TPU v7x, 256 devices: a whole 4x4x8 slice. The times are simulated.
256 devices in a mesh: ctx: 32 (over z, y), tp: 8 (over x, core).
Axes of the slice: x: 4, y: 4, z: 8, core: 2. Of those that a mesh axis runs over, the one named last changes fastest.
Arguments:
- queries: bfloat16 [4096, 5120], P('ctx', 'tp'), may hold values from -40 to 40
- keys: bfloat16 [4096, 1024], P('ctx', 'tp'), may hold values from -40 to 40
- values: bfloat16 [4096, 1024], P('ctx', 'tp'), may hold values from -6 to 6
- out_grad: bfloat16 [4096, 5120], P('ctx', 'tp'), may hold values from -6 to 6
- ancestry: int32 [32, 17], replicated, may hold values from 0 to 31, as said below
- w_query: bfloat16 [5120, 5120], P(None, 'tp'), may hold values from -0.078125 to 0.078125
- key_matrix: bfloat16 [5120, 1024], P(None, 'tp'), may hold values from -0.078125 to 0.078125
- value_matrix: bfloat16 [5120, 1024], P(None, 'tp'), may hold values from -0.078125 to 0.078125
Outputs:
- input_grad: bfloat16 [4096, 5120], P('ctx', 'tp')
Inputs may be any that keep to these rules, and one draw needn't show every extreme that they name: `ancestry`: row b holds b, then its ancestors in order parent, grandparent and so on (each an earlier block), then b again to fill the row. Blocks 0 to 16 form one chain, each the parent of the next; no block has more than 16 ancestors; every block descends from blocks 0 to 3 or is one of them.
All inputs are finite; a program needn't handle non-finite values.
Results may differ from a plain program's by a relative error of at most 0.024.
Values may be sent and summed in bfloat16 or wider, within the bound.
No kernel may reach another device: no remote copies, remote signals or barrier semaphores. Data moves between devices by JAX's collectives and lax.ppermute only.
A program may use at most 128 MiB of HBM per device.

v0:
```python
import math

import jax
import jax.numpy as jnp
from jax import lax
from jax.sharding import PartitionSpec as P

HEAD_SIZE = 128
TREE_BLOCK_SIZE = 128


ROPE_BASE = 1000000.0
MASKED = -1e30


def inverse_rotary(grads, token_places):
    half_width = grads.shape[-1] // 2
    frequencies = jnp.exp(
        jnp.arange(half_width, dtype=jnp.float32) * (-2.0 * math.log(ROPE_BASE) / grads.shape[-1])
    )
    angles = token_places[:, None] * frequencies[None, :]
    cosine = jnp.cos(angles)[:, None, :]
    sine_part = jnp.sin(angles)[:, None, :]
    front_half = grads[..., :half_width]
    second = grads[..., half_width:]
    return jnp.concatenate(
        [front_half * cosine + second * sine_part, second * cosine - front_half * sine_part],
        axis=-1,
    )


def to_rows(matrix, kv_local):
    row_count = matrix.shape[0]
    heads_per_group = matrix.shape[1] // HEAD_SIZE // kv_local
    return (
        matrix.reshape(row_count, kv_local, heads_per_group, HEAD_SIZE)
        .transpose(1, 2, 0, 3)
        .reshape(kv_local, heads_per_group * row_count, HEAD_SIZE)
    )


def spread_mask(seen_mask, kv_local, heads_per_group):
    reshaped_tensor = jnp.broadcast_to(
        seen_mask[None, None], (kv_local, heads_per_group) + seen_mask.shape
    )
    return reshaped_tensor.reshape(
        kv_local, heads_per_group * seen_mask.shape[0], seen_mask.shape[1]
    )


def visible_mask(ancestry, query_tok, key_tok):
    query_blk = query_tok // TREE_BLOCK_SIZE
    key_blk = key_tok // TREE_BLOCK_SIZE
    every_block = jnp.arange(ancestry.shape[0], dtype=jnp.int32)
    listed = jnp.any(ancestry[:, :, None] == key_blk[None, None, :], axis=1).astype(jnp.float32)
    picker = (query_blk[:, None] == every_block[None, :]).astype(jnp.float32)
    hit_rows = jnp.dot(picker, listed) > 0.5
    causal = (query_blk[:, None] != key_blk[None, :]) | (key_tok[None, :] <= query_tok[:, None])
    return hit_rows & causal


def local_fold(step_fn, initial, keys_all, values_all):
    all_tokens = keys_all.shape[0]
    span_rows = min(all_tokens, 4 * TREE_BLOCK_SIZE)

    def turn(turn_id, current):
        offset = turn_id * span_rows
        portion = (
            lax.dynamic_slice_in_dim(keys_all, offset, span_rows, 0),
            lax.dynamic_slice_in_dim(values_all, offset, span_rows, 0),
        )
        return step_fn(current, portion, offset)

    return lax.fori_loop(0, all_tokens // span_rows, turn, initial)


def shards(queries, keys, values, out_grad, ancestry, w_query, key_matrix, value_matrix):
    tok_local = queries.shape[0]
    kv_local = keys.shape[1] // HEAD_SIZE
    heads_local = queries.shape[1] // HEAD_SIZE
    heads_per_group = heads_local // kv_local
    factor = HEAD_SIZE ** (-0.5)
    all_tokens = tok_local * lax.axis_size("ctx")
    my_start = lax.axis_index("ctx") * tok_local
    own_tok = my_start + jnp.arange(tok_local, dtype=jnp.int32)
    every_block = jnp.arange(ancestry.shape[0], dtype=jnp.int32)
    depths = jnp.sum((ancestry != every_block[:, None]).astype(jnp.int32), axis=1)
    own_block = own_tok // TREE_BLOCK_SIZE
    own_depth = jnp.sum(
        jnp.where(own_block[:, None] == every_block[None, :], depths[None, :], 0), axis=1
    )
    token_places = (TREE_BLOCK_SIZE * own_depth + own_tok % TREE_BLOCK_SIZE).astype(jnp.float32)
    query_rows = to_rows(queries, kv_local)
    grad_rows = to_rows(out_grad, kv_local)
    row_count = heads_per_group * tok_local

    def forward_step(carry_state, portion, offset):
        keys_part, values_part = portion
        count_rows = keys_part.shape[0]
        key_tok = offset + jnp.arange(count_rows, dtype=jnp.int32)
        seen_mask = visible_mask(ancestry, own_tok, key_tok)

        def forward_update(current):
            maxima, totals, running = current
            heads_of_key = keys_part.reshape(count_rows, kv_local, HEAD_SIZE)
            heads_of_value = values_part.reshape(count_rows, kv_local, HEAD_SIZE)
            seen_rows = spread_mask(seen_mask, kv_local, heads_per_group)
            scores = (
                jnp.einsum(
                    "hrd,nhd->hrn", query_rows, heads_of_key, preferred_element_type=jnp.float32
                )
                * factor
            )
            scores = jnp.where(seen_rows, scores, MASKED)
            highest = jnp.maximum(maxima, jnp.max(scores, axis=-1))
            weights = jnp.where(seen_rows, jnp.exp(scores - highest[:, :, None]), 0.0)
            shrink = jnp.exp(maxima - highest)
            totals = totals * shrink + jnp.sum(weights, axis=-1)
            running = running * shrink[:, :, None] + jnp.einsum(
                "hrn,nhd->hrd",
                weights.astype(jnp.bfloat16),
                heads_of_value,
                preferred_element_type=jnp.float32,
            )
            return (highest, totals, running)

        return lax.cond(jnp.any(seen_mask), forward_update, lambda current: current, carry_state)

    start_state = (
        jnp.full((kv_local, row_count), MASKED, jnp.float32),
        jnp.zeros((kv_local, row_count), jnp.float32),
        jnp.zeros((kv_local, row_count, HEAD_SIZE), jnp.float32),
    )
    keys_all, values_all = (
        lax.all_gather(keys, "ctx", axis=0, tiled=True),
        lax.all_gather(values, "ctx", axis=0, tiled=True),
    )
    maxima, totals, running = local_fold(forward_step, start_state, keys_all, values_all)
    attended = (running / totals[:, :, None]).astype(jnp.bfloat16)
    log_totals = maxima + jnp.log(totals)
    row_dots = jnp.sum(grad_rows.astype(jnp.float32) * attended.astype(jnp.float32), axis=-1)
    pair_width = 2 * kv_local * HEAD_SIZE

    def backward_step(carry_state, portion, offset):
        keys_part, values_part = portion
        count_rows = keys_part.shape[0]
        key_tok = offset + jnp.arange(count_rows, dtype=jnp.int32)
        seen_mask = visible_mask(ancestry, own_tok, key_tok)

        def backward_update(current):
            heads_of_key = keys_part.reshape(count_rows, kv_local, HEAD_SIZE)
            heads_of_value = values_part.reshape(count_rows, kv_local, HEAD_SIZE)
            seen_rows = spread_mask(seen_mask, kv_local, heads_per_group)
            scores = (
                jnp.einsum(
                    "hrd,nhd->hrn", query_rows, heads_of_key, preferred_element_type=jnp.float32
                )
                * factor
            )
            weights = jnp.where(seen_rows, jnp.exp(scores - log_totals[:, :, None]), 0.0)
            prob_grads = jnp.einsum(
                "hrd,nhd->hrn", grad_rows, heads_of_value, preferred_element_type=jnp.float32
            )
            score_grads = (weights * (prob_grads - row_dots[:, :, None])).astype(jnp.bfloat16)
            query_grad = (
                current[0]
                + jnp.einsum(
                    "hrn,nhd->hrd", score_grads, heads_of_key, preferred_element_type=jnp.float32
                )
                * factor
            )
            key_grad = (
                jnp.einsum(
                    "hrn,hrd->nhd", score_grads, query_rows, preferred_element_type=jnp.float32
                )
                * factor
            )
            value_grad = jnp.einsum(
                "hrn,hrd->nhd",
                weights.astype(jnp.bfloat16),
                grad_rows,
                preferred_element_type=jnp.float32,
            )
            stacked = jnp.concatenate(
                [
                    key_grad.reshape(count_rows, kv_local * HEAD_SIZE),
                    value_grad.reshape(count_rows, kv_local * HEAD_SIZE),
                ],
                axis=1,
            )
            return (query_grad, lax.dynamic_update_slice_in_dim(current[1], stacked, offset, 0))

        return lax.cond(jnp.any(seen_mask), backward_update, lambda current: current, carry_state)

    back_state = (jnp.zeros((kv_local, row_count, HEAD_SIZE), jnp.float32),) + (
        jnp.zeros((all_tokens, pair_width), jnp.float32),
    )
    finished = local_fold(backward_step, back_state, keys_all, values_all)
    summed = lax.psum_scatter(
        finished[1].astype(jnp.bfloat16), "ctx", scatter_dimension=0, tiled=True
    ).astype(jnp.float32)
    key_own = summed[:, : kv_local * HEAD_SIZE].reshape(tok_local, kv_local, HEAD_SIZE)
    value_own = summed[:, kv_local * HEAD_SIZE :]
    query_total = (
        finished[0]
        .reshape(kv_local, heads_per_group, tok_local, HEAD_SIZE)
        .transpose(2, 0, 1, 3)
        .reshape(tok_local, heads_local, HEAD_SIZE)
    )
    query_low = (
        inverse_rotary(query_total, token_places)
        .astype(jnp.bfloat16)
        .reshape(tok_local, heads_local * HEAD_SIZE)
    )
    key_reduced = (
        inverse_rotary(key_own, token_places)
        .astype(jnp.bfloat16)
        .reshape(tok_local, kv_local * HEAD_SIZE)
    )
    value_reduced = value_own.astype(jnp.bfloat16)
    contract = (((1,), (1,)), ((), ()))
    partial_sum = lax.dot_general(query_low, w_query, contract, preferred_element_type=jnp.float32)
    partial_sum = partial_sum + lax.dot_general(
        key_reduced, key_matrix, contract, preferred_element_type=jnp.float32
    )
    partial_sum = partial_sum + lax.dot_general(
        value_reduced, value_matrix, contract, preferred_element_type=jnp.float32
    )
    return lax.psum_scatter(partial_sum.astype(jnp.bfloat16), "tp", scatter_dimension=1, tiled=True)


def solution(mesh):
    in_specs = (
        P("ctx", "tp"),
        P("ctx", "tp"),
        P("ctx", "tp"),
        P("ctx", "tp"),
        P(),
        P(None, "tp"),
        P(None, "tp"),
        P(None, "tp"),
    )
    out_specs = P("ctx", "tp")
    return jax.shard_map(shards, mesh=mesh, in_specs=in_specs, out_specs=out_specs, check_vma=False)
```

profile of v0, /device:TPU:1, one launch (start us, length us, event | category | flops | bytes accessed | tf_op | source)
XLA Modules:
  0.0 521.0 jit_solution(15357045312011004058)
XLA Ops:
  8.1 1.1 copy.45
  9.3 1.1 copy.47
  10.6 75.0 %all-gather.3.cloned.1.call-done = bf16[4096,128]{1,0:T(8,128)(2,1)} async-done(((bf16[128,128]{1,0:T(8,128)(2,1)}), bf16[4096,128]{1,0:T(8,128)(2,1)}) %all-gather.3.cloned.1.call-update) | async-done | bytes 1048592 | tf_op jit(solution)/shard_map/all_gather | solution.py:135
  85.6 76.5 %all-gather.5.cloned.1.call-done = bf16[4096,128]{1,0:T(8,128)(2,1)} async-done(((bf16[128,128]{1,0:T(8,128)(2,1)}), bf16[4096,128]{1,0:T(8,128)(2,1)}) %all-gather.5.cloned.1.call-update) | async-done | bytes 1048592 | tf_op jit(solution)/shard_map/all_gather | solution.py:136
  162.1 17.5 %while.42 = (s32[]{:T(128)}, f32[1,640]{1,0:T(1,128)S(1)}, f32[1,640]{1,0:T(1,128)S(1)}, f32[1,640,128]{2,1,0:T(8,128)S(1)}, s32[32,17]{0,1:T(8,128)S(1)}, /*ind...) while((s32[]{:T(128)}, f32[1,640]{1,0:T(1,128)S(1)}, ...), condition=%wide.region_7.8_spmd.clone.clone, body=%wide.region_0.7_spmd.clone.clone.sunk | while | flops 176029696 | bytes 7201713 | solution.py:74
  163.8 3.7 conditional.8
  164.3 1.3 fusion.79
  166.0 1.5 fusion.14
  180.7 1.6 broadcast_in_dim.108
  182.3 21.6 %while.43 = (s32[]{:T(128)}, f32[1,640,128]{2,1,0:T(8,128)}, bf16[4096,256]{0,1:T(8,128)(2,1)}, s32[32,17]{0,1:T(8,128)S(1)}, bf16[4096,128]{1,0:T(8,128)(2,1)},...) while((s32[]{:T(128)}, f32[1,640,128]{2,1,0:T(8,128)}, ...), condition=%wide.region_14.15_spmd.clone.clone, body=%wide.region_9.14_spmd.clone.clone.sunk | while | flops 427686016 | bytes 9893329 | solution.py:74
  182.5 0.9 fusion.102
  184.1 6.9 %conditional.9 = ((f32[1,640,128]{2,1,0:T(8,128)}, bf16[4096,256]{0,1:T(8,128)(2,1)})) conditional(s32[]{:T(128)} %convert_element_type.127, (f32[1,640,128]{2,1,0:T(8,128)}, bf16[4096,256]{0,1:T(8,128)(2,1)}) %tuple.160, (pred[128,512]{1,0:T(8,128)(4,1)S(1)}, s32[]{:T(128)}, bf16[4096,128]{1,0:T(8,128)(2,1)}, bf16[1,640,128]{2,1,0:T(8,128)(2,1)S(1)}, ...), branch_computations={%region_12.12_spmd, %region_13.13_spmd} | conditional | flops 422543360 | bytes 9780306 | solution.py:193
  184.6 1.4 fusion.38
  186.0 1.2 fusion.39
  187.3 2.1 fusion.41
  196.7 0.9 fusion.102
  203.9 4.1 copy.50
  208.5 1.2 add_convert_fusion
  210.0 6.6 %fusion.82 = f32[128,5120]{1,0:T(8,128)} fusion(bf16[128,640]{0,1:T(8,128)(2,1)S(1)} %bitcast.107, bf16[5120,640]{1,0:T(8,128)(2,1)} %param.21), kind=kOutput, calls=%fused_computation.140 | convolution fusion | flops 838860800 | bytes 9338880 | tf_op jit(solution)/shard_map/dot_general | solution.py:222
  216.6 254.6 %reduce-scatter.7.cloned.1.call-done = bf16[128,256]{1,0:T(8,128)(2,1)} async-done(((bf16[4096,256]{1,0:T(8,128)(2,1)}), bf16[128,256]{1,0:T(8,128)(2,1)}) %reduce-scatter.7.cloned.1.call-update) | async-done | bytes 65552
  472.4 2.4 convolution_add_fusion.1
  475.3 1.5 copy.52
  476.8 36.0 %reduce-scatter.9.cloned.1.call-done = bf16[640,128]{1,0:T(8,128)(2,1)} async-done(((bf16[5120,128]{1,0:T(8,128)(2,1)}), bf16[640,128]{1,0:T(8,128)(2,1)}) %reduce-scatter.9.cloned.1.call-update) | async-done | bytes 163856
  512.8 1.7 copy.53
  (127 shorter events, 24.6 us)
Async XLA Ops:
  6.5 465.8 %copy-start = (bf16[5120,128]{1,0:T(8,128)(2,1)S(1)}, bf16[5120,128]{1,0:T(8,128)(2,1)}, u32[]{:S(2)}) copy-start(bf16[5120,128]{1,0:T(8,128)(2,1)} %param.22) | copy-start | bytes 3932164
  6.5 155.5 %copy-start.1 = (s32[32,17]{0,1:T(8,128)S(1)}, s32[32,17]{0,1:T(8,128)}, u32[]{:S(2)}) copy-start(s32[32,17]{0,1:T(8,128)} %param.20) | copy-start | bytes 6532
  6.5 79.1 %all-gather.3.cloned.1.call-start = ((), (), s32[]{:S(2)}) async-start(), calls=%async_computation.2 | async-start | bytes 1081344 | tf_op jit(solution)/shard_map/all_gather | solution.py:135
  7.3 154.8 %all-gather.5.cloned.1.call-start = ((), (), s32[]{:S(2)}) async-start(), calls=%async_computation.3 | async-start | bytes 1081344 | tf_op jit(solution)/shard_map/all_gather | solution.py:136
  8.0 463.3 %reduce-scatter.7.cloned.1.call-start = ((), (), s32[]{:S(2)}) async-start(), calls=%async_computation.4 | async-start | bytes 2162688
  208.0 304.8 %reduce-scatter.9.cloned.1.call-start = ((), (), s32[]{:S(2)}) async-start(), calls=%async_computation.5 | async-start | bytes 1474560
  472.4 2.4 copy-start.2
  472.4 2.4 copy-start.3
Sparse Core Ops, SparseCore 0:
  9.9 75.6 all-gather.2
  88.2 73.8 all-gather.4
  208.1 263.1 reduce-scatter.6
  476.9 35.8 reduce-scatter.8
where the time goes:
time: 524 us; the launch traced here: 521 us
  waiting for transfers between devices  444 us (85%)
  matrix products  32.1 us (6%)
  local copies, waits for them, and re-layouts  14.2 us (3%)
  between operations  13.3 us (3%)
  loops' own time  10.7 us (2%)
  other arithmetic  7.16 us (1%)
    unnamed x6, waiting for transfers between devices  292 us
    all_gather x1, waiting for transfers between devices, shards(): lax.all_gather(values, 'ctx', axis=0, tiled=True)  76.5 us
    all_gather x1, waiting for transfers between devices, shards(): lax.all_gather(keys, 'ctx', axis=0, tiled=True)  75 us
    dot_general x16, matrix products, visible_mask(): hit_rows = jnp.dot(picker, listed) > 0.5  14.3 us
  transfers between devices with their start and end apart: 4, of which 4 were waited for; matrix products, arithmetic and copies ran while one was open for 2% of the time, Pallas kernels for 0%

commit v1 on v0

v1 whole, which is shorter than its diff:
```python
import math

import jax
import jax.numpy as jnp
from jax import lax
from jax.experimental import pallas as pl
from jax.experimental.pallas import tpu as pltpu
from jax.sharding import Mesh, PartitionSpec as P

HEAD = 128
BLOCK = 128
GROUP = 5
ROWS = GROUP * BLOCK
NZ, NY, NX, NC = 8, 4, 4, 2
ANC = 17
ROPE_BASE = 1000000.0
MASKED = -1e30
FACTOR = HEAD ** -0.5
NT = (((1,), (1,)), ((), ()))
NN = (((1,), (0,)), ((), ()))
VMEM_LIMIT = 48 << 20


def dot_nt(a, b):
    return lax.dot_general(a, b, NT, preferred_element_type=jnp.float32)


def dot_nn(a, b):
    return lax.dot_general(a, b, NN, preferred_element_type=jnp.float32)


def build_items(place_ref, anc_ref, list_ref, item_ref):
    z = place_ref[0]
    y = place_ref[1]
    base = jnp.int32(0)
    for j in range(NY):
        query_block = NY * z + (y - j) % NY
        bits = jnp.int32(0)
        for i in range(ANC):
            key_block = anc_ref[query_block, i]
            bits = bits | jnp.where(key_block % NY == y, jnp.int32(1) << (key_block // NY), 0)
        count = jnp.int32(0)
        for key_z in range(NZ):
            list_ref[count] = key_z
            count = count + ((bits >> key_z) & 1)
        for p in range(NZ // 2):
            first = jnp.where(2 * p < count, list_ref[2 * p], 0)
            both = 2 * p + 1 < count
            second = jnp.where(both, list_ref[2 * p + 1], first)
            item_ref[base + p, 0] = j
            item_ref[base + p, 1] = first
            item_ref[base + p, 2] = second
            if j == 0:
                item_ref[base + p, 3] = jnp.where(first == z, 1, 0)
                item_ref[base + p, 4] = jnp.where(both, jnp.where(second == z, 1, 0), 2)
            else:
                item_ref[base + p, 3] = 0
                item_ref[base + p, 4] = jnp.where(both, 0, 2)
        base = base + (count + 1) // 2
    return base


def stack_heads(groups, q_rows, g_rows):
    for j in range(NY):
        for h in range(GROUP):
            q_rows[j, h * BLOCK:(h + 1) * BLOCK, :] = groups[j][:, h * HEAD:(h + 1) * HEAD]
            g_rows[j, h * BLOCK:(h + 1) * BLOCK, :] = groups[j][:, ROWS + h * HEAD:ROWS + (h + 1) * HEAD]


def fill_bias(bias):
    key_row = lax.broadcasted_iota(jnp.int32, (BLOCK, ROWS), 0)
    query_row = lax.broadcasted_iota(jnp.int32, (BLOCK, ROWS), 1) % BLOCK
    bias[0] = jnp.zeros((BLOCK, ROWS), jnp.float32)
    bias[1] = jnp.where(key_row <= query_row, 0.0, MASKED)
    bias[2] = jnp.full((BLOCK, ROWS), MASKED, jnp.float32)


def load_item(p, item_ref, kv_ref, bias):
    j = item_ref[p, 0]
    first = item_ref[p, 1]
    second = item_ref[p, 2]
    kv = jnp.concatenate([kv_ref[first], kv_ref[second]], axis=0)
    both_bias = jnp.concatenate([bias[item_ref[p, 3]], bias[item_ref[p, 4]]], axis=0)
    return j, first, second, kv[:, :HEAD], kv[:, HEAD:], both_bias


def stats_kernel(place_ref, anc_ref, kv_ref, g0, g1, g2, g3, stat_ref, q_rows, g_rows, bias, list_ref, item_ref):
    stack_heads((g0, g1, g2, g3), q_rows, g_rows)
    fill_bias(bias)
    items = build_items(place_ref, anc_ref, list_ref, item_ref)
    for j in range(NY):
        stat_ref[j, 0:1, :] = jnp.full((1, ROWS), MASKED, jnp.float32)
        stat_ref[j, 1:4, :] = jnp.zeros((3, ROWS), jnp.float32)

    def step(p, carry):
        j, first, second, key_pair, value_pair, both_bias = load_item(p, item_ref, kv_ref, bias)
        scores = dot_nt(key_pair, q_rows[j]) * FACTOR + both_bias
        prob_grads = dot_nt(value_pair, g_rows[j])
        old = stat_ref[j, 0:1, :]
        highest = jnp.maximum(old, jnp.max(scores, axis=0, keepdims=True))
        weights = jnp.exp(scores - highest)
        shrink = jnp.exp(old - highest)
        stat_ref[j, 0:1, :] = highest
        stat_ref[j, 1:2, :] = stat_ref[j, 1:2, :] * shrink + jnp.sum(weights, axis=0, keepdims=True)
        stat_ref[j, 2:3, :] = stat_ref[j, 2:3, :] * shrink + jnp.sum(weights * prob_grads, axis=0, keepdims=True)
        return carry

    lax.fori_loop(0, items, step, 0)


def grads_kernel(place_ref, anc_ref, kv_ref, g0, g1, g2, g3, s0, s1, s2, s3,
                 dkv_ref, dq0, dq1, dq2, dq3,
                 q_rows, g_rows, bias, key_cols, rows, dk_acc, dv_acc, dq_acc, list_ref, item_ref):
    stack_heads((g0, g1, g2, g3), q_rows, g_rows)
    fill_bias(bias)
    items = build_items(place_ref, anc_ref, list_ref, item_ref)
    for a in range(NZ):
        key_cols[a] = kv_ref[a][:, :HEAD].T
    stats = (s0, s1, s2, s3)
    for j in range(NY):
        views = [stats[k][(j - k) % NY] for k in range(NY)]
        maxima = views[0][0:1]
        for k in range(1, NY):
            maxima = jnp.maximum(maxima, views[k][0:1])
        totals = jnp.zeros((1, ROWS), jnp.float32)
        dots = jnp.zeros((1, ROWS), jnp.float32)
        for k in range(NY):
            shrink = jnp.exp(views[k][0:1] - maxima)
            totals = totals + views[k][1:2] * shrink
            dots = dots + views[k][2:3] * shrink
        rows[j, 0:1, :] = maxima + jnp.log(totals)
        rows[j, 1:2, :] = dots / totals
    dk_acc[...] = jnp.zeros_like(dk_acc)
    dv_acc[...] = jnp.zeros_like(dv_acc)
    dq_acc[...] = jnp.zeros_like(dq_acc)

    def step(p, carry):
        j, first, second, key_pair, value_pair, both_bias = load_item(p, item_ref, kv_ref, bias)
        scores = dot_nt(key_pair, q_rows[j]) * FACTOR + both_bias
        prob_grads = dot_nt(value_pair, g_rows[j])
        probs = jnp.exp(scores - rows[j, 0:1, :])
        score_grads = (probs * (prob_grads - rows[j, 1:2, :])).astype(jnp.bfloat16)
        probs_low = probs.astype(jnp.bfloat16)
        dk_pair = dot_nn(score_grads, q_rows[j])
        dv_pair = dot_nn(probs_low, g_rows[j])
        dk_acc[first] += dk_pair[:BLOCK]
        dk_acc[second] += dk_pair[BLOCK:]
        dv_acc[first] += dv_pair[:BLOCK]
        dv_acc[second] += dv_pair[BLOCK:]
        cols = jnp.concatenate([key_cols[first], key_cols[second]], axis=1)
        dq_acc[j] += dot_nn(cols, score_grads)
        return carry

    lax.fori_loop(0, items, step, 0)
    for a in range(NZ):
        dkv_ref[a, :, :HEAD] = (dk_acc[a] * FACTOR).astype(jnp.bfloat16)
        dkv_ref[a, :, HEAD:] = dv_acc[a].astype(jnp.bfloat16)
    for j, out in enumerate((dq0, dq1, dq2, dq3)):
        for h in range(GROUP):
            part = dq_acc[j, :, h * BLOCK:(h + 1) * BLOCK].T * FACTOR
            out[:, h * HEAD:(h + 1) * HEAD] = part.astype(jnp.bfloat16)


def unrotate(x, cosine, sine):
    return x * cosine + pltpu.roll(x, HEAD // 2, 1) * sine


def first_half_kernel(place_ref, cos_ref, sin_ref, q0, q1, q2, q3, dkv_ref, wq, wk, wv, out_ref, low_ref):
    @pl.when(pl.program_id(0) == 0)
    def _():
        cosine = cos_ref[...]
        sine = sin_ref[...]
        for h in range(GROUP):
            cols = slice(h * HEAD, (h + 1) * HEAD)
            total = q0[:, cols].astype(jnp.float32)
            for part in (q1, q2, q3):
                total = total + part[:, cols].astype(jnp.float32)
            low_ref[:, cols] = unrotate(total, cosine, sine).astype(jnp.bfloat16)
        total = dkv_ref[0].astype(jnp.float32)
        for a in range(1, NZ):
            total = total + dkv_ref[a].astype(jnp.float32)
        low_ref[:, ROWS:ROWS + HEAD] = unrotate(total[:, :HEAD], cosine, sine).astype(jnp.bfloat16)
        low_ref[:, ROWS + HEAD:] = total[:, HEAD:].astype(jnp.bfloat16)

    out_ref[0] = project(low_ref, wq, wk, wv).astype(out_ref.dtype)


def second_half_kernel(place_ref, low_ref, wq, wk, wv, out_ref):
    out_ref[0] = project(low_ref, wq, wk, wv).astype(out_ref.dtype)


def project(low_ref, wq, wk, wv):
    total = dot_nt(low_ref[:, :ROWS], wq[...])
    total = total + dot_nt(low_ref[:, ROWS:ROWS + HEAD], wk[...])
    return total + dot_nt(low_ref[:, ROWS + HEAD:], wv[...])


def whole(shape):
    return pl.BlockSpec(shape, lambda *_: (0,) * len(shape))


def weight_specs(flip):
    def pick(i, place):
        core = 1 - place[3] if flip else place[3]
        return (2 * ((place[2] + i) % NX) + core, 0)

    return [pl.BlockSpec((ROWS, ROWS), pick), pl.BlockSpec((ROWS, HEAD), pick), pl.BlockSpec((ROWS, HEAD), pick)]


def shift(size, k):
    return [(i, (i + k) % size) for i in range(size)]


def shards(queries, keys, values, out_grad, ancestry, w_query, key_matrix, value_matrix):
    f32, bf16, i32 = jnp.float32, jnp.bfloat16, jnp.int32
    z, y, x, c = (lax.axis_index(name) for name in "zyxc")
    place = jnp.stack([z, y, x, c]).astype(i32)
    group = jnp.concatenate([queries, out_grad], axis=1)
    groups = [group] + [lax.ppermute(group, "y", shift(NY, k)) for k in range(1, NY)]
    kv = jnp.concatenate([keys, values], axis=1)
    kv_all = lax.all_to_all(jnp.broadcast_to(kv[None], (NZ,) + kv.shape), "z", 0, 0, tiled=True)

    own_block = NY * z + y
    own_row = lax.dynamic_slice_in_dim(ancestry, own_block, 1, 0)
    depth = jnp.sum((own_row != own_block).astype(i32))
    token_places = (BLOCK * depth + jnp.arange(BLOCK, dtype=i32)).astype(f32)
    frequencies = jnp.exp(jnp.arange(HEAD // 2, dtype=f32) * (-2.0 * math.log(ROPE_BASE) / HEAD))
    angles = token_places[:, None] * frequencies[None, :]
    cosine = jnp.cos(angles)
    sine = jnp.sin(angles)
    cosine = jnp.concatenate([cosine, cosine], axis=1)
    sine = jnp.concatenate([sine, -sine], axis=1)

    params = pltpu.CompilerParams(vmem_limit_bytes=VMEM_LIMIT)
    common = [
        pltpu.VMEM((NY, ROWS, HEAD), bf16),
        pltpu.VMEM((NY, ROWS, HEAD), bf16),
        pltpu.VMEM((3, BLOCK, ROWS), f32),
    ]
    lists = [pltpu.SMEM((NZ + 1,), i32), pltpu.SMEM((5 * NZ // 2, 5), i32)]
    in_shapes = [kv_all.shape] + [group.shape] * NY
    stats = pl.pallas_call(
        stats_kernel,
        out_shape=jax.ShapeDtypeStruct((NY, 4, ROWS), f32),
        grid_spec=pltpu.PrefetchScalarGridSpec(
            num_scalar_prefetch=2,
            grid=(1,),
            in_specs=[whole(s) for s in in_shapes],
            out_specs=whole((NY, 4, ROWS)),
            scratch_shapes=common + lists,
        ),
        compiler_params=params,
        name="stats",
    )(place, ancestry, kv_all, *groups)
    all_stats = [stats] + [lax.ppermute(stats, "y", shift(NY, k)) for k in range(1, NY)]
    dkv, *dq_parts = pl.pallas_call(
        grads_kernel,
        out_shape=[jax.ShapeDtypeStruct((NZ, BLOCK, 2 * HEAD), bf16)]
        + [jax.ShapeDtypeStruct((BLOCK, ROWS), bf16)] * NY,
        grid_spec=pltpu.PrefetchScalarGridSpec(
            num_scalar_prefetch=2,
            grid=(1,),
            in_specs=[whole(s) for s in in_shapes + [stats.shape] * NY],
            out_specs=[whole((NZ, BLOCK, 2 * HEAD))] + [whole((BLOCK, ROWS))] * NY,
            scratch_shapes=common
            + [
                pltpu.VMEM((NZ, HEAD, BLOCK), bf16),
                pltpu.VMEM((NY, 2, ROWS), f32),
                pltpu.VMEM((NZ, BLOCK, HEAD), f32),
                pltpu.VMEM((NZ, BLOCK, HEAD), f32),
                pltpu.VMEM((NY, HEAD, ROWS), f32),
            ]
            + lists,
        ),
        compiler_params=params,
        name="grads",
    )(place, ancestry, kv_all, *groups, *all_stats)
    dq_own = [dq_parts[0]] + [lax.ppermute(dq_parts[k], "y", shift(NY, -k)) for k in range(1, NY)]
    dkv_own = lax.all_to_all(dkv, "z", 0, 0, tiled=True)

    out_block = pl.BlockSpec((1, BLOCK, ROWS), lambda i, place: (i, 0, 0))
    low_shape = (BLOCK, ROWS + 2 * HEAD)
    away, low = pl.pallas_call(
        first_half_kernel,
        out_shape=[jax.ShapeDtypeStruct((NX, BLOCK, ROWS), bf16), jax.ShapeDtypeStruct(low_shape, bf16)],
        grid_spec=pltpu.PrefetchScalarGridSpec(
            num_scalar_prefetch=1,
            grid=(NX,),
            in_specs=[whole((BLOCK, HEAD))] * 2
            + [whole((BLOCK, ROWS))] * NY
            + [whole(dkv_own.shape)]
            + weight_specs(True),
            out_specs=[out_block, whole(low_shape)],
        ),
        compiler_params=params,
        name="first_half",
    )(place, cosine, sine, *dq_own, dkv_own, w_query, key_matrix, value_matrix)
    arrived = lax.ppermute(away, "c", shift(NC, 1))
    kept = pl.pallas_call(
        second_half_kernel,
        out_shape=jax.ShapeDtypeStruct((NX, BLOCK, ROWS), f32),
        grid_spec=pltpu.PrefetchScalarGridSpec(
            num_scalar_prefetch=1,
            grid=(NX,),
            in_specs=[whole(low_shape)] + weight_specs(False),
            out_specs=out_block,
        ),
        compiler_params=params,
        name="second_half",
    )(place, low, w_query, key_matrix, value_matrix)
    total = kept[0] + arrived[0].astype(f32)
    sent = [(kept[k] + arrived[k].astype(f32)).astype(bf16) for k in range(1, NX)]
    for k in range(1, NX):
        total = total + lax.ppermute(sent[k - 1], "x", shift(NX, k)).astype(f32)
    return total.astype(bf16)


def solution(mesh):
    grid = Mesh(mesh.devices.reshape(NZ, NY, NX, NC), ("z", "y", "x", "c"))
    split = P(("z", "y"), ("x", "c"))
    weight = P(None, ("x", "c"))
    return jax.shard_map(
        shards,
        mesh=grid,
        in_specs=(split, split, split, split, P(), weight, weight, weight),
        out_specs=split,
        check_vma=False,
    )
```

time: 524 us -> 102 us (0.19)
  waiting for transfers between devices: 444 us -> 31.2 us
  starting transfers between devices: 0.12 us -> 39.8 us
  matrix products: 32.1 us -> 0 us
  Pallas kernels: 0 us -> 17.2 us
  between operations: 13.3 us -> 0.82 us
  loops' own time: 10.7 us -> 0 us
  local copies, waits for them, and re-layouts: 14.2 us -> 8.5 us
    unnamed x6 -> x0, waiting for transfers between devices: 292 us -> none
    all_gather x2 -> x0, waiting for transfers between devices: 151 us -> none  [the longest x1 76.5 us: shards(): lax.all_gather(values, 'ctx', axis=0, tiled=True)]
    dot_general x26 -> x0, matrix products: 32.1 us -> none  [the longest x16 14.3 us: visible_mask(): hit_rows = jnp.dot(picker, listed) > 0.5]
    ppermute x0 -> x13, waiting for transfers between devices: none -> 26 us  [the longest x3 12.6 us: shards(): lax.ppermute(group, 'y', shift(NY, k))]
    all_to_all x0 -> x2, starting transfers between devices: none -> 20.7 us  [the longest x1 11.7 us: shards(): dkv_own = lax.all_to_all(dkv, 'z', 0, 0, tiled=True)]
    ppermute x0 -> x13, starting transfers between devices: none -> 19.1 us  [the longest x3 5.06 us: shards(): lax.ppermute(group, 'y', shift(NY, k))]
    pallas_call x0 -> x4, Pallas kernels: none -> 17.2 us  [the longest x1 4.77 us: shards(): pl.pallas_call(grads_kernel, out_shape=[jax.ShapeDtypeStruct((NZ, BLOCK,...]
    another operation x18 -> x0, loops' own time: 10.7 us -> none  [the longest x2 10.3 us: local_fold(): return lax.fori_loop(0, all_tokens // span_rows, turn, initial)]
  transfers between devices with their start and end apart: 4 -> 15, of which waited for: 4 -> 11; matrix products, arithmetic and copies ran while one was open for 2% -> 1% of each run, Pallas kernels for 0% -> 4%
where the time goes in v1:
time: 102 us; the launch traced here: 101 us
  starting transfers between devices  39.8 us (39%)
  waiting for transfers between devices  31.2 us (31%)
  Pallas kernels  17.2 us (17%)
  local copies, waits for them, and re-layouts  8.5 us (8%)
  other arithmetic  2.96 us (3%)
    ppermute x3, waiting for transfers between devices, shards(): lax.ppermute(group, 'y', shift(NY, k))  12.6 us
    all_to_all x1, starting transfers between devices, shards(): dkv_own = lax.all_to_all(dkv, 'z', 0, 0, tiled=True)  11.7 us
    all_to_all x1, starting transfers between devices, shards(): lax.all_to_all(jnp.broadcast_to(kv[None], (NZ,) + kv.shape), 'z', 0, 0, t...  9.01 us
    unnamed x32, local copies, waits for them, and re-layouts  7.64 us
    ppermute x3, waiting for transfers between devices, shards(): total = total + lax.ppermute(sent[k - 1], 'x', shift(NX, k)).astype(f32)  6.72 us
    all_to_all x1, waiting for transfers between devices, shards(): dkv_own = lax.all_to_all(dkv, 'z', 0, 0, tiled=True)  5.09 us
    ppermute x3, starting transfers between devices, shards(): lax.ppermute(group, 'y', shift(NY, k))  5.06 us
    ppermute x3, starting transfers between devices, shards(): total = total + lax.ppermute(sent[k - 1], 'x', shift(NX, k)).astype(f32)  4.89 us
  transfers between devices with their start and end apart: 15, of which 11 were waited for; matrix products, arithmetic and copies ran while one was open for 1% of the time, Pallas kernels for 4%

profile of v1, /device:TPU:1, one launch (start us, length us, event | category | flops | bytes accessed | tf_op | source)
XLA Modules:
  0.0 100.5 jit_solution(11464836922428612312)
XLA Ops:
  1.7 9.0 %all-to-all-start = ((bf16[8,128,256]{2,1,0:T(8,128)(2,1)}), bf16[8,128,256]{2,1,0:T(8,128)(2,1)S(1)}, u32[]{:S(2)}, u32[]{:S(2)}) async-start(bf16[8,128,256]{2,1,0:T(8,128)(2,1)} %broadcast_in_dim.2), calls=%async_computation | async-start | bytes 1048576 | tf_op jit(solution)/shard_map/all_to_all | solution.py:221
  10.8 1.4 %collective-permute-start = (bf16[128,1280]{1,0:T(8,128)(2,1)S(1)}, bf16[128,1280]{1,0:T(8,128)(2,1)S(1)}, u32[]{:S(2)}, u32[]{:S(2)}) collective-permute-start(bf16[128,1280]{1,0:T(8,128)(2,1)S(1)} %constant_dynamic-update-slice_fusion.g0), channel_id=1, source_target_pairs={{0,8},{8,16},{16,24},{24,0},{1,9},{9,17},{17,25},{25,1},{2,10},{10... | collective-permute-start | bytes 983048 | tf_op jit(solution)/shard_map/ppermute | solution.py:219
  12.1 2.6 %collective-permute-start.1 = (bf16[128,1280]{1,0:T(8,128)(2,1)S(1)}, bf16[128,1280]{1,0:T(8,128)(2,1)S(1)}, u32[]{:S(2)}, u32[]{:S(2)}) collective-permute-start(bf16[128,1280]{1,0:T(8,128)(2,1)S(1)} %constant_dynamic-update-slice_fusion.g0), channel_id=1, source_target_pairs={{0,16},{8,24},{16,0},{24,8},{1,17},{9,25},{17,1},{25,9},{2,18},{10... | collective-permute-start | bytes 983048 | tf_op jit(solution)/shard_map/ppermute | solution.py:219
  14.7 1.1 %collective-permute-start.2 = (bf16[128,1280]{1,0:T(8,128)(2,1)S(1)}, bf16[128,1280]{1,0:T(8,128)(2,1)S(1)}, u32[]{:S(2)}, u32[]{:S(2)}) collective-permute-start(bf16[128,1280]{1,0:T(8,128)(2,1)S(1)} %constant_dynamic-update-slice_fusion.g0), channel_id=1, source_target_pairs={{0,24},{8,0},{16,8},{24,16},{1,25},{9,1},{17,9},{25,17},{2,26},{10... | collective-permute-start | bytes 983048 | tf_op jit(solution)/shard_map/ppermute | solution.py:219
  16.0 4.5 %collective-permute-done.g1 = bf16[128,1280]{1,0:T(8,128)(2,1)S(1)} collective-permute-done((bf16[128,1280]{1,0:T(8,128)(2,1)S(1)}, bf16[128,1280]{1,0:T(8,128)(2,1)S(1)}, u32[]{:S(2)}, u32[]{:S(2)}) %collective-permute-start) | collective-permute-done | bytes 327712 | tf_op jit(solution)/shard_map/ppermute | solution.py:219
  20.4 8.1 %collective-permute-done.1.g2 = bf16[128,1280]{1,0:T(8,128)(2,1)S(1)} collective-permute-done((bf16[128,1280]{1,0:T(8,128)(2,1)S(1)}, bf16[128,1280]{1,0:T(8,128)(2,1)S(1)}, u32[]{:S(2)}, u32[]{:S(2)}) %collective-permute-start.1) | collective-permute-done | bytes 327712 | tf_op jit(solution)/shard_map/ppermute | solution.py:219
  28.6 3.3 %stats.1.s0 = f32[4,4,640]{2,1,0:T(4,128)S(1)} custom-call(s32[4]{0:T(128)S(1)} %pad_add_fusion.place_ref, s32[32,17]{1,0:T(8,128)S(1)} %copy.10.anc_ref, bf16[8,128,256]{2,1,0:T(8,128)(2,1)S(1)} %all-to-all-done.kv_ref, bf16[128,1280]{1,0:T(8,128)(2,1)S(1)} %constant_dynamic-update-slice_fusion.g0, bf16[128,1280]{1,0:T(8,128)(2,1)S(1)} %collective-permute-done.g1, ...), custom_call_target="tpu_custom_call" | custom-call | tf_op jit(solution)/shard_map/stats/pallas_call | solution.py:242
  32.0 1.2 %collective-permute-start.3 = (f32[4,4,640]{2,1,0:T(4,128)S(1)}, f32[4,4,640]{2,1,0:T(4,128)S(1)}, u32[]{:S(2)}, u32[]{:S(2)}) collective-permute-start(f32[4,4,640]{2,1,0:T(4,128)S(1)} %stats.1.s0), channel_id=1, source_target_pairs={{0,8},{8,16},{16,24},{24,0},{1,9},{9,17},{17,25},{25,1},{2,10},{10... | collective-permute-start | bytes 122888 | tf_op jit(solution)/shard_map/ppermute | solution.py:255
  33.2 2.0 %collective-permute-start.4 = (f32[4,4,640]{2,1,0:T(4,128)S(1)}, f32[4,4,640]{2,1,0:T(4,128)S(1)}, u32[]{:S(2)}, u32[]{:S(2)}) collective-permute-start(f32[4,4,640]{2,1,0:T(4,128)S(1)} %stats.1.s0), channel_id=1, source_target_pairs={{0,16},{8,24},{16,0},{24,8},{1,17},{9,25},{17,1},{25,9},{2,18},{10... | collective-permute-start | bytes 122888 | tf_op jit(solution)/shard_map/ppermute | solution.py:255
  36.2 1.7 %collective-permute-done.4.s2 = f32[4,4,640]{2,1,0:T(4,128)S(1)} collective-permute-done((f32[4,4,640]{2,1,0:T(4,128)S(1)}, f32[4,4,640]{2,1,0:T(4,128)S(1)}, u32[]{:S(2)}, u32[]{:S(2)}) %collective-permute-start.4) | collective-permute-done | bytes 40992 | tf_op jit(solution)/shard_map/ppermute | solution.py:255
  38.3 4.8 %grads.1 = (bf16[8,128,256]{2,1,0:T(8,128)(2,1)S(1)}, bf16[128,640]{1,0:T(8,128)(2,1)S(1)}, bf16[128,640]{1,0:T(8,128)(2,1)S(1)}, bf16[128,640]{1,0:T(8,128)(2,1)S(1)}, bf16[128,640]{1,0:T(8,128)(2,1)S(1)}) custom-call(s32[4]{0:T(128)S(1)} %pad_add_fusion.place_ref, s32[32,17]{1,0:T(8,128)S(1)} %copy.10.anc_ref, ...), custom_call_target="tpu_custom_call" | custom-call | tf_op jit(solution)/shard_map/grads/pallas_call | solution.py:256
  45.9 11.7 %all-to-all-start.1 = ((bf16[8,128,256]{2,1,0:T(8,128)(2,1)}), bf16[8,128,256]{2,1,0:T(8,128)(2,1)S(1)}, u32[]{:S(2)}, u32[]{:S(2)}) async-start(bf16[8,128,256]{2,1,0:T(8,128)(2,1)} %copy-done.2), calls=%async_computation.1 | async-start | bytes 1048576 | tf_op jit(solution)/shard_map/all_to_all | solution.py:279
  59.4 1.5 %collective-permute-start.7 = (bf16[128,640]{1,0:T(8,128)(2,1)}, bf16[128,640]{1,0:T(8,128)(2,1)S(1)}, u32[]{:S(2)}, u32[]{:S(2)}) collective-permute-start(bf16[128,640]{1,0:T(8,128)(2,1)} %copy-done.10), channel_id=1, source_target_pairs={{0,16},{8,24},{16,0},{24,8},{1,17},{9,25},{17,1},{25,9},{2,18},{10... | collective-permute-start | bytes 491528 | tf_op jit(solution)/shard_map/ppermute | solution.py:278
  61.4 2.4 %collective-permute-done.6.q1 = bf16[128,640]{1,0:T(8,128)(2,1)S(1)} collective-permute-done((bf16[128,640]{1,0:T(8,128)(2,1)}, bf16[128,640]{1,0:T(8,128)(2,1)S(1)}, u32[]{:S(2)}, u32[]{:S(2)}) %collective-permute-start.6) | collective-permute-done | bytes 163872 | tf_op jit(solution)/shard_map/ppermute | solution.py:278
  66.0 1.3 %collective-permute-done.8.q3 = bf16[128,640]{1,0:T(8,128)(2,1)S(1)} collective-permute-done((bf16[128,640]{1,0:T(8,128)(2,1)}, bf16[128,640]{1,0:T(8,128)(2,1)S(1)}, u32[]{:S(2)}, u32[]{:S(2)}) %collective-permute-start.8) | collective-permute-done | bytes 163872 | tf_op jit(solution)/shard_map/ppermute | solution.py:278
  68.0 5.1 %all-to-all-done.1.dkv_ref = bf16[8,128,256]{2,1,0:T(8,128)(2,1)S(1)} async-done(((bf16[8,128,256]{2,1,0:T(8,128)(2,1)}), bf16[8,128,256]{2,1,0:T(8,128)(2,1)S(1)}, u32[]{:S(2)}, u32[]{:S(2)}) %all-to-all-start.1) | async-done | bytes 524320 | tf_op jit(solution)/shard_map/all_to_all | solution.py:279
  75.9 4.7 %first_half.1 = (bf16[4,128,640]{2,1,0:T(8,128)(2,1)S(1)}, bf16[128,896]{1,0:T(8,128)(2,1)S(1)}) custom-call(s32[4]{0:T(128)S(1)} %pad_add_fusion.place_ref, f32[128,128]{1,0:T(8,128)S(1)} %get-tuple-element.25.cos_ref, f32[128,128]{1,0:T(8,128)S(1)} %get-tuple-element.26.sin_ref, bf16[128,640]{1,0:T(8,128)(2,1)S(1)} %get-tuple-element.12.q0, ...), custom_call_target="tpu_custom_call" | custom-call | tf_op jit(solution)/shard_map/first_half/pallas_call | solution.py:283
  80.6 3.0 %collective-permute-start.9 = (bf16[4,128,640]{2,1,0:T(8,128)(2,1)S(1)}, bf16[4,128,640]{2,1,0:T(8,128)(2,1)S(1)}, u32[]{:S(2)}, u32[]{:S(2)}) collective-permute-start(bf16[4,128,640]{2,1,0:T(8,128)(2,1)S(1)} %get-tuple-element.18), channel_id=1, source_target_pairs={{0,1},{1,0},{2,3},{3,2},{4,5},{5,4},{6,7},{7,6},{8,9},{9,8},{10,11... | collective-permute-start | bytes 1966088 | tf_op jit(solution)/shard_map/ppermute | solution.py:298
  83.6 4.4 %second_half.1 = f32[4,128,640]{2,1,0:T(8,128)S(1)} custom-call(s32[4]{0:T(128)S(1)} %pad_add_fusion.place_ref, bf16[128,896]{1,0:T(8,128)(2,1)S(1)} %get-tuple-element.17.low_ref, bf16[5120,640]{1,0:T(8,128)(2,1)} %wq.3, bf16[5120,128]{1,0:T(8,128)(2,1)S(1)} %copy-done, bf16[5120,128]{1,0:T(8,128)(2,1)S(1)} %copy-done.1), custom_call_target="tpu_custom_call" | custom-call | tf_op jit(solution)/shard_map/second_half/pallas_call | solution.py:299
  88.1 1.3 %collective-permute-start.10 = (bf16[128,640]{1,0:T(8,128)(2,1)S(1)}, bf16[128,640]{1,0:T(8,128)(2,1)S(1)}, u32[]{:S(2)}, u32[]{:S(2)}) collective-permute-start(bf16[128,640]{1,0:T(8,128)(2,1)S(1)} %get-tuple-element.19), channel_id=1, source_target_pairs={{0,2},{2,4},{4,6},{6,0},{1,3},{3,5},{5,7},{7,1},{8,10},{10,12},{12... | collective-permute-start | bytes 491528 | tf_op jit(solution)/shard_map/ppermute | solution.py:314
  89.4 2.5 %collective-permute-start.11 = (bf16[128,640]{1,0:T(8,128)(2,1)S(1)}, bf16[128,640]{1,0:T(8,128)(2,1)S(1)}, u32[]{:S(2)}, u32[]{:S(2)}) collective-permute-start(bf16[128,640]{1,0:T(8,128)(2,1)S(1)} %get-tuple-element.21), channel_id=1, source_target_pairs={{0,4},{2,6},{4,0},{6,2},{1,5},{3,7},{5,1},{7,3},{8,12},{10,14},{12... | collective-permute-start | bytes 491528 | tf_op jit(solution)/shard_map/ppermute | solution.py:314
  91.9 1.1 %collective-permute-start.12 = (bf16[128,640]{1,0:T(8,128)(2,1)S(1)}, bf16[128,640]{1,0:T(8,128)(2,1)S(1)}, u32[]{:S(2)}, u32[]{:S(2)}) collective-permute-start(bf16[128,640]{1,0:T(8,128)(2,1)S(1)} %get-tuple-element.20), channel_id=1, source_target_pairs={{0,6},{2,0},{4,2},{6,4},{1,7},{3,1},{5,3},{7,5},{8,14},{10,8},{12,... | collective-permute-start | bytes 491528 | tf_op jit(solution)/shard_map/ppermute | solution.py:314
  93.0 2.2 %collective-permute-done.10 = bf16[128,640]{1,0:T(8,128)(2,1)S(1)} collective-permute-done((bf16[128,640]{1,0:T(8,128)(2,1)S(1)}, bf16[128,640]{1,0:T(8,128)(2,1)S(1)}, u32[]{:S(2)}, u32[]{:S(2)}) %collective-permute-start.10) | collective-permute-done | bytes 163872 | tf_op jit(solution)/shard_map/ppermute | solution.py:314
  95.3 4.5 %collective-permute-done.11 = bf16[128,640]{1,0:T(8,128)(2,1)S(1)} collective-permute-done((bf16[128,640]{1,0:T(8,128)(2,1)S(1)}, bf16[128,640]{1,0:T(8,128)(2,1)S(1)}, u32[]{:S(2)}, u32[]{:S(2)}) %collective-permute-start.11) | collective-permute-done | bytes 163872 | tf_op jit(solution)/shard_map/ppermute | solution.py:314
  (53 shorter events, 14.2 us)
Async XLA Ops:
  0.0 10.7 %copy-start.12 = (bf16[128,640]{1,0:T(8,128)(2,1)S(1)}, bf16[128,640]{1,0:T(8,128)(2,1)}, u32[]{:S(2)}) copy-start(bf16[128,640]{1,0:T(8,128)(2,1)} %param.8) | copy-start | bytes 491524
  0.0 10.7 %copy-start.13 = (bf16[128,640]{1,0:T(8,128)(2,1)S(1)}, bf16[128,640]{1,0:T(8,128)(2,1)}, u32[]{:S(2)}) copy-start(bf16[128,640]{1,0:T(8,128)(2,1)} %param.11) | copy-start | bytes 491524
  0.0 15.8 %copy-start.14 = (s32[32,17]{0,1:T(8,128)S(1)}, s32[32,17]{0,1:T(8,128)}, u32[]{:S(2)}) copy-start(s32[32,17]{0,1:T(8,128)} %param.12) | copy-start | bytes 6532
  1.7 27.0 %all-to-all-start = ((bf16[8,128,256]{2,1,0:T(8,128)(2,1)}), bf16[8,128,256]{2,1,0:T(8,128)(2,1)S(1)}, u32[]{:S(2)}, u32[]{:S(2)}) async-start(bf16[8,128,256]{2,1,0:T(8,128)(2,1)} %broadcast_in_dim.2), calls=%async_computation | async-start | bytes 1048576 | tf_op jit(solution)/shard_map/all_to_all | solution.py:221
  10.8 9.7 %collective-permute-start = (bf16[128,1280]{1,0:T(8,128)(2,1)S(1)}, bf16[128,1280]{1,0:T(8,128)(2,1)S(1)}, u32[]{:S(2)}, u32[]{:S(2)}) collective-permute-start(bf16[128,1280]{1,0:T(8,128)(2,1)S(1)} %constant_dynamic-update-slice_fusion.g0), channel_id=1, source_target_pairs={{0,8},{8,16},{16,24},{24,0},{1,9},{9,17},{17,25},{25,1},{2,10},{10... | collective-permute-start | bytes 983048 | tf_op jit(solution)/shard_map/ppermute | solution.py:219
  12.1 16.4 %collective-permute-start.1 = (bf16[128,1280]{1,0:T(8,128)(2,1)S(1)}, bf16[128,1280]{1,0:T(8,128)(2,1)S(1)}, u32[]{:S(2)}, u32[]{:S(2)}) collective-permute-start(bf16[128,1280]{1,0:T(8,128)(2,1)S(1)} %constant_dynamic-update-slice_fusion.g0), channel_id=1, source_target_pairs={{0,16},{8,24},{16,0},{24,8},{1,17},{9,25},{17,1},{25,9},{2,18},{10... | collective-permute-start | bytes 983048 | tf_op jit(solution)/shard_map/ppermute | solution.py:219
  14.7 13.8 %collective-permute-start.2 = (bf16[128,1280]{1,0:T(8,128)(2,1)S(1)}, bf16[128,1280]{1,0:T(8,128)(2,1)S(1)}, u32[]{:S(2)}, u32[]{:S(2)}) collective-permute-start(bf16[128,1280]{1,0:T(8,128)(2,1)S(1)} %constant_dynamic-update-slice_fusion.g0), channel_id=1, source_target_pairs={{0,24},{8,0},{16,8},{24,16},{1,25},{9,1},{17,9},{25,17},{2,26},{10... | collective-permute-start | bytes 983048 | tf_op jit(solution)/shard_map/ppermute | solution.py:219
  32.0 4.2 %collective-permute-start.3 = (f32[4,4,640]{2,1,0:T(4,128)S(1)}, f32[4,4,640]{2,1,0:T(4,128)S(1)}, u32[]{:S(2)}, u32[]{:S(2)}) collective-permute-start(f32[4,4,640]{2,1,0:T(4,128)S(1)} %stats.1.s0), channel_id=1, source_target_pairs={{0,8},{8,16},{16,24},{24,0},{1,9},{9,17},{17,25},{25,1},{2,10},{10... | collective-permute-start | bytes 122888 | tf_op jit(solution)/shard_map/ppermute | solution.py:255
  33.2 4.8 %collective-permute-start.4 = (f32[4,4,640]{2,1,0:T(4,128)S(1)}, f32[4,4,640]{2,1,0:T(4,128)S(1)}, u32[]{:S(2)}, u32[]{:S(2)}) collective-permute-start(f32[4,4,640]{2,1,0:T(4,128)S(1)} %stats.1.s0), channel_id=1, source_target_pairs={{0,16},{8,24},{16,0},{24,8},{1,17},{9,25},{17,1},{25,9},{2,18},{10... | collective-permute-start | bytes 122888 | tf_op jit(solution)/shard_map/ppermute | solution.py:255
  35.2 3.1 %collective-permute-start.5 = (f32[4,4,640]{2,1,0:T(4,128)S(1)}, f32[4,4,640]{2,1,0:T(4,128)S(1)}, u32[]{:S(2)}, u32[]{:S(2)}) collective-permute-start(f32[4,4,640]{2,1,0:T(4,128)S(1)} %stats.1.s0), channel_id=1, source_target_pairs={{0,24},{8,0},{16,8},{24,16},{1,25},{9,1},{17,9},{25,17},{2,26},{10... | collective-permute-start | bytes 122888 | tf_op jit(solution)/shard_map/ppermute | solution.py:255
  38.3 34.8 %copy-start.1 = (bf16[5120,128]{1,0:T(8,128)(2,1)S(1)}, bf16[5120,128]{1,0:T(8,128)(2,1)}, u32[]{:S(2)}) copy-start(bf16[5120,128]{1,0:T(8,128)(2,1)} %wv.3) | copy-start | bytes 3932164
  43.1 0.8 copy-start.2
  45.9 27.3 %copy-start = (bf16[5120,128]{1,0:T(8,128)(2,1)S(1)}, bf16[5120,128]{1,0:T(8,128)(2,1)}, u32[]{:S(2)}) copy-start(bf16[5120,128]{1,0:T(8,128)(2,1)} %wk.3) | copy-start | bytes 3932164
  45.9 27.2 %all-to-all-start.1 = ((bf16[8,128,256]{2,1,0:T(8,128)(2,1)}), bf16[8,128,256]{2,1,0:T(8,128)(2,1)S(1)}, u32[]{:S(2)}, u32[]{:S(2)}) async-start(bf16[8,128,256]{2,1,0:T(8,128)(2,1)} %copy-done.2), calls=%async_computation.1 | async-start | bytes 1048576 | tf_op jit(solution)/shard_map/all_to_all | solution.py:279
  59.1 4.8 %collective-permute-start.6 = (bf16[128,640]{1,0:T(8,128)(2,1)}, bf16[128,640]{1,0:T(8,128)(2,1)S(1)}, u32[]{:S(2)}, u32[]{:S(2)}) collective-permute-start(bf16[128,640]{1,0:T(8,128)(2,1)} %copy-done.11), channel_id=1, source_target_pairs={{0,24},{8,0},{16,8},{24,16},{1,25},{9,1},{17,9},{25,17},{2,26},{10... | collective-permute-start | bytes 491528 | tf_op jit(solution)/shard_map/ppermute | solution.py:278
  59.4 5.9 %collective-permute-start.7 = (bf16[128,640]{1,0:T(8,128)(2,1)}, bf16[128,640]{1,0:T(8,128)(2,1)S(1)}, u32[]{:S(2)}, u32[]{:S(2)}) collective-permute-start(bf16[128,640]{1,0:T(8,128)(2,1)} %copy-done.10), channel_id=1, source_target_pairs={{0,16},{8,24},{16,0},{24,8},{1,17},{9,25},{17,1},{25,9},{2,18},{10... | collective-permute-start | bytes 491528 | tf_op jit(solution)/shard_map/ppermute | solution.py:278
  61.0 6.4 %collective-permute-start.8 = (bf16[128,640]{1,0:T(8,128)(2,1)}, bf16[128,640]{1,0:T(8,128)(2,1)S(1)}, u32[]{:S(2)}, u32[]{:S(2)}) collective-permute-start(bf16[128,640]{1,0:T(8,128)(2,1)} %copy-done.9), channel_id=1, source_target_pairs={{0,8},{8,16},{16,24},{24,0},{1,9},{9,17},{17,25},{25,1},{2,10},{10... | collective-permute-start | bytes 491528 | tf_op jit(solution)/shard_map/ppermute | solution.py:278
  73.1 0.9 copy-start.4
  74.1 0.9 copy-start.6
  75.0 0.9 copy-start.8
  80.6 7.5 %collective-permute-start.9 = (bf16[4,128,640]{2,1,0:T(8,128)(2,1)S(1)}, bf16[4,128,640]{2,1,0:T(8,128)(2,1)S(1)}, u32[]{:S(2)}, u32[]{:S(2)}) collective-permute-start(bf16[4,128,640]{2,1,0:T(8,128)(2,1)S(1)} %get-tuple-element.18), channel_id=1, source_target_pairs={{0,1},{1,0},{2,3},{3,2},{4,5},{5,4},{6,7},{7,6},{8,9},{9,8},{10,11... | collective-permute-start | bytes 1966088 | tf_op jit(solution)/shard_map/ppermute | solution.py:298
  88.1 7.1 %collective-permute-start.10 = (bf16[128,640]{1,0:T(8,128)(2,1)S(1)}, bf16[128,640]{1,0:T(8,128)(2,1)S(1)}, u32[]{:S(2)}, u32[]{:S(2)}) collective-permute-start(bf16[128,640]{1,0:T(8,128)(2,1)S(1)} %get-tuple-element.19), channel_id=1, source_target_pairs={{0,2},{2,4},{4,6},{6,0},{1,3},{3,5},{5,7},{7,1},{8,10},{10,12},{12... | collective-permute-start | bytes 491528 | tf_op jit(solution)/shard_map/ppermute | solution.py:314
  89.4 10.3 %collective-permute-start.11 = (bf16[128,640]{1,0:T(8,128)(2,1)S(1)}, bf16[128,640]{1,0:T(8,128)(2,1)S(1)}, u32[]{:S(2)}, u32[]{:S(2)}) collective-permute-start(bf16[128,640]{1,0:T(8,128)(2,1)S(1)} %get-tuple-element.21), channel_id=1, source_target_pairs={{0,4},{2,6},{4,0},{6,2},{1,5},{3,7},{5,1},{7,3},{8,12},{10,14},{12... | collective-permute-start | bytes 491528 | tf_op jit(solution)/shard_map/ppermute | solution.py:314
  91.9 7.9 %collective-permute-start.12 = (bf16[128,640]{1,0:T(8,128)(2,1)S(1)}, bf16[128,640]{1,0:T(8,128)(2,1)S(1)}, u32[]{:S(2)}, u32[]{:S(2)}) collective-permute-start(bf16[128,640]{1,0:T(8,128)(2,1)S(1)} %get-tuple-element.20), channel_id=1, source_target_pairs={{0,6},{2,0},{4,2},{6,4},{1,7},{3,1},{5,3},{7,5},{8,14},{10,8},{12,... | collective-permute-start | bytes 491528 | tf_op jit(solution)/shard_map/ppermute | solution.py:314
  (6 other events, 4.0 us)

commit v2 on v1

v2 whole, which is shorter than its diff:
```python
import math

import jax
import jax.numpy as jnp
from jax import lax
from jax.experimental import pallas as pl
from jax.experimental.pallas import tpu as pltpu
from jax.sharding import Mesh, PartitionSpec as P

HEAD = 128
BLOCK = 128
GROUP = 5
ROWS = GROUP * BLOCK
NZ, NY, NX, NC = 8, 4, 4, 2
PAIRS = NZ // 2
ANC = 17
ROPE_BASE = 1000000.0
MASKED = -1e30
FACTOR = HEAD ** -0.5
NT = (((1,), (1,)), ((), ()))
NN = (((1,), (0,)), ((), ()))
F32, BF16, I32 = jnp.float32, jnp.bfloat16, jnp.int32
VMEM_LIMIT = 16 << 20

VM = pl.BlockSpec(memory_space=pltpu.VMEM)
SM = pl.BlockSpec(memory_space=pltpu.SMEM)
HB = pl.BlockSpec(memory_space=pltpu.HBM)


def dot_nt(a, b):
    return lax.dot_general(a, b, NT, preferred_element_type=F32)


def dot_nn(a, b):
    return lax.dot_general(a, b, NN, preferred_element_type=F32)


def call(body, out_shape, in_specs, out_specs, name, scratch=()):
    return pl.pallas_call(
        body,
        out_shape=out_shape,
        in_specs=in_specs,
        out_specs=out_specs,
        scratch_shapes=list(scratch),
        compiler_params=pltpu.CompilerParams(vmem_limit_bytes=VMEM_LIMIT),
        name=name,
    )


def in_hbm(*arrays):
    return [pltpu.with_memory_space_constraint(a, pltpu.HBM) for a in arrays]


def pack_kernel(q_ref, g_ref, k_ref, v_ref, rows_ref, kv_ref, sem):
    copies = []
    for a in range(NZ):
        copies.append((k_ref, kv_ref.at[a, :, 0:HEAD]))
        copies.append((v_ref, kv_ref.at[a, :, HEAD:2 * HEAD]))
    for h in range(GROUP):
        cols = slice(h * HEAD, (h + 1) * HEAD)
        copies.append((q_ref.at[:, cols], rows_ref.at[h * BLOCK:(h + 1) * BLOCK, :]))
        copies.append((g_ref.at[:, cols], rows_ref.at[ROWS + h * BLOCK:ROWS + (h + 1) * BLOCK, :]))
    started = [pltpu.make_async_copy(src, dst, sem.at[i]) for i, (src, dst) in enumerate(copies)]
    for copy in started:
        copy.start()
    for copy in started:
        copy.wait()


def plan_kernel(place_ref, anc_ref, rows_ref, item_ref, list_ref):
    z = place_ref[0]
    y = place_ref[1]
    for j in range(NY):
        query_block = NY * z + ((y - j) & (NY - 1))
        bits = jnp.int32(0)
        for i in range(ANC):
            key_block = anc_ref[query_block, i]
            bits = bits | jnp.where((key_block & (NY - 1)) == y, jnp.int32(1) << (key_block >> 2), 0)
        count = jnp.int32(0)
        for key_z in range(NZ):
            list_ref[count] = key_z
            count = count + ((bits >> key_z) & 1)
        for p in range(PAIRS):
            row = PAIRS * j + p
            first = jnp.where(2 * p < count, list_ref[2 * p], 0)
            both = 2 * p + 1 < count
            second = jnp.where(both, list_ref[2 * p + 1], first)
            item_ref[row, 0] = first
            item_ref[row, 1] = second
            causal = jnp.int32(0) if j == 0 else jnp.int32(-BLOCK)
            item_ref[row, 2] = jnp.where(first == z, causal, -BLOCK)
            item_ref[row, 3] = jnp.where(both, jnp.where(second == z, causal, -BLOCK), BLOCK)
        item_ref[NY * PAIRS + j, 0] = (count + 1) // 2


def stats_kernel(item_ref, kv_ref, g0, g1, g2, g3, stat_ref, score_ref, pgrad_ref):
    key_row = lax.broadcasted_iota(I32, (BLOCK, ROWS), 0)
    query_row = lax.broadcasted_iota(I32, (BLOCK, ROWS), 1) % BLOCK
    gap = query_row - key_row
    for j, group in enumerate((g0, g1, g2, g3)):

        def step(p, carry, j=j, group=group):
            old, totals, dots = carry
            row = PAIRS * j + p
            first = item_ref[row, 0]
            second = item_ref[row, 1]
            kv = jnp.concatenate([kv_ref[first], kv_ref[second]], axis=0)
            scores = dot_nt(kv[:, :HEAD], group[:ROWS, :]) * FACTOR
            prob_grads = dot_nt(kv[:, HEAD:], group[ROWS:, :])
            upper = jnp.where(gap >= item_ref[row, 2], scores[:BLOCK], MASKED)
            lower = jnp.where(gap >= item_ref[row, 3], scores[BLOCK:], MASKED)
            scores = jnp.concatenate([upper, lower], axis=0)
            score_ref[row] = scores
            pgrad_ref[row] = prob_grads
            highest = jnp.maximum(old, jnp.max(scores, axis=0, keepdims=True))
            weights = jnp.exp(scores - highest)
            shrink = jnp.exp(old - highest)
            totals = totals * shrink + jnp.sum(weights, axis=0, keepdims=True)
            dots = dots * shrink + jnp.sum(weights * prob_grads, axis=0, keepdims=True)
            return highest, totals, dots

        zero = jnp.zeros((1, ROWS), F32)
        start = (jnp.full((1, ROWS), MASKED, F32), zero, zero)
        highest, totals, dots = lax.fori_loop(0, item_ref[NY * PAIRS + j, 0], step, start)
        stat_ref[j, 0:1, :] = highest
        stat_ref[j, 1:2, :] = totals
        stat_ref[j, 2:3, :] = dots
        stat_ref[j, 3:4, :] = zero


def turn_kernel(kv_ref, stat_ref, key_cols):
    for a in range(NZ):
        key_cols[a] = kv_ref[a, :, :HEAD].T


def grads_kernel(item_ref, cols_ref, score_ref, pgrad_ref, g0, g1, g2, g3, s0, s1, s2, s3,
                 dkv_hbm, dq0, dq1, dq2, dq3, dk_acc, dv_acc, dkv_low, sem):
    stats = (s0, s1, s2, s3)
    dk_acc[...] = jnp.zeros_like(dk_acc)
    dv_acc[...] = jnp.zeros_like(dv_acc)
    for j, (group, out) in enumerate(zip((g0, g1, g2, g3), (dq0, dq1, dq2, dq3))):
        views = [stats[k][(j - k) % NY] for k in range(NY)]
        maxima = views[0][0:1]
        for k in range(1, NY):
            maxima = jnp.maximum(maxima, views[k][0:1])
        totals = jnp.zeros((1, ROWS), F32)
        dots = jnp.zeros((1, ROWS), F32)
        for k in range(NY):
            shrink = jnp.exp(views[k][0:1] - maxima)
            totals = totals + views[k][1:2] * shrink
            dots = dots + views[k][2:3] * shrink
        log_totals = maxima + jnp.log(totals)
        row_dots = dots / totals

        def step(p, query_grad, j=j, group=group, log_totals=log_totals, row_dots=row_dots):
            row = PAIRS * j + p
            first = item_ref[row, 0]
            second = item_ref[row, 1]
            probs = jnp.exp(score_ref[row] - log_totals)
            score_grads = (probs * (pgrad_ref[row] - row_dots)).astype(BF16)
            dk_pair = dot_nn(score_grads, group[:ROWS, :])
            dv_pair = dot_nn(probs.astype(BF16), group[ROWS:, :])
            dk_acc[first] += dk_pair[:BLOCK]
            dk_acc[second] += dk_pair[BLOCK:]
            dv_acc[first] += dv_pair[:BLOCK]
            dv_acc[second] += dv_pair[BLOCK:]
            cols = jnp.concatenate([cols_ref[first], cols_ref[second]], axis=1)
            return query_grad + dot_nn(cols, score_grads)

        query_grad = lax.fori_loop(0, item_ref[NY * PAIRS + j, 0], step, jnp.zeros((HEAD, ROWS), F32))
        out[...] = (query_grad * FACTOR).astype(BF16)
    for a in range(NZ):
        dkv_low[a, :, :HEAD] = (dk_acc[a] * FACTOR).astype(BF16)
        dkv_low[a, :, HEAD:] = dv_acc[a].astype(BF16)
    copy = pltpu.make_async_copy(dkv_low, dkv_hbm, sem)
    copy.start()
    copy.wait()


def unrotate(x, cosine, sine):
    front = x[:HEAD // 2]
    back = x[HEAD // 2:]
    return jnp.concatenate([front * cosine + back * sine, back * cosine - front * sine], axis=0)


def query_part_kernel(place_ref, cos_ref, sin_ref, q0, q1, q2, q3, wq, out_ref, low_ref):
    @pl.when(pl.program_id(0) == 0)
    def _():
        cosine = cos_ref[...]
        sine = sin_ref[...]
        for h in range(GROUP):
            cols = slice(h * HEAD, (h + 1) * HEAD)
            total = q0[:, cols].astype(F32)
            for part in (q1, q2, q3):
                total = total + part[:, cols].astype(F32)
            low_ref[:, cols] = unrotate(total, cosine, sine).T.astype(BF16)

    out_ref[0] = dot_nt(low_ref[...], wq[...])


def add_key_value(low_ref, part_ref, wk, wv):
    total = part_ref[0] + dot_nt(low_ref[:, :HEAD], wk[...])
    return total + dot_nt(low_ref[:, HEAD:], wv[...])


def first_half_kernel(place_ref, cos_ref, sin_ref, dkv_ref, part_ref, wk, wv, out_ref, low_ref):
    @pl.when(pl.program_id(0) == 0)
    def _():
        total = dkv_ref[0].astype(F32)
        for a in range(1, NZ):
            total = total + dkv_ref[a].astype(F32)
        low_ref[:, :HEAD] = unrotate(total[:, :HEAD].T, cos_ref[...], sin_ref[...]).T.astype(BF16)
        low_ref[:, HEAD:] = total[:, HEAD:].astype(BF16)

    out_ref[0] = add_key_value(low_ref, part_ref, wk, wv).astype(BF16)


def second_half_kernel(place_ref, low_ref, part_ref, wk, wv, out_ref):
    out_ref[0] = add_key_value(low_ref, part_ref, wk, wv)


def weight_rows(first, width):
    def pick(i, place):
        step = i + first
        core = jnp.where(step < NX, 1 - place[3], place[3])
        return (2 * ((place[2] + step) & (NX - 1)) + core, 0)

    return pl.BlockSpec((ROWS, width), pick)


def out_rows(first):
    return pl.BlockSpec((1, BLOCK, ROWS), lambda i, place: (i + first, 0, 0))


def stepped(body, steps, out_shape, in_specs, out_specs, name, scratch=()):
    return pl.pallas_call(
        body,
        out_shape=out_shape,
        grid_spec=pltpu.PrefetchScalarGridSpec(
            num_scalar_prefetch=1,
            grid=(steps,),
            in_specs=in_specs,
            out_specs=out_specs,
            scratch_shapes=list(scratch),
        ),
        compiler_params=pltpu.CompilerParams(vmem_limit_bytes=VMEM_LIMIT),
        name=name,
    )


def shift(size, k):
    return [(i, (i + k) % size) for i in range(size)]


def shards(queries, keys, values, out_grad, ancestry, w_query, key_matrix, value_matrix):
    z, y, x, c = (lax.axis_index(name) for name in "zyxc")
    place = jnp.stack([z, y, x, c]).astype(I32)
    group, kv = call(
        pack_kernel,
        [pltpu.VMEM((2 * ROWS, HEAD), BF16), pltpu.HBM((NZ, BLOCK, 2 * HEAD), BF16)],
        [HB] * 4,
        [VM, HB],
        "pack",
        [pltpu.SemaphoreType.DMA((2 * NZ + 2 * GROUP,))],
    )(*in_hbm(queries, out_grad, keys, values))
    groups = [group] + [lax.ppermute(group, "y", shift(NY, k)) for k in range(1, NY)]
    kv_all = lax.all_to_all(kv, "z", 0, 0, tiled=True)

    own_block = NY * z + y
    own_row = lax.dynamic_slice_in_dim(ancestry, own_block, 1, 0)
    depth = jnp.sum((own_row != own_block).astype(I32))
    token_places = (BLOCK * depth + jnp.arange(BLOCK, dtype=I32)).astype(F32)
    frequencies = jnp.exp(jnp.arange(HEAD // 2, dtype=F32) * (-2.0 * math.log(ROPE_BASE) / HEAD))
    angles = frequencies[:, None] * token_places[None, :]
    cosine = jnp.cos(angles)
    sine = jnp.sin(angles)
    items = call(
        plan_kernel,
        jax.ShapeDtypeStruct((NY * PAIRS + NY, 4), I32),
        [SM, SM, VM],
        SM,
        "plan",
        [pltpu.SMEM((NZ + 1,), I32)],
    )(place, ancestry, group)
    items, cosine, sine = lax.optimization_barrier((items, cosine, sine))

    tiles = (NY * PAIRS, 2 * BLOCK, ROWS)
    stats, scores, prob_grads = call(
        stats_kernel,
        [jax.ShapeDtypeStruct((NY, 4, ROWS), F32), pltpu.VMEM(tiles, F32), pltpu.VMEM(tiles, F32)],
        [SM] + [VM] * (1 + NY),
        [VM] * 3,
        "stats",
    )(items, kv_all, *groups)
    all_stats = [stats] + [lax.ppermute(stats, "y", shift(NY, k)) for k in range(1, NY)]
    key_cols = call(
        turn_kernel, pltpu.VMEM((NZ, HEAD, BLOCK), BF16), [VM, VM], VM, "turn",
    )(kv_all, stats)
    dkv, *dq_parts = call(
        grads_kernel,
        [pltpu.HBM((NZ, BLOCK, 2 * HEAD), BF16)] + [pltpu.VMEM((HEAD, ROWS), BF16)] * NY,
        [SM] + [VM] * (3 + 2 * NY),
        [HB] + [VM] * NY,
        "grads",
        [
            pltpu.VMEM((NZ, BLOCK, HEAD), F32),
            pltpu.VMEM((NZ, BLOCK, HEAD), F32),
            pltpu.VMEM((NZ, BLOCK, 2 * HEAD), BF16),
            pltpu.SemaphoreType.DMA,
        ],
    )(items, key_cols, scores, prob_grads, *groups, *all_stats)
    dq_own = [dq_parts[0]] + [lax.ppermute(dq_parts[k], "y", shift(NY, -k)) for k in range(1, NY)]
    dkv_own = lax.all_to_all(dkv, "z", 0, 0, tiled=True)

    wq, wk, wv = in_hbm(w_query, key_matrix, value_matrix)
    query_part = stepped(
        query_part_kernel,
        2 * NX,
        pltpu.VMEM((2 * NX, BLOCK, ROWS), F32),
        [VM] * (2 + NY) + [weight_rows(0, ROWS)],
        out_rows(0),
        "query_part",
        [pltpu.VMEM((BLOCK, ROWS), BF16)],
    )(place, cosine, sine, *dq_own, wq)
    away, low = stepped(
        first_half_kernel,
        NX,
        [pltpu.VMEM((NX, BLOCK, ROWS), BF16), pltpu.VMEM((BLOCK, 2 * HEAD), BF16)],
        [VM] * 3 + [out_rows(0), weight_rows(0, HEAD), weight_rows(0, HEAD)],
        [out_rows(0), VM],
        "first_half",
    )(place, cosine, sine, dkv_own, query_part, wk, wv)
    arrived = lax.ppermute(away, "c", shift(NC, 1))
    kept = stepped(
        second_half_kernel,
        NX,
        pltpu.VMEM((NX, BLOCK, ROWS), F32),
        [VM, out_rows(NX), weight_rows(NX, HEAD), weight_rows(NX, HEAD)],
        out_rows(0),
        "second_half",
    )(place, low, query_part, wk, wv)
    total = kept[0] + arrived[0].astype(F32)
    sent = [(kept[k] + arrived[k].astype(F32)).astype(BF16) for k in range(1, NX)]
    for k in range(1, NX):
        total = total + lax.ppermute(sent[k - 1], "x", shift(NX, k)).astype(F32)
    return total.astype(BF16)


def solution(mesh):
    grid = Mesh(mesh.devices.reshape(NZ, NY, NX, NC), ("z", "y", "x", "c"))
    split = P(("z", "y"), ("x", "c"))
    weight = P(None, ("x", "c"))
    return jax.shard_map(
        shards,
        mesh=grid,
        in_specs=(split, split, split, split, P(), weight, weight, weight),
        out_specs=split,
        check_vma=False,
    )
```

time: 102 us -> 109 us (1.069); the launches traced: 101 us -> 109 us
  Pallas kernels: 17.2 us -> 40 us
  local copies, waits for them, and re-layouts: 8.5 us -> 0.09 us
  starting transfers between devices: 39.8 us -> 33 us
  waiting for transfers between devices: 31.2 us -> 33.3 us
    pallas_call x4 -> x8, Pallas kernels: 17.2 us -> 40 us  [the longest x1 17.2 us: shards(): call(pack_kernel, [pltpu.VMEM((2 * ROWS, HEAD), BF16), pltpu.HBM((NZ, BLO...]
    unnamed x32 -> x3, local copies, waits for them, and re-layouts: 7.64 us -> 0.09 us
    all_to_all x1, waiting for transfers between devices: 5.09 us -> 0.01 us  [shards(): dkv_own = lax.all_to_all(dkv, 'z', 0, 0, tiled=True)]
    ppermute x3, waiting for transfers between devices: 4.64 us -> 8.45 us  [shards(): lax.ppermute(dq_parts[k], 'y', shift(NY, -k))]
    ppermute x3, starting transfers between devices: 4.21 us -> 1.53 us  [shards(): lax.ppermute(stats, 'y', shift(NY, k))]
    ppermute x3, waiting for transfers between devices: 2.1 us -> 4.11 us  [shards(): lax.ppermute(stats, 'y', shift(NY, k))]
    ppermute x3, starting transfers between devices: 5.06 us -> 3.77 us  [shards(): lax.ppermute(group, 'y', shift(NY, k))]
  transfers between devices with their start and end apart: 15 -> 15, of which waited for: 11 -> 11; matrix products, arithmetic and copies ran while one was open for 1% -> 1% of each run, Pallas kernels for 4% -> 12%
where the time goes in v2:
time: 109 us
  Pallas kernels  40 us (37%)
  waiting for transfers between devices  33.3 us (31%)
  starting transfers between devices  33 us (30%)
  other arithmetic  1.96 us (2%)
    pallas_call x1, Pallas kernels, shards(): call(pack_kernel, [pltpu.VMEM((2 * ROWS, HEAD), BF16), pltpu.HBM((NZ, BLO...  17.2 us
    ppermute x3, waiting for transfers between devices, shards(): lax.ppermute(group, 'y', shift(NY, k))  13.4 us
    all_to_all x1, starting transfers between devices, shards(): dkv_own = lax.all_to_all(dkv, 'z', 0, 0, tiled=True)  10.8 us
    all_to_all x1, starting transfers between devices, shards(): kv_all = lax.all_to_all(kv, 'z', 0, 0, tiled=True)  9.03 us
    ppermute x3, waiting for transfers between devices, shards(): lax.ppermute(dq_parts[k], 'y', shift(NY, -k))  8.45 us
    pallas_call x1, Pallas kernels, shards(): stepped(query_part_kernel, 2 * NX, pltpu.VMEM((2 * NX, BLOCK, ROWS), F32)...  7.4 us
    ppermute x3, waiting for transfers between devices, shards(): total = total + lax.ppermute(sent[k - 1], 'x', shift(NX, k)).astype(F32)  7.32 us
    ppermute x3, starting transfers between devices, shards(): total = total + lax.ppermute(sent[k - 1], 'x', shift(NX, k)).astype(F32)  4.28 us
  transfers between devices with their start and end apart: 15, of which 11 were waited for; matrix products, arithmetic and copies ran while one was open for 1% of the time, Pallas kernels for 12%

profile of v2, /device:TPU:1, one launch (start us, length us, event | category | flops | bytes accessed | tf_op | source)
XLA Modules:
  0.0 109.1 jit_solution(10137453925001735827)
XLA Ops:
  0.0 17.2 %pack.1 = (bf16[1280,128]{1,0:T(8,128)(2,1)S(1)}, bf16[8,128,256]{2,1,0:T(8,128)(2,1)}) custom-call(bf16[128,640]{1,0:T(8,128)(2,1)} %q_ref.1, bf16[128,640]{1,0:T(8,128)(2,1)} %g_ref.1, bf16[128,128]{1,0:T(8,128)(2,1)} %k_ref.1, bf16[128,128]{1,0:T(8,128)(2,1)} %v_ref.1), custom_call_target="tpu_custom_call" | custom-call | tf_op jit(solution)/shard_map/pack/pallas_call | solution.py:258
  17.2 9.0 %all-to-all-start = ((bf16[8,128,256]{2,1,0:T(8,128)(2,1)}), bf16[8,128,256]{2,1,0:T(8,128)(2,1)S(1)}, u32[]{:S(2)}, u32[]{:S(2)}) async-start(bf16[8,128,256]{2,1,0:T(8,128)(2,1)} %get-tuple-element.24), calls=%async_computation | async-start | bytes 1048576 | tf_op jit(solution)/shard_map/all_to_all | solution.py:267
  26.3 2.7 %collective-permute-start.2 = (bf16[1280,128]{1,0:T(8,128)(2,1)S(1)}, bf16[1280,128]{1,0:T(8,128)(2,1)S(1)}, u32[]{:S(2)}, u32[]{:S(2)}) collective-permute-start(bf16[1280,128]{1,0:T(8,128)(2,1)S(1)} %get-tuple-element.20.rows_ref.g0), channel_id=1, source_target_pairs={{0,24},{8,0},{16,8},{24,16},{1,25},{9,1},{17,9},{25,17},{2,26},{10... | collective-permute-start | bytes 983048 | tf_op jit(solution)/shard_map/ppermute | solution.py:266
  31.7 1.8 %plan.1.item_ref = s32[20,4]{1,0:T(8,128)S(1)} custom-call(s32[4]{0:T(128)S(1)} %pad_add_fusion.place_ref, s32[32,17]{1,0:T(8,128)S(1)} %copy.9.anc_ref, bf16[1280,128]{1,0:T(8,128)(2,1)S(1)} %get-tuple-element.20.rows_ref.g0), custom_call_target="tpu_custom_call" | custom-call | tf_op jit(solution)/shard_map/plan/pallas_call | solution.py:277
  33.7 2.4 %collective-permute-done.2.g3 = bf16[1280,128]{1,0:T(8,128)(2,1)S(1)} collective-permute-done((bf16[1280,128]{1,0:T(8,128)(2,1)S(1)}, bf16[1280,128]{1,0:T(8,128)(2,1)S(1)}, u32[]{:S(2)}, u32[]{:S(2)}) %collective-permute-start.2) | collective-permute-done | bytes 327712 | tf_op jit(solution)/shard_map/ppermute | solution.py:266
  36.1 2.4 %collective-permute-done.1.g2 = bf16[1280,128]{1,0:T(8,128)(2,1)S(1)} collective-permute-done((bf16[1280,128]{1,0:T(8,128)(2,1)S(1)}, bf16[1280,128]{1,0:T(8,128)(2,1)S(1)}, u32[]{:S(2)}, u32[]{:S(2)}) %collective-permute-start.1) | collective-permute-done | bytes 327712 | tf_op jit(solution)/shard_map/ppermute | solution.py:266
  38.5 8.6 %collective-permute-done.g1 = bf16[1280,128]{1,0:T(8,128)(2,1)S(1)} collective-permute-done((bf16[1280,128]{1,0:T(8,128)(2,1)S(1)}, bf16[1280,128]{1,0:T(8,128)(2,1)S(1)}, u32[]{:S(2)}, u32[]{:S(2)}) %collective-permute-start) | collective-permute-done | bytes 327712 | tf_op jit(solution)/shard_map/ppermute | solution.py:266
  47.2 2.4 %stats.1 = (f32[4,4,640]{2,1,0:T(4,128)S(1)}, f32[16,256,640]{2,1,0:T(8,128)S(1)}, f32[16,256,640]{2,1,0:T(8,128)S(1)}) custom-call(s32[20,4]{1,0:T(8,128)S(1)} %plan.1.item_ref, bf16[8,128,256]{2,1,0:T(8,128)(2,1)S(1)} %all-to-all-done.kv_ref, bf16[1280,128]{1,0:T(8,128)(2,1)S(1)} %get-tuple-element.20.rows_ref.g0, ...), custom_call_target="tpu_custom_call" | custom-call | tf_op jit(solution)/shard_map/stats/pallas_call | solution.py:288
  49.8 1.4 %collective-permute-start.3 = (f32[4,4,640]{2,1,0:T(4,128)S(1)}, f32[4,4,640]{2,1,0:T(4,128)S(1)}, u32[]{:S(2)}, u32[]{:S(2)}) collective-permute-start(f32[4,4,640]{2,1,0:T(4,128)S(1)} %get-tuple-element.25.stat_ref.s0), channel_id=1, source_target_pairs={{0,8},{8,16},{16,24},{24,0},{1,9},{9,17},{17,25},{25,1},{2,10},{10... | collective-permute-start | bytes 122888 | tf_op jit(solution)/shard_map/ppermute | solution.py:295
  52.5 1.6 %collective-permute-done.4.s2 = f32[4,4,640]{2,1,0:T(4,128)S(1)} collective-permute-done((f32[4,4,640]{2,1,0:T(4,128)S(1)}, f32[4,4,640]{2,1,0:T(4,128)S(1)}, u32[]{:S(2)}, u32[]{:S(2)}) %collective-permute-start.4) | collective-permute-done | bytes 40992 | tf_op jit(solution)/shard_map/ppermute | solution.py:295
  55.4 3.8 %grads.1 = (bf16[8,128,256]{2,1,0:T(8,128)(2,1)}, bf16[128,640]{1,0:T(8,128)(2,1)S(1)}, bf16[128,640]{1,0:T(8,128)(2,1)S(1)}, bf16[128,640]{1,0:T(8,128)(2,1)S(1)}, bf16[128,640]{1,0:T(8,128)(2,1)S(1)}) custom-call(s32[20,4]{1,0:T(8,128)S(1)} %plan.1.item_ref, bf16[8,128,128]{2,1,0:T(8,128)(2,1)S(1)} %turn.1.cols_ref, ...), custom_call_target="tpu_custom_call" | custom-call | tf_op jit(solution)/shard_map/grads/pallas_call | solution.py:299
  59.2 10.8 %all-to-all-start.1 = ((bf16[8,128,256]{2,1,0:T(8,128)(2,1)}), bf16[8,128,256]{2,1,0:T(8,128)(2,1)S(1)}, u32[]{:S(2)}, u32[]{:S(2)}) async-start(bf16[8,128,256]{2,1,0:T(8,128)(2,1)} %get-tuple-element.28), calls=%async_computation.1 | async-start | bytes 1048576 | tf_op jit(solution)/shard_map/all_to_all | solution.py:313
  71.5 2.7 %collective-permute-done.6.q1 = bf16[128,640]{1,0:T(8,128)(2,1)S(1)} collective-permute-done((bf16[128,640]{1,0:T(8,128)(2,1)S(1)}, bf16[128,640]{1,0:T(8,128)(2,1)S(1)}, u32[]{:S(2)}, u32[]{:S(2)}) %collective-permute-start.6) | collective-permute-done | bytes 163872 | tf_op jit(solution)/shard_map/ppermute | solution.py:312
  74.2 1.7 %collective-permute-done.7.q2 = bf16[128,640]{1,0:T(8,128)(2,1)S(1)} collective-permute-done((bf16[128,640]{1,0:T(8,128)(2,1)S(1)}, bf16[128,640]{1,0:T(8,128)(2,1)S(1)}, u32[]{:S(2)}, u32[]{:S(2)}) %collective-permute-start.7) | collective-permute-done | bytes 163872 | tf_op jit(solution)/shard_map/ppermute | solution.py:312
  75.9 4.0 %collective-permute-done.8.q3 = bf16[128,640]{1,0:T(8,128)(2,1)S(1)} collective-permute-done((bf16[128,640]{1,0:T(8,128)(2,1)S(1)}, bf16[128,640]{1,0:T(8,128)(2,1)S(1)}, u32[]{:S(2)}, u32[]{:S(2)}) %collective-permute-start.8) | collective-permute-done | bytes 163872 | tf_op jit(solution)/shard_map/ppermute | solution.py:312
  80.0 7.4 %query_part.1.part_ref = f32[8,128,640]{2,1,0:T(8,128)S(1)} custom-call(s32[4]{0:T(128)S(1)} %pad_add_fusion.place_ref, f32[64,128]{1,0:T(8,128)S(1)} %get-tuple-element.21.cos_ref, f32[64,128]{1,0:T(8,128)S(1)} %get-tuple-element.22.sin_ref, bf16[128,640]{1,0:T(8,128)(2,1)S(1)} %get-tuple-element.29.q0, bf16[128,640]{1,0:T(8,128)(2,1)S(1)} %collective-permute-done.6.q1, ...), custom_call_target="tpu_custom_call" | custom-call | tf_op jit(solution)/shard_map/query_part/pallas_call | solution.py:316
  87.4 3.7 %first_half.1 = (bf16[4,128,640]{2,1,0:T(8,128)(2,1)S(1)}, bf16[128,256]{1,0:T(8,128)(2,1)S(1)}) custom-call(s32[4]{0:T(128)S(1)} %pad_add_fusion.place_ref, f32[64,128]{1,0:T(8,128)S(1)} %get-tuple-element.21.cos_ref, f32[64,128]{1,0:T(8,128)S(1)} %get-tuple-element.22.sin_ref, bf16[8,128,256]{2,1,0:T(8,128)(2,1)S(1)} %all-to-all-done.1.dkv_ref, ...), custom_call_target="tpu_custom_call" | custom-call | tf_op jit(solution)/shard_map/first_half/pallas_call | solution.py:325
  91.1 2.1 %collective-permute-start.9 = (bf16[4,128,640]{2,1,0:T(8,128)(2,1)S(1)}, bf16[4,128,640]{2,1,0:T(8,128)(2,1)S(1)}, u32[]{:S(2)}, u32[]{:S(2)}) collective-permute-start(bf16[4,128,640]{2,1,0:T(8,128)(2,1)S(1)} %get-tuple-element.34), channel_id=1, source_target_pairs={{0,1},{1,0},{2,3},{3,2},{4,5},{5,4},{6,7},{7,6},{8,9},{9,8},{10,11... | collective-permute-start | bytes 1966088 | tf_op jit(solution)/shard_map/ppermute | solution.py:333
  93.2 3.5 %second_half.1 = f32[4,128,640]{2,1,0:T(8,128)S(1)} custom-call(s32[4]{0:T(128)S(1)} %pad_add_fusion.place_ref, bf16[128,256]{1,0:T(8,128)(2,1)S(1)} %get-tuple-element.33.low_ref, f32[8,128,640]{2,1,0:T(8,128)S(1)} %query_part.1.part_ref, bf16[5120,128]{1,0:T(8,128)(2,1)} %wk.3, bf16[5120,128]{1,0:T(8,128)(2,1)} %wv.3), custom_call_target="tpu_custom_call" | custom-call | tf_op jit(solution)/shard_map/second_half/pallas_call | solution.py:334
  96.8 1.3 %collective-permute-start.10 = (bf16[128,640]{1,0:T(8,128)(2,1)S(1)}, bf16[128,640]{1,0:T(8,128)(2,1)S(1)}, u32[]{:S(2)}, u32[]{:S(2)}) collective-permute-start(bf16[128,640]{1,0:T(8,128)(2,1)S(1)} %get-tuple-element.35), channel_id=1, source_target_pairs={{0,2},{2,4},{4,6},{6,0},{1,3},{3,5},{5,7},{7,1},{8,10},{10,12},{12... | collective-permute-start | bytes 491528 | tf_op jit(solution)/shard_map/ppermute | solution.py:345
  98.0 1.5 %collective-permute-start.12 = (bf16[128,640]{1,0:T(8,128)(2,1)S(1)}, bf16[128,640]{1,0:T(8,128)(2,1)S(1)}, u32[]{:S(2)}, u32[]{:S(2)}) collective-permute-start(bf16[128,640]{1,0:T(8,128)(2,1)S(1)} %get-tuple-element.36), channel_id=1, source_target_pairs={{0,6},{2,0},{4,2},{6,4},{1,7},{3,1},{5,3},{7,5},{8,14},{10,8},{12,... | collective-permute-start | bytes 491528 | tf_op jit(solution)/shard_map/ppermute | solution.py:345
  99.5 1.5 %collective-permute-start.11 = (bf16[128,640]{1,0:T(8,128)(2,1)S(1)}, bf16[128,640]{1,0:T(8,128)(2,1)S(1)}, u32[]{:S(2)}, u32[]{:S(2)}) collective-permute-start(bf16[128,640]{1,0:T(8,128)(2,1)S(1)} %get-tuple-element.37), channel_id=1, source_target_pairs={{0,4},{2,6},{4,0},{6,2},{1,5},{3,7},{5,1},{7,3},{8,12},{10,14},{12... | collective-permute-start | bytes 491528 | tf_op jit(solution)/shard_map/ppermute | solution.py:345
  101.0 2.8 %collective-permute-done.10 = bf16[128,640]{1,0:T(8,128)(2,1)S(1)} collective-permute-done((bf16[128,640]{1,0:T(8,128)(2,1)S(1)}, bf16[128,640]{1,0:T(8,128)(2,1)S(1)}, u32[]{:S(2)}, u32[]{:S(2)}) %collective-permute-start.10) | collective-permute-done | bytes 163872 | tf_op jit(solution)/shard_map/ppermute | solution.py:345
  103.9 4.5 %collective-permute-done.11 = bf16[128,640]{1,0:T(8,128)(2,1)S(1)} collective-permute-done((bf16[128,640]{1,0:T(8,128)(2,1)S(1)}, bf16[128,640]{1,0:T(8,128)(2,1)S(1)}, u32[]{:S(2)}, u32[]{:S(2)}) %collective-permute-start.11) | collective-permute-done | bytes 163872 | tf_op jit(solution)/shard_map/ppermute | solution.py:345
  (24 shorter events, 7.4 us)
Async XLA Ops:
  0.0 30.0 %copy-start = (s32[32,17]{0,1:T(8,128)S(1)}, s32[32,17]{0,1:T(8,128)}, u32[]{:S(2)}) copy-start(s32[32,17]{0,1:T(8,128)} %param.12) | copy-start | bytes 6532
  17.2 29.9 %all-to-all-start = ((bf16[8,128,256]{2,1,0:T(8,128)(2,1)}), bf16[8,128,256]{2,1,0:T(8,128)(2,1)S(1)}, u32[]{:S(2)}, u32[]{:S(2)}) async-start(bf16[8,128,256]{2,1,0:T(8,128)(2,1)} %get-tuple-element.24), calls=%async_computation | async-start | bytes 1048576 | tf_op jit(solution)/shard_map/all_to_all | solution.py:267
  26.3 9.8 %collective-permute-start.2 = (bf16[1280,128]{1,0:T(8,128)(2,1)S(1)}, bf16[1280,128]{1,0:T(8,128)(2,1)S(1)}, u32[]{:S(2)}, u32[]{:S(2)}) collective-permute-start(bf16[1280,128]{1,0:T(8,128)(2,1)S(1)} %get-tuple-element.20.rows_ref.g0), channel_id=1, source_target_pairs={{0,24},{8,0},{16,8},{24,16},{1,25},{9,1},{17,9},{25,17},{2,26},{10... | collective-permute-start | bytes 983048 | tf_op jit(solution)/shard_map/ppermute | solution.py:266
  29.0 9.5 %collective-permute-start.1 = (bf16[1280,128]{1,0:T(8,128)(2,1)S(1)}, bf16[1280,128]{1,0:T(8,128)(2,1)S(1)}, u32[]{:S(2)}, u32[]{:S(2)}) collective-permute-start(bf16[1280,128]{1,0:T(8,128)(2,1)S(1)} %get-tuple-element.20.rows_ref.g0), channel_id=1, source_target_pairs={{0,16},{8,24},{16,0},{24,8},{1,17},{9,25},{17,1},{25,9},{2,18},{10... | collective-permute-start | bytes 983048 | tf_op jit(solution)/shard_map/ppermute | solution.py:266
  29.4 17.8 %collective-permute-start = (bf16[1280,128]{1,0:T(8,128)(2,1)S(1)}, bf16[1280,128]{1,0:T(8,128)(2,1)S(1)}, u32[]{:S(2)}, u32[]{:S(2)}) collective-permute-start(bf16[1280,128]{1,0:T(8,128)(2,1)S(1)} %get-tuple-element.20.rows_ref.g0), channel_id=1, source_target_pairs={{0,8},{8,16},{16,24},{24,0},{1,9},{9,17},{17,25},{25,1},{2,10},{10... | collective-permute-start | bytes 983048 | tf_op jit(solution)/shard_map/ppermute | solution.py:266
  49.6 2.9 %collective-permute-start.5 = (f32[4,4,640]{2,1,0:T(4,128)S(1)}, f32[4,4,640]{2,1,0:T(4,128)S(1)}, u32[]{:S(2)}, u32[]{:S(2)}) collective-permute-start(f32[4,4,640]{2,1,0:T(4,128)S(1)} %get-tuple-element.25.stat_ref.s0), channel_id=1, source_target_pairs={{0,24},{8,0},{16,8},{24,16},{1,25},{9,1},{17,9},{25,17},{2,26},{10... | collective-permute-start | bytes 122888 | tf_op jit(solution)/shard_map/ppermute | solution.py:295
  49.7 4.4 %collective-permute-start.4 = (f32[4,4,640]{2,1,0:T(4,128)S(1)}, f32[4,4,640]{2,1,0:T(4,128)S(1)}, u32[]{:S(2)}, u32[]{:S(2)}) collective-permute-start(f32[4,4,640]{2,1,0:T(4,128)S(1)} %get-tuple-element.25.stat_ref.s0), channel_id=1, source_target_pairs={{0,16},{8,24},{16,0},{24,8},{1,17},{9,25},{17,1},{25,9},{2,18},{10... | collective-permute-start | bytes 122888 | tf_op jit(solution)/shard_map/ppermute | solution.py:295
  49.8 5.6 %collective-permute-start.3 = (f32[4,4,640]{2,1,0:T(4,128)S(1)}, f32[4,4,640]{2,1,0:T(4,128)S(1)}, u32[]{:S(2)}, u32[]{:S(2)}) collective-permute-start(f32[4,4,640]{2,1,0:T(4,128)S(1)} %get-tuple-element.25.stat_ref.s0), channel_id=1, source_target_pairs={{0,8},{8,16},{16,24},{24,0},{1,9},{9,17},{17,25},{25,1},{2,10},{10... | collective-permute-start | bytes 122888 | tf_op jit(solution)/shard_map/ppermute | solution.py:295
  59.2 28.2 %all-to-all-start.1 = ((bf16[8,128,256]{2,1,0:T(8,128)(2,1)}), bf16[8,128,256]{2,1,0:T(8,128)(2,1)S(1)}, u32[]{:S(2)}, u32[]{:S(2)}) async-start(bf16[8,128,256]{2,1,0:T(8,128)(2,1)} %get-tuple-element.28), calls=%async_computation.1 | async-start | bytes 1048576 | tf_op jit(solution)/shard_map/all_to_all | solution.py:313
  70.1 4.2 %collective-permute-start.6 = (bf16[128,640]{1,0:T(8,128)(2,1)S(1)}, bf16[128,640]{1,0:T(8,128)(2,1)S(1)}, u32[]{:S(2)}, u32[]{:S(2)}) collective-permute-start(bf16[128,640]{1,0:T(8,128)(2,1)S(1)} %get-tuple-element.30), channel_id=1, source_target_pairs={{0,24},{8,0},{16,8},{24,16},{1,25},{9,1},{17,9},{25,17},{2,26},{10... | collective-permute-start | bytes 491528 | tf_op jit(solution)/shard_map/ppermute | solution.py:312
  70.1 5.9 %collective-permute-start.7 = (bf16[128,640]{1,0:T(8,128)(2,1)S(1)}, bf16[128,640]{1,0:T(8,128)(2,1)S(1)}, u32[]{:S(2)}, u32[]{:S(2)}) collective-permute-start(bf16[128,640]{1,0:T(8,128)(2,1)S(1)} %get-tuple-element.31), channel_id=1, source_target_pairs={{0,16},{8,24},{16,0},{24,8},{1,17},{9,25},{17,1},{25,9},{2,18},{10... | collective-permute-start | bytes 491528 | tf_op jit(solution)/shard_map/ppermute | solution.py:312
  70.6 9.3 %collective-permute-start.8 = (bf16[128,640]{1,0:T(8,128)(2,1)S(1)}, bf16[128,640]{1,0:T(8,128)(2,1)S(1)}, u32[]{:S(2)}, u32[]{:S(2)}) collective-permute-start(bf16[128,640]{1,0:T(8,128)(2,1)S(1)} %get-tuple-element.32), channel_id=1, source_target_pairs={{0,8},{8,16},{16,24},{24,0},{1,9},{9,17},{17,25},{25,1},{2,10},{10... | collective-permute-start | bytes 491528 | tf_op jit(solution)/shard_map/ppermute | solution.py:312
  91.1 5.5 %collective-permute-start.9 = (bf16[4,128,640]{2,1,0:T(8,128)(2,1)S(1)}, bf16[4,128,640]{2,1,0:T(8,128)(2,1)S(1)}, u32[]{:S(2)}, u32[]{:S(2)}) collective-permute-start(bf16[4,128,640]{2,1,0:T(8,128)(2,1)S(1)} %get-tuple-element.34), channel_id=1, source_target_pairs={{0,1},{1,0},{2,3},{3,2},{4,5},{5,4},{6,7},{7,6},{8,9},{9,8},{10,11... | collective-permute-start | bytes 1966088 | tf_op jit(solution)/shard_map/ppermute | solution.py:333
  96.8 7.1 %collective-permute-start.10 = (bf16[128,640]{1,0:T(8,128)(2,1)S(1)}, bf16[128,640]{1,0:T(8,128)(2,1)S(1)}, u32[]{:S(2)}, u32[]{:S(2)}) collective-permute-start(bf16[128,640]{1,0:T(8,128)(2,1)S(1)} %get-tuple-element.35), channel_id=1, source_target_pairs={{0,2},{2,4},{4,6},{6,0},{1,3},{3,5},{5,7},{7,1},{8,10},{10,12},{12... | collective-permute-start | bytes 491528 | tf_op jit(solution)/shard_map/ppermute | solution.py:345
  98.0 5.8 %collective-permute-start.12 = (bf16[128,640]{1,0:T(8,128)(2,1)S(1)}, bf16[128,640]{1,0:T(8,128)(2,1)S(1)}, u32[]{:S(2)}, u32[]{:S(2)}) collective-permute-start(bf16[128,640]{1,0:T(8,128)(2,1)S(1)} %get-tuple-element.36), channel_id=1, source_target_pairs={{0,6},{2,0},{4,2},{6,4},{1,7},{3,1},{5,3},{7,5},{8,14},{10,8},{12,... | collective-permute-start | bytes 491528 | tf_op jit(solution)/shard_map/ppermute | solution.py:345
  99.5 8.9 %collective-permute-start.11 = (bf16[128,640]{1,0:T(8,128)(2,1)S(1)}, bf16[128,640]{1,0:T(8,128)(2,1)S(1)}, u32[]{:S(2)}, u32[]{:S(2)}) collective-permute-start(bf16[128,640]{1,0:T(8,128)(2,1)S(1)} %get-tuple-element.37), channel_id=1, source_target_pairs={{0,4},{2,6},{4,0},{6,2},{1,5},{3,7},{5,1},{7,3},{8,12},{10,14},{12... | collective-permute-start | bytes 491528 | tf_op jit(solution)/shard_map/ppermute | solution.py:345

commit v3 on v2

--- a/solution.py
+++ b/solution.py
@@ -51,20 +51,30 @@
     return [pltpu.with_memory_space_constraint(a, pltpu.HBM) for a in arrays]
 
 
-def pack_kernel(q_ref, g_ref, k_ref, v_ref, rows_ref, kv_ref, sem):
-    copies = []
-    for a in range(NZ):
-        copies.append((k_ref, kv_ref.at[a, :, 0:HEAD]))
-        copies.append((v_ref, kv_ref.at[a, :, HEAD:2 * HEAD]))
-    for h in range(GROUP):
-        cols = slice(h * HEAD, (h + 1) * HEAD)
-        copies.append((q_ref.at[:, cols], rows_ref.at[h * BLOCK:(h + 1) * BLOCK, :]))
-        copies.append((g_ref.at[:, cols], rows_ref.at[ROWS + h * BLOCK:ROWS + (h + 1) * BLOCK, :]))
-    started = [pltpu.make_async_copy(src, dst, sem.at[i]) for i, (src, dst) in enumerate(copies)]
+def run_copies(pairs, sem):
+    started = [pltpu.make_async_copy(src, dst, sem.at[i]) for i, (src, dst) in enumerate(pairs)]
     for copy in started:
         copy.start()
     for copy in started:
         copy.wait()
+
+
+def stack_kernel(q_ref, g_ref, rows_ref, sem):
+    pairs = []
+    for h in range(GROUP):
+        cols = slice(h * HEAD, (h + 1) * HEAD)
+        pairs.append((q_ref.at[:, cols], rows_ref.at[h * BLOCK:(h + 1) * BLOCK, :]))
+        pairs.append((g_ref.at[:, cols], rows_ref.at[ROWS + h * BLOCK:ROWS + (h + 1) * BLOCK, :]))
+    run_copies(pairs, sem)
+
+
+def spread_kernel(k_ref, v_ref, rows_ref, kv_ref, pair_ref, sem):
+    run_copies([(k_ref, pair_ref.at[:, 0:HEAD]), (v_ref, pair_ref.at[:, HEAD:2 * HEAD])], sem)
+    run_copies([(pair_ref, kv_ref.at[a]) for a in range(NZ)], sem)
+
+
+def flush_kernel(low_ref, out_ref, sem):
+    run_copies([(low_ref, out_ref)], sem)
 
 
 def plan_kernel(place_ref, anc_ref, rows_ref, item_ref, list_ref):
@@ -134,7 +144,7 @@
 
 
 def grads_kernel(item_ref, cols_ref, score_ref, pgrad_ref, g0, g1, g2, g3, s0, s1, s2, s3,
-                 dkv_hbm, dq0, dq1, dq2, dq3, dk_acc, dv_acc, dkv_low, sem):
+                 dkv_ref, dq0, dq1, dq2, dq3, dk_acc, dv_acc):
     stats = (s0, s1, s2, s3)
     dk_acc[...] = jnp.zeros_like(dk_acc)
     dv_acc[...] = jnp.zeros_like(dv_acc)
@@ -170,11 +180,8 @@
         query_grad = lax.fori_loop(0, item_ref[NY * PAIRS + j, 0], step, jnp.zeros((HEAD, ROWS), F32))
         out[...] = (query_grad * FACTOR).astype(BF16)
     for a in range(NZ):
-        dkv_low[a, :, :HEAD] = (dk_acc[a] * FACTOR).astype(BF16)
-        dkv_low[a, :, HEAD:] = dv_acc[a].astype(BF16)
-    copy = pltpu.make_async_copy(dkv_low, dkv_hbm, sem)
-    copy.start()
-    copy.wait()
+        dkv_ref[a, :, :HEAD] = (dk_acc[a] * FACTOR).astype(BF16)
+        dkv_ref[a, :, HEAD:] = dv_acc[a].astype(BF16)
 
 
 def unrotate(x, cosine, sine):
@@ -193,14 +200,14 @@
             total = q0[:, cols].astype(F32)
             for part in (q1, q2, q3):
                 total = total + part[:, cols].astype(F32)
-            low_ref[:, cols] = unrotate(total, cosine, sine).T.astype(BF16)
-
-    out_ref[0] = dot_nt(low_ref[...], wq[...])
+            low_ref[cols, :] = unrotate(total, cosine, sine).astype(BF16)
+
+    out_ref[0] = dot_nn(wq[...], low_ref[...])
 
 
 def add_key_value(low_ref, part_ref, wk, wv):
-    total = part_ref[0] + dot_nt(low_ref[:, :HEAD], wk[...])
-    return total + dot_nt(low_ref[:, HEAD:], wv[...])
+    total = part_ref[0] + dot_nn(wk[...], low_ref[:HEAD, :])
+    return total + dot_nn(wv[...], low_ref[HEAD:, :])
 
 
 def first_half_kernel(place_ref, cos_ref, sin_ref, dkv_ref, part_ref, wk, wv, out_ref, low_ref):
@@ -209,14 +216,23 @@
         total = dkv_ref[0].astype(F32)
         for a in range(1, NZ):
             total = total + dkv_ref[a].astype(F32)
-        low_ref[:, :HEAD] = unrotate(total[:, :HEAD].T, cos_ref[...], sin_ref[...]).T.astype(BF16)
-        low_ref[:, HEAD:] = total[:, HEAD:].astype(BF16)
+        low_ref[:HEAD, :] = unrotate(total[:, :HEAD].T, cos_ref[...], sin_ref[...]).astype(BF16)
+        low_ref[HEAD:, :] = total[:, HEAD:].T.astype(BF16)
 
     out_ref[0] = add_key_value(low_ref, part_ref, wk, wv).astype(BF16)
 
 
 def second_half_kernel(place_ref, low_ref, part_ref, wk, wv, out_ref):
     out_ref[0] = add_key_value(low_ref, part_ref, wk, wv)
+
+
+def finish_kernel(kept_ref, arrived_ref, p0, p1, p2, out_ref):
+    for h in range(GROUP):
+        rows = slice(h * HEAD, (h + 1) * HEAD)
+        total = kept_ref[rows, :]
+        for part in (arrived_ref, p0, p1, p2):
+            total = total + part[rows, :].astype(F32)
+        out_ref[:, rows] = total.T.astype(BF16)
 
 
 def weight_rows(first, width):
@@ -229,7 +245,7 @@
 
 
 def out_rows(first):
-    return pl.BlockSpec((1, BLOCK, ROWS), lambda i, place: (i + first, 0, 0))
+    return pl.BlockSpec((1, ROWS, BLOCK), lambda i, place: (i + first, 0, 0))
 
 
 def stepped(body, steps, out_shape, in_specs, out_specs, name, scratch=()):
@@ -255,14 +271,14 @@
 def shards(queries, keys, values, out_grad, ancestry, w_query, key_matrix, value_matrix):
     z, y, x, c = (lax.axis_index(name) for name in "zyxc")
     place = jnp.stack([z, y, x, c]).astype(I32)
-    group, kv = call(
-        pack_kernel,
-        [pltpu.VMEM((2 * ROWS, HEAD), BF16), pltpu.HBM((NZ, BLOCK, 2 * HEAD), BF16)],
-        [HB] * 4,
-        [VM, HB],
-        "pack",
-        [pltpu.SemaphoreType.DMA((2 * NZ + 2 * GROUP,))],
-    )(*in_hbm(queries, out_grad, keys, values))
+    group = call(
+        stack_kernel, pltpu.VMEM((2 * ROWS, HEAD), BF16), [HB] * 2, VM, "stack",
+        [pltpu.SemaphoreType.DMA((2 * GROUP,))],
+    )(*in_hbm(queries, out_grad))
+    kv = call(
+        spread_kernel, pltpu.HBM((NZ, BLOCK, 2 * HEAD), BF16), [HB, HB, VM], HB, "spread",
+        [pltpu.VMEM((BLOCK, 2 * HEAD), BF16), pltpu.SemaphoreType.DMA((NZ,))],
+    )(*in_hbm(keys, values), group)
     groups = [group] + [lax.ppermute(group, "y", shift(NY, k)) for k in range(1, NY)]
     kv_all = lax.all_to_all(kv, "z", 0, 0, tiled=True)
 
@@ -298,34 +314,32 @@
     )(kv_all, stats)
     dkv, *dq_parts = call(
         grads_kernel,
-        [pltpu.HBM((NZ, BLOCK, 2 * HEAD), BF16)] + [pltpu.VMEM((HEAD, ROWS), BF16)] * NY,
+        [pltpu.VMEM((NZ, BLOCK, 2 * HEAD), BF16)] + [pltpu.VMEM((HEAD, ROWS), BF16)] * NY,
         [SM] + [VM] * (3 + 2 * NY),
-        [HB] + [VM] * NY,
+        [VM] * (1 + NY),
         "grads",
-        [
-            pltpu.VMEM((NZ, BLOCK, HEAD), F32),
-            pltpu.VMEM((NZ, BLOCK, HEAD), F32),
-            pltpu.VMEM((NZ, BLOCK, 2 * HEAD), BF16),
-            pltpu.SemaphoreType.DMA,
-        ],
+        [pltpu.VMEM((NZ, BLOCK, HEAD), F32), pltpu.VMEM((NZ, BLOCK, HEAD), F32)],
     )(items, key_cols, scores, prob_grads, *groups, *all_stats)
     dq_own = [dq_parts[0]] + [lax.ppermute(dq_parts[k], "y", shift(NY, -k)) for k in range(1, NY)]
+    dkv = call(
+        flush_kernel, pltpu.HBM(dkv.shape, BF16), [VM], HB, "flush", [pltpu.SemaphoreType.DMA((1,))],
+    )(dkv)
     dkv_own = lax.all_to_all(dkv, "z", 0, 0, tiled=True)
 
     wq, wk, wv = in_hbm(w_query, key_matrix, value_matrix)
     query_part = stepped(
         query_part_kernel,
         2 * NX,
-        pltpu.VMEM((2 * NX, BLOCK, ROWS), F32),
+        pltpu.VMEM((2 * NX, ROWS, BLOCK), F32),
         [VM] * (2 + NY) + [weight_rows(0, ROWS)],
         out_rows(0),
         "query_part",
-        [pltpu.VMEM((BLOCK, ROWS), BF16)],
+        [pltpu.VMEM((ROWS, BLOCK), BF16)],
     )(place, cosine, sine, *dq_own, wq)
     away, low = stepped(
         first_half_kernel,
         NX,
-        [pltpu.VMEM((NX, BLOCK, ROWS), BF16), pltpu.VMEM((BLOCK, 2 * HEAD), BF16)],
+        [pltpu.VMEM((NX, ROWS, BLOCK), BF16), pltpu.VMEM((2 * HEAD, BLOCK), BF16)],
         [VM] * 3 + [out_rows(0), weight_rows(0, HEAD), weight_rows(0, HEAD)],
         [out_rows(0), VM],
         "first_half",
@@ -334,16 +348,16 @@
     kept = stepped(
         second_half_kernel,
         NX,
-        pltpu.VMEM((NX, BLOCK, ROWS), F32),
+        pltpu.VMEM((NX, ROWS, BLOCK), F32),
         [VM, out_rows(NX), weight_rows(NX, HEAD), weight_rows(NX, HEAD)],
         out_rows(0),
         "second_half",
     )(place, low, query_part, wk, wv)
-    total = kept[0] + arrived[0].astype(F32)
     sent = [(kept[k] + arrived[k].astype(F32)).astype(BF16) for k in range(1, NX)]
-    for k in range(1, NX):
-        total = total + lax.ppermute(sent[k - 1], "x", shift(NX, k)).astype(F32)
-    return total.astype(BF16)
+    parts = [lax.ppermute(sent[k - 1], "x", shift(NX, k)) for k in range(1, NX)]
+    return call(
+        finish_kernel, jax.ShapeDtypeStruct((BLOCK, ROWS), BF16), [VM] * (2 + len(parts)), VM, "finish",
+    )(kept[0], arrived[0], *parts)
 
 
 def solution(mesh):

time: 109 us -> 95.9 us (0.88); the launches traced: 109 us -> 94.7 us
  Pallas kernels: 40 us -> 25.9 us
  waiting for transfers between devices: 33.3 us -> 36.5 us
  starting transfers between devices: 33 us -> 30.3 us
    pallas_call x5 -> x8, Pallas kernels: 35.6 us -> 21.5 us  [the longest x1 7.4 us: shards(): stepped(query_part_kernel, 2 * NX, pltpu.VMEM((2 * NX, ROWS, BLOCK), F32)...]
    ppermute x3, waiting for transfers between devices: 7.32 us -> 9.99 us  [shards(): parts = [lax.ppermute(sent[k - 1], 'x', shift(NX, k)) for k in range(1, NX)]]
    all_to_all x1, starting transfers between devices: 10.8 us -> 8.46 us  [shards(): dkv_own = lax.all_to_all(dkv, 'z', 0, 0, tiled=True)]
  transfers between devices with their start and end apart: 15 -> 15, of which waited for: 11 -> 12; matrix products, arithmetic and copies ran while one was open for 1% -> 1% of each run, Pallas kernels for 12% -> 13%
where the time goes in v3:
time: 95.9 us; the launch traced here: 94.7 us
  waiting for transfers between devices  36.5 us (38%)
  starting transfers between devices  30.3 us (32%)
  Pallas kernels  25.9 us (27%)
  other arithmetic  1.16 us (1%)
    ppermute x3, waiting for transfers between devices, shards(): lax.ppermute(group, 'y', shift(NY, k))  13.5 us
    ppermute x3, waiting for transfers between devices, shards(): parts = [lax.ppermute(sent[k - 1], 'x', shift(NX, k)) for k in range(1, NX)]  9.99 us
    all_to_all x1, starting transfers between devices, shards(): kv_all = lax.all_to_all(kv, 'z', 0, 0, tiled=True)  9.03 us
    ppermute x3, waiting for transfers between devices, shards(): lax.ppermute(dq_parts[k], 'y', shift(NY, -k))  8.84 us
    all_to_all x1, starting transfers between devices, shards(): dkv_own = lax.all_to_all(dkv, 'z', 0, 0, tiled=True)  8.46 us
    pallas_call x1, Pallas kernels, shards(): stepped(query_part_kernel, 2 * NX, pltpu.VMEM((2 * NX, ROWS, BLOCK), F32)...  7.4 us
    ppermute x3, waiting for transfers between devices, shards(): lax.ppermute(stats, 'y', shift(NY, k))  4.11 us
    ppermute x3, starting transfers between devices, shards(): lax.ppermute(group, 'y', shift(NY, k))  3.77 us
  transfers between devices with their start and end apart: 15, of which 12 were waited for; matrix products, arithmetic and copies ran while one was open for 1% of the time, Pallas kernels for 13%

profile of v3, /device:TPU:1, one launch (start us, length us, event | category | flops | bytes accessed | tf_op | source)
XLA Modules:
  0.0 94.7 jit_solution(5018219634641920331)
XLA Ops:
  1.0 1.6 %spread.1 = bf16[8,128,256]{2,1,0:T(8,128)(2,1)} custom-call(bf16[128,128]{1,0:T(8,128)(2,1)} %k_ref.1, bf16[128,128]{1,0:T(8,128)(2,1)} %v_ref.1, bf16[1280,128]{1,0:T(8,128)(2,1)S(1)} %stack.21.rows_ref.g0), custom_call_target="tpu_custom_call" | custom-call | tf_op jit(solution)/shard_map/spread/pallas_call | solution.py:278
  2.7 9.0 %all-to-all-start = ((bf16[8,128,256]{2,1,0:T(8,128)(2,1)}), bf16[8,128,256]{2,1,0:T(8,128)(2,1)S(1)}, u32[]{:S(2)}, u32[]{:S(2)}) async-start(bf16[8,128,256]{2,1,0:T(8,128)(2,1)} %spread.1), calls=%async_computation | async-start | bytes 1048576 | tf_op jit(solution)/shard_map/all_to_all | solution.py:283
  11.7 2.7 %collective-permute-start.2 = (bf16[1280,128]{1,0:T(8,128)(2,1)S(1)}, bf16[1280,128]{1,0:T(8,128)(2,1)S(1)}, u32[]{:S(2)}, u32[]{:S(2)}) collective-permute-start(bf16[1280,128]{1,0:T(8,128)(2,1)S(1)} %stack.21.rows_ref.g0), channel_id=1, source_target_pairs={{0,24},{8,0},{16,8},{24,16},{1,25},{9,1},{17,9},{25,17},{2,26},{10... | collective-permute-start | bytes 983048 | tf_op jit(solution)/shard_map/ppermute | solution.py:282
  17.0 1.8 %plan.1.item_ref = s32[20,4]{1,0:T(8,128)S(1)} custom-call(s32[4]{0:T(128)S(1)} %pad_add_fusion.place_ref, s32[32,17]{1,0:T(8,128)S(1)} %copy.9.anc_ref, bf16[1280,128]{1,0:T(8,128)(2,1)S(1)} %stack.21.rows_ref.g0), custom_call_target="tpu_custom_call" | custom-call | tf_op jit(solution)/shard_map/plan/pallas_call | solution.py:293
  19.1 2.5 %collective-permute-done.2.g3 = bf16[1280,128]{1,0:T(8,128)(2,1)S(1)} collective-permute-done((bf16[1280,128]{1,0:T(8,128)(2,1)S(1)}, bf16[1280,128]{1,0:T(8,128)(2,1)S(1)}, u32[]{:S(2)}, u32[]{:S(2)}) %collective-permute-start.2) | collective-permute-done | bytes 327712 | tf_op jit(solution)/shard_map/ppermute | solution.py:282
  21.5 2.4 %collective-permute-done.1.g2 = bf16[1280,128]{1,0:T(8,128)(2,1)S(1)} collective-permute-done((bf16[1280,128]{1,0:T(8,128)(2,1)S(1)}, bf16[1280,128]{1,0:T(8,128)(2,1)S(1)}, u32[]{:S(2)}, u32[]{:S(2)}) %collective-permute-start.1) | collective-permute-done | bytes 327712 | tf_op jit(solution)/shard_map/ppermute | solution.py:282
  24.0 8.6 %collective-permute-done.g1 = bf16[1280,128]{1,0:T(8,128)(2,1)S(1)} collective-permute-done((bf16[1280,128]{1,0:T(8,128)(2,1)S(1)}, bf16[1280,128]{1,0:T(8,128)(2,1)S(1)}, u32[]{:S(2)}, u32[]{:S(2)}) %collective-permute-start) | collective-permute-done | bytes 327712 | tf_op jit(solution)/shard_map/ppermute | solution.py:282
  32.6 2.4 %stats.1 = (f32[4,4,640]{2,1,0:T(4,128)S(1)}, f32[16,256,640]{2,1,0:T(8,128)S(1)}, f32[16,256,640]{2,1,0:T(8,128)S(1)}) custom-call(s32[20,4]{1,0:T(8,128)S(1)} %plan.1.item_ref, bf16[8,128,256]{2,1,0:T(8,128)(2,1)S(1)} %all-to-all-done.kv_ref, bf16[1280,128]{1,0:T(8,128)(2,1)S(1)} %stack.21.rows_ref.g0, bf16[1280,128]{1,0:T(8,128)(2,1)S(1)} %collective-permute-done.g1, ...), custom_call_target="tpu_custom_call" | custom-call | tf_op jit(solution)/shard_map/stats/pallas_call | solution.py:304
  35.2 1.4 %collective-permute-start.3 = (f32[4,4,640]{2,1,0:T(4,128)S(1)}, f32[4,4,640]{2,1,0:T(4,128)S(1)}, u32[]{:S(2)}, u32[]{:S(2)}) collective-permute-start(f32[4,4,640]{2,1,0:T(4,128)S(1)} %get-tuple-element.21.stat_ref.s0), channel_id=1, source_target_pairs={{0,8},{8,16},{16,24},{24,0},{1,9},{9,17},{17,25},{25,1},{2,10},{10... | collective-permute-start | bytes 122888 | tf_op jit(solution)/shard_map/ppermute | solution.py:311
  36.7 1.3 %collective-permute-done.5.s3 = f32[4,4,640]{2,1,0:T(4,128)S(1)} collective-permute-done((f32[4,4,640]{2,1,0:T(4,128)S(1)}, f32[4,4,640]{2,1,0:T(4,128)S(1)}, u32[]{:S(2)}, u32[]{:S(2)}) %collective-permute-start.5) | collective-permute-done | bytes 40992 | tf_op jit(solution)/shard_map/ppermute | solution.py:311
  38.0 1.6 %collective-permute-done.4.s2 = f32[4,4,640]{2,1,0:T(4,128)S(1)} collective-permute-done((f32[4,4,640]{2,1,0:T(4,128)S(1)}, f32[4,4,640]{2,1,0:T(4,128)S(1)}, u32[]{:S(2)}, u32[]{:S(2)}) %collective-permute-start.4) | collective-permute-done | bytes 40992 | tf_op jit(solution)/shard_map/ppermute | solution.py:311
  39.6 1.2 %collective-permute-done.3.s1 = f32[4,4,640]{2,1,0:T(4,128)S(1)} collective-permute-done((f32[4,4,640]{2,1,0:T(4,128)S(1)}, f32[4,4,640]{2,1,0:T(4,128)S(1)}, u32[]{:S(2)}, u32[]{:S(2)}) %collective-permute-start.3) | collective-permute-done | bytes 40992 | tf_op jit(solution)/shard_map/ppermute | solution.py:311
  40.8 3.0 %grads.1 = (bf16[8,128,256]{2,1,0:T(8,128)(2,1)S(1)}, bf16[128,640]{1,0:T(8,128)(2,1)S(1)}, bf16[128,640]{1,0:T(8,128)(2,1)S(1)}, bf16[128,640]{1,0:T(8,128)(2,1)S(1)}, bf16[128,640]{1,0:T(8,128)(2,1)S(1)}) custom-call(s32[20,4]{1,0:T(8,128)S(1)} %plan.1.item_ref, bf16[8,128,128]{2,1,0:T(8,128)(2,1)S(1)} %turn.1.cols_ref, ...), custom_call_target="tpu_custom_call" | custom-call | tf_op jit(solution)/shard_map/grads/pallas_call | solution.py:315
  44.6 8.5 %all-to-all-start.1 = ((bf16[8,128,256]{2,1,0:T(8,128)(2,1)}), bf16[8,128,256]{2,1,0:T(8,128)(2,1)S(1)}, u32[]{:S(2)}, u32[]{:S(2)}) async-start(bf16[8,128,256]{2,1,0:T(8,128)(2,1)} %flush.1), calls=%async_computation.1 | async-start | bytes 1048576 | tf_op jit(solution)/shard_map/all_to_all | solution.py:327
  54.6 2.7 %collective-permute-done.6.q1 = bf16[128,640]{1,0:T(8,128)(2,1)S(1)} collective-permute-done((bf16[128,640]{1,0:T(8,128)(2,1)S(1)}, bf16[128,640]{1,0:T(8,128)(2,1)S(1)}, u32[]{:S(2)}, u32[]{:S(2)}) %collective-permute-start.6) | collective-permute-done | bytes 163872 | tf_op jit(solution)/shard_map/ppermute | solution.py:323
  57.3 2.3 %collective-permute-done.7.q2 = bf16[128,640]{1,0:T(8,128)(2,1)S(1)} collective-permute-done((bf16[128,640]{1,0:T(8,128)(2,1)S(1)}, bf16[128,640]{1,0:T(8,128)(2,1)S(1)}, u32[]{:S(2)}, u32[]{:S(2)}) %collective-permute-start.7) | collective-permute-done | bytes 163872 | tf_op jit(solution)/shard_map/ppermute | solution.py:323
  59.6 3.8 %collective-permute-done.8.q3 = bf16[128,640]{1,0:T(8,128)(2,1)S(1)} collective-permute-done((bf16[128,640]{1,0:T(8,128)(2,1)S(1)}, bf16[128,640]{1,0:T(8,128)(2,1)S(1)}, u32[]{:S(2)}, u32[]{:S(2)}) %collective-permute-start.8) | collective-permute-done | bytes 163872 | tf_op jit(solution)/shard_map/ppermute | solution.py:323
  63.4 7.4 %query_part.1.part_ref = f32[8,640,128]{2,1,0:T(8,128)S(1)} custom-call(s32[4]{0:T(128)S(1)} %pad_add_fusion.place_ref, f32[64,128]{1,0:T(8,128)S(1)} %get-tuple-element.18.cos_ref, f32[64,128]{1,0:T(8,128)S(1)} %get-tuple-element.19.sin_ref, bf16[128,640]{1,0:T(8,128)(2,1)S(1)} %get-tuple-element.25.q0, bf16[128,640]{1,0:T(8,128)(2,1)S(1)} %collective-permute-done.6.q1, ...), custom_call_target="tpu_custom_call" | custom-call | tf_op jit(solution)/shard_map/query_part/pallas_call | solution.py:330
  70.8 3.5 %first_half.1 = (bf16[4,640,128]{2,1,0:T(8,128)(2,1)S(1)}, bf16[256,128]{1,0:T(8,128)(2,1)S(1)}) custom-call(s32[4]{0:T(128)S(1)} %pad_add_fusion.place_ref, f32[64,128]{1,0:T(8,128)S(1)} %get-tuple-element.18.cos_ref, f32[64,128]{1,0:T(8,128)S(1)} %get-tuple-element.19.sin_ref, bf16[8,128,256]{2,1,0:T(8,128)(2,1)S(1)} %all-to-all-done.1.dkv_ref, ...), custom_call_target="tpu_custom_call" | custom-call | tf_op jit(solution)/shard_map/first_half/pallas_call | solution.py:339
  74.3 2.3 %collective-permute-start.9 = (bf16[4,640,128]{2,1,0:T(8,128)(2,1)S(1)}, bf16[4,640,128]{2,1,0:T(8,128)(2,1)S(1)}, u32[]{:S(2)}, u32[]{:S(2)}) collective-permute-start(bf16[4,640,128]{2,1,0:T(8,128)(2,1)S(1)} %get-tuple-element.30), channel_id=1, source_target_pairs={{0,1},{1,0},{2,3},{3,2},{4,5},{5,4},{6,7},{7,6},{8,9},{9,8},{10,11... | collective-permute-start | bytes 1966088 | tf_op jit(solution)/shard_map/ppermute | solution.py:347
  76.7 3.3 %second_half.1 = f32[4,640,128]{2,1,0:T(8,128)S(1)} custom-call(s32[4]{0:T(128)S(1)} %pad_add_fusion.place_ref, bf16[256,128]{1,0:T(8,128)(2,1)S(1)} %get-tuple-element.29.low_ref, f32[8,640,128]{2,1,0:T(8,128)S(1)} %query_part.1.part_ref, bf16[5120,128]{1,0:T(8,128)(2,1)} %wk.3, bf16[5120,128]{1,0:T(8,128)(2,1)} %wv.3), custom_call_target="tpu_custom_call" | custom-call | tf_op jit(solution)/shard_map/second_half/pallas_call | solution.py:348
  80.1 2.6 %collective-permute-start.12 = (bf16[640,128]{1,0:T(8,128)(2,1)S(1)}, bf16[640,128]{1,0:T(8,128)(2,1)S(1)}, u32[]{:S(2)}, u32[]{:S(2)}) collective-permute-start(bf16[640,128]{1,0:T(8,128)(2,1)S(1)} %get-tuple-element.31), channel_id=1, source_target_pairs={{0,6},{2,0},{4,2},{6,4},{1,7},{3,1},{5,3},{7,5},{8,14},{10,8},{12,... | collective-permute-start | bytes 491528 | tf_op jit(solution)/shard_map/ppermute | solution.py:357
  83.8 5.8 %collective-permute-done.12.p2 = bf16[640,128]{1,0:T(8,128)(2,1)S(1)} collective-permute-done((bf16[640,128]{1,0:T(8,128)(2,1)S(1)}, bf16[640,128]{1,0:T(8,128)(2,1)S(1)}, u32[]{:S(2)}, u32[]{:S(2)}) %collective-permute-start.12) | collective-permute-done | bytes 163872 | tf_op jit(solution)/shard_map/ppermute | solution.py:357
  89.7 4.1 %collective-permute-done.10.p0 = bf16[640,128]{1,0:T(8,128)(2,1)S(1)} collective-permute-done((bf16[640,128]{1,0:T(8,128)(2,1)S(1)}, bf16[640,128]{1,0:T(8,128)(2,1)S(1)}, u32[]{:S(2)}, u32[]{:S(2)}) %collective-permute-start.10) | collective-permute-done | bytes 163872 | tf_op jit(solution)/shard_map/ppermute | solution.py:357
  (27 shorter events, 7.9 us)
Async XLA Ops:
  0.0 15.5 %copy-start = (s32[32,17]{0,1:T(8,128)S(1)}, s32[32,17]{0,1:T(8,128)}, u32[]{:S(2)}) copy-start(s32[32,17]{0,1:T(8,128)} %param.12) | copy-start | bytes 6532
  2.7 29.9 %all-to-all-start = ((bf16[8,128,256]{2,1,0:T(8,128)(2,1)}), bf16[8,128,256]{2,1,0:T(8,128)(2,1)S(1)}, u32[]{:S(2)}, u32[]{:S(2)}) async-start(bf16[8,128,256]{2,1,0:T(8,128)(2,1)} %spread.1), calls=%async_computation | async-start | bytes 1048576 | tf_op jit(solution)/shard_map/all_to_all | solution.py:283
  11.7 9.8 %collective-permute-start.2 = (bf16[1280,128]{1,0:T(8,128)(2,1)S(1)}, bf16[1280,128]{1,0:T(8,128)(2,1)S(1)}, u32[]{:S(2)}, u32[]{:S(2)}) collective-permute-start(bf16[1280,128]{1,0:T(8,128)(2,1)S(1)} %stack.21.rows_ref.g0), channel_id=1, source_target_pairs={{0,24},{8,0},{16,8},{24,16},{1,25},{9,1},{17,9},{25,17},{2,26},{10... | collective-permute-start | bytes 983048 | tf_op jit(solution)/shard_map/ppermute | solution.py:282
  14.4 9.5 %collective-permute-start.1 = (bf16[1280,128]{1,0:T(8,128)(2,1)S(1)}, bf16[1280,128]{1,0:T(8,128)(2,1)S(1)}, u32[]{:S(2)}, u32[]{:S(2)}) collective-permute-start(bf16[1280,128]{1,0:T(8,128)(2,1)S(1)} %stack.21.rows_ref.g0), channel_id=1, source_target_pairs={{0,16},{8,24},{16,0},{24,8},{1,17},{9,25},{17,1},{25,9},{2,18},{10... | collective-permute-start | bytes 983048 | tf_op jit(solution)/shard_map/ppermute | solution.py:282
  14.8 17.8 %collective-permute-start = (bf16[1280,128]{1,0:T(8,128)(2,1)S(1)}, bf16[1280,128]{1,0:T(8,128)(2,1)S(1)}, u32[]{:S(2)}, u32[]{:S(2)}) collective-permute-start(bf16[1280,128]{1,0:T(8,128)(2,1)S(1)} %stack.21.rows_ref.g0), channel_id=1, source_target_pairs={{0,8},{8,16},{16,24},{24,0},{1,9},{9,17},{17,25},{25,1},{2,10},{10... | collective-permute-start | bytes 983048 | tf_op jit(solution)/shard_map/ppermute | solution.py:282
  35.0 2.9 %collective-permute-start.5 = (f32[4,4,640]{2,1,0:T(4,128)S(1)}, f32[4,4,640]{2,1,0:T(4,128)S(1)}, u32[]{:S(2)}, u32[]{:S(2)}) collective-permute-start(f32[4,4,640]{2,1,0:T(4,128)S(1)} %get-tuple-element.21.stat_ref.s0), channel_id=1, source_target_pairs={{0,24},{8,0},{16,8},{24,16},{1,25},{9,1},{17,9},{25,17},{2,26},{10... | collective-permute-start | bytes 122888 | tf_op jit(solution)/shard_map/ppermute | solution.py:311
  35.1 4.4 %collective-permute-start.4 = (f32[4,4,640]{2,1,0:T(4,128)S(1)}, f32[4,4,640]{2,1,0:T(4,128)S(1)}, u32[]{:S(2)}, u32[]{:S(2)}) collective-permute-start(f32[4,4,640]{2,1,0:T(4,128)S(1)} %get-tuple-element.21.stat_ref.s0), channel_id=1, source_target_pairs={{0,16},{8,24},{16,0},{24,8},{1,17},{9,25},{17,1},{25,9},{2,18},{10... | collective-permute-start | bytes 122888 | tf_op jit(solution)/shard_map/ppermute | solution.py:311
  35.2 5.6 %collective-permute-start.3 = (f32[4,4,640]{2,1,0:T(4,128)S(1)}, f32[4,4,640]{2,1,0:T(4,128)S(1)}, u32[]{:S(2)}, u32[]{:S(2)}) collective-permute-start(f32[4,4,640]{2,1,0:T(4,128)S(1)} %get-tuple-element.21.stat_ref.s0), channel_id=1, source_target_pairs={{0,8},{8,16},{16,24},{24,0},{1,9},{9,17},{17,25},{25,1},{2,10},{10... | collective-permute-start | bytes 122888 | tf_op jit(solution)/shard_map/ppermute | solution.py:311
  44.6 26.2 %all-to-all-start.1 = ((bf16[8,128,256]{2,1,0:T(8,128)(2,1)}), bf16[8,128,256]{2,1,0:T(8,128)(2,1)S(1)}, u32[]{:S(2)}, u32[]{:S(2)}) async-start(bf16[8,128,256]{2,1,0:T(8,128)(2,1)} %flush.1), calls=%async_computation.1 | async-start | bytes 1048576 | tf_op jit(solution)/shard_map/all_to_all | solution.py:327
  53.1 4.2 %collective-permute-start.6 = (bf16[128,640]{1,0:T(8,128)(2,1)S(1)}, bf16[128,640]{1,0:T(8,128)(2,1)S(1)}, u32[]{:S(2)}, u32[]{:S(2)}) collective-permute-start(bf16[128,640]{1,0:T(8,128)(2,1)S(1)} %get-tuple-element.26), channel_id=1, source_target_pairs={{0,24},{8,0},{16,8},{24,16},{1,25},{9,1},{17,9},{25,17},{2,26},{10... | collective-permute-start | bytes 491528 | tf_op jit(solution)/shard_map/ppermute | solution.py:323
  53.8 5.8 %collective-permute-start.7 = (bf16[128,640]{1,0:T(8,128)(2,1)S(1)}, bf16[128,640]{1,0:T(8,128)(2,1)S(1)}, u32[]{:S(2)}, u32[]{:S(2)}) collective-permute-start(bf16[128,640]{1,0:T(8,128)(2,1)S(1)} %get-tuple-element.27), channel_id=1, source_target_pairs={{0,16},{8,24},{16,0},{24,8},{1,17},{9,25},{17,1},{25,9},{2,18},{10... | collective-permute-start | bytes 491528 | tf_op jit(solution)/shard_map/ppermute | solution.py:323
  54.5 8.9 %collective-permute-start.8 = (bf16[128,640]{1,0:T(8,128)(2,1)S(1)}, bf16[128,640]{1,0:T(8,128)(2,1)S(1)}, u32[]{:S(2)}, u32[]{:S(2)}) collective-permute-start(bf16[128,640]{1,0:T(8,128)(2,1)S(1)} %get-tuple-element.28), channel_id=1, source_target_pairs={{0,8},{8,16},{16,24},{24,0},{1,9},{9,17},{17,25},{25,1},{2,10},{10... | collective-permute-start | bytes 491528 | tf_op jit(solution)/shard_map/ppermute | solution.py:323
  74.3 5.7 %collective-permute-start.9 = (bf16[4,640,128]{2,1,0:T(8,128)(2,1)S(1)}, bf16[4,640,128]{2,1,0:T(8,128)(2,1)S(1)}, u32[]{:S(2)}, u32[]{:S(2)}) collective-permute-start(bf16[4,640,128]{2,1,0:T(8,128)(2,1)S(1)} %get-tuple-element.30), channel_id=1, source_target_pairs={{0,1},{1,0},{2,3},{3,2},{4,5},{5,4},{6,7},{7,6},{8,9},{9,8},{10,11... | collective-permute-start | bytes 1966088 | tf_op jit(solution)/shard_map/ppermute | solution.py:347
  80.1 9.5 %collective-permute-start.12 = (bf16[640,128]{1,0:T(8,128)(2,1)S(1)}, bf16[640,128]{1,0:T(8,128)(2,1)S(1)}, u32[]{:S(2)}, u32[]{:S(2)}) collective-permute-start(bf16[640,128]{1,0:T(8,128)(2,1)S(1)} %get-tuple-element.31), channel_id=1, source_target_pairs={{0,6},{2,0},{4,2},{6,4},{1,7},{3,1},{5,3},{7,5},{8,14},{10,8},{12,... | collective-permute-start | bytes 491528 | tf_op jit(solution)/shard_map/ppermute | solution.py:357
  82.7 7.0 %collective-permute-start.11 = (bf16[640,128]{1,0:T(8,128)(2,1)S(1)}, bf16[640,128]{1,0:T(8,128)(2,1)S(1)}, u32[]{:S(2)}, u32[]{:S(2)}) collective-permute-start(bf16[640,128]{1,0:T(8,128)(2,1)S(1)} %get-tuple-element.32), channel_id=1, source_target_pairs={{0,4},{2,6},{4,0},{6,2},{1,5},{3,7},{5,1},{7,3},{8,12},{10,14},{12... | collective-permute-start | bytes 491528 | tf_op jit(solution)/shard_map/ppermute | solution.py:357
  83.2 10.6 %collective-permute-start.10 = (bf16[640,128]{1,0:T(8,128)(2,1)S(1)}, bf16[640,128]{1,0:T(8,128)(2,1)S(1)}, u32[]{:S(2)}, u32[]{:S(2)}) collective-permute-start(bf16[640,128]{1,0:T(8,128)(2,1)S(1)} %get-tuple-element.33), channel_id=1, source_target_pairs={{0,2},{2,4},{4,6},{6,0},{1,3},{3,5},{5,7},{7,1},{8,10},{10,12},{12... | collective-permute-start | bytes 491528 | tf_op jit(solution)/shard_map/ppermute | solution.py:357

commit v4 on v3

--- a/solution.py
+++ b/solution.py
@@ -21,6 +21,7 @@
 NN = (((1,), (0,)), ((), ()))
 F32, BF16, I32 = jnp.float32, jnp.bfloat16, jnp.int32
 VMEM_LIMIT = 16 << 20
+PLAN_FLOPS = 15_000_000_000
 
 VM = pl.BlockSpec(memory_space=pltpu.VMEM)
 SM = pl.BlockSpec(memory_space=pltpu.SMEM)
@@ -35,7 +36,7 @@
     return lax.dot_general(a, b, NN, preferred_element_type=F32)
 
 
-def call(body, out_shape, in_specs, out_specs, name, scratch=()):
+def call(body, out_shape, in_specs, out_specs, name, scratch=(), flops=0):
     return pl.pallas_call(
         body,
         out_shape=out_shape,
@@ -43,6 +44,7 @@
         out_specs=out_specs,
         scratch_shapes=list(scratch),
         compiler_params=pltpu.CompilerParams(vmem_limit_bytes=VMEM_LIMIT),
+        cost_estimate=pl.CostEstimate(flops=flops, transcendentals=0, bytes_accessed=0) if flops else None,
         name=name,
     )
 
@@ -77,7 +79,7 @@
     run_copies([(low_ref, out_ref)], sem)
 
 
-def plan_kernel(place_ref, anc_ref, rows_ref, item_ref, list_ref):
+def plan_kernel(place_ref, anc_ref, g1, g2, g3, item_ref, list_ref):
     z = place_ref[0]
     y = place_ref[1]
     for j in range(NY):
@@ -190,40 +192,69 @@
     return jnp.concatenate([front * cosine + back * sine, back * cosine - front * sine], axis=0)
 
 
-def query_part_kernel(place_ref, cos_ref, sin_ref, q0, q1, q2, q3, wq, out_ref, low_ref):
-    @pl.when(pl.program_id(0) == 0)
-    def _():
-        cosine = cos_ref[...]
-        sine = sin_ref[...]
-        for h in range(GROUP):
-            cols = slice(h * HEAD, (h + 1) * HEAD)
-            total = q0[:, cols].astype(F32)
-            for part in (q1, q2, q3):
-                total = total + part[:, cols].astype(F32)
-            low_ref[cols, :] = unrotate(total, cosine, sine).astype(BF16)
-
-    out_ref[0] = dot_nn(wq[...], low_ref[...])
-
-
-def add_key_value(low_ref, part_ref, wk, wv):
-    total = part_ref[0] + dot_nn(wk[...], low_ref[:HEAD, :])
-    return total + dot_nn(wv[...], low_ref[HEAD:, :])
-
-
-def first_half_kernel(place_ref, cos_ref, sin_ref, dkv_ref, part_ref, wk, wv, out_ref, low_ref):
-    @pl.when(pl.program_id(0) == 0)
-    def _():
-        total = dkv_ref[0].astype(F32)
-        for a in range(1, NZ):
-            total = total + dkv_ref[a].astype(F32)
-        low_ref[:HEAD, :] = unrotate(total[:, :HEAD].T, cos_ref[...], sin_ref[...]).astype(BF16)
-        low_ref[HEAD:, :] = total[:, HEAD:].T.astype(BF16)
-
-    out_ref[0] = add_key_value(low_ref, part_ref, wk, wv).astype(BF16)
-
-
-def second_half_kernel(place_ref, low_ref, part_ref, wk, wv, out_ref):
-    out_ref[0] = add_key_value(low_ref, part_ref, wk, wv)
+def weight_rows(place_ref, step):
+    core = 1 - place_ref[3] if step < NX else place_ref[3]
+    return pl.ds(pl.multiple_of((2 * ((place_ref[2] + step) & (NX - 1)) + core) * ROWS, ROWS), ROWS)
+
+
+def query_part_kernel(place_ref, cos_ref, sin_ref, q0, q1, q2, q3, wq_hbm, out_ref, wq, sem):
+    copies = [
+        pltpu.make_async_copy(wq_hbm.at[weight_rows(place_ref, i), :], wq.at[i], sem.at[i]) for i in range(2 * NX)
+    ]
+    for copy in copies:
+        copy.start()
+    cosine = cos_ref[...]
+    sine = sin_ref[...]
+    low = []
+    for h in range(GROUP):
+        cols = slice(h * HEAD, (h + 1) * HEAD)
+        total = q0[:, cols].astype(F32)
+        for part in (q1, q2, q3):
+            total = total + part[:, cols].astype(F32)
+        low.append(unrotate(total, cosine, sine).astype(BF16))
+    low = jnp.concatenate(low, axis=0)
+    for i, copy in enumerate(copies):
+        copy.wait()
+        out_ref[i] = dot_nn(wq[i], low)
+
+
+def fetch_pair(place_ref, first, wk_hbm, wv_hbm, wk, wv, sem):
+    copies = []
+    for i in range(NX):
+        rows = weight_rows(place_ref, first + i)
+        copies.append(
+            (
+                pltpu.make_async_copy(wk_hbm.at[rows, :], wk.at[i], sem.at[2 * i]),
+                pltpu.make_async_copy(wv_hbm.at[rows, :], wv.at[i], sem.at[2 * i + 1]),
+            )
+        )
+    for pair in copies:
+        for copy in pair:
+            copy.start()
+    return copies
+
+
+def first_half_kernel(place_ref, cos_ref, sin_ref, dkv_ref, part_ref, wk_hbm, wv_hbm, out_ref, low_ref, wk, wv, sem):
+    copies = fetch_pair(place_ref, 0, wk_hbm, wv_hbm, wk, wv, sem)
+    total = dkv_ref[0].astype(F32)
+    for a in range(1, NZ):
+        total = total + dkv_ref[a].astype(F32)
+    low_ref[:HEAD, :] = unrotate(total[:, :HEAD].T, cos_ref[...], sin_ref[...]).astype(BF16)
+    low_ref[HEAD:, :] = total[:, HEAD:].T.astype(BF16)
+    for i, pair in enumerate(copies):
+        for copy in pair:
+            copy.wait()
+        total = part_ref[i] + dot_nn(wk[i], low_ref[:HEAD, :])
+        out_ref[i] = (total + dot_nn(wv[i], low_ref[HEAD:, :])).astype(BF16)
+
+
+def second_half_kernel(place_ref, low_ref, part_ref, wk_hbm, wv_hbm, out_ref, wk, wv, sem):
+    copies = fetch_pair(place_ref, NX, wk_hbm, wv_hbm, wk, wv, sem)
+    for i, pair in enumerate(copies):
+        for copy in pair:
+            copy.wait()
+        total = part_ref[NX + i] + dot_nn(wk[i], low_ref[:HEAD, :])
+        out_ref[i] = total + dot_nn(wv[i], low_ref[HEAD:, :])
 
 
 def finish_kernel(kept_ref, arrived_ref, p0, p1, p2, out_ref):
@@ -233,35 +264,6 @@
         for part in (arrived_ref, p0, p1, p2):
             total = total + part[rows, :].astype(F32)
         out_ref[:, rows] = total.T.astype(BF16)
-
-
-def weight_rows(first, width):
-    def pick(i, place):
-        step = i + first
-        core = jnp.where(step < NX, 1 - place[3], place[3])
-        return (2 * ((place[2] + step) & (NX - 1)) + core, 0)
-
-    return pl.BlockSpec((ROWS, width), pick)
-
-
-def out_rows(first):
-    return pl.BlockSpec((1, ROWS, BLOCK), lambda i, place: (i + first, 0, 0))
-
-
-def stepped(body, steps, out_shape, in_specs, out_specs, name, scratch=()):
-    return pl.pallas_call(
-        body,
-        out_shape=out_shape,
-        grid_spec=pltpu.PrefetchScalarGridSpec(
-            num_scalar_prefetch=1,
-            grid=(steps,),
-            in_specs=in_specs,
-            out_specs=out_specs,
-            scratch_shapes=list(scratch),
-        ),
-        compiler_params=pltpu.CompilerParams(vmem_limit_bytes=VMEM_LIMIT),
-        name=name,
-    )
 
 
 def shift(size, k):
@@ -293,11 +295,12 @@
     items = call(
         plan_kernel,
         jax.ShapeDtypeStruct((NY * PAIRS + NY, 4), I32),
-        [SM, SM, VM],
+        [SM, SM] + [VM] * 3,
         SM,
         "plan",
         [pltpu.SMEM((NZ + 1,), I32)],
-    )(place, ancestry, group)
+        PLAN_FLOPS,
+    )(place, ancestry, *groups[1:])
     items, cosine, sine = lax.optimization_barrier((items, cosine, sine))
 
     tiles = (NY * PAIRS, 2 * BLOCK, ROWS)
@@ -327,31 +330,31 @@
     dkv_own = lax.all_to_all(dkv, "z", 0, 0, tiled=True)
 
     wq, wk, wv = in_hbm(w_query, key_matrix, value_matrix)
-    query_part = stepped(
+    query_part = call(
         query_part_kernel,
-        2 * NX,
         pltpu.VMEM((2 * NX, ROWS, BLOCK), F32),
-        [VM] * (2 + NY) + [weight_rows(0, ROWS)],
-        out_rows(0),
+        [SM] + [VM] * (2 + NY) + [HB],
+        VM,
         "query_part",
-        [pltpu.VMEM((ROWS, BLOCK), BF16)],
+        [pltpu.VMEM((2 * NX, ROWS, ROWS), BF16), pltpu.SemaphoreType.DMA((2 * NX,))],
     )(place, cosine, sine, *dq_own, wq)
-    away, low = stepped(
+    pair_scratch = [pltpu.VMEM((NX, ROWS, HEAD), BF16)] * 2 + [pltpu.SemaphoreType.DMA((2 * NX,))]
+    away, low = call(
         first_half_kernel,
-        NX,
         [pltpu.VMEM((NX, ROWS, BLOCK), BF16), pltpu.VMEM((2 * HEAD, BLOCK), BF16)],
-        [VM] * 3 + [out_rows(0), weight_rows(0, HEAD), weight_rows(0, HEAD)],
-        [out_rows(0), VM],
+        [SM] + [VM] * 4 + [HB] * 2,
+        [VM, VM],
         "first_half",
+        pair_scratch,
     )(place, cosine, sine, dkv_own, query_part, wk, wv)
     arrived = lax.ppermute(away, "c", shift(NC, 1))
-    kept = stepped(
+    kept = call(
         second_half_kernel,
-        NX,
         pltpu.VMEM((NX, ROWS, BLOCK), F32),
-        [VM, out_rows(NX), weight_rows(NX, HEAD), weight_rows(NX, HEAD)],
-        out_rows(0),
+        [SM] + [VM] * 2 + [HB] * 2,
+        VM,
         "second_half",
+        pair_scratch,
     )(place, low, query_part, wk, wv)
     sent = [(kept[k] + arrived[k].astype(F32)).astype(BF16) for k in range(1, NX)]
     parts = [lax.ppermute(sent[k - 1], "x", shift(NX, k)) for k in range(1, NX)]

time: 95.9 us -> 92.2 us (0.961); the launches traced: 94.7 us -> 92 us
  starting transfers between devices: 30.3 us -> 33.8 us
  waiting for transfers between devices: 36.5 us -> 33.2 us
  Pallas kernels: 25.9 us -> 23.1 us
    ppermute x3, waiting for transfers between devices: 13.5 us -> 5.53 us  [shards(): lax.ppermute(group, 'y', shift(NY, k))]
    all_to_all x1, waiting for transfers between devices: 0.01 us -> 6.82 us  [shards(): kv_all = lax.all_to_all(kv, 'z', 0, 0, tiled=True)]
    ppermute x3, waiting for transfers between devices: 8.84 us -> 5.87 us  [shards(): lax.ppermute(dq_parts[k], 'y', shift(NY, -k))]
    pallas_call x3, Pallas kernels: 14.2 us -> 11.4 us  [the longest x1 5.67 us: shards(): call(query_part_kernel, pltpu.VMEM((2 * NX, ROWS, BLOCK), F32), [SM] + [V...]
    ppermute x1, starting transfers between devices: 2.31 us -> 4.29 us  [shards(): arrived = lax.ppermute(away, 'c', shift(NC, 1))]
    ppermute x3, starting transfers between devices: 1.53 us -> 3.06 us  [shards(): lax.ppermute(stats, 'y', shift(NY, k))]
    all_to_all x1, waiting for transfers between devices: 0.01 us -> 1.04 us  [shards(): dkv_own = lax.all_to_all(dkv, 'z', 0, 0, tiled=True)]
where the time goes in v4:
time: 92.2 us; the launch traced here: 92 us
  starting transfers between devices  33.8 us (37%)
  waiting for transfers between devices  33.2 us (36%)
  Pallas kernels  23.1 us (25%)
  other arithmetic  1.16 us (1%)
    ppermute x3, waiting for transfers between devices, shards(): parts = [lax.ppermute(sent[k - 1], 'x', shift(NX, k)) for k in range(1, NX)]  10 us
    all_to_all x1, starting transfers between devices, shards(): kv_all = lax.all_to_all(kv, 'z', 0, 0, tiled=True)  8.2 us
    all_to_all x1, starting transfers between devices, shards(): dkv_own = lax.all_to_all(dkv, 'z', 0, 0, tiled=True)  8.2 us
    all_to_all x1, waiting for transfers between devices, shards(): kv_all = lax.all_to_all(kv, 'z', 0, 0, tiled=True)  6.82 us
    ppermute x3, waiting for transfers between devices, shards(): lax.ppermute(dq_parts[k], 'y', shift(NY, -k))  5.87 us
    pallas_call x1, Pallas kernels, shards(): call(query_part_kernel, pltpu.VMEM((2 * NX, ROWS, BLOCK), F32), [SM] + [V...  5.67 us
    ppermute x3, waiting for transfers between devices, shards(): lax.ppermute(group, 'y', shift(NY, k))  5.53 us
    ppermute x3, starting transfers between devices, shards(): lax.ppermute(group, 'y', shift(NY, k))  4.68 us
  transfers between devices with their start and end apart: 15, of which 12 were waited for; matrix products, arithmetic and copies ran while one was open for 1% of the time, Pallas kernels for 13%

profile of v4, /device:TPU:1, one launch (start us, length us, event | category | flops | bytes accessed | tf_op | source)
XLA Modules:
  0.0 92.0 jit_solution(668761490503207201)
XLA Ops:
  1.0 3.6 %collective-permute-start.2 = (bf16[1280,128]{1,0:T(8,128)(2,1)S(1)}, bf16[1280,128]{1,0:T(8,128)(2,1)S(1)}, u32[]{:S(2)}, u32[]{:S(2)}) collective-permute-start(bf16[1280,128]{1,0:T(8,128)(2,1)S(1)} %stack.21.rows_ref.g0), channel_id=1, source_target_pairs={{0,24},{8,0},{16,8},{24,16},{1,25},{9,1},{17,9},{25,17},{2,26},{10... | collective-permute-start | bytes 983048 | tf_op jit(solution)/shard_map/ppermute | solution.py:284
  5.7 1.6 %spread.1 = bf16[8,128,256]{2,1,0:T(8,128)(2,1)} custom-call(bf16[128,128]{1,0:T(8,128)(2,1)} %k_ref.1, bf16[128,128]{1,0:T(8,128)(2,1)} %v_ref.1, bf16[1280,128]{1,0:T(8,128)(2,1)S(1)} %stack.21.rows_ref.g0), custom_call_target="tpu_custom_call" | custom-call | tf_op jit(solution)/shard_map/spread/pallas_call | solution.py:280
  7.3 8.2 %all-to-all-start = ((bf16[8,128,256]{2,1,0:T(8,128)(2,1)}), bf16[8,128,256]{2,1,0:T(8,128)(2,1)S(1)}, u32[]{:S(2)}, u32[]{:S(2)}) async-start(bf16[8,128,256]{2,1,0:T(8,128)(2,1)} %spread.1), calls=%async_computation | async-start | bytes 1048576 | tf_op jit(solution)/shard_map/all_to_all | solution.py:285
  17.9 4.9 %collective-permute-done.g1 = bf16[1280,128]{1,0:T(8,128)(2,1)S(1)} collective-permute-done((bf16[1280,128]{1,0:T(8,128)(2,1)S(1)}, bf16[1280,128]{1,0:T(8,128)(2,1)S(1)}, u32[]{:S(2)}, u32[]{:S(2)}) %collective-permute-start) | collective-permute-done | bytes 327712 | tf_op jit(solution)/shard_map/ppermute | solution.py:284
  22.8 1.8 %plan.1.item_ref = s32[20,4]{1,0:T(8,128)S(1)} custom-call(s32[4]{0:T(128)S(1)} %pad_add_fusion.place_ref, s32[32,17]{1,0:T(8,128)S(1)} %copy.9.anc_ref, bf16[1280,128]{1,0:T(8,128)(2,1)S(1)} %collective-permute-done.g1, bf16[1280,128]{1,0:T(8,128)(2,1)S(1)} %collective-permute-done.1.g2, bf16[1280,128]{1,0:T(8,128)(2,1)S(1)} %collective-permute-done.2.g3), custom_call_target="tpu_custom_call" | custom-call | flops 15000000512 | tf_op jit(solution)/shard_map/plan/pallas_call | solution.py:295
  24.7 6.8 %all-to-all-done.kv_ref = bf16[8,128,256]{2,1,0:T(8,128)(2,1)S(1)} async-done(((bf16[8,128,256]{2,1,0:T(8,128)(2,1)}), bf16[8,128,256]{2,1,0:T(8,128)(2,1)S(1)}, u32[]{:S(2)}, u32[]{:S(2)}) %all-to-all-start) | async-done | bytes 524320 | tf_op jit(solution)/shard_map/all_to_all | solution.py:285
  31.5 2.4 %stats.1 = (f32[4,4,640]{2,1,0:T(4,128)S(1)}, f32[16,256,640]{2,1,0:T(8,128)S(1)}, f32[16,256,640]{2,1,0:T(8,128)S(1)}) custom-call(s32[20,4]{1,0:T(8,128)S(1)} %plan.1.item_ref, bf16[8,128,256]{2,1,0:T(8,128)(2,1)S(1)} %all-to-all-done.kv_ref, bf16[1280,128]{1,0:T(8,128)(2,1)S(1)} %stack.21.rows_ref.g0, bf16[1280,128]{1,0:T(8,128)(2,1)S(1)} %collective-permute-done.g1, ...), custom_call_target="tpu_custom_call" | custom-call | tf_op jit(solution)/shard_map/stats/pallas_call | solution.py:307
  34.8 2.2 %collective-permute-start.4 = (f32[4,4,640]{2,1,0:T(4,128)S(1)}, f32[4,4,640]{2,1,0:T(4,128)S(1)}, u32[]{:S(2)}, u32[]{:S(2)}) collective-permute-start(f32[4,4,640]{2,1,0:T(4,128)S(1)} %get-tuple-element.21.stat_ref.s0), channel_id=1, source_target_pairs={{0,16},{8,24},{16,0},{24,8},{1,17},{9,25},{17,1},{25,9},{2,18},{10... | collective-permute-start | bytes 122888 | tf_op jit(solution)/shard_map/ppermute | solution.py:314
  37.1 2.0 %collective-permute-done.4.s2 = f32[4,4,640]{2,1,0:T(4,128)S(1)} collective-permute-done((f32[4,4,640]{2,1,0:T(4,128)S(1)}, f32[4,4,640]{2,1,0:T(4,128)S(1)}, u32[]{:S(2)}, u32[]{:S(2)}) %collective-permute-start.4) | collective-permute-done | bytes 40992 | tf_op jit(solution)/shard_map/ppermute | solution.py:314
  39.1 1.9 %collective-permute-done.3.s1 = f32[4,4,640]{2,1,0:T(4,128)S(1)} collective-permute-done((f32[4,4,640]{2,1,0:T(4,128)S(1)}, f32[4,4,640]{2,1,0:T(4,128)S(1)}, u32[]{:S(2)}, u32[]{:S(2)}) %collective-permute-start.3) | collective-permute-done | bytes 40992 | tf_op jit(solution)/shard_map/ppermute | solution.py:314
  41.0 3.0 %grads.1 = (bf16[8,128,256]{2,1,0:T(8,128)(2,1)S(1)}, bf16[128,640]{1,0:T(8,128)(2,1)S(1)}, bf16[128,640]{1,0:T(8,128)(2,1)S(1)}, bf16[128,640]{1,0:T(8,128)(2,1)S(1)}, bf16[128,640]{1,0:T(8,128)(2,1)S(1)}) custom-call(s32[20,4]{1,0:T(8,128)S(1)} %plan.1.item_ref, bf16[8,128,128]{2,1,0:T(8,128)(2,1)S(1)} %turn.1.cols_ref, ...), custom_call_target="tpu_custom_call" | custom-call | tf_op jit(solution)/shard_map/grads/pallas_call | solution.py:318
  44.9 8.2 %all-to-all-start.1 = ((bf16[8,128,256]{2,1,0:T(8,128)(2,1)}), bf16[8,128,256]{2,1,0:T(8,128)(2,1)S(1)}, u32[]{:S(2)}, u32[]{:S(2)}) async-start(bf16[8,128,256]{2,1,0:T(8,128)(2,1)} %flush.1), calls=%async_computation.1 | async-start | bytes 1048576 | tf_op jit(solution)/shard_map/all_to_all | solution.py:330
  53.1 1.6 %collective-permute-start.7 = (bf16[128,640]{1,0:T(8,128)(2,1)S(1)}, bf16[128,640]{1,0:T(8,128)(2,1)S(1)}, u32[]{:S(2)}, u32[]{:S(2)}) collective-permute-start(bf16[128,640]{1,0:T(8,128)(2,1)S(1)} %get-tuple-element.27), channel_id=1, source_target_pairs={{0,16},{8,24},{16,0},{24,8},{1,17},{9,25},{17,1},{25,9},{2,18},{10... | collective-permute-start | bytes 491528 | tf_op jit(solution)/shard_map/ppermute | solution.py:326
  54.7 2.5 %collective-permute-done.6.q1 = bf16[128,640]{1,0:T(8,128)(2,1)S(1)} collective-permute-done((bf16[128,640]{1,0:T(8,128)(2,1)S(1)}, bf16[128,640]{1,0:T(8,128)(2,1)S(1)}, u32[]{:S(2)}, u32[]{:S(2)}) %collective-permute-start.6) | collective-permute-done | bytes 163872 | tf_op jit(solution)/shard_map/ppermute | solution.py:326
  57.2 1.6 %collective-permute-done.7.q2 = bf16[128,640]{1,0:T(8,128)(2,1)S(1)} collective-permute-done((bf16[128,640]{1,0:T(8,128)(2,1)S(1)}, bf16[128,640]{1,0:T(8,128)(2,1)S(1)}, u32[]{:S(2)}, u32[]{:S(2)}) %collective-permute-start.7) | collective-permute-done | bytes 163872 | tf_op jit(solution)/shard_map/ppermute | solution.py:326
  58.9 1.7 %collective-permute-done.8.q3 = bf16[128,640]{1,0:T(8,128)(2,1)S(1)} collective-permute-done((bf16[128,640]{1,0:T(8,128)(2,1)S(1)}, bf16[128,640]{1,0:T(8,128)(2,1)S(1)}, u32[]{:S(2)}, u32[]{:S(2)}) %collective-permute-start.8) | collective-permute-done | bytes 163872 | tf_op jit(solution)/shard_map/ppermute | solution.py:326
  60.6 5.7 %query_part.1.part_ref = f32[8,640,128]{2,1,0:T(8,128)S(1)} custom-call(s32[4]{0:T(128)S(1)} %pad_add_fusion.place_ref, f32[64,128]{1,0:T(8,128)S(1)} %get-tuple-element.18.cos_ref, f32[64,128]{1,0:T(8,128)S(1)} %get-tuple-element.19.sin_ref, bf16[128,640]{1,0:T(8,128)(2,1)S(1)} %get-tuple-element.25.q0, bf16[128,640]{1,0:T(8,128)(2,1)S(1)} %collective-permute-done.6.q1, ...), custom_call_target="tpu_custom_call" | custom-call | tf_op jit(solution)/shard_map/query_part/pallas_call | solution.py:333
  66.3 1.0 %all-to-all-done.1.dkv_ref = bf16[8,128,256]{2,1,0:T(8,128)(2,1)S(1)} async-done(((bf16[8,128,256]{2,1,0:T(8,128)(2,1)}), bf16[8,128,256]{2,1,0:T(8,128)(2,1)S(1)}, u32[]{:S(2)}, u32[]{:S(2)}) %all-to-all-start.1) | async-done | bytes 524320 | tf_op jit(solution)/shard_map/all_to_all | solution.py:330
  67.3 2.9 %first_half.1 = (bf16[4,640,128]{2,1,0:T(8,128)(2,1)S(1)}, bf16[256,128]{1,0:T(8,128)(2,1)S(1)}) custom-call(s32[4]{0:T(128)S(1)} %pad_add_fusion.place_ref, f32[64,128]{1,0:T(8,128)S(1)} %get-tuple-element.18.cos_ref, f32[64,128]{1,0:T(8,128)S(1)} %get-tuple-element.19.sin_ref, bf16[8,128,256]{2,1,0:T(8,128)(2,1)S(1)} %all-to-all-done.1.dkv_ref, ...), custom_call_target="tpu_custom_call" | custom-call | tf_op jit(solution)/shard_map/first_half/pallas_call | solution.py:342
  70.2 4.3 %collective-permute-start.9 = (bf16[4,640,128]{2,1,0:T(8,128)(2,1)S(1)}, bf16[4,640,128]{2,1,0:T(8,128)(2,1)S(1)}, u32[]{:S(2)}, u32[]{:S(2)}) collective-permute-start(bf16[4,640,128]{2,1,0:T(8,128)(2,1)S(1)} %get-tuple-element.30), channel_id=1, source_target_pairs={{0,1},{1,0},{2,3},{3,2},{4,5},{5,4},{6,7},{7,6},{8,9},{9,8},{10,11... | collective-permute-start | bytes 1966088 | tf_op jit(solution)/shard_map/ppermute | solution.py:350
  74.5 2.8 %second_half.1 = f32[4,640,128]{2,1,0:T(8,128)S(1)} custom-call(s32[4]{0:T(128)S(1)} %pad_add_fusion.place_ref, bf16[256,128]{1,0:T(8,128)(2,1)S(1)} %get-tuple-element.29.low_ref, f32[8,640,128]{2,1,0:T(8,128)S(1)} %query_part.1.part_ref, bf16[5120,128]{1,0:T(8,128)(2,1)} %wk_hbm.3, bf16[5120,128]{1,0:T(8,128)(2,1)} %wv_hbm.3), custom_call_target="tpu_custom_call" | custom-call | tf_op jit(solution)/shard_map/second_half/pallas_call | solution.py:351
  77.5 2.6 %collective-permute-start.12 = (bf16[640,128]{1,0:T(8,128)(2,1)S(1)}, bf16[640,128]{1,0:T(8,128)(2,1)S(1)}, u32[]{:S(2)}, u32[]{:S(2)}) collective-permute-start(bf16[640,128]{1,0:T(8,128)(2,1)S(1)} %get-tuple-element.31), channel_id=1, source_target_pairs={{0,6},{2,0},{4,2},{6,4},{1,7},{3,1},{5,3},{7,5},{8,14},{10,8},{12,... | collective-permute-start | bytes 491528 | tf_op jit(solution)/shard_map/ppermute | solution.py:360
  81.2 5.9 %collective-permute-done.12.p2 = bf16[640,128]{1,0:T(8,128)(2,1)S(1)} collective-permute-done((bf16[640,128]{1,0:T(8,128)(2,1)S(1)}, bf16[640,128]{1,0:T(8,128)(2,1)S(1)}, u32[]{:S(2)}, u32[]{:S(2)}) %collective-permute-start.12) | collective-permute-done | bytes 163872 | tf_op jit(solution)/shard_map/ppermute | solution.py:360
  87.1 4.1 %collective-permute-done.10.p0 = bf16[640,128]{1,0:T(8,128)(2,1)S(1)} collective-permute-done((bf16[640,128]{1,0:T(8,128)(2,1)S(1)}, bf16[640,128]{1,0:T(8,128)(2,1)S(1)}, u32[]{:S(2)}, u32[]{:S(2)}) %collective-permute-start.10) | collective-permute-done | bytes 163872 | tf_op jit(solution)/shard_map/ppermute | solution.py:360
  (27 shorter events, 7.7 us)
Async XLA Ops:
  0.0 15.6 %copy-start = (s32[32,17]{0,1:T(8,128)S(1)}, s32[32,17]{0,1:T(8,128)}, u32[]{:S(2)}) copy-start(s32[32,17]{0,1:T(8,128)} %param.12) | copy-start | bytes 6532
  1.0 16.9 %collective-permute-start.2 = (bf16[1280,128]{1,0:T(8,128)(2,1)S(1)}, bf16[1280,128]{1,0:T(8,128)(2,1)S(1)}, u32[]{:S(2)}, u32[]{:S(2)}) collective-permute-start(bf16[1280,128]{1,0:T(8,128)(2,1)S(1)} %stack.21.rows_ref.g0), channel_id=1, source_target_pairs={{0,24},{8,0},{16,8},{24,16},{1,25},{9,1},{17,9},{25,17},{2,26},{10... | collective-permute-start | bytes 983048 | tf_op jit(solution)/shard_map/ppermute | solution.py:284
  4.7 13.3 %collective-permute-start.1 = (bf16[1280,128]{1,0:T(8,128)(2,1)S(1)}, bf16[1280,128]{1,0:T(8,128)(2,1)S(1)}, u32[]{:S(2)}, u32[]{:S(2)}) collective-permute-start(bf16[1280,128]{1,0:T(8,128)(2,1)S(1)} %stack.21.rows_ref.g0), channel_id=1, source_target_pairs={{0,16},{8,24},{16,0},{24,8},{1,17},{9,25},{17,1},{25,9},{2,18},{10... | collective-permute-start | bytes 983048 | tf_op jit(solution)/shard_map/ppermute | solution.py:284
  5.0 17.8 %collective-permute-start = (bf16[1280,128]{1,0:T(8,128)(2,1)S(1)}, bf16[1280,128]{1,0:T(8,128)(2,1)S(1)}, u32[]{:S(2)}, u32[]{:S(2)}) collective-permute-start(bf16[1280,128]{1,0:T(8,128)(2,1)S(1)} %stack.21.rows_ref.g0), channel_id=1, source_target_pairs={{0,8},{8,16},{16,24},{24,0},{1,9},{9,17},{17,25},{25,1},{2,10},{10... | collective-permute-start | bytes 983048 | tf_op jit(solution)/shard_map/ppermute | solution.py:284
  7.3 24.1 %all-to-all-start = ((bf16[8,128,256]{2,1,0:T(8,128)(2,1)}), bf16[8,128,256]{2,1,0:T(8,128)(2,1)S(1)}, u32[]{:S(2)}, u32[]{:S(2)}) async-start(bf16[8,128,256]{2,1,0:T(8,128)(2,1)} %spread.1), calls=%async_computation | async-start | bytes 1048576 | tf_op jit(solution)/shard_map/all_to_all | solution.py:285
  33.9 3.2 %collective-permute-start.5 = (f32[4,4,640]{2,1,0:T(4,128)S(1)}, f32[4,4,640]{2,1,0:T(4,128)S(1)}, u32[]{:S(2)}, u32[]{:S(2)}) collective-permute-start(f32[4,4,640]{2,1,0:T(4,128)S(1)} %get-tuple-element.21.stat_ref.s0), channel_id=1, source_target_pairs={{0,24},{8,0},{16,8},{24,16},{1,25},{9,1},{17,9},{25,17},{2,26},{10... | collective-permute-start | bytes 122888 | tf_op jit(solution)/shard_map/ppermute | solution.py:314
  34.8 4.4 %collective-permute-start.4 = (f32[4,4,640]{2,1,0:T(4,128)S(1)}, f32[4,4,640]{2,1,0:T(4,128)S(1)}, u32[]{:S(2)}, u32[]{:S(2)}) collective-permute-start(f32[4,4,640]{2,1,0:T(4,128)S(1)} %get-tuple-element.21.stat_ref.s0), channel_id=1, source_target_pairs={{0,16},{8,24},{16,0},{24,8},{1,17},{9,25},{17,1},{25,9},{2,18},{10... | collective-permute-start | bytes 122888 | tf_op jit(solution)/shard_map/ppermute | solution.py:314
  37.0 4.1 %collective-permute-start.3 = (f32[4,4,640]{2,1,0:T(4,128)S(1)}, f32[4,4,640]{2,1,0:T(4,128)S(1)}, u32[]{:S(2)}, u32[]{:S(2)}) collective-permute-start(f32[4,4,640]{2,1,0:T(4,128)S(1)} %get-tuple-element.21.stat_ref.s0), channel_id=1, source_target_pairs={{0,8},{8,16},{16,24},{24,0},{1,9},{9,17},{17,25},{25,1},{2,10},{10... | collective-permute-start | bytes 122888 | tf_op jit(solution)/shard_map/ppermute | solution.py:314
  44.9 22.4 %all-to-all-start.1 = ((bf16[8,128,256]{2,1,0:T(8,128)(2,1)}), bf16[8,128,256]{2,1,0:T(8,128)(2,1)S(1)}, u32[]{:S(2)}, u32[]{:S(2)}) async-start(bf16[8,128,256]{2,1,0:T(8,128)(2,1)} %flush.1), calls=%async_computation.1 | async-start | bytes 1048576 | tf_op jit(solution)/shard_map/all_to_all | solution.py:330
  53.1 4.2 %collective-permute-start.6 = (bf16[128,640]{1,0:T(8,128)(2,1)S(1)}, bf16[128,640]{1,0:T(8,128)(2,1)S(1)}, u32[]{:S(2)}, u32[]{:S(2)}) collective-permute-start(bf16[128,640]{1,0:T(8,128)(2,1)S(1)} %get-tuple-element.26), channel_id=1, source_target_pairs={{0,24},{8,0},{16,8},{24,16},{1,25},{9,1},{17,9},{25,17},{2,26},{10... | collective-permute-start | bytes 491528 | tf_op jit(solution)/shard_map/ppermute | solution.py:326
  53.1 5.8 %collective-permute-start.7 = (bf16[128,640]{1,0:T(8,128)(2,1)S(1)}, bf16[128,640]{1,0:T(8,128)(2,1)S(1)}, u32[]{:S(2)}, u32[]{:S(2)}) collective-permute-start(bf16[128,640]{1,0:T(8,128)(2,1)S(1)} %get-tuple-element.27), channel_id=1, source_target_pairs={{0,16},{8,24},{16,0},{24,8},{1,17},{9,25},{17,1},{25,9},{2,18},{10... | collective-permute-start | bytes 491528 | tf_op jit(solution)/shard_map/ppermute | solution.py:326
  54.7 5.9 %collective-permute-start.8 = (bf16[128,640]{1,0:T(8,128)(2,1)S(1)}, bf16[128,640]{1,0:T(8,128)(2,1)S(1)}, u32[]{:S(2)}, u32[]{:S(2)}) collective-permute-start(bf16[128,640]{1,0:T(8,128)(2,1)S(1)} %get-tuple-element.28), channel_id=1, source_target_pairs={{0,8},{8,16},{16,24},{24,0},{1,9},{9,17},{17,25},{25,1},{2,10},{10... | collective-permute-start | bytes 491528 | tf_op jit(solution)/shard_map/ppermute | solution.py:326
  70.2 7.1 %collective-permute-start.9 = (bf16[4,640,128]{2,1,0:T(8,128)(2,1)S(1)}, bf16[4,640,128]{2,1,0:T(8,128)(2,1)S(1)}, u32[]{:S(2)}, u32[]{:S(2)}) collective-permute-start(bf16[4,640,128]{2,1,0:T(8,128)(2,1)S(1)} %get-tuple-element.30), channel_id=1, source_target_pairs={{0,1},{1,0},{2,3},{3,2},{4,5},{5,4},{6,7},{7,6},{8,9},{9,8},{10,11... | collective-permute-start | bytes 1966088 | tf_op jit(solution)/shard_map/ppermute | solution.py:350
  77.5 9.5 %collective-permute-start.12 = (bf16[640,128]{1,0:T(8,128)(2,1)S(1)}, bf16[640,128]{1,0:T(8,128)(2,1)S(1)}, u32[]{:S(2)}, u32[]{:S(2)}) collective-permute-start(bf16[640,128]{1,0:T(8,128)(2,1)S(1)} %get-tuple-element.31), channel_id=1, source_target_pairs={{0,6},{2,0},{4,2},{6,4},{1,7},{3,1},{5,3},{7,5},{8,14},{10,8},{12,... | collective-permute-start | bytes 491528 | tf_op jit(solution)/shard_map/ppermute | solution.py:360
  80.1 7.0 %collective-permute-start.11 = (bf16[640,128]{1,0:T(8,128)(2,1)S(1)}, bf16[640,128]{1,0:T(8,128)(2,1)S(1)}, u32[]{:S(2)}, u32[]{:S(2)}) collective-permute-start(bf16[640,128]{1,0:T(8,128)(2,1)S(1)} %get-tuple-element.32), channel_id=1, source_target_pairs={{0,4},{2,6},{4,0},{6,2},{1,5},{3,7},{5,1},{7,3},{8,12},{10,14},{12... | collective-permute-start | bytes 491528 | tf_op jit(solution)/shard_map/ppermute | solution.py:360
  80.6 10.6 %collective-permute-start.10 = (bf16[640,128]{1,0:T(8,128)(2,1)S(1)}, bf16[640,128]{1,0:T(8,128)(2,1)S(1)}, u32[]{:S(2)}, u32[]{:S(2)}) collective-permute-start(bf16[640,128]{1,0:T(8,128)(2,1)S(1)} %get-tuple-element.33), channel_id=1, source_target_pairs={{0,2},{2,4},{4,6},{6,0},{1,3},{3,5},{5,7},{7,1},{8,10},{10,12},{12... | collective-permute-start | bytes 491528 | tf_op jit(solution)/shard_map/ppermute | solution.py:360

commit v5 on v4

--- a/solution.py
+++ b/solution.py
@@ -21,7 +21,9 @@
 NN = (((1,), (0,)), ((), ()))
 F32, BF16, I32 = jnp.float32, jnp.bfloat16, jnp.int32
 VMEM_LIMIT = 16 << 20
-PLAN_FLOPS = 15_000_000_000
+STATS_FLOPS = 2 * 2 * (NY * ROWS) * (NZ * BLOCK) * HEAD
+GRADS_FLOPS = 3 * 2 * (NY * ROWS) * (NZ * BLOCK) * HEAD
+QUERY_FLOPS = 2 * BLOCK * ROWS * 2 * NX * ROWS
 
 VM = pl.BlockSpec(memory_space=pltpu.VMEM)
 SM = pl.BlockSpec(memory_space=pltpu.SMEM)
@@ -61,8 +63,8 @@
         copy.wait()
 
 
-def stack_kernel(q_ref, g_ref, rows_ref, sem):
-    pairs = []
+def stack_kernel(q_ref, g_ref, k_ref, v_ref, rows_ref, kv_ref, sem):
+    pairs = [(k_ref, kv_ref.at[:, 0:HEAD]), (v_ref, kv_ref.at[:, HEAD:2 * HEAD])]
     for h in range(GROUP):
         cols = slice(h * HEAD, (h + 1) * HEAD)
         pairs.append((q_ref.at[:, cols], rows_ref.at[h * BLOCK:(h + 1) * BLOCK, :]))
@@ -70,16 +72,7 @@
     run_copies(pairs, sem)
 
 
-def spread_kernel(k_ref, v_ref, rows_ref, kv_ref, pair_ref, sem):
-    run_copies([(k_ref, pair_ref.at[:, 0:HEAD]), (v_ref, pair_ref.at[:, HEAD:2 * HEAD])], sem)
-    run_copies([(pair_ref, kv_ref.at[a]) for a in range(NZ)], sem)
-
-
-def flush_kernel(low_ref, out_ref, sem):
-    run_copies([(low_ref, out_ref)], sem)
-
-
-def plan_kernel(place_ref, anc_ref, g1, g2, g3, item_ref, list_ref):
+def plan_kernel(place_ref, anc_ref, rows_ref, item_ref, list_ref):
     z = place_ref[0]
     y = place_ref[1]
     for j in range(NY):
@@ -87,11 +80,13 @@
         bits = jnp.int32(0)
         for i in range(ANC):
             key_block = anc_ref[query_block, i]
-            bits = bits | jnp.where((key_block & (NY - 1)) == y, jnp.int32(1) << (key_block >> 2), 0)
+            key_z = key_block >> 2
+            slot = 2 * ((z >> 1) - (key_z >> 1)) + ((z ^ key_z) & 1)
+            bits = bits | jnp.where((key_block & (NY - 1)) == y, jnp.int32(1) << slot, 0)
         count = jnp.int32(0)
-        for key_z in range(NZ):
-            list_ref[count] = key_z
-            count = count + ((bits >> key_z) & 1)
+        for r in range(NZ):
+            list_ref[count] = r
+            count = count + ((bits >> r) & 1)
         for p in range(PAIRS):
             row = PAIRS * j + p
             first = jnp.where(2 * p < count, list_ref[2 * p], 0)
@@ -100,12 +95,15 @@
             item_ref[row, 0] = first
             item_ref[row, 1] = second
             causal = jnp.int32(0) if j == 0 else jnp.int32(-BLOCK)
-            item_ref[row, 2] = jnp.where(first == z, causal, -BLOCK)
-            item_ref[row, 3] = jnp.where(both, jnp.where(second == z, causal, -BLOCK), BLOCK)
+            item_ref[row, 2] = jnp.where(first == 0, causal, -BLOCK)
+            item_ref[row, 3] = jnp.where(both, jnp.where(second == 0, causal, -BLOCK), BLOCK)
         item_ref[NY * PAIRS + j, 0] = (count + 1) // 2
 
 
-def stats_kernel(item_ref, kv_ref, g0, g1, g2, g3, stat_ref, score_ref, pgrad_ref):
+def stats_kernel(item_ref, k0, k1, k2, k3, g0, g1, g2, g3, stat_ref, score_ref, pgrad_ref, kv_ref):
+    for k, part in enumerate((k0, k1, k2, k3)):
+        kv_ref[2 * k] = part[:BLOCK, :]
+        kv_ref[2 * k + 1] = part[BLOCK:, :]
     key_row = lax.broadcasted_iota(I32, (BLOCK, ROWS), 0)
     query_row = lax.broadcasted_iota(I32, (BLOCK, ROWS), 1) % BLOCK
     gap = query_row - key_row
@@ -140,13 +138,19 @@
         stat_ref[j, 3:4, :] = zero
 
 
-def turn_kernel(kv_ref, stat_ref, key_cols):
-    for a in range(NZ):
-        key_cols[a] = kv_ref[a, :, :HEAD].T
+def join_kernel(own_ref, beside_ref, pair_ref):
+    pair_ref[:BLOCK, :] = own_ref[...]
+    pair_ref[BLOCK:, :] = beside_ref[...]
+
+
+def turn_kernel(k0, k1, k2, k3, stat_ref, key_cols):
+    for k, part in enumerate((k0, k1, k2, k3)):
+        key_cols[2 * k] = part[:BLOCK, :HEAD].T
+        key_cols[2 * k + 1] = part[BLOCK:, :HEAD].T
 
 
 def grads_kernel(item_ref, cols_ref, score_ref, pgrad_ref, g0, g1, g2, g3, s0, s1, s2, s3,
-                 dkv_ref, dq0, dq1, dq2, dq3, dk_acc, dv_acc):
+                 d0, d1, d2, d3, dq0, dq1, dq2, dq3, dk_acc, dv_acc):
     stats = (s0, s1, s2, s3)
     dk_acc[...] = jnp.zeros_like(dk_acc)
     dv_acc[...] = jnp.zeros_like(dv_acc)
@@ -181,9 +185,11 @@
 
         query_grad = lax.fori_loop(0, item_ref[NY * PAIRS + j, 0], step, jnp.zeros((HEAD, ROWS), F32))
         out[...] = (query_grad * FACTOR).astype(BF16)
-    for a in range(NZ):
-        dkv_ref[a, :, :HEAD] = (dk_acc[a] * FACTOR).astype(BF16)
-        dkv_ref[a, :, HEAD:] = dv_acc[a].astype(BF16)
+    for slot in range(NZ):
+        out = (d0, d1, d2, d3)[slot // 2]
+        rows = slice((slot % 2) * BLOCK, (slot % 2 + 1) * BLOCK)
+        out[rows, :HEAD] = (dk_acc[slot] * FACTOR).astype(BF16)
+        out[rows, HEAD:] = dv_acc[slot].astype(BF16)
 
 
 def unrotate(x, cosine, sine):
@@ -218,43 +224,31 @@
         out_ref[i] = dot_nn(wq[i], low)
 
 
-def fetch_pair(place_ref, first, wk_hbm, wv_hbm, wk, wv, sem):
-    copies = []
-    for i in range(NX):
-        rows = weight_rows(place_ref, first + i)
-        copies.append(
-            (
-                pltpu.make_async_copy(wk_hbm.at[rows, :], wk.at[i], sem.at[2 * i]),
-                pltpu.make_async_copy(wv_hbm.at[rows, :], wv.at[i], sem.at[2 * i + 1]),
-            )
-        )
-    for pair in copies:
-        for copy in pair:
-            copy.start()
-    return copies
-
-
-def first_half_kernel(place_ref, cos_ref, sin_ref, dkv_ref, part_ref, wk_hbm, wv_hbm, out_ref, low_ref, wk, wv, sem):
-    copies = fetch_pair(place_ref, 0, wk_hbm, wv_hbm, wk, wv, sem)
-    total = dkv_ref[0].astype(F32)
-    for a in range(1, NZ):
-        total = total + dkv_ref[a].astype(F32)
+def fold_kernel(d0, d1, d2, d3, own_ref, beside_ref):
+    total = d0[...].astype(F32)
+    for part in (d1, d2, d3):
+        total = total + part[...].astype(F32)
+    own_ref[...] = total[:BLOCK]
+    beside_ref[...] = total[BLOCK:].astype(BF16)
+
+
+def first_half_kernel(place_ref, cos_ref, sin_ref, own_ref, beside_ref, part_ref, wk, wv, out_ref, low_ref):
+    total = own_ref[...] + beside_ref[...].astype(F32)
     low_ref[:HEAD, :] = unrotate(total[:, :HEAD].T, cos_ref[...], sin_ref[...]).astype(BF16)
     low_ref[HEAD:, :] = total[:, HEAD:].T.astype(BF16)
-    for i, pair in enumerate(copies):
-        for copy in pair:
-            copy.wait()
-        total = part_ref[i] + dot_nn(wk[i], low_ref[:HEAD, :])
-        out_ref[i] = (total + dot_nn(wv[i], low_ref[HEAD:, :])).astype(BF16)
-
-
-def second_half_kernel(place_ref, low_ref, part_ref, wk_hbm, wv_hbm, out_ref, wk, wv, sem):
-    copies = fetch_pair(place_ref, NX, wk_hbm, wv_hbm, wk, wv, sem)
-    for i, pair in enumerate(copies):
-        for copy in pair:
-            copy.wait()
-        total = part_ref[NX + i] + dot_nn(wk[i], low_ref[:HEAD, :])
-        out_ref[i] = total + dot_nn(wv[i], low_ref[HEAD:, :])
+    for i in range(NX):
+        out_ref[i] = add_key_value(place_ref, i, low_ref, part_ref, wk, wv).astype(BF16)
+
+
+def second_half_kernel(place_ref, low_ref, part_ref, wk, wv, out_ref):
+    for i in range(NX):
+        out_ref[i] = add_key_value(place_ref, NX + i, low_ref, part_ref, wk, wv)
+
+
+def add_key_value(place_ref, step, low_ref, part_ref, wk, wv):
+    rows = weight_rows(place_ref, step)
+    total = part_ref[step] + dot_nn(wk[rows, :], low_ref[:HEAD, :])
+    return total + dot_nn(wv[rows, :], low_ref[HEAD:, :])
 
 
 def finish_kernel(kept_ref, arrived_ref, p0, p1, p2, out_ref):
@@ -273,16 +267,20 @@
 def shards(queries, keys, values, out_grad, ancestry, w_query, key_matrix, value_matrix):
     z, y, x, c = (lax.axis_index(name) for name in "zyxc")
     place = jnp.stack([z, y, x, c]).astype(I32)
-    group = call(
-        stack_kernel, pltpu.VMEM((2 * ROWS, HEAD), BF16), [HB] * 2, VM, "stack",
-        [pltpu.SemaphoreType.DMA((2 * GROUP,))],
-    )(*in_hbm(queries, out_grad))
-    kv = call(
-        spread_kernel, pltpu.HBM((NZ, BLOCK, 2 * HEAD), BF16), [HB, HB, VM], HB, "spread",
-        [pltpu.VMEM((BLOCK, 2 * HEAD), BF16), pltpu.SemaphoreType.DMA((NZ,))],
-    )(*in_hbm(keys, values), group)
+    group, kv = call(
+        stack_kernel,
+        [pltpu.VMEM((2 * ROWS, HEAD), BF16), pltpu.VMEM((BLOCK, 2 * HEAD), BF16)],
+        [HB] * 4,
+        [VM] * 2,
+        "stack",
+        [pltpu.SemaphoreType.DMA((2 * GROUP + 2,))],
+    )(*in_hbm(queries, out_grad, keys, values))
     groups = [group] + [lax.ppermute(group, "y", shift(NY, k)) for k in range(1, NY)]
-    kv_all = lax.all_to_all(kv, "z", 0, 0, tiled=True)
+    beside = [(i, i ^ 1) for i in range(NZ)]
+    pair_shape = pltpu.VMEM((2 * BLOCK, 2 * HEAD), BF16)
+    pair = call(join_kernel, pair_shape, [VM] * 2, VM, "join")(kv, lax.ppermute(kv, "z", beside))
+    strides = range(2, NZ, 2)
+    kvs = [pair] + [lax.ppermute(pair, "z", [(i, i + k) for i in range(NZ - k)]) for k in strides]
 
     own_block = NY * z + y
     own_row = lax.dynamic_slice_in_dim(ancestry, own_block, 1, 0)
@@ -295,41 +293,50 @@
     items = call(
         plan_kernel,
         jax.ShapeDtypeStruct((NY * PAIRS + NY, 4), I32),
-        [SM, SM] + [VM] * 3,
+        [SM, SM, VM],
         SM,
         "plan",
         [pltpu.SMEM((NZ + 1,), I32)],
-        PLAN_FLOPS,
-    )(place, ancestry, *groups[1:])
+    )(place, ancestry, group)
     items, cosine, sine = lax.optimization_barrier((items, cosine, sine))
 
     tiles = (NY * PAIRS, 2 * BLOCK, ROWS)
     stats, scores, prob_grads = call(
         stats_kernel,
         [jax.ShapeDtypeStruct((NY, 4, ROWS), F32), pltpu.VMEM(tiles, F32), pltpu.VMEM(tiles, F32)],
-        [SM] + [VM] * (1 + NY),
+        [SM] + [VM] * (NZ // 2 + NY),
         [VM] * 3,
         "stats",
-    )(items, kv_all, *groups)
+        [pltpu.VMEM((NZ, BLOCK, 2 * HEAD), BF16)],
+        STATS_FLOPS,
+    )(items, *kvs, *groups)
     all_stats = [stats] + [lax.ppermute(stats, "y", shift(NY, k)) for k in range(1, NY)]
     key_cols = call(
-        turn_kernel, pltpu.VMEM((NZ, HEAD, BLOCK), BF16), [VM, VM], VM, "turn",
-    )(kv_all, stats)
-    dkv, *dq_parts = call(
+        turn_kernel, pltpu.VMEM((NZ, HEAD, BLOCK), BF16), [VM] * (NZ // 2 + 1), VM, "turn",
+    )(*kvs, stats)
+    grads = call(
         grads_kernel,
-        [pltpu.VMEM((NZ, BLOCK, 2 * HEAD), BF16)] + [pltpu.VMEM((HEAD, ROWS), BF16)] * NY,
+        [pair_shape] * (NZ // 2) + [pltpu.VMEM((HEAD, ROWS), BF16)] * NY,
         [SM] + [VM] * (3 + 2 * NY),
-        [VM] * (1 + NY),
+        [VM] * (NZ // 2 + NY),
         "grads",
         [pltpu.VMEM((NZ, BLOCK, HEAD), F32), pltpu.VMEM((NZ, BLOCK, HEAD), F32)],
+        GRADS_FLOPS,
     )(items, key_cols, scores, prob_grads, *groups, *all_stats)
+    dkv_parts, dq_parts = grads[:NZ // 2], grads[NZ // 2:]
     dq_own = [dq_parts[0]] + [lax.ppermute(dq_parts[k], "y", shift(NY, -k)) for k in range(1, NY)]
-    dkv = call(
-        flush_kernel, pltpu.HBM(dkv.shape, BF16), [VM], HB, "flush", [pltpu.SemaphoreType.DMA((1,))],
-    )(dkv)
-    dkv_own = lax.all_to_all(dkv, "z", 0, 0, tiled=True)
-
-    wq, wk, wv = in_hbm(w_query, key_matrix, value_matrix)
+    dkv_sent = [
+        lax.ppermute(part, "z", [(i, i - k) for i in range(k, NZ)]) for k, part in zip(strides, dkv_parts[1:])
+    ]
+    own_sum, beside_sum = call(
+        fold_kernel,
+        [pltpu.VMEM((BLOCK, 2 * HEAD), F32), pltpu.VMEM((BLOCK, 2 * HEAD), BF16)],
+        [VM] * (NZ // 2),
+        [VM] * 2,
+        "fold",
+    )(dkv_parts[0], *dkv_sent)
+    beside_sum = lax.ppermute(beside_sum, "z", beside)
+
     query_part = call(
         query_part_kernel,
         pltpu.VMEM((2 * NX, ROWS, BLOCK), F32),
@@ -337,25 +344,23 @@
         VM,
         "query_part",
         [pltpu.VMEM((2 * NX, ROWS, ROWS), BF16), pltpu.SemaphoreType.DMA((2 * NX,))],
-    )(place, cosine, sine, *dq_own, wq)
-    pair_scratch = [pltpu.VMEM((NX, ROWS, HEAD), BF16)] * 2 + [pltpu.SemaphoreType.DMA((2 * NX,))]
+        QUERY_FLOPS,
+    )(place, cosine, sine, *dq_own, *in_hbm(w_query))
     away, low = call(
         first_half_kernel,
         [pltpu.VMEM((NX, ROWS, BLOCK), BF16), pltpu.VMEM((2 * HEAD, BLOCK), BF16)],
-        [SM] + [VM] * 4 + [HB] * 2,
+        [SM] + [VM] * 7,
         [VM, VM],
         "first_half",
-        pair_scratch,
-    )(place, cosine, sine, dkv_own, query_part, wk, wv)
+    )(place, cosine, sine, own_sum, beside_sum, query_part, key_matrix, value_matrix)
     arrived = lax.ppermute(away, "c", shift(NC, 1))
     kept = call(
         second_half_kernel,
         pltpu.VMEM((NX, ROWS, BLOCK), F32),
-        [SM] + [VM] * 2 + [HB] * 2,
+        [SM] + [VM] * 4,
         VM,
         "second_half",
-        pair_scratch,
-    )(place, low, query_part, wk, wv)
+    )(place, low, query_part, key_matrix, value_matrix)
     sent = [(kept[k] + arrived[k].astype(F32)).astype(BF16) for k in range(1, NX)]
     parts = [lax.ppermute(sent[k - 1], "x", shift(NX, k)) for k in range(1, NX)]
     return call(

time: 92.2 us -> 98.8 us (1.072)
  starting transfers between devices: 33.8 us -> 41.4 us
  Pallas kernels: 23.1 us -> 17.6 us
  waiting for transfers between devices: 33.2 us -> 35.7 us
    ppermute x0 -> x8, starting transfers between devices: none -> 26.8 us  [the longest x3 13 us: shards(): lax.ppermute(pair, 'z', [(i, i + k) for i in range(NZ - k)])]
    ppermute x0 -> x8, waiting for transfers between devices: none -> 21.1 us  [the longest x3 16.9 us: shards(): lax.ppermute(part, 'z', [(i, i - k) for i in range(k, NZ)])]
    all_to_all x2 -> x0, starting transfers between devices: 16.4 us -> none  [the longest x1 8.2 us: shards(): kv_all = lax.all_to_all(kv, 'z', 0, 0, tiled=True)]
    all_to_all x2 -> x0, waiting for transfers between devices: 7.85 us -> none  [the longest x1 6.82 us: shards(): kv_all = lax.all_to_all(kv, 'z', 0, 0, tiled=True)]
    ppermute x3, waiting for transfers between devices: 5.87 us -> 0.01 us  [shards(): lax.ppermute(dq_parts[k], 'y', shift(NY, -k))]
    ppermute x3, waiting for transfers between devices: 5.53 us -> 0.01 us  [shards(): lax.ppermute(group, 'y', shift(NY, k))]
    ppermute x1, starting transfers between devices: 4.29 us -> 1.64 us  [shards(): arrived = lax.ppermute(away, 'c', shift(NC, 1))]
    pallas_call x5, Pallas kernels: 6.57 us -> 4.27 us  [the longest x1 3.02 us: shards(): call(grads_kernel, [pair_shape] * (NZ // 2) + [pltpu.VMEM((HEAD, ROWS), B...]
  transfers between devices with their start and end apart: 15 -> 21, of which waited for: 12 -> 11; matrix products, arithmetic and copies ran while one was open for 1% -> 3% of each run, Pallas kernels for 13% -> 9%
where the time goes in v5:
time: 98.8 us; the launch traced here: 98.2 us
  starting transfers between devices  41.4 us (42%)
  waiting for transfers between devices  35.7 us (36%)
  Pallas kernels  17.6 us (18%)
  other arithmetic  1.81 us (2%)
    ppermute x3, waiting for transfers between devices, shards(): lax.ppermute(part, 'z', [(i, i - k) for i in range(k, NZ)])  16.9 us
    ppermute x3, starting transfers between devices, shards(): lax.ppermute(pair, 'z', [(i, i + k) for i in range(NZ - k)])  13 us
    ppermute x3, waiting for transfers between devices, shards(): parts = [lax.ppermute(sent[k - 1], 'x', shift(NX, k)) for k in range(1, NX)]  10 us
    ppermute x1, starting transfers between devices, shards(): beside_sum = lax.ppermute(beside_sum, 'z', beside)  8.29 us
    pallas_call x1, Pallas kernels, shards(): call(query_part_kernel, pltpu.VMEM((2 * NX, ROWS, BLOCK), F32), [SM] + [V...  5.89 us
    ppermute x3, starting transfers between devices, shards(): lax.ppermute(group, 'y', shift(NY, k))  4.68 us
    ppermute x3, waiting for transfers between devices, shards(): lax.ppermute(stats, 'y', shift(NY, k))  3.93 us
    ppermute x3, starting transfers between devices, shards(): lax.ppermute(part, 'z', [(i, i - k) for i in range(k, NZ)])  3.85 us
  transfers between devices with their start and end apart: 21, of which 11 were waited for; matrix products, arithmetic and copies ran while one was open for 3% of the time, Pallas kernels for 9%

profile of v5, /device:TPU:1, one launch (start us, length us, event | category | flops | bytes accessed | tf_op | source)
XLA Modules:
  0.0 98.2 jit_solution(15006576691585739014)
XLA Ops:
  1.1 3.6 %collective-permute-start.6 = (bf16[1280,128]{1,0:T(8,128)(2,1)S(1)}, bf16[1280,128]{1,0:T(8,128)(2,1)S(1)}, u32[]{:S(2)}, u32[]{:S(2)}) collective-permute-start(bf16[1280,128]{1,0:T(8,128)(2,1)S(1)} %get-tuple-element.25.rows_ref.g0), channel_id=1, source_target_pairs={{0,24},{8,0},{16,8},{24,16},{1,25},{9,1},{17,9},{25,17},{2,26},{10... | collective-permute-start | bytes 983048 | tf_op jit(solution)/shard_map/ppermute | solution.py:278
  5.7 1.6 %collective-permute-start = (bf16[128,256]{1,0:T(8,128)(2,1)S(1)}, bf16[128,256]{1,0:T(8,128)(2,1)S(1)}, u32[]{:S(2)}, u32[]{:S(2)}) collective-permute-start(bf16[128,256]{1,0:T(8,128)(2,1)S(1)} %get-tuple-element.29.own_ref), channel_id=1, source_target_pairs={{0,32},{32,0},{64,96},{96,64},{128,160},{160,128},{192,224},{224,1... | collective-permute-start | bytes 196616 | tf_op jit(solution)/shard_map/ppermute | solution.py:281
  7.4 1.9 %collective-permute-done.beside_ref = bf16[128,256]{1,0:T(8,128)(2,1)S(1)} collective-permute-done((bf16[128,256]{1,0:T(8,128)(2,1)S(1)}, bf16[128,256]{1,0:T(8,128)(2,1)S(1)}, u32[]{:S(2)}, u32[]{:S(2)}) %collective-permute-start) | collective-permute-done | bytes 65568 | tf_op jit(solution)/shard_map/ppermute | solution.py:281
  9.3 7.8 %collective-permute-start.3 = (bf16[256,256]{1,0:T(8,128)(2,1)S(1)}, bf16[256,256]{1,0:T(8,128)(2,1)S(1)}, u32[]{:S(2)}, u32[]{:S(2)}) collective-permute-start(bf16[256,256]{1,0:T(8,128)(2,1)S(1)} %join.1.k0), channel_id=1, source_target_pairs={{0,192},{32,224},{1,193},{33,225},{2,194},{34,226},{3,195},{35,227... | collective-permute-start | bytes 393224 | tf_op jit(solution)/shard_map/ppermute | solution.py:283
  18.0 1.4 %convert_reduce_fusion = s32[]{:T(128)} fusion(s32[32,17]{0,1:T(8,128)} %param.12, s32[]{:T(128)S(6)} %select_n.3, s32[]{:T(128)S(6)} %add.28), kind=kLoop, calls=%fused_computation.13 | loop fusion | flops 50 | bytes 80 | tf_op jit(solution)/shard_map/reduce_sum | solution.py:287
  20.0 2.0 %plan.1.item_ref = s32[20,4]{1,0:T(8,128)S(1)} custom-call(s32[4]{0:T(128)S(1)} %pad_add_fusion.place_ref, s32[32,17]{1,0:T(8,128)S(1)} %copy.9.anc_ref, bf16[1280,128]{1,0:T(8,128)(2,1)S(1)} %get-tuple-element.25.rows_ref.g0), custom_call_target="tpu_custom_call" | custom-call | tf_op jit(solution)/shard_map/plan/pallas_call | solution.py:293
  22.0 1.6 %collective-permute-start.2 = (bf16[256,256]{1,0:T(8,128)(2,1)S(1)}, bf16[256,256]{1,0:T(8,128)(2,1)S(1)}, u32[]{:S(2)}, u32[]{:S(2)}) collective-permute-start(bf16[256,256]{1,0:T(8,128)(2,1)S(1)} %join.1.k0), channel_id=1, source_target_pairs={{0,128},{32,160},{64,192},{96,224},{1,129},{33,161},{65,193},{97,2... | collective-permute-start | bytes 393224 | tf_op jit(solution)/shard_map/ppermute | solution.py:283
  23.6 3.7 %collective-permute-start.1 = (bf16[256,256]{1,0:T(8,128)(2,1)S(1)}, bf16[256,256]{1,0:T(8,128)(2,1)S(1)}, u32[]{:S(2)}, u32[]{:S(2)}) collective-permute-start(bf16[256,256]{1,0:T(8,128)(2,1)S(1)} %join.1.k0), channel_id=1, source_target_pairs={{0,64},{32,96},{64,128},{96,160},{128,192},{160,224},{1,65},{33,97... | collective-permute-start | bytes 393224 | tf_op jit(solution)/shard_map/ppermute | solution.py:283
  27.5 2.2 %collective-permute-done.1.k1 = bf16[256,256]{1,0:T(8,128)(2,1)S(1)} collective-permute-done((bf16[256,256]{1,0:T(8,128)(2,1)S(1)}, bf16[256,256]{1,0:T(8,128)(2,1)S(1)}, u32[]{:S(2)}, u32[]{:S(2)}) %collective-permute-start.1) | collective-permute-done | bytes 131104 | tf_op jit(solution)/shard_map/ppermute | solution.py:283
  29.8 2.5 %stats.1 = (f32[4,4,640]{2,1,0:T(4,128)S(1)}, f32[16,256,640]{2,1,0:T(8,128)S(1)}, f32[16,256,640]{2,1,0:T(8,128)S(1)}) custom-call(s32[20,4]{1,0:T(8,128)S(1)} %plan.1.item_ref, bf16[256,256]{1,0:T(8,128)(2,1)S(1)} %join.1.k0, bf16[256,256]{1,0:T(8,128)(2,1)S(1)} %collective-permute-done.1.k1, bf16[256,256]{1,0:T(8,128)(2,1)S(1)} %collective-permute-done.2.k2, ...), custom_call_target="tpu_custom_call" | custom-call | flops 1342177280 | tf_op jit(solution)/shard_map/stats/pallas_call | solution.py:304
  33.1 2.2 %collective-permute-start.8 = (f32[4,4,640]{2,1,0:T(4,128)S(1)}, f32[4,4,640]{2,1,0:T(4,128)S(1)}, u32[]{:S(2)}, u32[]{:S(2)}) collective-permute-start(f32[4,4,640]{2,1,0:T(4,128)S(1)} %get-tuple-element.30.stat_ref.s0), channel_id=1, source_target_pairs={{0,16},{8,24},{16,0},{24,8},{1,17},{9,25},{17,1},{25,9},{2,18},{10... | collective-permute-start | bytes 122888 | tf_op jit(solution)/shard_map/ppermute | solution.py:313
  35.5 2.0 %collective-permute-done.8.s2 = f32[4,4,640]{2,1,0:T(4,128)S(1)} collective-permute-done((f32[4,4,640]{2,1,0:T(4,128)S(1)}, f32[4,4,640]{2,1,0:T(4,128)S(1)}, u32[]{:S(2)}, u32[]{:S(2)}) %collective-permute-start.8) | collective-permute-done | bytes 40992 | tf_op jit(solution)/shard_map/ppermute | solution.py:313
  37.5 1.9 %collective-permute-done.7.s1 = f32[4,4,640]{2,1,0:T(4,128)S(1)} collective-permute-done((f32[4,4,640]{2,1,0:T(4,128)S(1)}, f32[4,4,640]{2,1,0:T(4,128)S(1)}, u32[]{:S(2)}, u32[]{:S(2)}) %collective-permute-start.7) | collective-permute-done | bytes 40992 | tf_op jit(solution)/shard_map/ppermute | solution.py:313
  39.4 3.0 %grads.1 = (bf16[256,256]{1,0:T(8,128)(2,1)S(1)}, bf16[256,256]{1,0:T(8,128)(2,1)S(1)}, bf16[256,256]{1,0:T(8,128)(2,1)S(1)}, bf16[256,256]{1,0:T(8,128)(2,1)S(1...) custom-call(s32[20,4]{1,0:T(8,128)S(1)} %plan.1.item_ref, ...), custom_call_target="tpu_custom_call" | custom-call | flops 2013265920 | tf_op jit(solution)/shard_map/grads/pallas_call | solution.py:317
  42.4 1.3 %collective-permute-start.10 = (bf16[256,256]{1,0:T(8,128)(2,1)S(1)}, bf16[256,256]{1,0:T(8,128)(2,1)S(1)}, u32[]{:S(2)}, u32[]{:S(2)}) collective-permute-start(bf16[256,256]{1,0:T(8,128)(2,1)S(1)} %get-tuple-element.34), channel_id=1, source_target_pairs={{64,0},{96,32},{128,64},{160,96},{192,128},{224,160},{65,1},{97,33... | collective-permute-start | bytes 393224 | tf_op jit(solution)/shard_map/ppermute | solution.py:329
  46.6 8.1 %collective-permute-done.10.d1 = bf16[256,256]{1,0:T(8,128)(2,1)S(1)} collective-permute-done((bf16[256,256]{1,0:T(8,128)(2,1)S(1)}, bf16[256,256]{1,0:T(8,128)(2,1)S(1)}, u32[]{:S(2)}, u32[]{:S(2)}) %collective-permute-start.10) | collective-permute-done | bytes 131104 | tf_op jit(solution)/shard_map/ppermute | solution.py:329
  56.0 6.0 %collective-permute-done.11.d2 = bf16[256,256]{1,0:T(8,128)(2,1)S(1)} collective-permute-done((bf16[256,256]{1,0:T(8,128)(2,1)S(1)}, bf16[256,256]{1,0:T(8,128)(2,1)S(1)}, u32[]{:S(2)}, u32[]{:S(2)}) %collective-permute-start.11) | collective-permute-done | bytes 131104 | tf_op jit(solution)/shard_map/ppermute | solution.py:329
  62.0 2.7 %collective-permute-done.12.d3 = bf16[256,256]{1,0:T(8,128)(2,1)S(1)} collective-permute-done((bf16[256,256]{1,0:T(8,128)(2,1)S(1)}, bf16[256,256]{1,0:T(8,128)(2,1)S(1)}, u32[]{:S(2)}, u32[]{:S(2)}) %collective-permute-start.12) | collective-permute-done | bytes 131104 | tf_op jit(solution)/shard_map/ppermute | solution.py:329
  64.8 8.3 %collective-permute-start.13 = (bf16[128,256]{1,0:T(8,128)(2,1)S(1)}, bf16[128,256]{1,0:T(8,128)(2,1)S(1)}, u32[]{:S(2)}, u32[]{:S(2)}) collective-permute-start(bf16[128,256]{1,0:T(8,128)(2,1)S(1)} %get-tuple-element.38), channel_id=1, source_target_pairs={{0,32},{32,0},{64,96},{96,64},{128,160},{160,128},{192,224},{224,1... | collective-permute-start | bytes 196616 | tf_op jit(solution)/shard_map/ppermute | solution.py:338
  73.2 5.9 %query_part.1.part_ref = f32[8,640,128]{2,1,0:T(8,128)S(1)} custom-call(s32[4]{0:T(128)S(1)} %pad_add_fusion.place_ref, f32[64,128]{1,0:T(8,128)S(1)} %get-tuple-element.26.cos_ref, f32[64,128]{1,0:T(8,128)S(1)} %get-tuple-element.27.sin_ref, bf16[128,640]{1,0:T(8,128)(2,1)S(1)} %get-tuple-element.39.q0, bf16[128,640]{1,0:T(8,128)(2,1)S(1)} %collective-permute-done.14.q1, ...), custom_call_target="tpu_custom_call" | custom-call | flops 838860800 | tf_op jit(solution)/shard_map/query_part/pallas_call | solution.py:340
  80.2 1.6 %collective-permute-start.17 = (bf16[4,640,128]{2,1,0:T(8,128)(2,1)S(1)}, bf16[4,640,128]{2,1,0:T(8,128)(2,1)S(1)}, u32[]{:S(2)}, u32[]{:S(2)}) collective-permute-start(bf16[4,640,128]{2,1,0:T(8,128)(2,1)S(1)} %get-tuple-element.44), channel_id=1, source_target_pairs={{0,1},{1,0},{2,3},{3,2},{4,5},{5,4},{6,7},{7,6},{8,9},{9,8},{10,11... | collective-permute-start | bytes 1966088 | tf_op jit(solution)/shard_map/ppermute | solution.py:356
  83.7 2.6 %collective-permute-start.20 = (bf16[640,128]{1,0:T(8,128)(2,1)S(1)}, bf16[640,128]{1,0:T(8,128)(2,1)S(1)}, u32[]{:S(2)}, u32[]{:S(2)}) collective-permute-start(bf16[640,128]{1,0:T(8,128)(2,1)S(1)} %get-tuple-element.45), channel_id=1, source_target_pairs={{0,6},{2,0},{4,2},{6,4},{1,7},{3,1},{5,3},{7,5},{8,14},{10,8},{12,... | collective-permute-start | bytes 491528 | tf_op jit(solution)/shard_map/ppermute | solution.py:365
  87.4 5.4 %collective-permute-done.20.p2 = bf16[640,128]{1,0:T(8,128)(2,1)S(1)} collective-permute-done((bf16[640,128]{1,0:T(8,128)(2,1)S(1)}, bf16[640,128]{1,0:T(8,128)(2,1)S(1)}, u32[]{:S(2)}, u32[]{:S(2)}) %collective-permute-start.20) | collective-permute-done | bytes 163872 | tf_op jit(solution)/shard_map/ppermute | solution.py:365
  92.9 4.5 %collective-permute-done.18.p0 = bf16[640,128]{1,0:T(8,128)(2,1)S(1)} collective-permute-done((bf16[640,128]{1,0:T(8,128)(2,1)S(1)}, bf16[640,128]{1,0:T(8,128)(2,1)S(1)}, u32[]{:S(2)}, u32[]{:S(2)}) %collective-permute-start.18) | collective-permute-done | bytes 163872 | tf_op jit(solution)/shard_map/ppermute | solution.py:365
  (41 shorter events, 13.3 us)
Async XLA Ops:
  1.1 28.7 %collective-permute-start.6 = (bf16[1280,128]{1,0:T(8,128)(2,1)S(1)}, bf16[1280,128]{1,0:T(8,128)(2,1)S(1)}, u32[]{:S(2)}, u32[]{:S(2)}) collective-permute-start(bf16[1280,128]{1,0:T(8,128)(2,1)S(1)} %get-tuple-element.25.rows_ref.g0), channel_id=1, source_target_pairs={{0,24},{8,0},{16,8},{24,16},{1,25},{9,1},{17,9},{25,17},{2,26},{10... | collective-permute-start | bytes 983048 | tf_op jit(solution)/shard_map/ppermute | solution.py:278
  4.7 25.1 %collective-permute-start.5 = (bf16[1280,128]{1,0:T(8,128)(2,1)S(1)}, bf16[1280,128]{1,0:T(8,128)(2,1)S(1)}, u32[]{:S(2)}, u32[]{:S(2)}) collective-permute-start(bf16[1280,128]{1,0:T(8,128)(2,1)S(1)} %get-tuple-element.25.rows_ref.g0), channel_id=1, source_target_pairs={{0,16},{8,24},{16,0},{24,8},{1,17},{9,25},{17,1},{25,9},{2,18},{10... | collective-permute-start | bytes 983048 | tf_op jit(solution)/shard_map/ppermute | solution.py:278
  5.0 24.8 %collective-permute-start.4 = (bf16[1280,128]{1,0:T(8,128)(2,1)S(1)}, bf16[1280,128]{1,0:T(8,128)(2,1)S(1)}, u32[]{:S(2)}, u32[]{:S(2)}) collective-permute-start(bf16[1280,128]{1,0:T(8,128)(2,1)S(1)} %get-tuple-element.25.rows_ref.g0), channel_id=1, source_target_pairs={{0,8},{8,16},{16,24},{24,0},{1,9},{9,17},{17,25},{25,1},{2,10},{10... | collective-permute-start | bytes 983048 | tf_op jit(solution)/shard_map/ppermute | solution.py:278
  5.7 3.6 %collective-permute-start = (bf16[128,256]{1,0:T(8,128)(2,1)S(1)}, bf16[128,256]{1,0:T(8,128)(2,1)S(1)}, u32[]{:S(2)}, u32[]{:S(2)}) collective-permute-start(bf16[128,256]{1,0:T(8,128)(2,1)S(1)} %get-tuple-element.29.own_ref), channel_id=1, source_target_pairs={{0,32},{32,0},{64,96},{96,64},{128,160},{160,128},{192,224},{224,1... | collective-permute-start | bytes 196616 | tf_op jit(solution)/shard_map/ppermute | solution.py:281
  9.3 14.3 %collective-permute-start.3 = (bf16[256,256]{1,0:T(8,128)(2,1)S(1)}, bf16[256,256]{1,0:T(8,128)(2,1)S(1)}, u32[]{:S(2)}, u32[]{:S(2)}) collective-permute-start(bf16[256,256]{1,0:T(8,128)(2,1)S(1)} %join.1.k0), channel_id=1, source_target_pairs={{0,192},{32,224},{1,193},{33,225},{2,194},{34,226},{3,195},{35,227... | collective-permute-start | bytes 393224 | tf_op jit(solution)/shard_map/ppermute | solution.py:283
  22.0 5.5 %collective-permute-start.2 = (bf16[256,256]{1,0:T(8,128)(2,1)S(1)}, bf16[256,256]{1,0:T(8,128)(2,1)S(1)}, u32[]{:S(2)}, u32[]{:S(2)}) collective-permute-start(bf16[256,256]{1,0:T(8,128)(2,1)S(1)} %join.1.k0), channel_id=1, source_target_pairs={{0,128},{32,160},{64,192},{96,224},{1,129},{33,161},{65,193},{97,2... | collective-permute-start | bytes 393224 | tf_op jit(solution)/shard_map/ppermute | solution.py:283
  23.6 6.2 %collective-permute-start.1 = (bf16[256,256]{1,0:T(8,128)(2,1)S(1)}, bf16[256,256]{1,0:T(8,128)(2,1)S(1)}, u32[]{:S(2)}, u32[]{:S(2)}) collective-permute-start(bf16[256,256]{1,0:T(8,128)(2,1)S(1)} %join.1.k0), channel_id=1, source_target_pairs={{0,64},{32,96},{64,128},{96,160},{128,192},{160,224},{1,65},{33,97... | collective-permute-start | bytes 393224 | tf_op jit(solution)/shard_map/ppermute | solution.py:283
  32.3 3.2 %collective-permute-start.9 = (f32[4,4,640]{2,1,0:T(4,128)S(1)}, f32[4,4,640]{2,1,0:T(4,128)S(1)}, u32[]{:S(2)}, u32[]{:S(2)}) collective-permute-start(f32[4,4,640]{2,1,0:T(4,128)S(1)} %get-tuple-element.30.stat_ref.s0), channel_id=1, source_target_pairs={{0,24},{8,0},{16,8},{24,16},{1,25},{9,1},{17,9},{25,17},{2,26},{10... | collective-permute-start | bytes 122888 | tf_op jit(solution)/shard_map/ppermute | solution.py:313
  33.1 4.4 %collective-permute-start.8 = (f32[4,4,640]{2,1,0:T(4,128)S(1)}, f32[4,4,640]{2,1,0:T(4,128)S(1)}, u32[]{:S(2)}, u32[]{:S(2)}) collective-permute-start(f32[4,4,640]{2,1,0:T(4,128)S(1)} %get-tuple-element.30.stat_ref.s0), channel_id=1, source_target_pairs={{0,16},{8,24},{16,0},{24,8},{1,17},{9,25},{17,1},{25,9},{2,18},{10... | collective-permute-start | bytes 122888 | tf_op jit(solution)/shard_map/ppermute | solution.py:313
  35.3 4.1 %collective-permute-start.7 = (f32[4,4,640]{2,1,0:T(4,128)S(1)}, f32[4,4,640]{2,1,0:T(4,128)S(1)}, u32[]{:S(2)}, u32[]{:S(2)}) collective-permute-start(f32[4,4,640]{2,1,0:T(4,128)S(1)} %get-tuple-element.30.stat_ref.s0), channel_id=1, source_target_pairs={{0,8},{8,16},{16,24},{24,0},{1,9},{9,17},{17,25},{25,1},{2,10},{10... | collective-permute-start | bytes 122888 | tf_op jit(solution)/shard_map/ppermute | solution.py:313
  42.4 12.3 %collective-permute-start.10 = (bf16[256,256]{1,0:T(8,128)(2,1)S(1)}, bf16[256,256]{1,0:T(8,128)(2,1)S(1)}, u32[]{:S(2)}, u32[]{:S(2)}) collective-permute-start(bf16[256,256]{1,0:T(8,128)(2,1)S(1)} %get-tuple-element.34), channel_id=1, source_target_pairs={{64,0},{96,32},{128,64},{160,96},{192,128},{224,160},{65,1},{97,33... | collective-permute-start | bytes 393224 | tf_op jit(solution)/shard_map/ppermute | solution.py:329
  43.7 29.4 %collective-permute-start.14 = (bf16[128,640]{1,0:T(8,128)(2,1)S(1)}, bf16[128,640]{1,0:T(8,128)(2,1)S(1)}, u32[]{:S(2)}, u32[]{:S(2)}) collective-permute-start(bf16[128,640]{1,0:T(8,128)(2,1)S(1)} %get-tuple-element.40), channel_id=1, source_target_pairs={{0,24},{8,0},{16,8},{24,16},{1,25},{9,1},{17,9},{25,17},{2,26},{10... | collective-permute-start | bytes 491528 | tf_op jit(solution)/shard_map/ppermute | solution.py:327
  43.8 29.3 %collective-permute-start.15 = (bf16[128,640]{1,0:T(8,128)(2,1)S(1)}, bf16[128,640]{1,0:T(8,128)(2,1)S(1)}, u32[]{:S(2)}, u32[]{:S(2)}) collective-permute-start(bf16[128,640]{1,0:T(8,128)(2,1)S(1)} %get-tuple-element.41), channel_id=1, source_target_pairs={{0,16},{8,24},{16,0},{24,8},{1,17},{9,25},{17,1},{25,9},{2,18},{10... | collective-permute-start | bytes 491528 | tf_op jit(solution)/shard_map/ppermute | solution.py:327
  44.4 28.8 %collective-permute-start.16 = (bf16[128,640]{1,0:T(8,128)(2,1)S(1)}, bf16[128,640]{1,0:T(8,128)(2,1)S(1)}, u32[]{:S(2)}, u32[]{:S(2)}) collective-permute-start(bf16[128,640]{1,0:T(8,128)(2,1)S(1)} %get-tuple-element.42), channel_id=1, source_target_pairs={{0,8},{8,16},{16,24},{24,0},{1,9},{9,17},{17,25},{25,1},{2,10},{10... | collective-permute-start | bytes 491528 | tf_op jit(solution)/shard_map/ppermute | solution.py:327
  45.3 16.8 %collective-permute-start.11 = (bf16[256,256]{1,0:T(8,128)(2,1)S(1)}, bf16[256,256]{1,0:T(8,128)(2,1)S(1)}, u32[]{:S(2)}, u32[]{:S(2)}) collective-permute-start(bf16[256,256]{1,0:T(8,128)(2,1)S(1)} %get-tuple-element.35), channel_id=1, source_target_pairs={{128,0},{160,32},{192,64},{224,96},{129,1},{161,33},{193,65},{225,... | collective-permute-start | bytes 393224 | tf_op jit(solution)/shard_map/ppermute | solution.py:329
  54.7 10.0 %collective-permute-start.12 = (bf16[256,256]{1,0:T(8,128)(2,1)S(1)}, bf16[256,256]{1,0:T(8,128)(2,1)S(1)}, u32[]{:S(2)}, u32[]{:S(2)}) collective-permute-start(bf16[256,256]{1,0:T(8,128)(2,1)S(1)} %get-tuple-element.36), channel_id=1, source_target_pairs={{192,0},{224,32},{193,1},{225,33},{194,2},{226,34},{195,3},{227,35... | collective-permute-start | bytes 393224 | tf_op jit(solution)/shard_map/ppermute | solution.py:329
  64.8 14.2 %collective-permute-start.13 = (bf16[128,256]{1,0:T(8,128)(2,1)S(1)}, bf16[128,256]{1,0:T(8,128)(2,1)S(1)}, u32[]{:S(2)}, u32[]{:S(2)}) collective-permute-start(bf16[128,256]{1,0:T(8,128)(2,1)S(1)} %get-tuple-element.38), channel_id=1, source_target_pairs={{0,32},{32,0},{64,96},{96,64},{128,160},{160,128},{192,224},{224,1... | collective-permute-start | bytes 196616 | tf_op jit(solution)/shard_map/ppermute | solution.py:338
  73.1 5.9 %copy-start = (bf16[5120,128]{1,0:T(8,128)(2,1)S(1)}, bf16[5120,128]{1,0:T(8,128)(2,1)}, u32[]{:S(2)}) copy-start(bf16[5120,128]{1,0:T(8,128)(2,1)} %wk.3) | copy-start | bytes 3932164
  73.1 5.9 %copy-start.1 = (bf16[5120,128]{1,0:T(8,128)(2,1)S(1)}, bf16[5120,128]{1,0:T(8,128)(2,1)}, u32[]{:S(2)}) copy-start(bf16[5120,128]{1,0:T(8,128)(2,1)} %wv.3) | copy-start | bytes 3932164
  80.2 3.4 %collective-permute-start.17 = (bf16[4,640,128]{2,1,0:T(8,128)(2,1)S(1)}, bf16[4,640,128]{2,1,0:T(8,128)(2,1)S(1)}, u32[]{:S(2)}, u32[]{:S(2)}) collective-permute-start(bf16[4,640,128]{2,1,0:T(8,128)(2,1)S(1)} %get-tuple-element.44), channel_id=1, source_target_pairs={{0,1},{1,0},{2,3},{3,2},{4,5},{5,4},{6,7},{7,6},{8,9},{9,8},{10,11... | collective-permute-start | bytes 1966088 | tf_op jit(solution)/shard_map/ppermute | solution.py:356
  83.7 9.1 %collective-permute-start.20 = (bf16[640,128]{1,0:T(8,128)(2,1)S(1)}, bf16[640,128]{1,0:T(8,128)(2,1)S(1)}, u32[]{:S(2)}, u32[]{:S(2)}) collective-permute-start(bf16[640,128]{1,0:T(8,128)(2,1)S(1)} %get-tuple-element.45), channel_id=1, source_target_pairs={{0,6},{2,0},{4,2},{6,4},{1,7},{3,1},{5,3},{7,5},{8,14},{10,8},{12,... | collective-permute-start | bytes 491528 | tf_op jit(solution)/shard_map/ppermute | solution.py:365
  86.3 6.6 %collective-permute-start.19 = (bf16[640,128]{1,0:T(8,128)(2,1)S(1)}, bf16[640,128]{1,0:T(8,128)(2,1)S(1)}, u32[]{:S(2)}, u32[]{:S(2)}) collective-permute-start(bf16[640,128]{1,0:T(8,128)(2,1)S(1)} %get-tuple-element.46), channel_id=1, source_target_pairs={{0,4},{2,6},{4,0},{6,2},{1,5},{3,7},{5,1},{7,3},{8,12},{10,14},{12... | collective-permute-start | bytes 491528 | tf_op jit(solution)/shard_map/ppermute | solution.py:365
  86.8 10.6 %collective-permute-start.18 = (bf16[640,128]{1,0:T(8,128)(2,1)S(1)}, bf16[640,128]{1,0:T(8,128)(2,1)S(1)}, u32[]{:S(2)}, u32[]{:S(2)}) collective-permute-start(bf16[640,128]{1,0:T(8,128)(2,1)S(1)} %get-tuple-element.47), channel_id=1, source_target_pairs={{0,2},{2,4},{4,6},{6,0},{1,3},{3,5},{5,7},{7,1},{8,10},{10,12},{12... | collective-permute-start | bytes 491528 | tf_op jit(solution)/shard_map/ppermute | solution.py:365

commit v6 on v4

--- a/solution.py
+++ b/solution.py
@@ -21,7 +21,9 @@
 NN = (((1,), (0,)), ((), ()))
 F32, BF16, I32 = jnp.float32, jnp.bfloat16, jnp.int32
 VMEM_LIMIT = 16 << 20
-PLAN_FLOPS = 15_000_000_000
+STATS_FLOPS = 2 * 2 * (NY * ROWS) * (NZ * BLOCK) * HEAD
+GRADS_FLOPS = 3 * 2 * (NY * ROWS) * (NZ * BLOCK) * HEAD
+QUERY_FLOPS = 2 * BLOCK * ROWS * 2 * NX * ROWS
 
 VM = pl.BlockSpec(memory_space=pltpu.VMEM)
 SM = pl.BlockSpec(memory_space=pltpu.SMEM)
@@ -61,8 +63,8 @@
         copy.wait()
 
 
-def stack_kernel(q_ref, g_ref, rows_ref, sem):
-    pairs = []
+def stack_kernel(q_ref, g_ref, k_ref, v_ref, rows_ref, kv_ref, sem):
+    pairs = [(k_ref, kv_ref.at[:, 0:HEAD]), (v_ref, kv_ref.at[:, HEAD:2 * HEAD])]
     for h in range(GROUP):
         cols = slice(h * HEAD, (h + 1) * HEAD)
         pairs.append((q_ref.at[:, cols], rows_ref.at[h * BLOCK:(h + 1) * BLOCK, :]))
@@ -70,16 +72,7 @@
     run_copies(pairs, sem)
 
 
-def spread_kernel(k_ref, v_ref, rows_ref, kv_ref, pair_ref, sem):
-    run_copies([(k_ref, pair_ref.at[:, 0:HEAD]), (v_ref, pair_ref.at[:, HEAD:2 * HEAD])], sem)
-    run_copies([(pair_ref, kv_ref.at[a]) for a in range(NZ)], sem)
-
-
-def flush_kernel(low_ref, out_ref, sem):
-    run_copies([(low_ref, out_ref)], sem)
-
-
-def plan_kernel(place_ref, anc_ref, g1, g2, g3, item_ref, list_ref):
+def plan_kernel(place_ref, anc_ref, rows_ref, item_ref, list_ref):
     z = place_ref[0]
     y = place_ref[1]
     for j in range(NY):
@@ -145,6 +138,10 @@
         key_cols[a] = kv_ref[a, :, :HEAD].T
 
 
+def flush_kernel(low_ref, out_ref, sem):
+    run_copies([(low_ref, out_ref)], sem)
+
+
 def grads_kernel(item_ref, cols_ref, score_ref, pgrad_ref, g0, g1, g2, g3, s0, s1, s2, s3,
                  dkv_ref, dq0, dq1, dq2, dq3, dk_acc, dv_acc):
     stats = (s0, s1, s2, s3)
@@ -197,12 +194,25 @@
     return pl.ds(pl.multiple_of((2 * ((place_ref[2] + step) & (NX - 1)) + core) * ROWS, ROWS), ROWS)
 
 
-def query_part_kernel(place_ref, cos_ref, sin_ref, q0, q1, q2, q3, wq_hbm, out_ref, wq, sem):
-    copies = [
-        pltpu.make_async_copy(wq_hbm.at[weight_rows(place_ref, i), :], wq.at[i], sem.at[i]) for i in range(2 * NX)
-    ]
+def fetch_kernel(place_ref, dq_ref, wq_hbm, *refs):
+    blocks, sem = refs[:-1], refs[-1]
+    run_copies([(wq_hbm.at[weight_rows(place_ref, i), :], block) for i, block in enumerate(blocks)], sem)
+
+
+def start_pair(place_ref, first, wk_hbm, wv_hbm, wk, wv, sem):
+    copies = []
+    for i in range(NX):
+        rows = weight_rows(place_ref, first + i)
+        copies.append(pltpu.make_async_copy(wk_hbm.at[rows, :], wk.at[i], sem.at[2 * i]))
+        copies.append(pltpu.make_async_copy(wv_hbm.at[rows, :], wv.at[i], sem.at[2 * i + 1]))
     for copy in copies:
         copy.start()
+    return copies
+
+
+def query_part_kernel(place_ref, cos_ref, sin_ref, q0, q1, q2, q3, wk_hbm, wv_hbm, *refs):
+    blocks, out_ref, wk, wv, sem = refs[:2 * NX], *refs[2 * NX:]
+    copies = start_pair(place_ref, 0, wk_hbm, wv_hbm, wk, wv, sem)
     cosine = cos_ref[...]
     sine = sin_ref[...]
     low = []
@@ -213,48 +223,33 @@
             total = total + part[:, cols].astype(F32)
         low.append(unrotate(total, cosine, sine).astype(BF16))
     low = jnp.concatenate(low, axis=0)
-    for i, copy in enumerate(copies):
+    for i, block in enumerate(blocks):
+        out_ref[i] = dot_nn(block[...], low).astype(BF16)
+    for copy in copies:
         copy.wait()
-        out_ref[i] = dot_nn(wq[i], low)
-
-
-def fetch_pair(place_ref, first, wk_hbm, wv_hbm, wk, wv, sem):
-    copies = []
-    for i in range(NX):
-        rows = weight_rows(place_ref, first + i)
-        copies.append(
-            (
-                pltpu.make_async_copy(wk_hbm.at[rows, :], wk.at[i], sem.at[2 * i]),
-                pltpu.make_async_copy(wv_hbm.at[rows, :], wv.at[i], sem.at[2 * i + 1]),
-            )
-        )
-    for pair in copies:
-        for copy in pair:
-            copy.start()
-    return copies
-
-
-def first_half_kernel(place_ref, cos_ref, sin_ref, dkv_ref, part_ref, wk_hbm, wv_hbm, out_ref, low_ref, wk, wv, sem):
-    copies = fetch_pair(place_ref, 0, wk_hbm, wv_hbm, wk, wv, sem)
+
+
+def first_half_kernel(place_ref, cos_ref, sin_ref, dkv_ref, part_ref, wk, wv, wk_hbm, wv_hbm,
+                      out_ref, low_ref, wk_kept, wv_kept, sem):
+    copies = start_pair(place_ref, NX, wk_hbm, wv_hbm, wk_kept, wv_kept, sem)
     total = dkv_ref[0].astype(F32)
     for a in range(1, NZ):
         total = total + dkv_ref[a].astype(F32)
     low_ref[:HEAD, :] = unrotate(total[:, :HEAD].T, cos_ref[...], sin_ref[...]).astype(BF16)
     low_ref[HEAD:, :] = total[:, HEAD:].T.astype(BF16)
-    for i, pair in enumerate(copies):
-        for copy in pair:
-            copy.wait()
-        total = part_ref[i] + dot_nn(wk[i], low_ref[:HEAD, :])
-        out_ref[i] = (total + dot_nn(wv[i], low_ref[HEAD:, :])).astype(BF16)
-
-
-def second_half_kernel(place_ref, low_ref, part_ref, wk_hbm, wv_hbm, out_ref, wk, wv, sem):
-    copies = fetch_pair(place_ref, NX, wk_hbm, wv_hbm, wk, wv, sem)
-    for i, pair in enumerate(copies):
-        for copy in pair:
-            copy.wait()
-        total = part_ref[NX + i] + dot_nn(wk[i], low_ref[:HEAD, :])
-        out_ref[i] = total + dot_nn(wv[i], low_ref[HEAD:, :])
+    for i in range(NX):
+        out_ref[i] = (part_ref[i] + key_value_part(low_ref, wk[i], wv[i])).astype(BF16)
+    for copy in copies:
+        copy.wait()
+
+
+def second_half_kernel(low_ref, part_ref, wk, wv, out_ref):
+    for i in range(NX):
+        out_ref[i] = part_ref[NX + i] + key_value_part(low_ref, wk[i], wv[i])
+
+
+def key_value_part(low_ref, wk, wv):
+    return dot_nn(wk, low_ref[:HEAD, :]) + dot_nn(wv, low_ref[HEAD:, :])
 
 
 def finish_kernel(kept_ref, arrived_ref, p0, p1, p2, out_ref):
@@ -273,16 +268,16 @@
 def shards(queries, keys, values, out_grad, ancestry, w_query, key_matrix, value_matrix):
     z, y, x, c = (lax.axis_index(name) for name in "zyxc")
     place = jnp.stack([z, y, x, c]).astype(I32)
-    group = call(
-        stack_kernel, pltpu.VMEM((2 * ROWS, HEAD), BF16), [HB] * 2, VM, "stack",
-        [pltpu.SemaphoreType.DMA((2 * GROUP,))],
-    )(*in_hbm(queries, out_grad))
-    kv = call(
-        spread_kernel, pltpu.HBM((NZ, BLOCK, 2 * HEAD), BF16), [HB, HB, VM], HB, "spread",
-        [pltpu.VMEM((BLOCK, 2 * HEAD), BF16), pltpu.SemaphoreType.DMA((NZ,))],
-    )(*in_hbm(keys, values), group)
+    group, kv = call(
+        stack_kernel,
+        [pltpu.VMEM((2 * ROWS, HEAD), BF16), pltpu.VMEM((BLOCK, 2 * HEAD), BF16)],
+        [HB] * 4,
+        [VM] * 2,
+        "stack",
+        [pltpu.SemaphoreType.DMA((2 * GROUP + 2,))],
+    )(*in_hbm(queries, out_grad, keys, values))
     groups = [group] + [lax.ppermute(group, "y", shift(NY, k)) for k in range(1, NY)]
-    kv_all = lax.all_to_all(kv, "z", 0, 0, tiled=True)
+    kv_all = lax.all_gather(kv, "z", axis=0, tiled=False)
 
     own_block = NY * z + y
     own_row = lax.dynamic_slice_in_dim(ancestry, own_block, 1, 0)
@@ -295,12 +290,11 @@
     items = call(
         plan_kernel,
         jax.ShapeDtypeStruct((NY * PAIRS + NY, 4), I32),
-        [SM, SM] + [VM] * 3,
+        [SM, SM, VM],
         SM,
         "plan",
         [pltpu.SMEM((NZ + 1,), I32)],
-        PLAN_FLOPS,
-    )(place, ancestry, *groups[1:])
+    )(place, ancestry, group)
     items, cosine, sine = lax.optimization_barrier((items, cosine, sine))
 
     tiles = (NY * PAIRS, 2 * BLOCK, ROWS)
@@ -310,10 +304,12 @@
         [SM] + [VM] * (1 + NY),
         [VM] * 3,
         "stats",
+        (),
+        STATS_FLOPS,
     )(items, kv_all, *groups)
     all_stats = [stats] + [lax.ppermute(stats, "y", shift(NY, k)) for k in range(1, NY)]
     key_cols = call(
-        turn_kernel, pltpu.VMEM((NZ, HEAD, BLOCK), BF16), [VM, VM], VM, "turn",
+        turn_kernel, pltpu.VMEM((NZ, HEAD, BLOCK), BF16), [VM] * 2, VM, "turn",
     )(kv_all, stats)
     dkv, *dq_parts = call(
         grads_kernel,
@@ -322,6 +318,7 @@
         [VM] * (1 + NY),
         "grads",
         [pltpu.VMEM((NZ, BLOCK, HEAD), F32), pltpu.VMEM((NZ, BLOCK, HEAD), F32)],
+        GRADS_FLOPS,
     )(items, key_cols, scores, prob_grads, *groups, *all_stats)
     dq_own = [dq_parts[0]] + [lax.ppermute(dq_parts[k], "y", shift(NY, -k)) for k in range(1, NY)]
     dkv = call(
@@ -330,32 +327,40 @@
     dkv_own = lax.all_to_all(dkv, "z", 0, 0, tiled=True)
 
     wq, wk, wv = in_hbm(w_query, key_matrix, value_matrix)
-    query_part = call(
+    blocks = call(
+        fetch_kernel,
+        [pltpu.VMEM((ROWS, ROWS), BF16)] * (2 * NX),
+        [SM, VM, HB],
+        [VM] * (2 * NX),
+        "fetch",
+        [pltpu.SemaphoreType.DMA((2 * NX,))],
+    )(place, dq_parts[0], wq)
+    pair_shapes = [pltpu.VMEM((NX, ROWS, HEAD), BF16)] * 2
+    query_part, wk_away, wv_away = call(
         query_part_kernel,
-        pltpu.VMEM((2 * NX, ROWS, BLOCK), F32),
-        [SM] + [VM] * (2 + NY) + [HB],
-        VM,
+        [pltpu.VMEM((2 * NX, ROWS, BLOCK), BF16)] + pair_shapes,
+        [SM] + [VM] * (2 + NY) + [HB] * 2 + [VM] * (2 * NX),
+        [VM] * 3,
         "query_part",
-        [pltpu.VMEM((2 * NX, ROWS, ROWS), BF16), pltpu.SemaphoreType.DMA((2 * NX,))],
-    )(place, cosine, sine, *dq_own, wq)
-    pair_scratch = [pltpu.VMEM((NX, ROWS, HEAD), BF16)] * 2 + [pltpu.SemaphoreType.DMA((2 * NX,))]
-    away, low = call(
+        [pltpu.SemaphoreType.DMA((2 * NX,))],
+        QUERY_FLOPS,
+    )(place, cosine, sine, *dq_own, wk, wv, *blocks)
+    away, low, wk_kept, wv_kept = call(
         first_half_kernel,
-        [pltpu.VMEM((NX, ROWS, BLOCK), BF16), pltpu.VMEM((2 * HEAD, BLOCK), BF16)],
-        [SM] + [VM] * 4 + [HB] * 2,
-        [VM, VM],
+        [pltpu.VMEM((NX, ROWS, BLOCK), BF16), pltpu.VMEM((2 * HEAD, BLOCK), BF16)] + pair_shapes,
+        [SM] + [VM] * 6 + [HB] * 2,
+        [VM] * 4,
         "first_half",
-        pair_scratch,
-    )(place, cosine, sine, dkv_own, query_part, wk, wv)
+        [pltpu.SemaphoreType.DMA((2 * NX,))],
+    )(place, cosine, sine, dkv_own, query_part, wk_away, wv_away, wk, wv)
     arrived = lax.ppermute(away, "c", shift(NC, 1))
     kept = call(
         second_half_kernel,
         pltpu.VMEM((NX, ROWS, BLOCK), F32),
-        [SM] + [VM] * 2 + [HB] * 2,
+        [VM] * 4,
         VM,
         "second_half",
-        pair_scratch,
-    )(place, low, query_part, wk, wv)
+    )(low, query_part, wk_kept, wv_kept)
     sent = [(kept[k] + arrived[k].astype(F32)).astype(BF16) for k in range(1, NX)]
     parts = [lax.ppermute(sent[k - 1], "x", shift(NX, k)) for k in range(1, NX)]
     return call(

time: 92.2 us -> 97.9 us (1.062)
  blocking collectives: 0 us -> 23.8 us
  waiting for transfers between devices: 33.2 us -> 18.5 us
  Pallas kernels: 23.1 us -> 20.2 us
  starting transfers between devices: 33.8 us -> 31.1 us
    all_gather x0 -> x1, blocking collectives: none -> 23.8 us  [shards(): kv_all = lax.all_gather(kv, 'z', axis=0, tiled=False)]
    all_to_all x1 -> x0, starting transfers between devices: 8.2 us -> none  [shards(): kv_all = lax.all_to_all(kv, 'z', 0, 0, tiled=True)]
    all_to_all x1 -> x0, waiting for transfers between devices: 6.82 us -> none  [shards(): kv_all = lax.all_to_all(kv, 'z', 0, 0, tiled=True)]
    ppermute x1, starting transfers between devices: 4.29 us -> 10.2 us  [shards(): arrived = lax.ppermute(away, 'c', shift(NC, 1))]
    ppermute x3, waiting for transfers between devices: 5.53 us -> 0.01 us  [shards(): lax.ppermute(group, 'y', shift(NY, k))]
    ppermute x3, waiting for transfers between devices: 5.87 us -> 2.55 us  [shards(): lax.ppermute(dq_parts[k], 'y', shift(NY, -k))]
    pallas_call x5, Pallas kernels: 11.3 us -> 8.92 us  [the longest x1 3.8 us: shards(): call(query_part_kernel, [pltpu.VMEM((2 * NX, ROWS, BLOCK), BF16)] + pair_...]
    ppermute x1, waiting for transfers between devices: 0.01 us -> 1.24 us  [shards(): arrived = lax.ppermute(away, 'c', shift(NC, 1))]
  transfers between devices with their start and end apart: 15 -> 14, of which waited for: 12 -> 10; matrix products, arithmetic and copies ran while one was open for 1% -> 3% of each run, Pallas kernels for 13% -> 10%
where the time goes in v6:
time: 97.9 us; the launch traced here: 97 us
  starting transfers between devices  31.1 us (32%)
  blocking collectives  23.8 us (24%)
  Pallas kernels  20.2 us (21%)
  waiting for transfers between devices  18.5 us (19%)
  other arithmetic  1.88 us (2%)
    all_gather x1, blocking collectives, shards(): kv_all = lax.all_gather(kv, 'z', axis=0, tiled=False)  23.8 us
    ppermute x1, starting transfers between devices, shards(): arrived = lax.ppermute(away, 'c', shift(NC, 1))  10.2 us
    ppermute x3, waiting for transfers between devices, shards(): parts = [lax.ppermute(sent[k - 1], 'x', shift(NX, k)) for k in range(1, NX)]  10 us
    all_to_all x1, starting transfers between devices, shards(): dkv_own = lax.all_to_all(dkv, 'z', 0, 0, tiled=True)  8.22 us
    ppermute x3, starting transfers between devices, shards(): lax.ppermute(group, 'y', shift(NY, k))  4.68 us
    ppermute x3, waiting for transfers between devices, shards(): lax.ppermute(stats, 'y', shift(NY, k))  3.93 us
    pallas_call x1, Pallas kernels, shards(): call(query_part_kernel, [pltpu.VMEM((2 * NX, ROWS, BLOCK), BF16)] + pair_...  3.8 us
    ppermute x3, starting transfers between devices, shards(): parts = [lax.ppermute(sent[k - 1], 'x', shift(NX, k)) for k in range(1, NX)]  3.68 us
  transfers between devices with their start and end apart: 14, of which 10 were waited for; matrix products, arithmetic and copies ran while one was open for 3% of the time, Pallas kernels for 10%

profile of v6, /device:TPU:1, one launch (start us, length us, event | category | flops | bytes accessed | tf_op | source)
XLA Modules:
  0.0 97.0 jit_solution(13773950608770978327)
XLA Ops:
  0.0 1.0 %stack.21 = (bf16[1280,128]{1,0:T(8,128)(2,1)S(1)}, bf16[128,256]{1,0:T(8,128)(2,1)S(1)}) custom-call(bf16[128,640]{1,0:T(8,128)(2,1)} %q_ref.1, bf16[128,640]{1,0:T(8,128)(2,1)} %g_ref.1, bf16[128,128]{1,0:T(8,128)(2,1)} %k_ref.1, bf16[128,128]{1,0:T(8,128)(2,1)} %v_ref.1), custom_call_target="tpu_custom_call" | custom-call | tf_op jit(solution)/shard_map/stack/pallas_call | solution.py:271
  1.1 3.6 %collective-permute-start.2 = (bf16[1280,128]{1,0:T(8,128)(2,1)S(1)}, bf16[1280,128]{1,0:T(8,128)(2,1)S(1)}, u32[]{:S(2)}, u32[]{:S(2)}) collective-permute-start(bf16[1280,128]{1,0:T(8,128)(2,1)S(1)} %get-tuple-element.33.rows_ref.g0), channel_id=1, source_target_pairs={{0,24},{8,0},{16,8},{24,16},{1,25},{9,1},{17,9},{25,17},{2,26},{10... | collective-permute-start | bytes 983048 | tf_op jit(solution)/shard_map/ppermute | solution.py:279
  6.5 1.5 %convert_reduce_fusion = s32[]{:T(128)} fusion(s32[32,17]{0,1:T(8,128)} %param.12, s32[]{:T(128)S(6)} %select_n.3, s32[]{:T(128)S(6)} %add.28), kind=kLoop, calls=%fused_computation.13 | loop fusion | flops 50 | bytes 80 | tf_op jit(solution)/shard_map/reduce_sum | solution.py:284
  8.9 1.8 %plan.1.item_ref = s32[20,4]{1,0:T(8,128)S(1)} custom-call(s32[4]{0:T(128)S(1)} %pad_add_fusion.place_ref, s32[32,17]{1,0:T(8,128)S(1)} %copy.9.anc_ref, bf16[1280,128]{1,0:T(8,128)(2,1)S(1)} %get-tuple-element.33.rows_ref.g0), custom_call_target="tpu_custom_call" | custom-call | tf_op jit(solution)/shard_map/plan/pallas_call | solution.py:290
  10.8 23.8 %all-gather = bf16[1024,256]{1,0:T(8,128)(2,1)S(1)} all-gather(bf16[128,256]{1,0:T(8,128)(2,1)S(1)} %get-tuple-element.37), channel_id=2, replica_groups=mesh['z'=8,'y'=4,'x'=4,'c'=2] {'z'}, dimensions={0}, use_global_device_ids=true | all-gather | bytes 589824 | tf_op jit(solution)/shard_map/all_gather | solution.py:280
  34.6 2.5 %stats.1 = (f32[4,4,640]{2,1,0:T(4,128)S(1)}, f32[16,256,640]{2,1,0:T(8,128)S(1)}, f32[16,256,640]{2,1,0:T(8,128)S(1)}) custom-call(s32[20,4]{1,0:T(8,128)S(1)} %plan.1.item_ref, bf16[8,128,256]{2,1,0:T(8,128)(2,1)S(1)} %bitcast.15, bf16[1280,128]{1,0:T(8,128)(2,1)S(1)} %get-tuple-element.33.rows_ref.g0, bf16[1280,128]{1,0:T(8,128)(2,1)S(1)} %collective-permute-done.g1, ...), custom_call_target="tpu_custom_call" | custom-call | flops 1342177280 | tf_op jit(solution)/shard_map/stats/pallas_call | solution.py:301
  37.8 2.1 %collective-permute-start.4 = (f32[4,4,640]{2,1,0:T(4,128)S(1)}, f32[4,4,640]{2,1,0:T(4,128)S(1)}, u32[]{:S(2)}, u32[]{:S(2)}) collective-permute-start(f32[4,4,640]{2,1,0:T(4,128)S(1)} %get-tuple-element.38.stat_ref.s0), channel_id=1, source_target_pairs={{0,16},{8,24},{16,0},{24,8},{1,17},{9,25},{17,1},{25,9},{2,18},{10... | collective-permute-start | bytes 122888 | tf_op jit(solution)/shard_map/ppermute | solution.py:310
  40.3 1.9 %collective-permute-done.4.s2 = f32[4,4,640]{2,1,0:T(4,128)S(1)} collective-permute-done((f32[4,4,640]{2,1,0:T(4,128)S(1)}, f32[4,4,640]{2,1,0:T(4,128)S(1)}, u32[]{:S(2)}, u32[]{:S(2)}) %collective-permute-start.4) | collective-permute-done | bytes 40992 | tf_op jit(solution)/shard_map/ppermute | solution.py:310
  42.2 1.8 %collective-permute-done.3.s1 = f32[4,4,640]{2,1,0:T(4,128)S(1)} collective-permute-done((f32[4,4,640]{2,1,0:T(4,128)S(1)}, f32[4,4,640]{2,1,0:T(4,128)S(1)}, u32[]{:S(2)}, u32[]{:S(2)}) %collective-permute-start.3) | collective-permute-done | bytes 40992 | tf_op jit(solution)/shard_map/ppermute | solution.py:310
  44.0 3.0 %grads.1 = (bf16[8,128,256]{2,1,0:T(8,128)(2,1)S(1)}, bf16[128,640]{1,0:T(8,128)(2,1)S(1)}, bf16[128,640]{1,0:T(8,128)(2,1)S(1)}, bf16[128,640]{1,0:T(8,128)(2,1)S(1)}, bf16[128,640]{1,0:T(8,128)(2,1)S(1)}) custom-call(s32[20,4]{1,0:T(8,128)S(1)} %plan.1.item_ref, bf16[8,128,128]{2,1,0:T(8,128)(2,1)S(1)} %turn.1.cols_ref, ...), custom_call_target="tpu_custom_call" | custom-call | flops 2013265920 | tf_op jit(solution)/shard_map/grads/pallas_call | solution.py:314
  47.8 8.2 %all-to-all-start = ((bf16[8,128,256]{2,1,0:T(8,128)(2,1)}), bf16[8,128,256]{2,1,0:T(8,128)(2,1)S(1)}, u32[]{:S(2)}, u32[]{:S(2)}) async-start(bf16[8,128,256]{2,1,0:T(8,128)(2,1)} %flush.1), calls=%async_computation | async-start | bytes 1048576 | tf_op jit(solution)/shard_map/all_to_all | solution.py:327
  56.6 0.9 collective-permute-start.8
  57.5 3.5 %fetch.1 = (bf16[640,640]{1,0:T(8,128)(2,1)S(1)}, bf16[640,640]{1,0:T(8,128)(2,1)S(1)}, bf16[640,640]{1,0:T(8,128)(2,1)S(1)}, bf16[640,640]{1,0:T(8,128)(2,1)S(1...) custom-call(s32[4]{0:T(128)S(1)} %pad_add_fusion.place_ref, ...), custom_call_target="tpu_custom_call" | custom-call | tf_op jit(solution)/shard_map/fetch/pallas_call | solution.py:330
  61.0 0.9 collective-permute-done.7.q2
  61.9 1.7 %collective-permute-done.8.q3 = bf16[128,640]{1,0:T(8,128)(2,1)S(1)} collective-permute-done((bf16[128,640]{1,0:T(8,128)(2,1)S(1)}, bf16[128,640]{1,0:T(8,128)(2,1)S(1)}, u32[]{:S(2)}, u32[]{:S(2)}) %collective-permute-start.8) | collective-permute-done | bytes 163872 | tf_op jit(solution)/shard_map/ppermute | solution.py:323
  63.5 3.8 %query_part.1 = (bf16[8,640,128]{2,1,0:T(8,128)(2,1)S(1)}, bf16[4,640,128]{2,1,0:T(8,128)(2,1)S(1)}, bf16[4,640,128]{2,1,0:T(8,128)(2,1)S(1)}) custom-call(s32[4]{0:T(128)S(1)} %pad_add_fusion.place_ref, f32[64,128]{1,0:T(8,128)S(1)} %get-tuple-element.34.cos_ref, f32[64,128]{1,0:T(8,128)S(1)} %get-tuple-element.35.sin_ref, ...), custom_call_target="tpu_custom_call" | custom-call | flops 838860800 | tf_op jit(solution)/shard_map/query_part/pallas_call | solution.py:339
  67.3 0.8 all-to-all-done.dkv_ref
  68.2 2.3 %first_half.1 = (bf16[4,640,128]{2,1,0:T(8,128)(2,1)S(1)}, bf16[256,128]{1,0:T(8,128)(2,1)S(1)}, bf16[4,640,128]{2,1,0:T(8,128)(2,1)S(1)}, bf16[4,640,128]{2,1,0:T(8,128)(2,1)S(1)}) custom-call(s32[4]{0:T(128)S(1)} %pad_add_fusion.place_ref, f32[64,128]{1,0:T(8,128)S(1)} %get-tuple-element.34.cos_ref, f32[64,128]{1,0:T(8,128)S(1)} %get-tuple-element.35.sin_ref, ...), custom_call_target="tpu_custom_call" | custom-call | tf_op jit(solution)/shard_map/first_half/pallas_call | solution.py:348
  70.5 10.2 %collective-permute-start.9 = (bf16[4,640,128]{2,1,0:T(8,128)(2,1)S(1)}, bf16[4,640,128]{2,1,0:T(8,128)(2,1)S(1)}, u32[]{:S(2)}, u32[]{:S(2)}) collective-permute-start(bf16[4,640,128]{2,1,0:T(8,128)(2,1)S(1)} %get-tuple-element.60), channel_id=1, source_target_pairs={{0,1},{1,0},{2,3},{3,2},{4,5},{5,4},{6,7},{7,6},{8,9},{9,8},{10,11... | collective-permute-start | bytes 1966088 | tf_op jit(solution)/shard_map/ppermute | solution.py:356
  81.2 1.2 %collective-permute-done.9 = bf16[4,640,128]{2,1,0:T(8,128)(2,1)S(1)} collective-permute-done((bf16[4,640,128]{2,1,0:T(8,128)(2,1)S(1)}, bf16[4,640,128]{2,1,0:T(8,128)(2,1)S(1)}, u32[]{:S(2)}, u32[]{:S(2)}) %collective-permute-start.9) | collective-permute-done | bytes 655392 | tf_op jit(solution)/shard_map/ppermute | solution.py:356
  82.5 2.6 %collective-permute-start.12 = (bf16[640,128]{1,0:T(8,128)(2,1)S(1)}, bf16[640,128]{1,0:T(8,128)(2,1)S(1)}, u32[]{:S(2)}, u32[]{:S(2)}) collective-permute-start(bf16[640,128]{1,0:T(8,128)(2,1)S(1)} %get-tuple-element.61), channel_id=1, source_target_pairs={{0,6},{2,0},{4,2},{6,4},{1,7},{3,1},{5,3},{7,5},{8,14},{10,8},{12,... | collective-permute-start | bytes 491528 | tf_op jit(solution)/shard_map/ppermute | solution.py:365
  86.2 5.4 %collective-permute-done.12.p2 = bf16[640,128]{1,0:T(8,128)(2,1)S(1)} collective-permute-done((bf16[640,128]{1,0:T(8,128)(2,1)S(1)}, bf16[640,128]{1,0:T(8,128)(2,1)S(1)}, u32[]{:S(2)}, u32[]{:S(2)}) %collective-permute-start.12) | collective-permute-done | bytes 163872 | tf_op jit(solution)/shard_map/ppermute | solution.py:365
  91.7 4.5 %collective-permute-done.10.p0 = bf16[640,128]{1,0:T(8,128)(2,1)S(1)} collective-permute-done((bf16[640,128]{1,0:T(8,128)(2,1)S(1)}, bf16[640,128]{1,0:T(8,128)(2,1)S(1)}, u32[]{:S(2)}, u32[]{:S(2)}) %collective-permute-start.10) | collective-permute-done | bytes 163872 | tf_op jit(solution)/shard_map/ppermute | solution.py:365
  96.2 0.8 finish.1
  (24 shorter events, 6.4 us)
Async XLA Ops:
  1.1 33.5 %collective-permute-start.2 = (bf16[1280,128]{1,0:T(8,128)(2,1)S(1)}, bf16[1280,128]{1,0:T(8,128)(2,1)S(1)}, u32[]{:S(2)}, u32[]{:S(2)}) collective-permute-start(bf16[1280,128]{1,0:T(8,128)(2,1)S(1)} %get-tuple-element.33.rows_ref.g0), channel_id=1, source_target_pairs={{0,24},{8,0},{16,8},{24,16},{1,25},{9,1},{17,9},{25,17},{2,26},{10... | collective-permute-start | bytes 983048 | tf_op jit(solution)/shard_map/ppermute | solution.py:279
  4.7 29.9 %collective-permute-start.1 = (bf16[1280,128]{1,0:T(8,128)(2,1)S(1)}, bf16[1280,128]{1,0:T(8,128)(2,1)S(1)}, u32[]{:S(2)}, u32[]{:S(2)}) collective-permute-start(bf16[1280,128]{1,0:T(8,128)(2,1)S(1)} %get-tuple-element.33.rows_ref.g0), channel_id=1, source_target_pairs={{0,16},{8,24},{16,0},{24,8},{1,17},{9,25},{17,1},{25,9},{2,18},{10... | collective-permute-start | bytes 983048 | tf_op jit(solution)/shard_map/ppermute | solution.py:279
  5.0 29.5 %collective-permute-start = (bf16[1280,128]{1,0:T(8,128)(2,1)S(1)}, bf16[1280,128]{1,0:T(8,128)(2,1)S(1)}, u32[]{:S(2)}, u32[]{:S(2)}) collective-permute-start(bf16[1280,128]{1,0:T(8,128)(2,1)S(1)} %get-tuple-element.33.rows_ref.g0), channel_id=1, source_target_pairs={{0,8},{8,16},{16,24},{24,0},{1,9},{9,17},{17,25},{25,1},{2,10},{10... | collective-permute-start | bytes 983048 | tf_op jit(solution)/shard_map/ppermute | solution.py:279
  37.0 3.2 %collective-permute-start.5 = (f32[4,4,640]{2,1,0:T(4,128)S(1)}, f32[4,4,640]{2,1,0:T(4,128)S(1)}, u32[]{:S(2)}, u32[]{:S(2)}) collective-permute-start(f32[4,4,640]{2,1,0:T(4,128)S(1)} %get-tuple-element.38.stat_ref.s0), channel_id=1, source_target_pairs={{0,24},{8,0},{16,8},{24,16},{1,25},{9,1},{17,9},{25,17},{2,26},{10... | collective-permute-start | bytes 122888 | tf_op jit(solution)/shard_map/ppermute | solution.py:310
  37.8 4.4 %collective-permute-start.4 = (f32[4,4,640]{2,1,0:T(4,128)S(1)}, f32[4,4,640]{2,1,0:T(4,128)S(1)}, u32[]{:S(2)}, u32[]{:S(2)}) collective-permute-start(f32[4,4,640]{2,1,0:T(4,128)S(1)} %get-tuple-element.38.stat_ref.s0), channel_id=1, source_target_pairs={{0,16},{8,24},{16,0},{24,8},{1,17},{9,25},{17,1},{25,9},{2,18},{10... | collective-permute-start | bytes 122888 | tf_op jit(solution)/shard_map/ppermute | solution.py:310
  39.9 4.1 %collective-permute-start.3 = (f32[4,4,640]{2,1,0:T(4,128)S(1)}, f32[4,4,640]{2,1,0:T(4,128)S(1)}, u32[]{:S(2)}, u32[]{:S(2)}) collective-permute-start(f32[4,4,640]{2,1,0:T(4,128)S(1)} %get-tuple-element.38.stat_ref.s0), channel_id=1, source_target_pairs={{0,8},{8,16},{16,24},{24,0},{1,9},{9,17},{17,25},{25,1},{2,10},{10... | collective-permute-start | bytes 122888 | tf_op jit(solution)/shard_map/ppermute | solution.py:310
  47.8 20.4 %all-to-all-start = ((bf16[8,128,256]{2,1,0:T(8,128)(2,1)}), bf16[8,128,256]{2,1,0:T(8,128)(2,1)S(1)}, u32[]{:S(2)}, u32[]{:S(2)}) async-start(bf16[8,128,256]{2,1,0:T(8,128)(2,1)} %flush.1), calls=%async_computation | async-start | bytes 1048576 | tf_op jit(solution)/shard_map/all_to_all | solution.py:327
  56.0 5.0 %collective-permute-start.6 = (bf16[128,640]{1,0:T(8,128)(2,1)S(1)}, bf16[128,640]{1,0:T(8,128)(2,1)S(1)}, u32[]{:S(2)}, u32[]{:S(2)}) collective-permute-start(bf16[128,640]{1,0:T(8,128)(2,1)S(1)} %get-tuple-element.43), channel_id=1, source_target_pairs={{0,24},{8,0},{16,8},{24,16},{1,25},{9,1},{17,9},{25,17},{2,26},{10... | collective-permute-start | bytes 491528 | tf_op jit(solution)/shard_map/ppermute | solution.py:323
  56.0 5.9 %collective-permute-start.7 = (bf16[128,640]{1,0:T(8,128)(2,1)S(1)}, bf16[128,640]{1,0:T(8,128)(2,1)S(1)}, u32[]{:S(2)}, u32[]{:S(2)}) collective-permute-start(bf16[128,640]{1,0:T(8,128)(2,1)S(1)} %get-tuple-element.44), channel_id=1, source_target_pairs={{0,16},{8,24},{16,0},{24,8},{1,17},{9,25},{17,1},{25,9},{2,18},{10... | collective-permute-start | bytes 491528 | tf_op jit(solution)/shard_map/ppermute | solution.py:323
  56.6 7.0 %collective-permute-start.8 = (bf16[128,640]{1,0:T(8,128)(2,1)S(1)}, bf16[128,640]{1,0:T(8,128)(2,1)S(1)}, u32[]{:S(2)}, u32[]{:S(2)}) collective-permute-start(bf16[128,640]{1,0:T(8,128)(2,1)S(1)} %get-tuple-element.45), channel_id=1, source_target_pairs={{0,8},{8,16},{16,24},{24,0},{1,9},{9,17},{17,25},{25,1},{2,10},{10... | collective-permute-start | bytes 491528 | tf_op jit(solution)/shard_map/ppermute | solution.py:323
  70.5 11.9 %collective-permute-start.9 = (bf16[4,640,128]{2,1,0:T(8,128)(2,1)S(1)}, bf16[4,640,128]{2,1,0:T(8,128)(2,1)S(1)}, u32[]{:S(2)}, u32[]{:S(2)}) collective-permute-start(bf16[4,640,128]{2,1,0:T(8,128)(2,1)S(1)} %get-tuple-element.60), channel_id=1, source_target_pairs={{0,1},{1,0},{2,3},{3,2},{4,5},{5,4},{6,7},{7,6},{8,9},{9,8},{10,11... | collective-permute-start | bytes 1966088 | tf_op jit(solution)/shard_map/ppermute | solution.py:356
  82.5 9.1 %collective-permute-start.12 = (bf16[640,128]{1,0:T(8,128)(2,1)S(1)}, bf16[640,128]{1,0:T(8,128)(2,1)S(1)}, u32[]{:S(2)}, u32[]{:S(2)}) collective-permute-start(bf16[640,128]{1,0:T(8,128)(2,1)S(1)} %get-tuple-element.61), channel_id=1, source_target_pairs={{0,6},{2,0},{4,2},{6,4},{1,7},{3,1},{5,3},{7,5},{8,14},{10,8},{12,... | collective-permute-start | bytes 491528 | tf_op jit(solution)/shard_map/ppermute | solution.py:365
  85.1 6.6 %collective-permute-start.11 = (bf16[640,128]{1,0:T(8,128)(2,1)S(1)}, bf16[640,128]{1,0:T(8,128)(2,1)S(1)}, u32[]{:S(2)}, u32[]{:S(2)}) collective-permute-start(bf16[640,128]{1,0:T(8,128)(2,1)S(1)} %get-tuple-element.62), channel_id=1, source_target_pairs={{0,4},{2,6},{4,0},{6,2},{1,5},{3,7},{5,1},{7,3},{8,12},{10,14},{12... | collective-permute-start | bytes 491528 | tf_op jit(solution)/shard_map/ppermute | solution.py:365
  85.6 10.6 %collective-permute-start.10 = (bf16[640,128]{1,0:T(8,128)(2,1)S(1)}, bf16[640,128]{1,0:T(8,128)(2,1)S(1)}, u32[]{:S(2)}, u32[]{:S(2)}) collective-permute-start(bf16[640,128]{1,0:T(8,128)(2,1)S(1)} %get-tuple-element.63), channel_id=1, source_target_pairs={{0,2},{2,4},{4,6},{6,0},{1,3},{3,5},{5,7},{7,1},{8,10},{10,12},{12... | collective-permute-start | bytes 491528 | tf_op jit(solution)/shard_map/ppermute | solution.py:365

commit v7 on v6

--- a/solution.py
+++ b/solution.py
@@ -96,9 +96,13 @@
             item_ref[row, 2] = jnp.where(first == z, causal, -BLOCK)
             item_ref[row, 3] = jnp.where(both, jnp.where(second == z, causal, -BLOCK), BLOCK)
         item_ref[NY * PAIRS + j, 0] = (count + 1) // 2
-
-
-def stats_kernel(item_ref, kv_ref, g0, g1, g2, g3, stat_ref, score_ref, pgrad_ref):
+        item_ref[NY * PAIRS + j, 1] = z
+
+
+def stats_kernel(item_ref, k0, k1, k2, k3, k4, k5, k6, k7, g0, g1, g2, g3, stat_ref, score_ref, pgrad_ref, kv_ref):
+    z = item_ref[NY * PAIRS, 1]
+    for r, part in enumerate((k0, k1, k2, k3, k4, k5, k6, k7)):
+        kv_ref[(z - r) & (NZ - 1)] = part[...]
     key_row = lax.broadcasted_iota(I32, (BLOCK, ROWS), 0)
     query_row = lax.broadcasted_iota(I32, (BLOCK, ROWS), 1) % BLOCK
     gap = query_row - key_row
@@ -133,9 +137,10 @@
         stat_ref[j, 3:4, :] = zero
 
 
-def turn_kernel(kv_ref, stat_ref, key_cols):
-    for a in range(NZ):
-        key_cols[a] = kv_ref[a, :, :HEAD].T
+def turn_kernel(item_ref, k0, k1, k2, k3, k4, k5, k6, k7, stat_ref, key_cols):
+    z = item_ref[NY * PAIRS, 1]
+    for r, part in enumerate((k0, k1, k2, k3, k4, k5, k6, k7)):
+        key_cols[(z - r) & (NZ - 1)] = part[:, :HEAD].T
 
 
 def flush_kernel(low_ref, out_ref, sem):
@@ -277,7 +282,11 @@
         [pltpu.SemaphoreType.DMA((2 * GROUP + 2,))],
     )(*in_hbm(queries, out_grad, keys, values))
     groups = [group] + [lax.ppermute(group, "y", shift(NY, k)) for k in range(1, NY)]
-    kv_all = lax.all_gather(kv, "z", axis=0, tiled=False)
+    below, above = [kv], [kv]
+    for r in range(1, NZ // 2):
+        below.append(lax.ppermute(below[-1], "z", shift(NZ, 1)))
+        above.append(lax.ppermute(above[-1], "z", shift(NZ, -1)))
+    kvs = below + [lax.ppermute(below[-1], "z", shift(NZ, 1))] + above[:0:-1]
 
     own_block = NY * z + y
     own_row = lax.dynamic_slice_in_dim(ancestry, own_block, 1, 0)
@@ -301,16 +310,16 @@
     stats, scores, prob_grads = call(
         stats_kernel,
         [jax.ShapeDtypeStruct((NY, 4, ROWS), F32), pltpu.VMEM(tiles, F32), pltpu.VMEM(tiles, F32)],
-        [SM] + [VM] * (1 + NY),
+        [SM] + [VM] * (NZ + NY),
         [VM] * 3,
         "stats",
-        (),
+        [pltpu.VMEM((NZ, BLOCK, 2 * HEAD), BF16)],
         STATS_FLOPS,
-    )(items, kv_all, *groups)
+    )(items, *kvs, *groups)
     all_stats = [stats] + [lax.ppermute(stats, "y", shift(NY, k)) for k in range(1, NY)]
     key_cols = call(
-        turn_kernel, pltpu.VMEM((NZ, HEAD, BLOCK), BF16), [VM] * 2, VM, "turn",
-    )(kv_all, stats)
+        turn_kernel, pltpu.VMEM((NZ, HEAD, BLOCK), BF16), [SM] + [VM] * (NZ + 1), VM, "turn",
+    )(items, *kvs, stats)
     dkv, *dq_parts = call(
         grads_kernel,
         [pltpu.VMEM((NZ, BLOCK, 2 * HEAD), BF16)] + [pltpu.VMEM((HEAD, ROWS), BF16)] * NY,

time: 97.9 us -> 86.3 us (0.88)
  blocking collectives: 23.8 us -> 0 us
  starting transfers between devices: 31.1 us -> 37.7 us
  waiting for transfers between devices: 18.5 us -> 24 us
    all_gather x1 -> x0, blocking collectives: 23.8 us -> none  [shards(): kv_all = lax.all_gather(kv, 'z', axis=0, tiled=False)]
    ppermute x0 -> x7, starting transfers between devices: none -> 12 us  [the longest x3 11.9 us: shards(): above.append(lax.ppermute(above[-1], 'z', shift(NZ, -1)))]
    ppermute x0 -> x7, waiting for transfers between devices: none -> 5.46 us  [the longest x3 2.77 us: shards(): below.append(lax.ppermute(below[-1], 'z', shift(NZ, 1)))]
    ppermute x1, starting transfers between devices: 10.2 us -> 7.77 us  [shards(): arrived = lax.ppermute(away, 'c', shift(NC, 1))]
    ppermute x3, starting transfers between devices: 2.86 us -> 1.54 us  [shards(): lax.ppermute(stats, 'y', shift(NY, k))]
    ppermute x3, waiting for transfers between devices: 0.01 us -> 1.08 us  [shards(): lax.ppermute(group, 'y', shift(NY, k))]
    ppermute x3, waiting for transfers between devices: 3.93 us -> 2.92 us  [shards(): lax.ppermute(stats, 'y', shift(NY, k))]
  transfers between devices with their start and end apart: 14 -> 21, of which waited for: 10 -> 14; matrix products, arithmetic and copies ran while one was open for 3% -> 3% of each run, Pallas kernels for 10% -> 12%
where the time goes in v7:
time: 86.3 us; the launch traced here: 86.4 us
  starting transfers between devices  37.7 us (44%)
  waiting for transfers between devices  24 us (28%)
  Pallas kernels  21.1 us (24%)
  other arithmetic  1.81 us (2%)
    ppermute x3, starting transfers between devices, shards(): above.append(lax.ppermute(above[-1], 'z', shift(NZ, -1)))  11.9 us
    ppermute x3, waiting for transfers between devices, shards(): parts = [lax.ppermute(sent[k - 1], 'x', shift(NX, k)) for k in range(1, NX)]  9.99 us
    ppermute x1, starting transfers between devices, shards(): arrived = lax.ppermute(away, 'c', shift(NC, 1))  7.77 us
    all_to_all x1, starting transfers between devices, shards(): dkv_own = lax.all_to_all(dkv, 'z', 0, 0, tiled=True)  7.39 us
    pallas_call x1, Pallas kernels, shards(): call(query_part_kernel, [pltpu.VMEM((2 * NX, ROWS, BLOCK), BF16)] + pair_...  3.8 us
    ppermute x3, starting transfers between devices, shards(): lax.ppermute(group, 'y', shift(NY, k))  3.77 us
    ppermute x3, starting transfers between devices, shards(): parts = [lax.ppermute(sent[k - 1], 'x', shift(NX, k)) for k in range(1, NX)]  3.69 us
    pallas_call x1, Pallas kernels, shards(): call(fetch_kernel, [pltpu.VMEM((ROWS, ROWS), BF16)] * (2 * NX), [SM, VM,...  3.49 us
  transfers between devices with their start and end apart: 21, of which 14 were waited for; matrix products, arithmetic and copies ran while one was open for 3% of the time, Pallas kernels for 12%

profile of v7, /device:TPU:1, one launch (start us, length us, event | category | flops | bytes accessed | tf_op | source)
XLA Modules:
  0.0 86.4 jit_solution(9846909228877242293)
XLA Ops:
  1.1 6.5 %collective-permute-start.4 = (bf16[128,256]{1,0:T(8,128)(2,1)S(1)}, bf16[128,256]{1,0:T(8,128)(2,1)S(1)}, u32[]{:S(2)}, u32[]{:S(2)}) collective-permute-start(bf16[128,256]{1,0:T(8,128)(2,1)S(1)} %get-tuple-element.37.k0), channel_id=1, source_target_pairs={{0,224},{32,0},{64,32},{96,64},{128,96},{160,128},{192,160},{224,1... | collective-permute-start | bytes 196616 | tf_op jit(solution)/shard_map/ppermute | solution.py:288
  7.5 2.7 %collective-permute-start.9 = (bf16[1280,128]{1,0:T(8,128)(2,1)S(1)}, bf16[1280,128]{1,0:T(8,128)(2,1)S(1)}, u32[]{:S(2)}, u32[]{:S(2)}) collective-permute-start(bf16[1280,128]{1,0:T(8,128)(2,1)S(1)} %get-tuple-element.33.rows_ref.g0), channel_id=1, source_target_pairs={{0,24},{8,0},{16,8},{24,16},{1,25},{9,1},{17,9},{25,17},{2,26},{10... | collective-permute-start | bytes 983048 | tf_op jit(solution)/shard_map/ppermute | solution.py:284
  11.3 1.4 %convert_reduce_fusion = s32[]{:T(128)} fusion(s32[32,17]{0,1:T(8,128)} %param.12, s32[]{:T(128)S(6)} %select_n.3, s32[]{:T(128)S(6)} %add.28), kind=kLoop, calls=%fused_computation.13 | loop fusion | flops 50 | bytes 80 | tf_op jit(solution)/shard_map/reduce_sum | solution.py:293
  13.5 2.7 %collective-permute-start.5 = (bf16[128,256]{1,0:T(8,128)(2,1)S(1)}, bf16[128,256]{1,0:T(8,128)(2,1)S(1)}, u32[]{:S(2)}, u32[]{:S(2)}) collective-permute-start(bf16[128,256]{1,0:T(8,128)(2,1)S(1)} %collective-permute-done.4.k7), channel_id=1, source_target_pairs={{0,224},{32,0},{64,32},{96,64},{128,96},{160,128},{192,160},{224,1... | collective-permute-start | bytes 196616 | tf_op jit(solution)/shard_map/ppermute | solution.py:288
  16.3 1.8 %collective-permute-done.1.k2 = bf16[128,256]{1,0:T(8,128)(2,1)S(1)} collective-permute-done((bf16[128,256]{1,0:T(8,128)(2,1)S(1)}, bf16[128,256]{1,0:T(8,128)(2,1)S(1)}, u32[]{:S(2)}, u32[]{:S(2)}) %collective-permute-start.1) | collective-permute-done | bytes 65568 | tf_op jit(solution)/shard_map/ppermute | solution.py:287
  19.1 2.7 %collective-permute-start.6 = (bf16[128,256]{1,0:T(8,128)(2,1)S(1)}, bf16[128,256]{1,0:T(8,128)(2,1)S(1)}, u32[]{:S(2)}, u32[]{:S(2)}) collective-permute-start(bf16[128,256]{1,0:T(8,128)(2,1)S(1)} %collective-permute-done.5.k6), channel_id=1, source_target_pairs={{0,224},{32,0},{64,32},{96,64},{128,96},{160,128},{192,160},{224,1... | collective-permute-start | bytes 196616 | tf_op jit(solution)/shard_map/ppermute | solution.py:288
  22.8 1.8 %plan.1.item_ref = s32[20,4]{1,0:T(8,128)S(1)} custom-call(s32[4]{0:T(128)S(1)} %pad_add_fusion.place_ref, s32[32,17]{1,0:T(8,128)S(1)} %copy.9.anc_ref, bf16[1280,128]{1,0:T(8,128)(2,1)S(1)} %get-tuple-element.33.rows_ref.g0), custom_call_target="tpu_custom_call" | custom-call | tf_op jit(solution)/shard_map/plan/pallas_call | solution.py:299
  24.7 2.7 %collective-permute-done.3.k4 = bf16[128,256]{1,0:T(8,128)(2,1)S(1)} collective-permute-done((bf16[128,256]{1,0:T(8,128)(2,1)S(1)}, bf16[128,256]{1,0:T(8,128)(2,1)S(1)}, u32[]{:S(2)}, u32[]{:S(2)}) %collective-permute-start.3) | collective-permute-done | bytes 65568 | tf_op jit(solution)/shard_map/ppermute | solution.py:289
  27.4 1.1 %collective-permute-done.7.g1 = bf16[1280,128]{1,0:T(8,128)(2,1)S(1)} collective-permute-done((bf16[1280,128]{1,0:T(8,128)(2,1)S(1)}, bf16[1280,128]{1,0:T(8,128)(2,1)S(1)}, u32[]{:S(2)}, u32[]{:S(2)}) %collective-permute-start.7) | collective-permute-done | bytes 327712 | tf_op jit(solution)/shard_map/ppermute | solution.py:284
  28.4 2.5 %stats.1 = (f32[4,4,640]{2,1,0:T(4,128)S(1)}, f32[16,256,640]{2,1,0:T(8,128)S(1)}, f32[16,256,640]{2,1,0:T(8,128)S(1)}) custom-call(s32[20,4]{1,0:T(8,128)S(1)} %plan.1.item_ref, bf16[128,256]{1,0:T(8,128)(2,1)S(1)} %get-tuple-element.37.k0, bf16[128,256]{1,0:T(8,128)(2,1)S(1)} %collective-permute-done.k1, bf16[128,256]{1,0:T(8,128)(2,1)S(1)} %collective-permute-done.1.k2, ...), custom_call_target="tpu_custom_call" | custom-call | flops 1342177280 | tf_op jit(solution)/shard_map/stats/pallas_call | solution.py:310
  31.0 1.2 %collective-permute-start.11 = (f32[4,4,640]{2,1,0:T(4,128)S(1)}, f32[4,4,640]{2,1,0:T(4,128)S(1)}, u32[]{:S(2)}, u32[]{:S(2)}) collective-permute-start(f32[4,4,640]{2,1,0:T(4,128)S(1)} %get-tuple-element.38.stat_ref.s0), channel_id=1, source_target_pairs={{0,16},{8,24},{16,0},{24,8},{1,17},{9,25},{17,1},{25,9},{2,18},{10... | collective-permute-start | bytes 122888 | tf_op jit(solution)/shard_map/ppermute | solution.py:319
  33.8 1.6 %collective-permute-done.11.s2 = f32[4,4,640]{2,1,0:T(4,128)S(1)} collective-permute-done((f32[4,4,640]{2,1,0:T(4,128)S(1)}, f32[4,4,640]{2,1,0:T(4,128)S(1)}, u32[]{:S(2)}, u32[]{:S(2)}) %collective-permute-start.11) | collective-permute-done | bytes 40992 | tf_op jit(solution)/shard_map/ppermute | solution.py:319
  36.2 3.2 %grads.1 = (bf16[8,128,256]{2,1,0:T(8,128)(2,1)S(1)}, bf16[128,640]{1,0:T(8,128)(2,1)S(1)}, bf16[128,640]{1,0:T(8,128)(2,1)S(1)}, bf16[128,640]{1,0:T(8,128)(2,1)S(1)}, bf16[128,640]{1,0:T(8,128)(2,1)S(1)}) custom-call(s32[20,4]{1,0:T(8,128)S(1)} %plan.1.item_ref, bf16[8,128,128]{2,1,0:T(8,128)(2,1)S(1)} %turn.1.cols_ref, ...), custom_call_target="tpu_custom_call" | custom-call | flops 2013265920 | tf_op jit(solution)/shard_map/grads/pallas_call | solution.py:323
  40.3 7.4 %all-to-all-start = ((bf16[8,128,256]{2,1,0:T(8,128)(2,1)}), bf16[8,128,256]{2,1,0:T(8,128)(2,1)S(1)}, u32[]{:S(2)}, u32[]{:S(2)}) async-start(bf16[8,128,256]{2,1,0:T(8,128)(2,1)} %flush.1), calls=%async_computation | async-start | bytes 1048576 | tf_op jit(solution)/shard_map/all_to_all | solution.py:336
  49.2 3.5 %fetch.1 = (bf16[640,640]{1,0:T(8,128)(2,1)S(1)}, bf16[640,640]{1,0:T(8,128)(2,1)S(1)}, bf16[640,640]{1,0:T(8,128)(2,1)S(1)}, bf16[640,640]{1,0:T(8,128)(2,1)S(1...) custom-call(s32[4]{0:T(128)S(1)} %pad_add_fusion.place_ref, ...), custom_call_target="tpu_custom_call" | custom-call | tf_op jit(solution)/shard_map/fetch/pallas_call | solution.py:339
  52.7 1.2 %collective-permute-done.14.q2 = bf16[128,640]{1,0:T(8,128)(2,1)S(1)} collective-permute-done((bf16[128,640]{1,0:T(8,128)(2,1)S(1)}, bf16[128,640]{1,0:T(8,128)(2,1)S(1)}, u32[]{:S(2)}, u32[]{:S(2)}) %collective-permute-start.14) | collective-permute-done | bytes 163872 | tf_op jit(solution)/shard_map/ppermute | solution.py:332
  54.0 1.7 %collective-permute-done.15.q3 = bf16[128,640]{1,0:T(8,128)(2,1)S(1)} collective-permute-done((bf16[128,640]{1,0:T(8,128)(2,1)S(1)}, bf16[128,640]{1,0:T(8,128)(2,1)S(1)}, u32[]{:S(2)}, u32[]{:S(2)}) %collective-permute-start.15) | collective-permute-done | bytes 163872 | tf_op jit(solution)/shard_map/ppermute | solution.py:332
  55.6 3.8 %query_part.1 = (bf16[8,640,128]{2,1,0:T(8,128)(2,1)S(1)}, bf16[4,640,128]{2,1,0:T(8,128)(2,1)S(1)}, bf16[4,640,128]{2,1,0:T(8,128)(2,1)S(1)}) custom-call(s32[4]{0:T(128)S(1)} %pad_add_fusion.place_ref, f32[64,128]{1,0:T(8,128)S(1)} %get-tuple-element.34.cos_ref, f32[64,128]{1,0:T(8,128)S(1)} %get-tuple-element.35.sin_ref, ...), custom_call_target="tpu_custom_call" | custom-call | flops 838860800 | tf_op jit(solution)/shard_map/query_part/pallas_call | solution.py:348
  59.9 2.3 %first_half.1 = (bf16[4,640,128]{2,1,0:T(8,128)(2,1)S(1)}, bf16[256,128]{1,0:T(8,128)(2,1)S(1)}, bf16[4,640,128]{2,1,0:T(8,128)(2,1)S(1)}, bf16[4,640,128]{2,1,0:T(8,128)(2,1)S(1)}) custom-call(s32[4]{0:T(128)S(1)} %pad_add_fusion.place_ref, f32[64,128]{1,0:T(8,128)S(1)} %get-tuple-element.34.cos_ref, f32[64,128]{1,0:T(8,128)S(1)} %get-tuple-element.35.sin_ref, ...), custom_call_target="tpu_custom_call" | custom-call | tf_op jit(solution)/shard_map/first_half/pallas_call | solution.py:357
  62.2 7.8 %collective-permute-start.16 = (bf16[4,640,128]{2,1,0:T(8,128)(2,1)S(1)}, bf16[4,640,128]{2,1,0:T(8,128)(2,1)S(1)}, u32[]{:S(2)}, u32[]{:S(2)}) collective-permute-start(bf16[4,640,128]{2,1,0:T(8,128)(2,1)S(1)} %get-tuple-element.60), channel_id=1, source_target_pairs={{0,1},{1,0},{2,3},{3,2},{4,5},{5,4},{6,7},{7,6},{8,9},{9,8},{10,11... | collective-permute-start | bytes 1966088 | tf_op jit(solution)/shard_map/ppermute | solution.py:365
  70.5 1.2 %collective-permute-done.16 = bf16[4,640,128]{2,1,0:T(8,128)(2,1)S(1)} collective-permute-done((bf16[4,640,128]{2,1,0:T(8,128)(2,1)S(1)}, bf16[4,640,128]{2,1,0:T(8,128)(2,1)S(1)}, u32[]{:S(2)}, u32[]{:S(2)}) %collective-permute-start.16) | collective-permute-done | bytes 655392 | tf_op jit(solution)/shard_map/ppermute | solution.py:365
  71.8 2.6 %collective-permute-start.19 = (bf16[640,128]{1,0:T(8,128)(2,1)S(1)}, bf16[640,128]{1,0:T(8,128)(2,1)S(1)}, u32[]{:S(2)}, u32[]{:S(2)}) collective-permute-start(bf16[640,128]{1,0:T(8,128)(2,1)S(1)} %get-tuple-element.61), channel_id=1, source_target_pairs={{0,6},{2,0},{4,2},{6,4},{1,7},{3,1},{5,3},{7,5},{8,14},{10,8},{12,... | collective-permute-start | bytes 491528 | tf_op jit(solution)/shard_map/ppermute | solution.py:374
  75.5 5.4 %collective-permute-done.19.p2 = bf16[640,128]{1,0:T(8,128)(2,1)S(1)} collective-permute-done((bf16[640,128]{1,0:T(8,128)(2,1)S(1)}, bf16[640,128]{1,0:T(8,128)(2,1)S(1)}, u32[]{:S(2)}, u32[]{:S(2)}) %collective-permute-start.19) | collective-permute-done | bytes 163872 | tf_op jit(solution)/shard_map/ppermute | solution.py:374
  81.0 4.5 %collective-permute-done.17.p0 = bf16[640,128]{1,0:T(8,128)(2,1)S(1)} collective-permute-done((bf16[640,128]{1,0:T(8,128)(2,1)S(1)}, bf16[640,128]{1,0:T(8,128)(2,1)S(1)}, u32[]{:S(2)}, u32[]{:S(2)}) %collective-permute-start.17) | collective-permute-done | bytes 163872 | tf_op jit(solution)/shard_map/ppermute | solution.py:374
  (37 shorter events, 12.2 us)
Async XLA Ops:
  1.1 12.5 %collective-permute-start.4 = (bf16[128,256]{1,0:T(8,128)(2,1)S(1)}, bf16[128,256]{1,0:T(8,128)(2,1)S(1)}, u32[]{:S(2)}, u32[]{:S(2)}) collective-permute-start(bf16[128,256]{1,0:T(8,128)(2,1)S(1)} %get-tuple-element.37.k0), channel_id=1, source_target_pairs={{0,224},{32,0},{64,32},{96,64},{128,96},{160,128},{192,160},{224,1... | collective-permute-start | bytes 196616 | tf_op jit(solution)/shard_map/ppermute | solution.py:288
  7.5 5.9 %collective-permute-start = (bf16[128,256]{1,0:T(8,128)(2,1)S(1)}, bf16[128,256]{1,0:T(8,128)(2,1)S(1)}, u32[]{:S(2)}, u32[]{:S(2)}) collective-permute-start(bf16[128,256]{1,0:T(8,128)(2,1)S(1)} %get-tuple-element.37.k0), channel_id=1, source_target_pairs={{0,32},{32,64},{64,96},{96,128},{128,160},{160,192},{192,224},{224... | collective-permute-start | bytes 196616 | tf_op jit(solution)/shard_map/ppermute | solution.py:287
  7.5 19.8 %collective-permute-start.9 = (bf16[1280,128]{1,0:T(8,128)(2,1)S(1)}, bf16[1280,128]{1,0:T(8,128)(2,1)S(1)}, u32[]{:S(2)}, u32[]{:S(2)}) collective-permute-start(bf16[1280,128]{1,0:T(8,128)(2,1)S(1)} %get-tuple-element.33.rows_ref.g0), channel_id=1, source_target_pairs={{0,24},{8,0},{16,8},{24,16},{1,25},{9,1},{17,9},{25,17},{2,26},{10... | collective-permute-start | bytes 983048 | tf_op jit(solution)/shard_map/ppermute | solution.py:284
  10.3 17.1 %collective-permute-start.8 = (bf16[1280,128]{1,0:T(8,128)(2,1)S(1)}, bf16[1280,128]{1,0:T(8,128)(2,1)S(1)}, u32[]{:S(2)}, u32[]{:S(2)}) collective-permute-start(bf16[1280,128]{1,0:T(8,128)(2,1)S(1)} %get-tuple-element.33.rows_ref.g0), channel_id=1, source_target_pairs={{0,16},{8,24},{16,0},{24,8},{1,17},{9,25},{17,1},{25,9},{2,18},{10... | collective-permute-start | bytes 983048 | tf_op jit(solution)/shard_map/ppermute | solution.py:284
  10.6 17.8 %collective-permute-start.7 = (bf16[1280,128]{1,0:T(8,128)(2,1)S(1)}, bf16[1280,128]{1,0:T(8,128)(2,1)S(1)}, u32[]{:S(2)}, u32[]{:S(2)}) collective-permute-start(bf16[1280,128]{1,0:T(8,128)(2,1)S(1)} %get-tuple-element.33.rows_ref.g0), channel_id=1, source_target_pairs={{0,8},{8,16},{16,24},{24,0},{1,9},{9,17},{17,25},{25,1},{2,10},{10... | collective-permute-start | bytes 983048 | tf_op jit(solution)/shard_map/ppermute | solution.py:284
  13.4 4.7 %collective-permute-start.1 = (bf16[128,256]{1,0:T(8,128)(2,1)S(1)}, bf16[128,256]{1,0:T(8,128)(2,1)S(1)}, u32[]{:S(2)}, u32[]{:S(2)}) collective-permute-start(bf16[128,256]{1,0:T(8,128)(2,1)S(1)} %collective-permute-done.k1), channel_id=1, source_target_pairs={{0,32},{32,64},{64,96},{96,128},{128,160},{160,192},{192,224},{224... | collective-permute-start | bytes 196616 | tf_op jit(solution)/shard_map/ppermute | solution.py:287
  13.5 5.6 %collective-permute-start.5 = (bf16[128,256]{1,0:T(8,128)(2,1)S(1)}, bf16[128,256]{1,0:T(8,128)(2,1)S(1)}, u32[]{:S(2)}, u32[]{:S(2)}) collective-permute-start(bf16[128,256]{1,0:T(8,128)(2,1)S(1)} %collective-permute-done.4.k7), channel_id=1, source_target_pairs={{0,224},{32,0},{64,32},{96,64},{128,96},{160,128},{192,160},{224,1... | collective-permute-start | bytes 196616 | tf_op jit(solution)/shard_map/ppermute | solution.py:288
  18.1 4.6 %collective-permute-start.2 = (bf16[128,256]{1,0:T(8,128)(2,1)S(1)}, bf16[128,256]{1,0:T(8,128)(2,1)S(1)}, u32[]{:S(2)}, u32[]{:S(2)}) collective-permute-start(bf16[128,256]{1,0:T(8,128)(2,1)S(1)} %collective-permute-done.1.k2), channel_id=1, source_target_pairs={{0,32},{32,64},{64,96},{96,128},{128,160},{160,192},{192,224},{224... | collective-permute-start | bytes 196616 | tf_op jit(solution)/shard_map/ppermute | solution.py:287
  19.1 5.6 %collective-permute-start.6 = (bf16[128,256]{1,0:T(8,128)(2,1)S(1)}, bf16[128,256]{1,0:T(8,128)(2,1)S(1)}, u32[]{:S(2)}, u32[]{:S(2)}) collective-permute-start(bf16[128,256]{1,0:T(8,128)(2,1)S(1)} %collective-permute-done.5.k6), channel_id=1, source_target_pairs={{0,224},{32,0},{64,32},{96,64},{128,96},{160,128},{192,160},{224,1... | collective-permute-start | bytes 196616 | tf_op jit(solution)/shard_map/ppermute | solution.py:288
  22.7 4.6 %collective-permute-start.3 = (bf16[128,256]{1,0:T(8,128)(2,1)S(1)}, bf16[128,256]{1,0:T(8,128)(2,1)S(1)}, u32[]{:S(2)}, u32[]{:S(2)}) collective-permute-start(bf16[128,256]{1,0:T(8,128)(2,1)S(1)} %collective-permute-done.2.k3), channel_id=1, source_target_pairs={{0,32},{32,64},{64,96},{96,128},{128,160},{160,192},{192,224},{224... | collective-permute-start | bytes 196616 | tf_op jit(solution)/shard_map/ppermute | solution.py:289
  30.9 2.9 %collective-permute-start.12 = (f32[4,4,640]{2,1,0:T(4,128)S(1)}, f32[4,4,640]{2,1,0:T(4,128)S(1)}, u32[]{:S(2)}, u32[]{:S(2)}) collective-permute-start(f32[4,4,640]{2,1,0:T(4,128)S(1)} %get-tuple-element.38.stat_ref.s0), channel_id=1, source_target_pairs={{0,24},{8,0},{16,8},{24,16},{1,25},{9,1},{17,9},{25,17},{2,26},{10... | collective-permute-start | bytes 122888 | tf_op jit(solution)/shard_map/ppermute | solution.py:319
  31.0 4.4 %collective-permute-start.11 = (f32[4,4,640]{2,1,0:T(4,128)S(1)}, f32[4,4,640]{2,1,0:T(4,128)S(1)}, u32[]{:S(2)}, u32[]{:S(2)}) collective-permute-start(f32[4,4,640]{2,1,0:T(4,128)S(1)} %get-tuple-element.38.stat_ref.s0), channel_id=1, source_target_pairs={{0,16},{8,24},{16,0},{24,8},{1,17},{9,25},{17,1},{25,9},{2,18},{10... | collective-permute-start | bytes 122888 | tf_op jit(solution)/shard_map/ppermute | solution.py:319
  32.2 4.1 %collective-permute-start.10 = (f32[4,4,640]{2,1,0:T(4,128)S(1)}, f32[4,4,640]{2,1,0:T(4,128)S(1)}, u32[]{:S(2)}, u32[]{:S(2)}) collective-permute-start(f32[4,4,640]{2,1,0:T(4,128)S(1)} %get-tuple-element.38.stat_ref.s0), channel_id=1, source_target_pairs={{0,8},{8,16},{16,24},{24,0},{1,9},{9,17},{17,25},{25,1},{2,10},{10... | collective-permute-start | bytes 122888 | tf_op jit(solution)/shard_map/ppermute | solution.py:319
  40.3 19.6 %all-to-all-start = ((bf16[8,128,256]{2,1,0:T(8,128)(2,1)}), bf16[8,128,256]{2,1,0:T(8,128)(2,1)S(1)}, u32[]{:S(2)}, u32[]{:S(2)}) async-start(bf16[8,128,256]{2,1,0:T(8,128)(2,1)} %flush.1), calls=%async_computation | async-start | bytes 1048576 | tf_op jit(solution)/shard_map/all_to_all | solution.py:336
  47.7 5.1 %collective-permute-start.13 = (bf16[128,640]{1,0:T(8,128)(2,1)S(1)}, bf16[128,640]{1,0:T(8,128)(2,1)S(1)}, u32[]{:S(2)}, u32[]{:S(2)}) collective-permute-start(bf16[128,640]{1,0:T(8,128)(2,1)S(1)} %get-tuple-element.43), channel_id=1, source_target_pairs={{0,24},{8,0},{16,8},{24,16},{1,25},{9,1},{17,9},{25,17},{2,26},{10... | collective-permute-start | bytes 491528 | tf_op jit(solution)/shard_map/ppermute | solution.py:332
  48.2 5.8 %collective-permute-start.14 = (bf16[128,640]{1,0:T(8,128)(2,1)S(1)}, bf16[128,640]{1,0:T(8,128)(2,1)S(1)}, u32[]{:S(2)}, u32[]{:S(2)}) collective-permute-start(bf16[128,640]{1,0:T(8,128)(2,1)S(1)} %get-tuple-element.44), channel_id=1, source_target_pairs={{0,16},{8,24},{16,0},{24,8},{1,17},{9,25},{17,1},{25,9},{2,18},{10... | collective-permute-start | bytes 491528 | tf_op jit(solution)/shard_map/ppermute | solution.py:332
  49.2 6.4 %collective-permute-start.15 = (bf16[128,640]{1,0:T(8,128)(2,1)S(1)}, bf16[128,640]{1,0:T(8,128)(2,1)S(1)}, u32[]{:S(2)}, u32[]{:S(2)}) collective-permute-start(bf16[128,640]{1,0:T(8,128)(2,1)S(1)} %get-tuple-element.45), channel_id=1, source_target_pairs={{0,8},{8,16},{16,24},{24,0},{1,9},{9,17},{17,25},{25,1},{2,10},{10... | collective-permute-start | bytes 491528 | tf_op jit(solution)/shard_map/ppermute | solution.py:332
  62.2 9.5 %collective-permute-start.16 = (bf16[4,640,128]{2,1,0:T(8,128)(2,1)S(1)}, bf16[4,640,128]{2,1,0:T(8,128)(2,1)S(1)}, u32[]{:S(2)}, u32[]{:S(2)}) collective-permute-start(bf16[4,640,128]{2,1,0:T(8,128)(2,1)S(1)} %get-tuple-element.60), channel_id=1, source_target_pairs={{0,1},{1,0},{2,3},{3,2},{4,5},{5,4},{6,7},{7,6},{8,9},{9,8},{10,11... | collective-permute-start | bytes 1966088 | tf_op jit(solution)/shard_map/ppermute | solution.py:365
  71.8 9.1 %collective-permute-start.19 = (bf16[640,128]{1,0:T(8,128)(2,1)S(1)}, bf16[640,128]{1,0:T(8,128)(2,1)S(1)}, u32[]{:S(2)}, u32[]{:S(2)}) collective-permute-start(bf16[640,128]{1,0:T(8,128)(2,1)S(1)} %get-tuple-element.61), channel_id=1, source_target_pairs={{0,6},{2,0},{4,2},{6,4},{1,7},{3,1},{5,3},{7,5},{8,14},{10,8},{12,... | collective-permute-start | bytes 491528 | tf_op jit(solution)/shard_map/ppermute | solution.py:374
  74.4 6.6 %collective-permute-start.18 = (bf16[640,128]{1,0:T(8,128)(2,1)S(1)}, bf16[640,128]{1,0:T(8,128)(2,1)S(1)}, u32[]{:S(2)}, u32[]{:S(2)}) collective-permute-start(bf16[640,128]{1,0:T(8,128)(2,1)S(1)} %get-tuple-element.62), channel_id=1, source_target_pairs={{0,4},{2,6},{4,0},{6,2},{1,5},{3,7},{5,1},{7,3},{8,12},{10,14},{12... | collective-permute-start | bytes 491528 | tf_op jit(solution)/shard_map/ppermute | solution.py:374
  74.9 10.6 %collective-permute-start.17 = (bf16[640,128]{1,0:T(8,128)(2,1)S(1)}, bf16[640,128]{1,0:T(8,128)(2,1)S(1)}, u32[]{:S(2)}, u32[]{:S(2)}) collective-permute-start(bf16[640,128]{1,0:T(8,128)(2,1)S(1)} %get-tuple-element.63), channel_id=1, source_target_pairs={{0,2},{2,4},{4,6},{6,0},{1,3},{3,5},{5,7},{7,1},{8,10},{10,12},{12... | collective-permute-start | bytes 491528 | tf_op jit(solution)/shard_map/ppermute | solution.py:374

commit v8 on v7

--- a/solution.py
+++ b/solution.py
@@ -79,7 +79,7 @@
         query_block = NY * z + ((y - j) & (NY - 1))
         bits = jnp.int32(0)
         for i in range(ANC):
-            key_block = anc_ref[query_block, i]
+            key_block = anc_ref[i, query_block]
             bits = bits | jnp.where((key_block & (NY - 1)) == y, jnp.int32(1) << (key_block >> 2), 0)
         count = jnp.int32(0)
         for key_z in range(NZ):
@@ -199,9 +199,26 @@
     return pl.ds(pl.multiple_of((2 * ((place_ref[2] + step) & (NX - 1)) + core) * ROWS, ROWS), ROWS)
 
 
-def fetch_kernel(place_ref, dq_ref, wq_hbm, *refs):
+def fetch_kernel(place_ref, anc_ref, dq_ref, wq_hbm, cos_ref, sin_ref, *refs):
     blocks, sem = refs[:-1], refs[-1]
-    run_copies([(wq_hbm.at[weight_rows(place_ref, i), :], block) for i, block in enumerate(blocks)], sem)
+    copies = [
+        pltpu.make_async_copy(wq_hbm.at[weight_rows(place_ref, i), :], block, sem.at[i])
+        for i, block in enumerate(blocks)
+    ]
+    for copy in copies:
+        copy.start()
+    own_block = NY * place_ref[0] + place_ref[1]
+    depth = jnp.int32(0)
+    for i in range(ANC):
+        depth = depth + jnp.where(anc_ref[i, own_block] != own_block, 1, 0)
+    half = (HEAD // 2, BLOCK)
+    pair = lax.broadcasted_iota(I32, half, 0).astype(F32)
+    token_place = (lax.broadcasted_iota(I32, half, 1) + BLOCK * depth).astype(F32)
+    angles = jnp.exp(pair * (-2.0 * math.log(ROPE_BASE) / HEAD)) * token_place
+    cos_ref[...] = jnp.cos(angles)
+    sin_ref[...] = jnp.sin(angles)
+    for copy in copies:
+        copy.wait()
 
 
 def start_pair(place_ref, first, wk_hbm, wv_hbm, wk, wv, sem):
@@ -234,9 +251,7 @@
         copy.wait()
 
 
-def first_half_kernel(place_ref, cos_ref, sin_ref, dkv_ref, part_ref, wk, wv, wk_hbm, wv_hbm,
-                      out_ref, low_ref, wk_kept, wv_kept, sem):
-    copies = start_pair(place_ref, NX, wk_hbm, wv_hbm, wk_kept, wv_kept, sem)
+def first_half_kernel(cos_ref, sin_ref, dkv_ref, part_ref, wk, wv, out_ref, low_ref):
     total = dkv_ref[0].astype(F32)
     for a in range(1, NZ):
         total = total + dkv_ref[a].astype(F32)
@@ -244,12 +259,13 @@
     low_ref[HEAD:, :] = total[:, HEAD:].T.astype(BF16)
     for i in range(NX):
         out_ref[i] = (part_ref[i] + key_value_part(low_ref, wk[i], wv[i])).astype(BF16)
-    for copy in copies:
-        copy.wait()
-
-
-def second_half_kernel(low_ref, part_ref, wk, wv, out_ref):
+
+
+def second_half_kernel(place_ref, low_ref, part_ref, wk_hbm, wv_hbm, out_ref, wk, wv, sem):
+    copies = start_pair(place_ref, NX, wk_hbm, wv_hbm, wk, wv, sem)
     for i in range(NX):
+        for copy in copies[2 * i:2 * i + 2]:
+            copy.wait()
         out_ref[i] = part_ref[NX + i] + key_value_part(low_ref, wk[i], wv[i])
 
 
@@ -288,14 +304,6 @@
         above.append(lax.ppermute(above[-1], "z", shift(NZ, -1)))
     kvs = below + [lax.ppermute(below[-1], "z", shift(NZ, 1))] + above[:0:-1]
 
-    own_block = NY * z + y
-    own_row = lax.dynamic_slice_in_dim(ancestry, own_block, 1, 0)
-    depth = jnp.sum((own_row != own_block).astype(I32))
-    token_places = (BLOCK * depth + jnp.arange(BLOCK, dtype=I32)).astype(F32)
-    frequencies = jnp.exp(jnp.arange(HEAD // 2, dtype=F32) * (-2.0 * math.log(ROPE_BASE) / HEAD))
-    angles = frequencies[:, None] * token_places[None, :]
-    cosine = jnp.cos(angles)
-    sine = jnp.sin(angles)
     items = call(
         plan_kernel,
         jax.ShapeDtypeStruct((NY * PAIRS + NY, 4), I32),
@@ -303,8 +311,7 @@
         SM,
         "plan",
         [pltpu.SMEM((NZ + 1,), I32)],
-    )(place, ancestry, group)
-    items, cosine, sine = lax.optimization_barrier((items, cosine, sine))
+    )(place, ancestry.T, group)
 
     tiles = (NY * PAIRS, 2 * BLOCK, ROWS)
     stats, scores, prob_grads = call(
@@ -336,14 +343,14 @@
     dkv_own = lax.all_to_all(dkv, "z", 0, 0, tiled=True)
 
     wq, wk, wv = in_hbm(w_query, key_matrix, value_matrix)
-    blocks = call(
+    cosine, sine, *blocks = call(
         fetch_kernel,
-        [pltpu.VMEM((ROWS, ROWS), BF16)] * (2 * NX),
-        [SM, VM, HB],
-        [VM] * (2 * NX),
+        [pltpu.VMEM((HEAD // 2, BLOCK), F32)] * 2 + [pltpu.VMEM((ROWS, ROWS), BF16)] * (2 * NX),
+        [SM, SM, VM, HB],
+        [VM] * (2 * NX + 2),
         "fetch",
         [pltpu.SemaphoreType.DMA((2 * NX,))],
-    )(place, dq_parts[0], wq)
+    )(place, ancestry.T, dq_parts[0], wq)
     pair_shapes = [pltpu.VMEM((NX, ROWS, HEAD), BF16)] * 2
     query_part, wk_away, wv_away = call(
         query_part_kernel,
@@ -354,22 +361,22 @@
         [pltpu.SemaphoreType.DMA((2 * NX,))],
         QUERY_FLOPS,
     )(place, cosine, sine, *dq_own, wk, wv, *blocks)
-    away, low, wk_kept, wv_kept = call(
+    away, low = call(
         first_half_kernel,
-        [pltpu.VMEM((NX, ROWS, BLOCK), BF16), pltpu.VMEM((2 * HEAD, BLOCK), BF16)] + pair_shapes,
-        [SM] + [VM] * 6 + [HB] * 2,
-        [VM] * 4,
+        [pltpu.VMEM((NX, ROWS, BLOCK), BF16), pltpu.VMEM((2 * HEAD, BLOCK), BF16)],
+        [VM] * 6,
+        [VM] * 2,
         "first_half",
-        [pltpu.SemaphoreType.DMA((2 * NX,))],
-    )(place, cosine, sine, dkv_own, query_part, wk_away, wv_away, wk, wv)
+    )(cosine, sine, dkv_own, query_part, wk_away, wv_away)
     arrived = lax.ppermute(away, "c", shift(NC, 1))
     kept = call(
         second_half_kernel,
         pltpu.VMEM((NX, ROWS, BLOCK), F32),
-        [VM] * 4,
+        [SM] + [VM] * 2 + [HB] * 2,
         VM,
         "second_half",
-    )(low, query_part, wk_kept, wv_kept)
+        pair_shapes + [pltpu.SemaphoreType.DMA((2 * NX,))],
+    )(place, low, query_part, wk, wv)
     sent = [(kept[k] + arrived[k].astype(F32)).astype(BF16) for k in range(1, NX)]
     parts = [lax.ppermute(sent[k - 1], "x", shift(NX, k)) for k in range(1, NX)]
     return call(

time: 86.3 us -> 87 us (level)
  starting transfers between devices: 37.7 us -> 40.5 us
  other arithmetic: 1.81 us -> 0.21 us
    ppermute x3, waiting for transfers between devices: 2.77 us -> 5.83 us  [shards(): below.append(lax.ppermute(below[-1], 'z', shift(NZ, 1)))]
    ppermute x3, starting transfers between devices: 11.9 us -> 9.29 us  [shards(): above.append(lax.ppermute(above[-1], 'z', shift(NZ, -1)))]
    pallas_call x2, Pallas kernels: 3.97 us -> 6.5 us  [the longest x1 3.68 us: shards(): call(fetch_kernel, [pltpu.VMEM((HEAD // 2, BLOCK), F32)] * 2 + [pltpu.VME...]
    pallas_call x1, Pallas kernels: 2.32 us -> 0.62 us  [shards(): call(first_half_kernel, [pltpu.VMEM((NX, ROWS, BLOCK), BF16), pltpu.VMEM(...]
    ppermute x3, starting transfers between devices: 0.09 us -> 1.64 us  [shards(): below.append(lax.ppermute(below[-1], 'z', shift(NZ, 1)))]
    reduce_sum x1 -> x0, other arithmetic: 1.42 us -> none  [shards(): depth = jnp.sum((own_row != own_block).astype(I32))]
    ppermute x1, starting transfers between devices: 7.77 us -> 9.06 us  [shards(): arrived = lax.ppermute(away, 'c', shift(NC, 1))]
    ppermute x1, waiting for transfers between devices: 1.24 us -> 0.01 us  [shards(): arrived = lax.ppermute(away, 'c', shift(NC, 1))]
  transfers between devices with their start and end apart: 21 -> 21, of which waited for: 14 -> 12; matrix products, arithmetic and copies ran while one was open for 3% -> 0% of each run, Pallas kernels for 12% -> 15%
where the time goes in v8:
time: 87 us; the launch traced here: 87.5 us
  starting transfers between devices  40.5 us (47%)
  waiting for transfers between devices  23.9 us (27%)
  Pallas kernels  21.9 us (25%)
    ppermute x3, waiting for transfers between devices, shards(): parts = [lax.ppermute(sent[k - 1], 'x', shift(NX, k)) for k in range(1, NX)]  9.98 us
    ppermute x3, starting transfers between devices, shards(): above.append(lax.ppermute(above[-1], 'z', shift(NZ, -1)))  9.29 us
    ppermute x1, starting transfers between devices, shards(): arrived = lax.ppermute(away, 'c', shift(NC, 1))  9.06 us
    all_to_all x1, starting transfers between devices, shards(): dkv_own = lax.all_to_all(dkv, 'z', 0, 0, tiled=True)  8.15 us
    ppermute x3, waiting for transfers between devices, shards(): below.append(lax.ppermute(below[-1], 'z', shift(NZ, 1)))  5.83 us
    ppermute x3, starting transfers between devices, shards(): lax.ppermute(group, 'y', shift(NY, k))  4.68 us
    pallas_call x1, Pallas kernels, shards(): call(query_part_kernel, [pltpu.VMEM((2 * NX, ROWS, BLOCK), BF16)] + pair_...  3.78 us
    ppermute x3, starting transfers between devices, shards(): parts = [lax.ppermute(sent[k - 1], 'x', shift(NX, k)) for k in range(1, NX)]  3.69 us
  transfers between devices with their start and end apart: 21, of which 12 were waited for; matrix products, arithmetic and copies ran while one was open for 0% of the time, Pallas kernels for 15%

profile of v8, /device:TPU:1, one launch (start us, length us, event | category | flops | bytes accessed | tf_op | source)
XLA Modules:
  0.0 87.5 jit_solution(13374825086259541250)
XLA Ops:
  1.1 3.6 %collective-permute-start.9 = (bf16[1280,128]{1,0:T(8,128)(2,1)S(1)}, bf16[1280,128]{1,0:T(8,128)(2,1)S(1)}, u32[]{:S(2)}, u32[]{:S(2)}) collective-permute-start(bf16[1280,128]{1,0:T(8,128)(2,1)S(1)} %get-tuple-element.30.rows_ref.g0), channel_id=1, source_target_pairs={{0,24},{8,0},{16,8},{24,16},{1,25},{9,1},{17,9},{25,17},{2,26},{10... | collective-permute-start | bytes 983048 | tf_op jit(solution)/shard_map/ppermute | solution.py:300
  5.7 1.6 %collective-permute-start = (bf16[128,256]{1,0:T(8,128)(2,1)S(1)}, bf16[128,256]{1,0:T(8,128)(2,1)S(1)}, u32[]{:S(2)}, u32[]{:S(2)}) collective-permute-start(bf16[128,256]{1,0:T(8,128)(2,1)S(1)} %get-tuple-element.31.k0), channel_id=1, source_target_pairs={{0,32},{32,64},{64,96},{96,128},{128,160},{160,192},{192,224},{224... | collective-permute-start | bytes 196616 | tf_op jit(solution)/shard_map/ppermute | solution.py:303
  7.4 3.9 %collective-permute-start.4 = (bf16[128,256]{1,0:T(8,128)(2,1)S(1)}, bf16[128,256]{1,0:T(8,128)(2,1)S(1)}, u32[]{:S(2)}, u32[]{:S(2)}) collective-permute-start(bf16[128,256]{1,0:T(8,128)(2,1)S(1)} %get-tuple-element.31.k0), channel_id=1, source_target_pairs={{0,224},{32,0},{64,32},{96,64},{128,96},{160,128},{192,160},{224,1... | collective-permute-start | bytes 196616 | tf_op jit(solution)/shard_map/ppermute | solution.py:304
  11.3 1.9 %collective-permute-done.k1 = bf16[128,256]{1,0:T(8,128)(2,1)S(1)} collective-permute-done((bf16[128,256]{1,0:T(8,128)(2,1)S(1)}, bf16[128,256]{1,0:T(8,128)(2,1)S(1)}, u32[]{:S(2)}, u32[]{:S(2)}) %collective-permute-start) | collective-permute-done | bytes 65568 | tf_op jit(solution)/shard_map/ppermute | solution.py:303
  13.3 2.7 %collective-permute-start.5 = (bf16[128,256]{1,0:T(8,128)(2,1)S(1)}, bf16[128,256]{1,0:T(8,128)(2,1)S(1)}, u32[]{:S(2)}, u32[]{:S(2)}) collective-permute-start(bf16[128,256]{1,0:T(8,128)(2,1)S(1)} %collective-permute-done.4.k7), channel_id=1, source_target_pairs={{0,224},{32,0},{64,32},{96,64},{128,96},{160,128},{192,160},{224,1... | collective-permute-start | bytes 196616 | tf_op jit(solution)/shard_map/ppermute | solution.py:304
  15.9 1.9 %collective-permute-done.1.k2 = bf16[128,256]{1,0:T(8,128)(2,1)S(1)} collective-permute-done((bf16[128,256]{1,0:T(8,128)(2,1)S(1)}, bf16[128,256]{1,0:T(8,128)(2,1)S(1)}, u32[]{:S(2)}, u32[]{:S(2)}) %collective-permute-start.1) | collective-permute-done | bytes 65568 | tf_op jit(solution)/shard_map/ppermute | solution.py:303
  17.9 2.7 %collective-permute-start.6 = (bf16[128,256]{1,0:T(8,128)(2,1)S(1)}, bf16[128,256]{1,0:T(8,128)(2,1)S(1)}, u32[]{:S(2)}, u32[]{:S(2)}) collective-permute-start(bf16[128,256]{1,0:T(8,128)(2,1)S(1)} %collective-permute-done.5.k6), channel_id=1, source_target_pairs={{0,224},{32,0},{64,32},{96,64},{128,96},{160,128},{192,160},{224,1... | collective-permute-start | bytes 196616 | tf_op jit(solution)/shard_map/ppermute | solution.py:304
  20.6 1.9 %collective-permute-done.2.k3 = bf16[128,256]{1,0:T(8,128)(2,1)S(1)} collective-permute-done((bf16[128,256]{1,0:T(8,128)(2,1)S(1)}, bf16[128,256]{1,0:T(8,128)(2,1)S(1)}, u32[]{:S(2)}, u32[]{:S(2)}) %collective-permute-start.2) | collective-permute-done | bytes 65568 | tf_op jit(solution)/shard_map/ppermute | solution.py:303
  23.3 1.8 %plan.1.item_ref = s32[20,4]{1,0:T(8,128)S(1)} custom-call(s32[4]{0:T(128)S(1)} %pad_add_fusion.place_ref, s32[17,32]{1,0:T(8,128)S(1)} %bitcast.15, bf16[1280,128]{1,0:T(8,128)(2,1)S(1)} %get-tuple-element.30.rows_ref.g0), custom_call_target="tpu_custom_call" | custom-call | tf_op jit(solution)/shard_map/plan/pallas_call | solution.py:307
  25.1 1.7 %collective-permute-done.3.k4 = bf16[128,256]{1,0:T(8,128)(2,1)S(1)} collective-permute-done((bf16[128,256]{1,0:T(8,128)(2,1)S(1)}, bf16[128,256]{1,0:T(8,128)(2,1)S(1)}, u32[]{:S(2)}, u32[]{:S(2)}) %collective-permute-start.3) | collective-permute-done | bytes 65568 | tf_op jit(solution)/shard_map/ppermute | solution.py:305
  26.8 2.5 %stats.1 = (f32[4,4,640]{2,1,0:T(4,128)S(1)}, f32[16,256,640]{2,1,0:T(8,128)S(1)}, f32[16,256,640]{2,1,0:T(8,128)S(1)}) custom-call(s32[20,4]{1,0:T(8,128)S(1)} %plan.1.item_ref, bf16[128,256]{1,0:T(8,128)(2,1)S(1)} %get-tuple-element.31.k0, bf16[128,256]{1,0:T(8,128)(2,1)S(1)} %collective-permute-done.k1, bf16[128,256]{1,0:T(8,128)(2,1)S(1)} %collective-permute-done.1.k2, ...), custom_call_target="tpu_custom_call" | custom-call | flops 1342177280 | tf_op jit(solution)/shard_map/stats/pallas_call | solution.py:317
  29.9 2.0 %collective-permute-start.11 = (f32[4,4,640]{2,1,0:T(4,128)S(1)}, f32[4,4,640]{2,1,0:T(4,128)S(1)}, u32[]{:S(2)}, u32[]{:S(2)}) collective-permute-start(f32[4,4,640]{2,1,0:T(4,128)S(1)} %get-tuple-element.32.stat_ref.s0), channel_id=1, source_target_pairs={{0,16},{8,24},{16,0},{24,8},{1,17},{9,25},{17,1},{25,9},{2,18},{10... | collective-permute-start | bytes 122888 | tf_op jit(solution)/shard_map/ppermute | solution.py:326
  32.7 1.5 %collective-permute-done.11.s2 = f32[4,4,640]{2,1,0:T(4,128)S(1)} collective-permute-done((f32[4,4,640]{2,1,0:T(4,128)S(1)}, f32[4,4,640]{2,1,0:T(4,128)S(1)}, u32[]{:S(2)}, u32[]{:S(2)}) %collective-permute-start.11) | collective-permute-done | bytes 40992 | tf_op jit(solution)/shard_map/ppermute | solution.py:326
  34.2 1.7 %collective-permute-done.10.s1 = f32[4,4,640]{2,1,0:T(4,128)S(1)} collective-permute-done((f32[4,4,640]{2,1,0:T(4,128)S(1)}, f32[4,4,640]{2,1,0:T(4,128)S(1)}, u32[]{:S(2)}, u32[]{:S(2)}) %collective-permute-start.10) | collective-permute-done | bytes 40992 | tf_op jit(solution)/shard_map/ppermute | solution.py:326
  35.9 3.2 %grads.1 = (bf16[8,128,256]{2,1,0:T(8,128)(2,1)S(1)}, bf16[128,640]{1,0:T(8,128)(2,1)S(1)}, bf16[128,640]{1,0:T(8,128)(2,1)S(1)}, bf16[128,640]{1,0:T(8,128)(2,1)S(1)}, bf16[128,640]{1,0:T(8,128)(2,1)S(1)}) custom-call(s32[20,4]{1,0:T(8,128)S(1)} %plan.1.item_ref, bf16[8,128,128]{2,1,0:T(8,128)(2,1)S(1)} %turn.1.cols_ref, ...), custom_call_target="tpu_custom_call" | custom-call | flops 2013265920 | tf_op jit(solution)/shard_map/grads/pallas_call | solution.py:330
  40.0 8.2 %all-to-all-start = ((bf16[8,128,256]{2,1,0:T(8,128)(2,1)}), bf16[8,128,256]{2,1,0:T(8,128)(2,1)S(1)}, u32[]{:S(2)}, u32[]{:S(2)}) async-start(bf16[8,128,256]{2,1,0:T(8,128)(2,1)} %flush.1), calls=%async_computation | async-start | bytes 1048576 | tf_op jit(solution)/shard_map/all_to_all | solution.py:343
  49.6 3.7 %fetch.1 = (f32[64,128]{1,0:T(8,128)S(1)}, f32[64,128]{1,0:T(8,128)S(1)}, bf16[640,640]{1,0:T(8,128)(2,1)S(1)}, bf16[640,640]{1,0:T(8,128)(2,1)S(1)}, bf16[640,6...) custom-call(s32[4]{0:T(128)S(1)} %pad_add_fusion.place_ref, ...), custom_call_target="tpu_custom_call" | custom-call | tf_op jit(solution)/shard_map/fetch/pallas_call | solution.py:346
  54.0 1.7 %collective-permute-done.15.q3 = bf16[128,640]{1,0:T(8,128)(2,1)S(1)} collective-permute-done((bf16[128,640]{1,0:T(8,128)(2,1)S(1)}, bf16[128,640]{1,0:T(8,128)(2,1)S(1)}, u32[]{:S(2)}, u32[]{:S(2)}) %collective-permute-start.15) | collective-permute-done | bytes 163872 | tf_op jit(solution)/shard_map/ppermute | solution.py:339
  55.7 3.8 %query_part.1 = (bf16[8,640,128]{2,1,0:T(8,128)(2,1)S(1)}, bf16[4,640,128]{2,1,0:T(8,128)(2,1)S(1)}, bf16[4,640,128]{2,1,0:T(8,128)(2,1)S(1)}) custom-call(s32[4]{0:T(128)S(1)} %pad_add_fusion.place_ref, f32[64,128]{1,0:T(8,128)S(1)} %get-tuple-element.36.cos_ref, f32[64,128]{1,0:T(8,128)S(1)} %get-tuple-element.37.sin_ref, ...), custom_call_target="tpu_custom_call" | custom-call | flops 838860800 | tf_op jit(solution)/shard_map/query_part/pallas_call | solution.py:355
  60.9 9.1 %collective-permute-start.16 = (bf16[4,640,128]{2,1,0:T(8,128)(2,1)S(1)}, bf16[4,640,128]{2,1,0:T(8,128)(2,1)S(1)}, u32[]{:S(2)}, u32[]{:S(2)}) collective-permute-start(bf16[4,640,128]{2,1,0:T(8,128)(2,1)S(1)} %get-tuple-element.54), channel_id=1, source_target_pairs={{0,1},{1,0},{2,3},{3,2},{4,5},{5,4},{6,7},{7,6},{8,9},{9,8},{10,11... | collective-permute-start | bytes 1966088 | tf_op jit(solution)/shard_map/ppermute | solution.py:371
  70.0 2.8 %second_half.1 = f32[4,640,128]{2,1,0:T(8,128)S(1)} custom-call(s32[4]{0:T(128)S(1)} %pad_add_fusion.place_ref, bf16[256,128]{1,0:T(8,128)(2,1)S(1)} %get-tuple-element.53.low_ref, bf16[8,640,128]{2,1,0:T(8,128)(2,1)S(1)} %get-tuple-element.50.part_ref, bf16[5120,128]{1,0:T(8,128)(2,1)} %wk_hbm.3, bf16[5120,128]{1,0:T(8,128)(2,1)} %wv_hbm.3), custom_call_target="tpu_custom_call" | custom-call | tf_op jit(solution)/shard_map/second_half/pallas_call | solution.py:372
  72.9 2.5 %collective-permute-start.19 = (bf16[640,128]{1,0:T(8,128)(2,1)S(1)}, bf16[640,128]{1,0:T(8,128)(2,1)S(1)}, u32[]{:S(2)}, u32[]{:S(2)}) collective-permute-start(bf16[640,128]{1,0:T(8,128)(2,1)S(1)} %get-tuple-element.55), channel_id=1, source_target_pairs={{0,6},{2,0},{4,2},{6,4},{1,7},{3,1},{5,3},{7,5},{8,14},{10,8},{12,... | collective-permute-start | bytes 491528 | tf_op jit(solution)/shard_map/ppermute | solution.py:381
  76.7 5.8 %collective-permute-done.19.p2 = bf16[640,128]{1,0:T(8,128)(2,1)S(1)} collective-permute-done((bf16[640,128]{1,0:T(8,128)(2,1)S(1)}, bf16[640,128]{1,0:T(8,128)(2,1)S(1)}, u32[]{:S(2)}, u32[]{:S(2)}) %collective-permute-start.19) | collective-permute-done | bytes 163872 | tf_op jit(solution)/shard_map/ppermute | solution.py:381
  82.5 4.1 %collective-permute-done.17.p0 = bf16[640,128]{1,0:T(8,128)(2,1)S(1)} collective-permute-done((bf16[640,128]{1,0:T(8,128)(2,1)S(1)}, bf16[640,128]{1,0:T(8,128)(2,1)S(1)}, u32[]{:S(2)}, u32[]{:S(2)}) %collective-permute-start.17) | collective-permute-done | bytes 163872 | tf_op jit(solution)/shard_map/ppermute | solution.py:381
  (36 shorter events, 10.9 us)
Async XLA Ops:
  1.1 25.8 %collective-permute-start.9 = (bf16[1280,128]{1,0:T(8,128)(2,1)S(1)}, bf16[1280,128]{1,0:T(8,128)(2,1)S(1)}, u32[]{:S(2)}, u32[]{:S(2)}) collective-permute-start(bf16[1280,128]{1,0:T(8,128)(2,1)S(1)} %get-tuple-element.30.rows_ref.g0), channel_id=1, source_target_pairs={{0,24},{8,0},{16,8},{24,16},{1,25},{9,1},{17,9},{25,17},{2,26},{10... | collective-permute-start | bytes 983048 | tf_op jit(solution)/shard_map/ppermute | solution.py:300
  4.7 22.1 %collective-permute-start.8 = (bf16[1280,128]{1,0:T(8,128)(2,1)S(1)}, bf16[1280,128]{1,0:T(8,128)(2,1)S(1)}, u32[]{:S(2)}, u32[]{:S(2)}) collective-permute-start(bf16[1280,128]{1,0:T(8,128)(2,1)S(1)} %get-tuple-element.30.rows_ref.g0), channel_id=1, source_target_pairs={{0,16},{8,24},{16,0},{24,8},{1,17},{9,25},{17,1},{25,9},{2,18},{10... | collective-permute-start | bytes 983048 | tf_op jit(solution)/shard_map/ppermute | solution.py:300
  5.0 21.8 %collective-permute-start.7 = (bf16[1280,128]{1,0:T(8,128)(2,1)S(1)}, bf16[1280,128]{1,0:T(8,128)(2,1)S(1)}, u32[]{:S(2)}, u32[]{:S(2)}) collective-permute-start(bf16[1280,128]{1,0:T(8,128)(2,1)S(1)} %get-tuple-element.30.rows_ref.g0), channel_id=1, source_target_pairs={{0,8},{8,16},{16,24},{24,0},{1,9},{9,17},{17,25},{25,1},{2,10},{10... | collective-permute-start | bytes 983048 | tf_op jit(solution)/shard_map/ppermute | solution.py:300
  5.7 7.5 %collective-permute-start = (bf16[128,256]{1,0:T(8,128)(2,1)S(1)}, bf16[128,256]{1,0:T(8,128)(2,1)S(1)}, u32[]{:S(2)}, u32[]{:S(2)}) collective-permute-start(bf16[128,256]{1,0:T(8,128)(2,1)S(1)} %get-tuple-element.31.k0), channel_id=1, source_target_pairs={{0,32},{32,64},{64,96},{96,128},{128,160},{160,192},{192,224},{224... | collective-permute-start | bytes 196616 | tf_op jit(solution)/shard_map/ppermute | solution.py:303
  7.4 5.9 %collective-permute-start.4 = (bf16[128,256]{1,0:T(8,128)(2,1)S(1)}, bf16[128,256]{1,0:T(8,128)(2,1)S(1)}, u32[]{:S(2)}, u32[]{:S(2)}) collective-permute-start(bf16[128,256]{1,0:T(8,128)(2,1)S(1)} %get-tuple-element.31.k0), channel_id=1, source_target_pairs={{0,224},{32,0},{64,32},{96,64},{128,96},{160,128},{192,160},{224,1... | collective-permute-start | bytes 196616 | tf_op jit(solution)/shard_map/ppermute | solution.py:304
  13.3 4.6 %collective-permute-start.1 = (bf16[128,256]{1,0:T(8,128)(2,1)S(1)}, bf16[128,256]{1,0:T(8,128)(2,1)S(1)}, u32[]{:S(2)}, u32[]{:S(2)}) collective-permute-start(bf16[128,256]{1,0:T(8,128)(2,1)S(1)} %collective-permute-done.k1), channel_id=1, source_target_pairs={{0,32},{32,64},{64,96},{96,128},{128,160},{160,192},{192,224},{224... | collective-permute-start | bytes 196616 | tf_op jit(solution)/shard_map/ppermute | solution.py:303
  13.3 4.6 %collective-permute-start.5 = (bf16[128,256]{1,0:T(8,128)(2,1)S(1)}, bf16[128,256]{1,0:T(8,128)(2,1)S(1)}, u32[]{:S(2)}, u32[]{:S(2)}) collective-permute-start(bf16[128,256]{1,0:T(8,128)(2,1)S(1)} %collective-permute-done.4.k7), channel_id=1, source_target_pairs={{0,224},{32,0},{64,32},{96,64},{128,96},{160,128},{192,160},{224,1... | collective-permute-start | bytes 196616 | tf_op jit(solution)/shard_map/ppermute | solution.py:304
  17.9 4.6 %collective-permute-start.2 = (bf16[128,256]{1,0:T(8,128)(2,1)S(1)}, bf16[128,256]{1,0:T(8,128)(2,1)S(1)}, u32[]{:S(2)}, u32[]{:S(2)}) collective-permute-start(bf16[128,256]{1,0:T(8,128)(2,1)S(1)} %collective-permute-done.1.k2), channel_id=1, source_target_pairs={{0,32},{32,64},{64,96},{96,128},{128,160},{160,192},{192,224},{224... | collective-permute-start | bytes 196616 | tf_op jit(solution)/shard_map/ppermute | solution.py:303
  17.9 7.2 %collective-permute-start.6 = (bf16[128,256]{1,0:T(8,128)(2,1)S(1)}, bf16[128,256]{1,0:T(8,128)(2,1)S(1)}, u32[]{:S(2)}, u32[]{:S(2)}) collective-permute-start(bf16[128,256]{1,0:T(8,128)(2,1)S(1)} %collective-permute-done.5.k6), channel_id=1, source_target_pairs={{0,224},{32,0},{64,32},{96,64},{128,96},{160,128},{192,160},{224,1... | collective-permute-start | bytes 196616 | tf_op jit(solution)/shard_map/ppermute | solution.py:304
  22.5 4.3 %collective-permute-start.3 = (bf16[128,256]{1,0:T(8,128)(2,1)S(1)}, bf16[128,256]{1,0:T(8,128)(2,1)S(1)}, u32[]{:S(2)}, u32[]{:S(2)}) collective-permute-start(bf16[128,256]{1,0:T(8,128)(2,1)S(1)} %collective-permute-done.2.k3), channel_id=1, source_target_pairs={{0,32},{32,64},{64,96},{96,128},{128,160},{160,192},{192,224},{224... | collective-permute-start | bytes 196616 | tf_op jit(solution)/shard_map/ppermute | solution.py:305
  22.6 0.7 copy-start
  29.3 3.4 %collective-permute-start.12 = (f32[4,4,640]{2,1,0:T(4,128)S(1)}, f32[4,4,640]{2,1,0:T(4,128)S(1)}, u32[]{:S(2)}, u32[]{:S(2)}) collective-permute-start(f32[4,4,640]{2,1,0:T(4,128)S(1)} %get-tuple-element.32.stat_ref.s0), channel_id=1, source_target_pairs={{0,24},{8,0},{16,8},{24,16},{1,25},{9,1},{17,9},{25,17},{2,26},{10... | collective-permute-start | bytes 122888 | tf_op jit(solution)/shard_map/ppermute | solution.py:326
  29.9 4.4 %collective-permute-start.11 = (f32[4,4,640]{2,1,0:T(4,128)S(1)}, f32[4,4,640]{2,1,0:T(4,128)S(1)}, u32[]{:S(2)}, u32[]{:S(2)}) collective-permute-start(f32[4,4,640]{2,1,0:T(4,128)S(1)} %get-tuple-element.32.stat_ref.s0), channel_id=1, source_target_pairs={{0,16},{8,24},{16,0},{24,8},{1,17},{9,25},{17,1},{25,9},{2,18},{10... | collective-permute-start | bytes 122888 | tf_op jit(solution)/shard_map/ppermute | solution.py:326
  31.9 4.1 %collective-permute-start.10 = (f32[4,4,640]{2,1,0:T(4,128)S(1)}, f32[4,4,640]{2,1,0:T(4,128)S(1)}, u32[]{:S(2)}, u32[]{:S(2)}) collective-permute-start(f32[4,4,640]{2,1,0:T(4,128)S(1)} %get-tuple-element.32.stat_ref.s0), channel_id=1, source_target_pairs={{0,8},{8,16},{16,24},{24,0},{1,9},{9,17},{17,25},{25,1},{2,10},{10... | collective-permute-start | bytes 122888 | tf_op jit(solution)/shard_map/ppermute | solution.py:326
  39.1 10.5 %copy-start.1 = (s32[32,17]{0,1:T(8,128)S(1)}, s32[32,17]{0,1:T(8,128)}, u32[]{:S(2)}) copy-start(s32[32,17]{0,1:T(8,128)} %param.12) | copy-start | bytes 6532
  40.0 20.3 %all-to-all-start = ((bf16[8,128,256]{2,1,0:T(8,128)(2,1)}), bf16[8,128,256]{2,1,0:T(8,128)(2,1)S(1)}, u32[]{:S(2)}, u32[]{:S(2)}) async-start(bf16[8,128,256]{2,1,0:T(8,128)(2,1)} %flush.1), calls=%async_computation | async-start | bytes 1048576 | tf_op jit(solution)/shard_map/all_to_all | solution.py:343
  48.1 5.2 %collective-permute-start.13 = (bf16[128,640]{1,0:T(8,128)(2,1)S(1)}, bf16[128,640]{1,0:T(8,128)(2,1)S(1)}, u32[]{:S(2)}, u32[]{:S(2)}) collective-permute-start(bf16[128,640]{1,0:T(8,128)(2,1)S(1)} %get-tuple-element.39), channel_id=1, source_target_pairs={{0,24},{8,0},{16,8},{24,16},{1,25},{9,1},{17,9},{25,17},{2,26},{10... | collective-permute-start | bytes 491528 | tf_op jit(solution)/shard_map/ppermute | solution.py:339
  48.2 5.9 %collective-permute-start.14 = (bf16[128,640]{1,0:T(8,128)(2,1)S(1)}, bf16[128,640]{1,0:T(8,128)(2,1)S(1)}, u32[]{:S(2)}, u32[]{:S(2)}) collective-permute-start(bf16[128,640]{1,0:T(8,128)(2,1)S(1)} %get-tuple-element.40), channel_id=1, source_target_pairs={{0,16},{8,24},{16,0},{24,8},{1,17},{9,25},{17,1},{25,9},{2,18},{10... | collective-permute-start | bytes 491528 | tf_op jit(solution)/shard_map/ppermute | solution.py:339
  49.1 6.5 %collective-permute-start.15 = (bf16[128,640]{1,0:T(8,128)(2,1)S(1)}, bf16[128,640]{1,0:T(8,128)(2,1)S(1)}, u32[]{:S(2)}, u32[]{:S(2)}) collective-permute-start(bf16[128,640]{1,0:T(8,128)(2,1)S(1)} %get-tuple-element.41), channel_id=1, source_target_pairs={{0,8},{8,16},{16,24},{24,0},{1,9},{9,17},{17,25},{25,1},{2,10},{10... | collective-permute-start | bytes 491528 | tf_op jit(solution)/shard_map/ppermute | solution.py:339
  60.9 11.9 %collective-permute-start.16 = (bf16[4,640,128]{2,1,0:T(8,128)(2,1)S(1)}, bf16[4,640,128]{2,1,0:T(8,128)(2,1)S(1)}, u32[]{:S(2)}, u32[]{:S(2)}) collective-permute-start(bf16[4,640,128]{2,1,0:T(8,128)(2,1)S(1)} %get-tuple-element.54), channel_id=1, source_target_pairs={{0,1},{1,0},{2,3},{3,2},{4,5},{5,4},{6,7},{7,6},{8,9},{9,8},{10,11... | collective-permute-start | bytes 1966088 | tf_op jit(solution)/shard_map/ppermute | solution.py:371
  72.9 9.5 %collective-permute-start.19 = (bf16[640,128]{1,0:T(8,128)(2,1)S(1)}, bf16[640,128]{1,0:T(8,128)(2,1)S(1)}, u32[]{:S(2)}, u32[]{:S(2)}) collective-permute-start(bf16[640,128]{1,0:T(8,128)(2,1)S(1)} %get-tuple-element.55), channel_id=1, source_target_pairs={{0,6},{2,0},{4,2},{6,4},{1,7},{3,1},{5,3},{7,5},{8,14},{10,8},{12,... | collective-permute-start | bytes 491528 | tf_op jit(solution)/shard_map/ppermute | solution.py:381
  75.5 7.0 %collective-permute-start.18 = (bf16[640,128]{1,0:T(8,128)(2,1)S(1)}, bf16[640,128]{1,0:T(8,128)(2,1)S(1)}, u32[]{:S(2)}, u32[]{:S(2)}) collective-permute-start(bf16[640,128]{1,0:T(8,128)(2,1)S(1)} %get-tuple-element.56), channel_id=1, source_target_pairs={{0,4},{2,6},{4,0},{6,2},{1,5},{3,7},{5,1},{7,3},{8,12},{10,14},{12... | collective-permute-start | bytes 491528 | tf_op jit(solution)/shard_map/ppermute | solution.py:381
  76.0 10.6 %collective-permute-start.17 = (bf16[640,128]{1,0:T(8,128)(2,1)S(1)}, bf16[640,128]{1,0:T(8,128)(2,1)S(1)}, u32[]{:S(2)}, u32[]{:S(2)}) collective-permute-start(bf16[640,128]{1,0:T(8,128)(2,1)S(1)} %get-tuple-element.57), channel_id=1, source_target_pairs={{0,2},{2,4},{4,6},{6,0},{1,3},{3,5},{5,7},{7,1},{8,10},{10,12},{12... | collective-permute-start | bytes 491528 | tf_op jit(solution)/shard_map/ppermute | solution.py:381

commit v9 on v8

--- a/solution.py
+++ b/solution.py
@@ -21,6 +21,7 @@
 NN = (((1,), (0,)), ((), ()))
 F32, BF16, I32 = jnp.float32, jnp.bfloat16, jnp.int32
 VMEM_LIMIT = 16 << 20
+PLAN_FLOPS = 1_000_000_000
 STATS_FLOPS = 2 * 2 * (NY * ROWS) * (NZ * BLOCK) * HEAD
 GRADS_FLOPS = 3 * 2 * (NY * ROWS) * (NZ * BLOCK) * HEAD
 QUERY_FLOPS = 2 * BLOCK * ROWS * 2 * NX * ROWS
@@ -195,7 +196,7 @@
 
 
 def weight_rows(place_ref, step):
-    core = 1 - place_ref[3] if step < NX else place_ref[3]
+    core = place_ref[3] if step < NX else 1 - place_ref[3]
     return pl.ds(pl.multiple_of((2 * ((place_ref[2] + step) & (NX - 1)) + core) * ROWS, ROWS), ROWS)
 
 
@@ -251,33 +252,33 @@
         copy.wait()
 
 
-def first_half_kernel(cos_ref, sin_ref, dkv_ref, part_ref, wk, wv, out_ref, low_ref):
+def first_half_kernel(cos_ref, sin_ref, dkv_ref, part_ref, wk, wv, kept_ref, b1, b2, b3, low_ref):
     total = dkv_ref[0].astype(F32)
     for a in range(1, NZ):
         total = total + dkv_ref[a].astype(F32)
     low_ref[:HEAD, :] = unrotate(total[:, :HEAD].T, cos_ref[...], sin_ref[...]).astype(BF16)
     low_ref[HEAD:, :] = total[:, HEAD:].T.astype(BF16)
-    for i in range(NX):
-        out_ref[i] = (part_ref[i] + key_value_part(low_ref, wk[i], wv[i])).astype(BF16)
-
-
-def second_half_kernel(place_ref, low_ref, part_ref, wk_hbm, wv_hbm, out_ref, wk, wv, sem):
+    for i, out_ref in enumerate((kept_ref, b1, b2, b3)):
+        out_ref[...] = (part_ref[i] + key_value_part(low_ref, wk[i], wv[i])).astype(out_ref.dtype)
+
+
+def second_half_kernel(place_ref, low_ref, part_ref, wk_hbm, wv_hbm, b4, b5, b6, b7, wk, wv, sem):
     copies = start_pair(place_ref, NX, wk_hbm, wv_hbm, wk, wv, sem)
-    for i in range(NX):
+    for i, out_ref in enumerate((b4, b5, b6, b7)):
         for copy in copies[2 * i:2 * i + 2]:
             copy.wait()
-        out_ref[i] = part_ref[NX + i] + key_value_part(low_ref, wk[i], wv[i])
+        out_ref[...] = (part_ref[NX + i] + key_value_part(low_ref, wk[i], wv[i])).astype(out_ref.dtype)
 
 
 def key_value_part(low_ref, wk, wv):
     return dot_nn(wk, low_ref[:HEAD, :]) + dot_nn(wv, low_ref[HEAD:, :])
 
 
-def finish_kernel(kept_ref, arrived_ref, p0, p1, p2, out_ref):
+def finish_kernel(kept_ref, p1, p2, p3, p4, p5, p6, p7, out_ref):
     for h in range(GROUP):
         rows = slice(h * HEAD, (h + 1) * HEAD)
         total = kept_ref[rows, :]
-        for part in (arrived_ref, p0, p1, p2):
+        for part in (p1, p2, p3, p4, p5, p6, p7):
             total = total + part[rows, :].astype(F32)
         out_ref[:, rows] = total.T.astype(BF16)
 
@@ -297,13 +298,13 @@
         "stack",
         [pltpu.SemaphoreType.DMA((2 * GROUP + 2,))],
     )(*in_hbm(queries, out_grad, keys, values))
-    groups = [group] + [lax.ppermute(group, "y", shift(NY, k)) for k in range(1, NY)]
     below, above = [kv], [kv]
     for r in range(1, NZ // 2):
         below.append(lax.ppermute(below[-1], "z", shift(NZ, 1)))
         above.append(lax.ppermute(above[-1], "z", shift(NZ, -1)))
     kvs = below + [lax.ppermute(below[-1], "z", shift(NZ, 1))] + above[:0:-1]
 
+    groups = [group] + [lax.ppermute(group, "y", shift(NY, k)) for k in range(1, NY)]
     items = call(
         plan_kernel,
         jax.ShapeDtypeStruct((NY * PAIRS + NY, 4), I32),
@@ -311,6 +312,7 @@
         SM,
         "plan",
         [pltpu.SMEM((NZ + 1,), I32)],
+        PLAN_FLOPS,
     )(place, ancestry.T, group)
 
     tiles = (NY * PAIRS, 2 * BLOCK, ROWS)
@@ -352,7 +354,7 @@
         [pltpu.SemaphoreType.DMA((2 * NX,))],
     )(place, ancestry.T, dq_parts[0], wq)
     pair_shapes = [pltpu.VMEM((NX, ROWS, HEAD), BF16)] * 2
-    query_part, wk_away, wv_away = call(
+    query_part, wk_first, wv_first = call(
         query_part_kernel,
         [pltpu.VMEM((2 * NX, ROWS, BLOCK), BF16)] + pair_shapes,
         [SM] + [VM] * (2 + NY) + [HB] * 2 + [VM] * (2 * NX),
@@ -361,27 +363,30 @@
         [pltpu.SemaphoreType.DMA((2 * NX,))],
         QUERY_FLOPS,
     )(place, cosine, sine, *dq_own, wk, wv, *blocks)
-    away, low = call(
+    block = pltpu.VMEM((ROWS, BLOCK), BF16)
+    kept, b1, b2, b3, low = call(
         first_half_kernel,
-        [pltpu.VMEM((NX, ROWS, BLOCK), BF16), pltpu.VMEM((2 * HEAD, BLOCK), BF16)],
+        [pltpu.VMEM((ROWS, BLOCK), F32), block, block, block, pltpu.VMEM((2 * HEAD, BLOCK), BF16)],
         [VM] * 6,
-        [VM] * 2,
+        [VM] * 5,
         "first_half",
-    )(cosine, sine, dkv_own, query_part, wk_away, wv_away)
-    arrived = lax.ppermute(away, "c", shift(NC, 1))
-    kept = call(
+    )(cosine, sine, dkv_own, query_part, wk_first, wv_first)
+    others = call(
         second_half_kernel,
-        pltpu.VMEM((NX, ROWS, BLOCK), F32),
+        [block] * NX,
         [SM] + [VM] * 2 + [HB] * 2,
-        VM,
+        [VM] * NX,
         "second_half",
         pair_shapes + [pltpu.SemaphoreType.DMA((2 * NX,))],
     )(place, low, query_part, wk, wv)
-    sent = [(kept[k] + arrived[k].astype(F32)).astype(BF16) for k in range(1, NX)]
-    parts = [lax.ppermute(sent[k - 1], "x", shift(NX, k)) for k in range(1, NX)]
+    parts = []
+    for step, sent in enumerate([b1, b2, b3, *others], start=1):
+        flip, dx = divmod(step, NX)
+        pairs = [(NC * a + core, NC * ((a + dx) % NX) + (core ^ flip)) for a in range(NX) for core in range(NC)]
+        parts.append(lax.ppermute(sent, ("x", "c"), pairs))
     return call(
-        finish_kernel, jax.ShapeDtypeStruct((BLOCK, ROWS), BF16), [VM] * (2 + len(parts)), VM, "finish",
-    )(kept[0], arrived[0], *parts)
+        finish_kernel, jax.ShapeDtypeStruct((BLOCK, ROWS), BF16), [VM] * (1 + len(parts)), VM, "finish",
+    )(kept, *parts)
 
 
 def solution(mesh):

time: 87 us -> 90.3 us (1.038); the launches traced: 87.5 us -> 89.5 us
  starting transfers between devices: 40.5 us -> 47.6 us
  waiting for transfers between devices: 23.9 us -> 19 us
    ppermute x3, waiting for transfers between devices: 5.83 us -> 0.6 us  [shards(): below.append(lax.ppermute(below[-1], 'z', shift(NZ, 1)))]
    ppermute x4 -> x7, starting transfers between devices: 12.7 us -> 16.6 us  [shards(): parts.append(lax.ppermute(sent, ('x', 'c'), pairs))]
    ppermute x3, waiting for transfers between devices: 0.01 us -> 2.28 us  [shards(): above.append(lax.ppermute(above[-1], 'z', shift(NZ, -1)))]
    ppermute x4 -> x7, waiting for transfers between devices: 9.98 us -> 8.62 us  [shards(): parts.append(lax.ppermute(sent, ('x', 'c'), pairs))]
    all_to_all x1, starting transfers between devices: 8.15 us -> 9.32 us  [shards(): dkv_own = lax.all_to_all(dkv, 'z', 0, 0, tiled=True)]
    ppermute x3, starting transfers between devices: 9.29 us -> 10.3 us  [shards(): above.append(lax.ppermute(above[-1], 'z', shift(NZ, -1)))]
    ppermute x3, starting transfers between devices: 1.64 us -> 2.55 us  [shards(): below.append(lax.ppermute(below[-1], 'z', shift(NZ, 1)))]
    ppermute x3, starting transfers between devices: 4.68 us -> 3.77 us  [shards(): lax.ppermute(group, 'y', shift(NY, k))]
  transfers between devices with their start and end apart: 21 -> 24, of which waited for: 12 -> 12; matrix products, arithmetic and copies ran while one was open for 0% -> 0% of each run, Pallas kernels for 15% -> 14%
where the time goes in v9:
time: 90.3 us; the launch traced here: 89.5 us
  starting transfers between devices  47.6 us (53%)
  Pallas kernels  22 us (24%)
  waiting for transfers between devices  19 us (21%)
    ppermute x7, starting transfers between devices, shards(): parts.append(lax.ppermute(sent, ('x', 'c'), pairs))  16.6 us
    ppermute x3, starting transfers between devices, shards(): above.append(lax.ppermute(above[-1], 'z', shift(NZ, -1)))  10.3 us
    all_to_all x1, starting transfers between devices, shards(): dkv_own = lax.all_to_all(dkv, 'z', 0, 0, tiled=True)  9.32 us
    ppermute x7, waiting for transfers between devices, shards(): parts.append(lax.ppermute(sent, ('x', 'c'), pairs))  8.62 us
    pallas_call x1, Pallas kernels, shards(): call(query_part_kernel, [pltpu.VMEM((2 * NX, ROWS, BLOCK), BF16)] + pair_...  3.78 us
    ppermute x3, starting transfers between devices, shards(): lax.ppermute(group, 'y', shift(NY, k))  3.77 us
    pallas_call x1, Pallas kernels, shards(): call(fetch_kernel, [pltpu.VMEM((HEAD // 2, BLOCK), F32)] * 2 + [pltpu.VME...  3.68 us
    pallas_call x1, Pallas kernels, shards(): call(grads_kernel, [pltpu.VMEM((NZ, BLOCK, 2 * HEAD), BF16)] + [pltpu.VME...  3.2 us
  transfers between devices with their start and end apart: 24, of which 12 were waited for; matrix products, arithmetic and copies ran while one was open for 0% of the time, Pallas kernels for 14%

profile of v9, /device:TPU:1, one launch (start us, length us, event | category | flops | bytes accessed | tf_op | source)
XLA Modules:
  0.0 89.5 jit_solution(5846953092411081334)
XLA Ops:
  1.1 2.5 %collective-permute-start = (bf16[128,256]{1,0:T(8,128)(2,1)S(1)}, bf16[128,256]{1,0:T(8,128)(2,1)S(1)}, u32[]{:S(2)}, u32[]{:S(2)}) collective-permute-start(bf16[128,256]{1,0:T(8,128)(2,1)S(1)} %get-tuple-element.38.k0), channel_id=1, source_target_pairs={{0,32},{32,64},{64,96},{96,128},{128,160},{160,192},{192,224},{224... | collective-permute-start | bytes 196616 | tf_op jit(solution)/shard_map/ppermute | solution.py:303
  3.6 2.7 %collective-permute-start.9 = (bf16[1280,128]{1,0:T(8,128)(2,1)S(1)}, bf16[1280,128]{1,0:T(8,128)(2,1)S(1)}, u32[]{:S(2)}, u32[]{:S(2)}) collective-permute-start(bf16[1280,128]{1,0:T(8,128)(2,1)S(1)} %get-tuple-element.37.rows_ref.g0), channel_id=1, source_target_pairs={{0,24},{8,0},{16,8},{24,16},{1,25},{9,1},{17,9},{25,17},{2,26},{10... | collective-permute-start | bytes 983048 | tf_op jit(solution)/shard_map/ppermute | solution.py:307
  7.4 4.0 %collective-permute-start.4 = (bf16[128,256]{1,0:T(8,128)(2,1)S(1)}, bf16[128,256]{1,0:T(8,128)(2,1)S(1)}, u32[]{:S(2)}, u32[]{:S(2)}) collective-permute-start(bf16[128,256]{1,0:T(8,128)(2,1)S(1)} %get-tuple-element.38.k0), channel_id=1, source_target_pairs={{0,224},{32,0},{64,32},{96,64},{128,96},{160,128},{192,160},{224,1... | collective-permute-start | bytes 196616 | tf_op jit(solution)/shard_map/ppermute | solution.py:304
  11.4 1.3 %collective-permute-done.4.k7 = bf16[128,256]{1,0:T(8,128)(2,1)S(1)} collective-permute-done((bf16[128,256]{1,0:T(8,128)(2,1)S(1)}, bf16[128,256]{1,0:T(8,128)(2,1)S(1)}, u32[]{:S(2)}, u32[]{:S(2)}) %collective-permute-start.4) | collective-permute-done | bytes 65568 | tf_op jit(solution)/shard_map/ppermute | solution.py:304
  12.7 3.0 %collective-permute-start.5 = (bf16[128,256]{1,0:T(8,128)(2,1)S(1)}, bf16[128,256]{1,0:T(8,128)(2,1)S(1)}, u32[]{:S(2)}, u32[]{:S(2)}) collective-permute-start(bf16[128,256]{1,0:T(8,128)(2,1)S(1)} %collective-permute-done.4.k7), channel_id=1, source_target_pairs={{0,224},{32,0},{64,32},{96,64},{128,96},{160,128},{192,160},{224,1... | collective-permute-start | bytes 196616 | tf_op jit(solution)/shard_map/ppermute | solution.py:304
  17.1 3.3 %collective-permute-start.6 = (bf16[128,256]{1,0:T(8,128)(2,1)S(1)}, bf16[128,256]{1,0:T(8,128)(2,1)S(1)}, u32[]{:S(2)}, u32[]{:S(2)}) collective-permute-start(bf16[128,256]{1,0:T(8,128)(2,1)S(1)} %collective-permute-done.5.k6), channel_id=1, source_target_pairs={{0,224},{32,0},{64,32},{96,64},{128,96},{160,128},{192,160},{224,1... | collective-permute-start | bytes 196616 | tf_op jit(solution)/shard_map/ppermute | solution.py:304
  21.4 1.8 %plan.1.item_ref = s32[20,4]{1,0:T(8,128)S(1)} custom-call(s32[4]{0:T(128)S(1)} %pad_add_fusion.place_ref, s32[17,32]{1,0:T(8,128)S(1)} %bitcast.5, bf16[1280,128]{1,0:T(8,128)(2,1)S(1)} %get-tuple-element.37.rows_ref.g0), custom_call_target="tpu_custom_call" | custom-call | flops 1000000000 | tf_op jit(solution)/shard_map/plan/pallas_call | solution.py:308
  23.2 1.8 %collective-permute-done.3.k4 = bf16[128,256]{1,0:T(8,128)(2,1)S(1)} collective-permute-done((bf16[128,256]{1,0:T(8,128)(2,1)S(1)}, bf16[128,256]{1,0:T(8,128)(2,1)S(1)}, u32[]{:S(2)}, u32[]{:S(2)}) %collective-permute-start.3) | collective-permute-done | bytes 65568 | tf_op jit(solution)/shard_map/ppermute | solution.py:305
  25.0 2.5 %stats.1 = (f32[4,4,640]{2,1,0:T(4,128)S(1)}, f32[16,256,640]{2,1,0:T(8,128)S(1)}, f32[16,256,640]{2,1,0:T(8,128)S(1)}) custom-call(s32[20,4]{1,0:T(8,128)S(1)} %plan.1.item_ref, bf16[128,256]{1,0:T(8,128)(2,1)S(1)} %get-tuple-element.38.k0, bf16[128,256]{1,0:T(8,128)(2,1)S(1)} %collective-permute-done.k1, bf16[128,256]{1,0:T(8,128)(2,1)S(1)} %collective-permute-done.1.k2, ...), custom_call_target="tpu_custom_call" | custom-call | flops 1342177280 | tf_op jit(solution)/shard_map/stats/pallas_call | solution.py:319
  28.3 1.9 %collective-permute-start.11 = (f32[4,4,640]{2,1,0:T(4,128)S(1)}, f32[4,4,640]{2,1,0:T(4,128)S(1)}, u32[]{:S(2)}, u32[]{:S(2)}) collective-permute-start(f32[4,4,640]{2,1,0:T(4,128)S(1)} %get-tuple-element.39.stat_ref.s0), channel_id=1, source_target_pairs={{0,16},{8,24},{16,0},{24,8},{1,17},{9,25},{17,1},{25,9},{2,18},{10... | collective-permute-start | bytes 122888 | tf_op jit(solution)/shard_map/ppermute | solution.py:328
  31.1 1.6 %collective-permute-done.11.s2 = f32[4,4,640]{2,1,0:T(4,128)S(1)} collective-permute-done((f32[4,4,640]{2,1,0:T(4,128)S(1)}, f32[4,4,640]{2,1,0:T(4,128)S(1)}, u32[]{:S(2)}, u32[]{:S(2)}) %collective-permute-start.11) | collective-permute-done | bytes 40992 | tf_op jit(solution)/shard_map/ppermute | solution.py:328
  32.7 1.6 %collective-permute-done.10.s1 = f32[4,4,640]{2,1,0:T(4,128)S(1)} collective-permute-done((f32[4,4,640]{2,1,0:T(4,128)S(1)}, f32[4,4,640]{2,1,0:T(4,128)S(1)}, u32[]{:S(2)}, u32[]{:S(2)}) %collective-permute-start.10) | collective-permute-done | bytes 40992 | tf_op jit(solution)/shard_map/ppermute | solution.py:328
  34.3 3.2 %grads.1 = (bf16[8,128,256]{2,1,0:T(8,128)(2,1)S(1)}, bf16[128,640]{1,0:T(8,128)(2,1)S(1)}, bf16[128,640]{1,0:T(8,128)(2,1)S(1)}, bf16[128,640]{1,0:T(8,128)(2,1)S(1)}, bf16[128,640]{1,0:T(8,128)(2,1)S(1)}) custom-call(s32[20,4]{1,0:T(8,128)S(1)} %plan.1.item_ref, bf16[8,128,128]{2,1,0:T(8,128)(2,1)S(1)} %turn.1.cols_ref, ...), custom_call_target="tpu_custom_call" | custom-call | flops 2013265920 | tf_op jit(solution)/shard_map/grads/pallas_call | solution.py:332
  38.3 9.3 %all-to-all-start = ((bf16[8,128,256]{2,1,0:T(8,128)(2,1)}), bf16[8,128,256]{2,1,0:T(8,128)(2,1)S(1)}, u32[]{:S(2)}, u32[]{:S(2)}) async-start(bf16[8,128,256]{2,1,0:T(8,128)(2,1)} %flush.1), calls=%async_computation | async-start | bytes 1048576 | tf_op jit(solution)/shard_map/all_to_all | solution.py:345
  48.1 1.8 %collective-permute-start.14 = (bf16[128,640]{1,0:T(8,128)(2,1)S(1)}, bf16[128,640]{1,0:T(8,128)(2,1)S(1)}, u32[]{:S(2)}, u32[]{:S(2)}) collective-permute-start(bf16[128,640]{1,0:T(8,128)(2,1)S(1)} %get-tuple-element.47), channel_id=1, source_target_pairs={{0,16},{8,24},{16,0},{24,8},{1,17},{9,25},{17,1},{25,9},{2,18},{10... | collective-permute-start | bytes 491528 | tf_op jit(solution)/shard_map/ppermute | solution.py:341
  49.9 3.7 %fetch.1 = (f32[64,128]{1,0:T(8,128)S(1)}, f32[64,128]{1,0:T(8,128)S(1)}, bf16[640,640]{1,0:T(8,128)(2,1)S(1)}, bf16[640,640]{1,0:T(8,128)(2,1)S(1)}, bf16[640,6...) custom-call(s32[4]{0:T(128)S(1)} %pad_add_fusion.place_ref, ...), custom_call_target="tpu_custom_call" | custom-call | tf_op jit(solution)/shard_map/fetch/pallas_call | solution.py:348
  53.7 1.7 %collective-permute-done.15.q3 = bf16[128,640]{1,0:T(8,128)(2,1)S(1)} collective-permute-done((bf16[128,640]{1,0:T(8,128)(2,1)S(1)}, bf16[128,640]{1,0:T(8,128)(2,1)S(1)}, u32[]{:S(2)}, u32[]{:S(2)}) %collective-permute-start.15) | collective-permute-done | bytes 163872 | tf_op jit(solution)/shard_map/ppermute | solution.py:341
  55.5 3.8 %query_part.1 = (bf16[8,640,128]{2,1,0:T(8,128)(2,1)S(1)}, bf16[4,640,128]{2,1,0:T(8,128)(2,1)S(1)}, bf16[4,640,128]{2,1,0:T(8,128)(2,1)S(1)}) custom-call(s32[4]{0:T(128)S(1)} %pad_add_fusion.place_ref, f32[64,128]{1,0:T(8,128)S(1)} %get-tuple-element.43.cos_ref, f32[64,128]{1,0:T(8,128)S(1)} %get-tuple-element.44.sin_ref, ...), custom_call_target="tpu_custom_call" | custom-call | flops 838860800 | tf_op jit(solution)/shard_map/query_part/pallas_call | solution.py:357
  60.5 1.3 %collective-permute-start.16 = (bf16[640,128]{1,0:T(8,128)(2,1)S(1)}, bf16[640,128]{1,0:T(8,128)(2,1)S(1)}, u32[]{:S(2)}, u32[]{:S(2)}) collective-permute-start(bf16[640,128]{1,0:T(8,128)(2,1)S(1)} %get-tuple-element.61), channel_id=1, source_target_pairs={{0,2},{1,3},{2,4},{3,5},{4,6},{5,7},{6,0},{7,1},{8,10},{9,11},{10,... | collective-permute-start | bytes 491528 | tf_op jit(solution)/shard_map/ppermute | solution.py:386
  61.8 2.5 %collective-permute-start.17 = (bf16[640,128]{1,0:T(8,128)(2,1)S(1)}, bf16[640,128]{1,0:T(8,128)(2,1)S(1)}, u32[]{:S(2)}, u32[]{:S(2)}) collective-permute-start(bf16[640,128]{1,0:T(8,128)(2,1)S(1)} %get-tuple-element.62), channel_id=1, source_target_pairs={{0,4},{1,5},{2,6},{3,7},{4,0},{5,1},{6,2},{7,3},{8,12},{9,13},{10,... | collective-permute-start | bytes 491528 | tf_op jit(solution)/shard_map/ppermute | solution.py:386
  64.2 2.8 %second_half.1 = (bf16[640,128]{1,0:T(8,128)(2,1)S(1)}, bf16[640,128]{1,0:T(8,128)(2,1)S(1)}, bf16[640,128]{1,0:T(8,128)(2,1)S(1)}, bf16[640,128]{1,0:T(8,128)(2,1)S(1)}) custom-call(s32[4]{0:T(128)S(1)} %pad_add_fusion.place_ref, bf16[256,128]{1,0:T(8,128)(2,1)S(1)} %get-tuple-element.64.low_ref, bf16[8,640,128]{2,1,0:T(8,128)(2,1)S(1)} %get-tuple-element.57.part_ref, ...), custom_call_target="tpu_custom_call" | custom-call | tf_op jit(solution)/shard_map/second_half/pallas_call | solution.py:374
  68.3 8.6 %collective-permute-start.19 = (bf16[640,128]{1,0:T(8,128)(2,1)S(1)}, bf16[640,128]{1,0:T(8,128)(2,1)S(1)}, u32[]{:S(2)}, u32[]{:S(2)}) collective-permute-start(bf16[640,128]{1,0:T(8,128)(2,1)S(1)} %get-tuple-element.65), channel_id=1, source_target_pairs={{0,1},{1,0},{2,3},{3,2},{4,5},{5,4},{6,7},{7,6},{8,9},{9,8},{10,11... | collective-permute-start | bytes 491528 | tf_op jit(solution)/shard_map/ppermute | solution.py:386
  78.2 1.7 %collective-permute-start.22 = (bf16[640,128]{1,0:T(8,128)(2,1)S(1)}, bf16[640,128]{1,0:T(8,128)(2,1)S(1)}, u32[]{:S(2)}, u32[]{:S(2)}) collective-permute-start(bf16[640,128]{1,0:T(8,128)(2,1)S(1)} %get-tuple-element.68), channel_id=1, source_target_pairs={{0,7},{1,6},{2,1},{3,0},{4,3},{5,2},{6,5},{7,4},{8,15},{9,14},{10,... | collective-permute-start | bytes 491528 | tf_op jit(solution)/shard_map/ppermute | solution.py:386
  80.0 7.5 %collective-permute-done.20.p5 = bf16[640,128]{1,0:T(8,128)(2,1)S(1)} collective-permute-done((bf16[640,128]{1,0:T(8,128)(2,1)S(1)}, bf16[640,128]{1,0:T(8,128)(2,1)S(1)}, u32[]{:S(2)}, u32[]{:S(2)}) %collective-permute-start.20) | collective-permute-done | bytes 163872 | tf_op jit(solution)/shard_map/ppermute | solution.py:386
  (40 shorter events, 13.3 us)
Async XLA Ops:
  1.1 10.4 %collective-permute-start = (bf16[128,256]{1,0:T(8,128)(2,1)S(1)}, bf16[128,256]{1,0:T(8,128)(2,1)S(1)}, u32[]{:S(2)}, u32[]{:S(2)}) collective-permute-start(bf16[128,256]{1,0:T(8,128)(2,1)S(1)} %get-tuple-element.38.k0), channel_id=1, source_target_pairs={{0,32},{32,64},{64,96},{96,128},{128,160},{160,192},{192,224},{224... | collective-permute-start | bytes 196616 | tf_op jit(solution)/shard_map/ppermute | solution.py:303
  3.6 21.4 %collective-permute-start.9 = (bf16[1280,128]{1,0:T(8,128)(2,1)S(1)}, bf16[1280,128]{1,0:T(8,128)(2,1)S(1)}, u32[]{:S(2)}, u32[]{:S(2)}) collective-permute-start(bf16[1280,128]{1,0:T(8,128)(2,1)S(1)} %get-tuple-element.37.rows_ref.g0), channel_id=1, source_target_pairs={{0,24},{8,0},{16,8},{24,16},{1,25},{9,1},{17,9},{25,17},{2,26},{10... | collective-permute-start | bytes 983048 | tf_op jit(solution)/shard_map/ppermute | solution.py:307
  6.3 18.7 %collective-permute-start.8 = (bf16[1280,128]{1,0:T(8,128)(2,1)S(1)}, bf16[1280,128]{1,0:T(8,128)(2,1)S(1)}, u32[]{:S(2)}, u32[]{:S(2)}) collective-permute-start(bf16[1280,128]{1,0:T(8,128)(2,1)S(1)} %get-tuple-element.37.rows_ref.g0), channel_id=1, source_target_pairs={{0,16},{8,24},{16,0},{24,8},{1,17},{9,25},{17,1},{25,9},{2,18},{10... | collective-permute-start | bytes 983048 | tf_op jit(solution)/shard_map/ppermute | solution.py:307
  6.7 18.3 %collective-permute-start.7 = (bf16[1280,128]{1,0:T(8,128)(2,1)S(1)}, bf16[1280,128]{1,0:T(8,128)(2,1)S(1)}, u32[]{:S(2)}, u32[]{:S(2)}) collective-permute-start(bf16[1280,128]{1,0:T(8,128)(2,1)S(1)} %get-tuple-element.37.rows_ref.g0), channel_id=1, source_target_pairs={{0,8},{8,16},{16,24},{24,0},{1,9},{9,17},{17,25},{25,1},{2,10},{10... | collective-permute-start | bytes 983048 | tf_op jit(solution)/shard_map/ppermute | solution.py:307
  7.4 5.4 %collective-permute-start.4 = (bf16[128,256]{1,0:T(8,128)(2,1)S(1)}, bf16[128,256]{1,0:T(8,128)(2,1)S(1)}, u32[]{:S(2)}, u32[]{:S(2)}) collective-permute-start(bf16[128,256]{1,0:T(8,128)(2,1)S(1)} %get-tuple-element.38.k0), channel_id=1, source_target_pairs={{0,224},{32,0},{64,32},{96,64},{128,96},{160,128},{192,160},{224,1... | collective-permute-start | bytes 196616 | tf_op jit(solution)/shard_map/ppermute | solution.py:304
  11.4 4.6 %collective-permute-start.1 = (bf16[128,256]{1,0:T(8,128)(2,1)S(1)}, bf16[128,256]{1,0:T(8,128)(2,1)S(1)}, u32[]{:S(2)}, u32[]{:S(2)}) collective-permute-start(bf16[128,256]{1,0:T(8,128)(2,1)S(1)} %collective-permute-done.k1), channel_id=1, source_target_pairs={{0,32},{32,64},{64,96},{96,128},{128,160},{160,192},{192,224},{224... | collective-permute-start | bytes 196616 | tf_op jit(solution)/shard_map/ppermute | solution.py:303
  12.7 4.3 %collective-permute-start.5 = (bf16[128,256]{1,0:T(8,128)(2,1)S(1)}, bf16[128,256]{1,0:T(8,128)(2,1)S(1)}, u32[]{:S(2)}, u32[]{:S(2)}) collective-permute-start(bf16[128,256]{1,0:T(8,128)(2,1)S(1)} %collective-permute-done.4.k7), channel_id=1, source_target_pairs={{0,224},{32,0},{64,32},{96,64},{128,96},{160,128},{192,160},{224,1... | collective-permute-start | bytes 196616 | tf_op jit(solution)/shard_map/ppermute | solution.py:304
  16.0 4.6 %collective-permute-start.2 = (bf16[128,256]{1,0:T(8,128)(2,1)S(1)}, bf16[128,256]{1,0:T(8,128)(2,1)S(1)}, u32[]{:S(2)}, u32[]{:S(2)}) collective-permute-start(bf16[128,256]{1,0:T(8,128)(2,1)S(1)} %collective-permute-done.1.k2), channel_id=1, source_target_pairs={{0,32},{32,64},{64,96},{96,128},{128,160},{160,192},{192,224},{224... | collective-permute-start | bytes 196616 | tf_op jit(solution)/shard_map/ppermute | solution.py:303
  17.1 6.1 %collective-permute-start.6 = (bf16[128,256]{1,0:T(8,128)(2,1)S(1)}, bf16[128,256]{1,0:T(8,128)(2,1)S(1)}, u32[]{:S(2)}, u32[]{:S(2)}) collective-permute-start(bf16[128,256]{1,0:T(8,128)(2,1)S(1)} %collective-permute-done.5.k6), channel_id=1, source_target_pairs={{0,224},{32,0},{64,32},{96,64},{128,96},{160,128},{192,160},{224,1... | collective-permute-start | bytes 196616 | tf_op jit(solution)/shard_map/ppermute | solution.py:304
  20.6 4.3 %collective-permute-start.3 = (bf16[128,256]{1,0:T(8,128)(2,1)S(1)}, bf16[128,256]{1,0:T(8,128)(2,1)S(1)}, u32[]{:S(2)}, u32[]{:S(2)}) collective-permute-start(bf16[128,256]{1,0:T(8,128)(2,1)S(1)} %collective-permute-done.2.k3), channel_id=1, source_target_pairs={{0,32},{32,64},{64,96},{96,128},{128,160},{160,192},{192,224},{224... | collective-permute-start | bytes 196616 | tf_op jit(solution)/shard_map/ppermute | solution.py:305
  27.5 3.6 %collective-permute-start.12 = (f32[4,4,640]{2,1,0:T(4,128)S(1)}, f32[4,4,640]{2,1,0:T(4,128)S(1)}, u32[]{:S(2)}, u32[]{:S(2)}) collective-permute-start(f32[4,4,640]{2,1,0:T(4,128)S(1)} %get-tuple-element.39.stat_ref.s0), channel_id=1, source_target_pairs={{0,24},{8,0},{16,8},{24,16},{1,25},{9,1},{17,9},{25,17},{2,26},{10... | collective-permute-start | bytes 122888 | tf_op jit(solution)/shard_map/ppermute | solution.py:328
  28.3 4.4 %collective-permute-start.11 = (f32[4,4,640]{2,1,0:T(4,128)S(1)}, f32[4,4,640]{2,1,0:T(4,128)S(1)}, u32[]{:S(2)}, u32[]{:S(2)}) collective-permute-start(f32[4,4,640]{2,1,0:T(4,128)S(1)} %get-tuple-element.39.stat_ref.s0), channel_id=1, source_target_pairs={{0,16},{8,24},{16,0},{24,8},{1,17},{9,25},{17,1},{25,9},{2,18},{10... | collective-permute-start | bytes 122888 | tf_op jit(solution)/shard_map/ppermute | solution.py:328
  30.2 4.1 %collective-permute-start.10 = (f32[4,4,640]{2,1,0:T(4,128)S(1)}, f32[4,4,640]{2,1,0:T(4,128)S(1)}, u32[]{:S(2)}, u32[]{:S(2)}) collective-permute-start(f32[4,4,640]{2,1,0:T(4,128)S(1)} %get-tuple-element.39.stat_ref.s0), channel_id=1, source_target_pairs={{0,8},{8,16},{16,24},{24,0},{1,9},{9,17},{17,25},{25,1},{2,10},{10... | collective-permute-start | bytes 122888 | tf_op jit(solution)/shard_map/ppermute | solution.py:328
  38.3 21.6 %all-to-all-start = ((bf16[8,128,256]{2,1,0:T(8,128)(2,1)}), bf16[8,128,256]{2,1,0:T(8,128)(2,1)S(1)}, u32[]{:S(2)}, u32[]{:S(2)}) async-start(bf16[8,128,256]{2,1,0:T(8,128)(2,1)} %flush.1), calls=%async_computation | async-start | bytes 1048576 | tf_op jit(solution)/shard_map/all_to_all | solution.py:345
  47.6 5.9 %collective-permute-start.13 = (bf16[128,640]{1,0:T(8,128)(2,1)S(1)}, bf16[128,640]{1,0:T(8,128)(2,1)S(1)}, u32[]{:S(2)}, u32[]{:S(2)}) collective-permute-start(bf16[128,640]{1,0:T(8,128)(2,1)S(1)} %get-tuple-element.46), channel_id=1, source_target_pairs={{0,24},{8,0},{16,8},{24,16},{1,25},{9,1},{17,9},{25,17},{2,26},{10... | collective-permute-start | bytes 491528 | tf_op jit(solution)/shard_map/ppermute | solution.py:341
  48.1 5.7 %collective-permute-start.14 = (bf16[128,640]{1,0:T(8,128)(2,1)S(1)}, bf16[128,640]{1,0:T(8,128)(2,1)S(1)}, u32[]{:S(2)}, u32[]{:S(2)}) collective-permute-start(bf16[128,640]{1,0:T(8,128)(2,1)S(1)} %get-tuple-element.47), channel_id=1, source_target_pairs={{0,16},{8,24},{16,0},{24,8},{1,17},{9,25},{17,1},{25,9},{2,18},{10... | collective-permute-start | bytes 491528 | tf_op jit(solution)/shard_map/ppermute | solution.py:341
  49.8 5.6 %collective-permute-start.15 = (bf16[128,640]{1,0:T(8,128)(2,1)S(1)}, bf16[128,640]{1,0:T(8,128)(2,1)S(1)}, u32[]{:S(2)}, u32[]{:S(2)}) collective-permute-start(bf16[128,640]{1,0:T(8,128)(2,1)S(1)} %get-tuple-element.48), channel_id=1, source_target_pairs={{0,8},{8,16},{16,24},{24,0},{1,9},{9,17},{17,25},{25,1},{2,10},{10... | collective-permute-start | bytes 491528 | tf_op jit(solution)/shard_map/ppermute | solution.py:341
  60.5 16.6 %collective-permute-start.16 = (bf16[640,128]{1,0:T(8,128)(2,1)S(1)}, bf16[640,128]{1,0:T(8,128)(2,1)S(1)}, u32[]{:S(2)}, u32[]{:S(2)}) collective-permute-start(bf16[640,128]{1,0:T(8,128)(2,1)S(1)} %get-tuple-element.61), channel_id=1, source_target_pairs={{0,2},{1,3},{2,4},{3,5},{4,6},{5,7},{6,0},{7,1},{8,10},{9,11},{10,... | collective-permute-start | bytes 491528 | tf_op jit(solution)/shard_map/ppermute | solution.py:386
  61.8 16.4 %collective-permute-start.17 = (bf16[640,128]{1,0:T(8,128)(2,1)S(1)}, bf16[640,128]{1,0:T(8,128)(2,1)S(1)}, u32[]{:S(2)}, u32[]{:S(2)}) collective-permute-start(bf16[640,128]{1,0:T(8,128)(2,1)S(1)} %get-tuple-element.62), channel_id=1, source_target_pairs={{0,4},{1,5},{2,6},{3,7},{4,0},{5,1},{6,2},{7,3},{8,12},{9,13},{10,... | collective-permute-start | bytes 491528 | tf_op jit(solution)/shard_map/ppermute | solution.py:386
  67.1 12.9 %collective-permute-start.18 = (bf16[640,128]{1,0:T(8,128)(2,1)S(1)}, bf16[640,128]{1,0:T(8,128)(2,1)S(1)}, u32[]{:S(2)}, u32[]{:S(2)}) collective-permute-start(bf16[640,128]{1,0:T(8,128)(2,1)S(1)} %get-tuple-element.63), channel_id=1, source_target_pairs={{0,6},{1,7},{2,0},{3,1},{4,2},{5,3},{6,4},{7,5},{8,14},{9,15},{10,... | collective-permute-start | bytes 491528 | tf_op jit(solution)/shard_map/ppermute | solution.py:386
  68.3 11.7 %collective-permute-start.19 = (bf16[640,128]{1,0:T(8,128)(2,1)S(1)}, bf16[640,128]{1,0:T(8,128)(2,1)S(1)}, u32[]{:S(2)}, u32[]{:S(2)}) collective-permute-start(bf16[640,128]{1,0:T(8,128)(2,1)S(1)} %get-tuple-element.65), channel_id=1, source_target_pairs={{0,1},{1,0},{2,3},{3,2},{4,5},{5,4},{6,7},{7,6},{8,9},{9,8},{10,11... | collective-permute-start | bytes 491528 | tf_op jit(solution)/shard_map/ppermute | solution.py:386
  76.9 10.5 %collective-permute-start.20 = (bf16[640,128]{1,0:T(8,128)(2,1)S(1)}, bf16[640,128]{1,0:T(8,128)(2,1)S(1)}, u32[]{:S(2)}, u32[]{:S(2)}) collective-permute-start(bf16[640,128]{1,0:T(8,128)(2,1)S(1)} %get-tuple-element.66), channel_id=1, source_target_pairs={{0,3},{1,2},{2,5},{3,4},{4,7},{5,6},{6,1},{7,0},{8,11},{9,10},{10,... | collective-permute-start | bytes 491528 | tf_op jit(solution)/shard_map/ppermute | solution.py:386
  77.1 10.3 %collective-permute-start.21 = (bf16[640,128]{1,0:T(8,128)(2,1)S(1)}, bf16[640,128]{1,0:T(8,128)(2,1)S(1)}, u32[]{:S(2)}, u32[]{:S(2)}) collective-permute-start(bf16[640,128]{1,0:T(8,128)(2,1)S(1)} %get-tuple-element.67), channel_id=1, source_target_pairs={{0,5},{1,4},{2,7},{3,6},{4,1},{5,0},{6,3},{7,2},{8,13},{9,12},{10,... | collective-permute-start | bytes 491528 | tf_op jit(solution)/shard_map/ppermute | solution.py:386
  78.2 10.4 %collective-permute-start.22 = (bf16[640,128]{1,0:T(8,128)(2,1)S(1)}, bf16[640,128]{1,0:T(8,128)(2,1)S(1)}, u32[]{:S(2)}, u32[]{:S(2)}) collective-permute-start(bf16[640,128]{1,0:T(8,128)(2,1)S(1)} %get-tuple-element.68), channel_id=1, source_target_pairs={{0,7},{1,6},{2,1},{3,0},{4,3},{5,2},{6,5},{7,4},{8,15},{9,14},{10,... | collective-permute-start | bytes 491528 | tf_op jit(solution)/shard_map/ppermute | solution.py:386
  (2 other events, 16.3 us)

commit v10 on v8

--- a/solution.py
+++ b/solution.py
@@ -21,6 +21,7 @@
 NN = (((1,), (0,)), ((), ()))
 F32, BF16, I32 = jnp.float32, jnp.bfloat16, jnp.int32
 VMEM_LIMIT = 16 << 20
+PLAN_FLOPS = 1_000_000_000
 STATS_FLOPS = 2 * 2 * (NY * ROWS) * (NZ * BLOCK) * HEAD
 GRADS_FLOPS = 3 * 2 * (NY * ROWS) * (NZ * BLOCK) * HEAD
 QUERY_FLOPS = 2 * BLOCK * ROWS * 2 * NX * ROWS
@@ -97,6 +98,7 @@
             item_ref[row, 3] = jnp.where(both, jnp.where(second == z, causal, -BLOCK), BLOCK)
         item_ref[NY * PAIRS + j, 0] = (count + 1) // 2
         item_ref[NY * PAIRS + j, 1] = z
+        item_ref[NY * PAIRS + j, 2] = y
 
 
 def stats_kernel(item_ref, k0, k1, k2, k3, k4, k5, k6, k7, g0, g1, g2, g3, stat_ref, score_ref, pgrad_ref, kv_ref):
@@ -137,6 +139,25 @@
         stat_ref[j, 3:4, :] = zero
 
 
+def merged(mine, other):
+    highest = jnp.maximum(mine[0:1], other[0:1])
+    shrink_mine = jnp.exp(mine[0:1] - highest)
+    shrink_other = jnp.exp(other[0:1] - highest)
+    totals = mine[1:2] * shrink_mine + other[1:2] * shrink_other
+    dots = mine[2:3] * shrink_mine + other[2:3] * shrink_other
+    return highest, totals, dots
+
+
+def merge_kernel(item_ref, mine_ref, other_ref, out_ref):
+    step = 1 - 2 * (item_ref[NY * PAIRS, 2] & 1)
+    for j in range(NY):
+        highest, totals, dots = merged(mine_ref[j], other_ref[(j + step) & (NY - 1)])
+        out_ref[j, 0:1, :] = highest
+        out_ref[j, 1:2, :] = totals
+        out_ref[j, 2:3, :] = dots
+        out_ref[j, 3:4, :] = dots
+
+
 def turn_kernel(item_ref, k0, k1, k2, k3, k4, k5, k6, k7, stat_ref, key_cols):
     z = item_ref[NY * PAIRS, 1]
     for r, part in enumerate((k0, k1, k2, k3, k4, k5, k6, k7)):
@@ -147,22 +168,13 @@
     run_copies([(low_ref, out_ref)], sem)
 
 
-def grads_kernel(item_ref, cols_ref, score_ref, pgrad_ref, g0, g1, g2, g3, s0, s1, s2, s3,
+def grads_kernel(item_ref, cols_ref, score_ref, pgrad_ref, g0, g1, g2, g3, mine_ref, other_ref,
                  dkv_ref, dq0, dq1, dq2, dq3, dk_acc, dv_acc):
-    stats = (s0, s1, s2, s3)
+    step_to_other = NY - 1 - 2 * item_ref[NY * PAIRS, 2]
     dk_acc[...] = jnp.zeros_like(dk_acc)
     dv_acc[...] = jnp.zeros_like(dv_acc)
     for j, (group, out) in enumerate(zip((g0, g1, g2, g3), (dq0, dq1, dq2, dq3))):
-        views = [stats[k][(j - k) % NY] for k in range(NY)]
-        maxima = views[0][0:1]
-        for k in range(1, NY):
-            maxima = jnp.maximum(maxima, views[k][0:1])
-        totals = jnp.zeros((1, ROWS), F32)
-        dots = jnp.zeros((1, ROWS), F32)
-        for k in range(NY):
-            shrink = jnp.exp(views[k][0:1] - maxima)
-            totals = totals + views[k][1:2] * shrink
-            dots = dots + views[k][2:3] * shrink
+        maxima, totals, dots = merged(mine_ref[j], other_ref[(j + step_to_other) & (NY - 1)])
         log_totals = maxima + jnp.log(totals)
         row_dots = dots / totals
 
@@ -311,6 +323,7 @@
         SM,
         "plan",
         [pltpu.SMEM((NZ + 1,), I32)],
+        PLAN_FLOPS,
     )(place, ancestry.T, group)
 
     tiles = (NY * PAIRS, 2 * BLOCK, ROWS)
@@ -323,19 +336,23 @@
         [pltpu.VMEM((NZ, BLOCK, 2 * HEAD), BF16)],
         STATS_FLOPS,
     )(items, *kvs, *groups)
-    all_stats = [stats] + [lax.ppermute(stats, "y", shift(NY, k)) for k in range(1, NY)]
+    beside = lax.ppermute(stats, "y", [(i, i ^ 1) for i in range(NY)])
+    half_stats = call(
+        merge_kernel, jax.ShapeDtypeStruct(stats.shape, F32), [SM] + [VM] * 2, VM, "merge",
+    )(items, stats, beside)
+    other_half = lax.ppermute(half_stats, "y", [(i, NY - 1 - i) for i in range(NY)])
     key_cols = call(
         turn_kernel, pltpu.VMEM((NZ, HEAD, BLOCK), BF16), [SM] + [VM] * (NZ + 1), VM, "turn",
     )(items, *kvs, stats)
     dkv, *dq_parts = call(
         grads_kernel,
         [pltpu.VMEM((NZ, BLOCK, 2 * HEAD), BF16)] + [pltpu.VMEM((HEAD, ROWS), BF16)] * NY,
-        [SM] + [VM] * (3 + 2 * NY),
+        [SM] + [VM] * (5 + NY),
         [VM] * (1 + NY),
         "grads",
         [pltpu.VMEM((NZ, BLOCK, HEAD), F32), pltpu.VMEM((NZ, BLOCK, HEAD), F32)],
         GRADS_FLOPS,
-    )(items, key_cols, scores, prob_grads, *groups, *all_stats)
+    )(items, key_cols, scores, prob_grads, *groups, half_stats, other_half)
     dq_own = [dq_parts[0]] + [lax.ppermute(dq_parts[k], "y", shift(NY, -k)) for k in range(1, NY)]
     dkv = call(
         flush_kernel, pltpu.HBM(dkv.shape, BF16), [VM], HB, "flush", [pltpu.SemaphoreType.DMA((1,))],

time: 87 us -> 87.9 us (1.010); the launches traced: 87.5 us -> 86.8 us
  waiting for transfers between devices: 23.9 us -> 22.4 us
    ppermute x3, waiting for transfers between devices: 5.83 us -> 0.6 us  [shards(): below.append(lax.ppermute(below[-1], 'z', shift(NZ, 1)))]
    ppermute x3, waiting for transfers between devices: 0.01 us -> 2.28 us  [shards(): above.append(lax.ppermute(above[-1], 'z', shift(NZ, -1)))]
    ppermute x1, starting transfers between devices: 9.06 us -> 7.19 us  [shards(): arrived = lax.ppermute(away, 'c', shift(NC, 1))]
    all_to_all x1, starting transfers between devices: 8.15 us -> 9.77 us  [shards(): dkv_own = lax.all_to_all(dkv, 'z', 0, 0, tiled=True)]
    ppermute x3 -> x2, waiting for transfers between devices: 3.19 us -> 4.36 us  [the longest x1 2.39 us: shards(): lax.ppermute(half_stats, 'y', [(i, NY - 1 - i) for i in range(NY)])]
    ppermute x3, starting transfers between devices: 9.29 us -> 10.3 us  [shards(): above.append(lax.ppermute(above[-1], 'z', shift(NZ, -1)))]
    ppermute x3, starting transfers between devices: 1.64 us -> 2.55 us  [shards(): below.append(lax.ppermute(below[-1], 'z', shift(NZ, 1)))]
    ppermute x3, starting transfers between devices: 4.68 us -> 3.77 us  [shards(): lax.ppermute(group, 'y', shift(NY, k))]
  transfers between devices with their start and end apart: 21 -> 20, of which waited for: 12 -> 13; matrix products, arithmetic and copies ran while one was open for 0% -> 0% of each run, Pallas kernels for 15% -> 15%
where the time goes in v10:
time: 87.9 us; the launch traced here: 86.8 us
  starting transfers between devices  40.6 us (46%)
  Pallas kernels  22.7 us (26%)
  waiting for transfers between devices  22.4 us (25%)
    ppermute x3, starting transfers between devices, shards(): above.append(lax.ppermute(above[-1], 'z', shift(NZ, -1)))  10.3 us
    ppermute x3, waiting for transfers between devices, shards(): parts = [lax.ppermute(sent[k - 1], 'x', shift(NX, k)) for k in range(1, NX)]  9.99 us
    all_to_all x1, starting transfers between devices, shards(): dkv_own = lax.all_to_all(dkv, 'z', 0, 0, tiled=True)  9.77 us
    ppermute x1, starting transfers between devices, shards(): arrived = lax.ppermute(away, 'c', shift(NC, 1))  7.19 us
    pallas_call x1, Pallas kernels, shards(): call(query_part_kernel, [pltpu.VMEM((2 * NX, ROWS, BLOCK), BF16)] + pair_...  3.78 us
    ppermute x3, starting transfers between devices, shards(): lax.ppermute(group, 'y', shift(NY, k))  3.77 us
    ppermute x3, starting transfers between devices, shards(): parts = [lax.ppermute(sent[k - 1], 'x', shift(NX, k)) for k in range(1, NX)]  3.69 us
    pallas_call x1, Pallas kernels, shards(): call(fetch_kernel, [pltpu.VMEM((HEAD // 2, BLOCK), F32)] * 2 + [pltpu.VME...  3.68 us
  transfers between devices with their start and end apart: 20, of which 13 were waited for; matrix products, arithmetic and copies ran while one was open for 0% of the time, Pallas kernels for 15%

profile of v10, /device:TPU:1, one launch (start us, length us, event | category | flops | bytes accessed | tf_op | source)
XLA Modules:
  0.0 86.8 jit_solution(7642433499046295145)
XLA Ops:
  0.0 1.0 %stack.21 = (bf16[1280,128]{1,0:T(8,128)(2,1)S(1)}, bf16[128,256]{1,0:T(8,128)(2,1)S(1)}) custom-call(bf16[128,640]{1,0:T(8,128)(2,1)} %q_ref.1, bf16[128,640]{1,0:T(8,128)(2,1)} %g_ref.1, bf16[128,128]{1,0:T(8,128)(2,1)} %k_ref.1, bf16[128,128]{1,0:T(8,128)(2,1)} %v_ref.1), custom_call_target="tpu_custom_call" | custom-call | tf_op jit(solution)/shard_map/stack/pallas_call | solution.py:304
  1.1 2.5 %collective-permute-start = (bf16[128,256]{1,0:T(8,128)(2,1)S(1)}, bf16[128,256]{1,0:T(8,128)(2,1)S(1)}, u32[]{:S(2)}, u32[]{:S(2)}) collective-permute-start(bf16[128,256]{1,0:T(8,128)(2,1)S(1)} %get-tuple-element.31.k0), channel_id=1, source_target_pairs={{0,32},{32,64},{64,96},{96,128},{128,160},{160,192},{192,224},{224... | collective-permute-start | bytes 196616 | tf_op jit(solution)/shard_map/ppermute | solution.py:315
  3.6 2.7 %collective-permute-start.9 = (bf16[1280,128]{1,0:T(8,128)(2,1)S(1)}, bf16[1280,128]{1,0:T(8,128)(2,1)S(1)}, u32[]{:S(2)}, u32[]{:S(2)}) collective-permute-start(bf16[1280,128]{1,0:T(8,128)(2,1)S(1)} %get-tuple-element.30.rows_ref.g0), channel_id=1, source_target_pairs={{0,24},{8,0},{16,8},{24,16},{1,25},{9,1},{17,9},{25,17},{2,26},{10... | collective-permute-start | bytes 983048 | tf_op jit(solution)/shard_map/ppermute | solution.py:312
  7.4 4.0 %collective-permute-start.4 = (bf16[128,256]{1,0:T(8,128)(2,1)S(1)}, bf16[128,256]{1,0:T(8,128)(2,1)S(1)}, u32[]{:S(2)}, u32[]{:S(2)}) collective-permute-start(bf16[128,256]{1,0:T(8,128)(2,1)S(1)} %get-tuple-element.31.k0), channel_id=1, source_target_pairs={{0,224},{32,0},{64,32},{96,64},{128,96},{160,128},{192,160},{224,1... | collective-permute-start | bytes 196616 | tf_op jit(solution)/shard_map/ppermute | solution.py:316
  11.4 1.3 %collective-permute-done.4.k7 = bf16[128,256]{1,0:T(8,128)(2,1)S(1)} collective-permute-done((bf16[128,256]{1,0:T(8,128)(2,1)S(1)}, bf16[128,256]{1,0:T(8,128)(2,1)S(1)}, u32[]{:S(2)}, u32[]{:S(2)}) %collective-permute-start.4) | collective-permute-done | bytes 65568 | tf_op jit(solution)/shard_map/ppermute | solution.py:316
  12.7 3.0 %collective-permute-start.5 = (bf16[128,256]{1,0:T(8,128)(2,1)S(1)}, bf16[128,256]{1,0:T(8,128)(2,1)S(1)}, u32[]{:S(2)}, u32[]{:S(2)}) collective-permute-start(bf16[128,256]{1,0:T(8,128)(2,1)S(1)} %collective-permute-done.4.k7), channel_id=1, source_target_pairs={{0,224},{32,0},{64,32},{96,64},{128,96},{160,128},{192,160},{224,1... | collective-permute-start | bytes 196616 | tf_op jit(solution)/shard_map/ppermute | solution.py:316
  17.1 3.3 %collective-permute-start.6 = (bf16[128,256]{1,0:T(8,128)(2,1)S(1)}, bf16[128,256]{1,0:T(8,128)(2,1)S(1)}, u32[]{:S(2)}, u32[]{:S(2)}) collective-permute-start(bf16[128,256]{1,0:T(8,128)(2,1)S(1)} %collective-permute-done.5.k6), channel_id=1, source_target_pairs={{0,224},{32,0},{64,32},{96,64},{128,96},{160,128},{192,160},{224,1... | collective-permute-start | bytes 196616 | tf_op jit(solution)/shard_map/ppermute | solution.py:316
  21.4 1.8 %plan.1.item_ref = s32[20,4]{1,0:T(8,128)S(1)} custom-call(s32[4]{0:T(128)S(1)} %pad_add_fusion.place_ref, s32[17,32]{1,0:T(8,128)S(1)} %bitcast.15, bf16[1280,128]{1,0:T(8,128)(2,1)S(1)} %get-tuple-element.30.rows_ref.g0), custom_call_target="tpu_custom_call" | custom-call | flops 1000000000 | tf_op jit(solution)/shard_map/plan/pallas_call | solution.py:319
  23.2 1.8 %collective-permute-done.3.k4 = bf16[128,256]{1,0:T(8,128)(2,1)S(1)} collective-permute-done((bf16[128,256]{1,0:T(8,128)(2,1)S(1)}, bf16[128,256]{1,0:T(8,128)(2,1)S(1)}, u32[]{:S(2)}, u32[]{:S(2)}) %collective-permute-start.3) | collective-permute-done | bytes 65568 | tf_op jit(solution)/shard_map/ppermute | solution.py:317
  25.0 2.5 %stats.1 = (f32[4,4,640]{2,1,0:T(4,128)S(1)}, f32[16,256,640]{2,1,0:T(8,128)S(1)}, f32[16,256,640]{2,1,0:T(8,128)S(1)}) custom-call(s32[20,4]{1,0:T(8,128)S(1)} %plan.1.item_ref, bf16[128,256]{1,0:T(8,128)(2,1)S(1)} %get-tuple-element.31.k0, bf16[128,256]{1,0:T(8,128)(2,1)S(1)} %collective-permute-done.k1, bf16[128,256]{1,0:T(8,128)(2,1)S(1)} %collective-permute-done.1.k2, ...), custom_call_target="tpu_custom_call" | custom-call | flops 1342177280 | tf_op jit(solution)/shard_map/stats/pallas_call | solution.py:330
  27.5 1.0 %collective-permute-start.10 = (f32[4,4,640]{2,1,0:T(4,128)S(1)}, f32[4,4,640]{2,1,0:T(4,128)S(1)}, u32[]{:S(2)}, u32[]{:S(2)}) collective-permute-start(f32[4,4,640]{2,1,0:T(4,128)S(1)} %get-tuple-element.32.stat_ref.mine_ref), channel_id=1, source_target_pairs={{0,8},{8,0},{16,24},{24,16},{1,9},{9,1},{17,25},{25,17},{2,10},{10... | collective-permute-start | bytes 122888 | tf_op jit(solution)/shard_map/ppermute | solution.py:339
  28.4 2.0 %collective-permute-done.10.other_ref = f32[4,4,640]{2,1,0:T(4,128)S(1)} collective-permute-done((f32[4,4,640]{2,1,0:T(4,128)S(1)}, f32[4,4,640]{2,1,0:T(4,128)S(1)}, u32[]{:S(2)}, u32[]{:S(2)}) %collective-permute-start.10) | collective-permute-done | bytes 40992 | tf_op jit(solution)/shard_map/ppermute | solution.py:339
  33.0 2.4 %collective-permute-done.11.other_ref = f32[4,4,640]{2,1,0:T(4,128)S(1)} collective-permute-done((f32[4,4,640]{2,1,0:T(4,128)S(1)}, f32[4,4,640]{2,1,0:T(4,128)S(1)}, u32[]{:S(2)}, u32[]{:S(2)}) %collective-permute-start.11) | collective-permute-done | bytes 40992 | tf_op jit(solution)/shard_map/ppermute | solution.py:343
  35.4 3.2 %grads.1 = (bf16[8,128,256]{2,1,0:T(8,128)(2,1)S(1)}, bf16[128,640]{1,0:T(8,128)(2,1)S(1)}, bf16[128,640]{1,0:T(8,128)(2,1)S(1)}, bf16[128,640]{1,0:T(8,128)(2,1)S(1)}, bf16[128,640]{1,0:T(8,128)(2,1)S(1)}) custom-call(s32[20,4]{1,0:T(8,128)S(1)} %plan.1.item_ref, bf16[8,128,128]{2,1,0:T(8,128)(2,1)S(1)} %turn.1.cols_ref, ...), custom_call_target="tpu_custom_call" | custom-call | flops 2013265920 | tf_op jit(solution)/shard_map/grads/pallas_call | solution.py:347
  39.4 9.8 %all-to-all-start = ((bf16[8,128,256]{2,1,0:T(8,128)(2,1)}), bf16[8,128,256]{2,1,0:T(8,128)(2,1)S(1)}, u32[]{:S(2)}, u32[]{:S(2)}) async-start(bf16[8,128,256]{2,1,0:T(8,128)(2,1)} %flush.1), calls=%async_computation | async-start | bytes 1048576 | tf_op jit(solution)/shard_map/all_to_all | solution.py:360
  50.6 3.7 %fetch.1 = (f32[64,128]{1,0:T(8,128)S(1)}, f32[64,128]{1,0:T(8,128)S(1)}, bf16[640,640]{1,0:T(8,128)(2,1)S(1)}, bf16[640,640]{1,0:T(8,128)(2,1)S(1)}, bf16[640,6...) custom-call(s32[4]{0:T(128)S(1)} %pad_add_fusion.place_ref, ...), custom_call_target="tpu_custom_call" | custom-call | tf_op jit(solution)/shard_map/fetch/pallas_call | solution.py:363
  55.0 1.7 %collective-permute-done.14.q3 = bf16[128,640]{1,0:T(8,128)(2,1)S(1)} collective-permute-done((bf16[128,640]{1,0:T(8,128)(2,1)S(1)}, bf16[128,640]{1,0:T(8,128)(2,1)S(1)}, u32[]{:S(2)}, u32[]{:S(2)}) %collective-permute-start.14) | collective-permute-done | bytes 163872 | tf_op jit(solution)/shard_map/ppermute | solution.py:356
  56.7 3.8 %query_part.1 = (bf16[8,640,128]{2,1,0:T(8,128)(2,1)S(1)}, bf16[4,640,128]{2,1,0:T(8,128)(2,1)S(1)}, bf16[4,640,128]{2,1,0:T(8,128)(2,1)S(1)}) custom-call(s32[4]{0:T(128)S(1)} %pad_add_fusion.place_ref, f32[64,128]{1,0:T(8,128)S(1)} %get-tuple-element.36.cos_ref, f32[64,128]{1,0:T(8,128)S(1)} %get-tuple-element.37.sin_ref, ...), custom_call_target="tpu_custom_call" | custom-call | flops 838860800 | tf_op jit(solution)/shard_map/query_part/pallas_call | solution.py:372
  60.5 1.0 %all-to-all-done.dkv_ref = bf16[8,128,256]{2,1,0:T(8,128)(2,1)S(1)} async-done(((bf16[8,128,256]{2,1,0:T(8,128)(2,1)}), bf16[8,128,256]{2,1,0:T(8,128)(2,1)S(1)}, u32[]{:S(2)}, u32[]{:S(2)}) %all-to-all-start) | async-done | bytes 524320 | tf_op jit(solution)/shard_map/all_to_all | solution.py:360
  62.1 7.2 %collective-permute-start.15 = (bf16[4,640,128]{2,1,0:T(8,128)(2,1)S(1)}, bf16[4,640,128]{2,1,0:T(8,128)(2,1)S(1)}, u32[]{:S(2)}, u32[]{:S(2)}) collective-permute-start(bf16[4,640,128]{2,1,0:T(8,128)(2,1)S(1)} %get-tuple-element.54), channel_id=1, source_target_pairs={{0,1},{1,0},{2,3},{3,2},{4,5},{5,4},{6,7},{7,6},{8,9},{9,8},{10,11... | collective-permute-start | bytes 1966088 | tf_op jit(solution)/shard_map/ppermute | solution.py:388
  69.3 2.8 %second_half.1 = f32[4,640,128]{2,1,0:T(8,128)S(1)} custom-call(s32[4]{0:T(128)S(1)} %pad_add_fusion.place_ref, bf16[256,128]{1,0:T(8,128)(2,1)S(1)} %get-tuple-element.53.low_ref, bf16[8,640,128]{2,1,0:T(8,128)(2,1)S(1)} %get-tuple-element.50.part_ref, bf16[5120,128]{1,0:T(8,128)(2,1)} %wk_hbm.3, bf16[5120,128]{1,0:T(8,128)(2,1)} %wv_hbm.3), custom_call_target="tpu_custom_call" | custom-call | tf_op jit(solution)/shard_map/second_half/pallas_call | solution.py:389
  72.3 2.6 %collective-permute-start.18 = (bf16[640,128]{1,0:T(8,128)(2,1)S(1)}, bf16[640,128]{1,0:T(8,128)(2,1)S(1)}, u32[]{:S(2)}, u32[]{:S(2)}) collective-permute-start(bf16[640,128]{1,0:T(8,128)(2,1)S(1)} %get-tuple-element.55), channel_id=1, source_target_pairs={{0,6},{2,0},{4,2},{6,4},{1,7},{3,1},{5,3},{7,5},{8,14},{10,8},{12,... | collective-permute-start | bytes 491528 | tf_op jit(solution)/shard_map/ppermute | solution.py:398
  76.0 5.8 %collective-permute-done.18.p2 = bf16[640,128]{1,0:T(8,128)(2,1)S(1)} collective-permute-done((bf16[640,128]{1,0:T(8,128)(2,1)S(1)}, bf16[640,128]{1,0:T(8,128)(2,1)S(1)}, u32[]{:S(2)}, u32[]{:S(2)}) %collective-permute-start.18) | collective-permute-done | bytes 163872 | tf_op jit(solution)/shard_map/ppermute | solution.py:398
  81.9 4.1 %collective-permute-done.16.p0 = bf16[640,128]{1,0:T(8,128)(2,1)S(1)} collective-permute-done((bf16[640,128]{1,0:T(8,128)(2,1)S(1)}, bf16[640,128]{1,0:T(8,128)(2,1)S(1)}, u32[]{:S(2)}, u32[]{:S(2)}) %collective-permute-start.16) | collective-permute-done | bytes 163872 | tf_op jit(solution)/shard_map/ppermute | solution.py:398
  (35 shorter events, 11.7 us)
Async XLA Ops:
  1.1 10.4 %collective-permute-start = (bf16[128,256]{1,0:T(8,128)(2,1)S(1)}, bf16[128,256]{1,0:T(8,128)(2,1)S(1)}, u32[]{:S(2)}, u32[]{:S(2)}) collective-permute-start(bf16[128,256]{1,0:T(8,128)(2,1)S(1)} %get-tuple-element.31.k0), channel_id=1, source_target_pairs={{0,32},{32,64},{64,96},{96,128},{128,160},{160,192},{192,224},{224... | collective-permute-start | bytes 196616 | tf_op jit(solution)/shard_map/ppermute | solution.py:315
  3.6 21.4 %collective-permute-start.9 = (bf16[1280,128]{1,0:T(8,128)(2,1)S(1)}, bf16[1280,128]{1,0:T(8,128)(2,1)S(1)}, u32[]{:S(2)}, u32[]{:S(2)}) collective-permute-start(bf16[1280,128]{1,0:T(8,128)(2,1)S(1)} %get-tuple-element.30.rows_ref.g0), channel_id=1, source_target_pairs={{0,24},{8,0},{16,8},{24,16},{1,25},{9,1},{17,9},{25,17},{2,26},{10... | collective-permute-start | bytes 983048 | tf_op jit(solution)/shard_map/ppermute | solution.py:312
  6.3 18.7 %collective-permute-start.8 = (bf16[1280,128]{1,0:T(8,128)(2,1)S(1)}, bf16[1280,128]{1,0:T(8,128)(2,1)S(1)}, u32[]{:S(2)}, u32[]{:S(2)}) collective-permute-start(bf16[1280,128]{1,0:T(8,128)(2,1)S(1)} %get-tuple-element.30.rows_ref.g0), channel_id=1, source_target_pairs={{0,16},{8,24},{16,0},{24,8},{1,17},{9,25},{17,1},{25,9},{2,18},{10... | collective-permute-start | bytes 983048 | tf_op jit(solution)/shard_map/ppermute | solution.py:312
  6.7 18.3 %collective-permute-start.7 = (bf16[1280,128]{1,0:T(8,128)(2,1)S(1)}, bf16[1280,128]{1,0:T(8,128)(2,1)S(1)}, u32[]{:S(2)}, u32[]{:S(2)}) collective-permute-start(bf16[1280,128]{1,0:T(8,128)(2,1)S(1)} %get-tuple-element.30.rows_ref.g0), channel_id=1, source_target_pairs={{0,8},{8,16},{16,24},{24,0},{1,9},{9,17},{17,25},{25,1},{2,10},{10... | collective-permute-start | bytes 983048 | tf_op jit(solution)/shard_map/ppermute | solution.py:312
  7.4 5.4 %collective-permute-start.4 = (bf16[128,256]{1,0:T(8,128)(2,1)S(1)}, bf16[128,256]{1,0:T(8,128)(2,1)S(1)}, u32[]{:S(2)}, u32[]{:S(2)}) collective-permute-start(bf16[128,256]{1,0:T(8,128)(2,1)S(1)} %get-tuple-element.31.k0), channel_id=1, source_target_pairs={{0,224},{32,0},{64,32},{96,64},{128,96},{160,128},{192,160},{224,1... | collective-permute-start | bytes 196616 | tf_op jit(solution)/shard_map/ppermute | solution.py:316
  11.4 4.6 %collective-permute-start.1 = (bf16[128,256]{1,0:T(8,128)(2,1)S(1)}, bf16[128,256]{1,0:T(8,128)(2,1)S(1)}, u32[]{:S(2)}, u32[]{:S(2)}) collective-permute-start(bf16[128,256]{1,0:T(8,128)(2,1)S(1)} %collective-permute-done.k1), channel_id=1, source_target_pairs={{0,32},{32,64},{64,96},{96,128},{128,160},{160,192},{192,224},{224... | collective-permute-start | bytes 196616 | tf_op jit(solution)/shard_map/ppermute | solution.py:315
  12.7 4.3 %collective-permute-start.5 = (bf16[128,256]{1,0:T(8,128)(2,1)S(1)}, bf16[128,256]{1,0:T(8,128)(2,1)S(1)}, u32[]{:S(2)}, u32[]{:S(2)}) collective-permute-start(bf16[128,256]{1,0:T(8,128)(2,1)S(1)} %collective-permute-done.4.k7), channel_id=1, source_target_pairs={{0,224},{32,0},{64,32},{96,64},{128,96},{160,128},{192,160},{224,1... | collective-permute-start | bytes 196616 | tf_op jit(solution)/shard_map/ppermute | solution.py:316
  16.0 4.6 %collective-permute-start.2 = (bf16[128,256]{1,0:T(8,128)(2,1)S(1)}, bf16[128,256]{1,0:T(8,128)(2,1)S(1)}, u32[]{:S(2)}, u32[]{:S(2)}) collective-permute-start(bf16[128,256]{1,0:T(8,128)(2,1)S(1)} %collective-permute-done.1.k2), channel_id=1, source_target_pairs={{0,32},{32,64},{64,96},{96,128},{128,160},{160,192},{192,224},{224... | collective-permute-start | bytes 196616 | tf_op jit(solution)/shard_map/ppermute | solution.py:315
  17.1 6.1 %collective-permute-start.6 = (bf16[128,256]{1,0:T(8,128)(2,1)S(1)}, bf16[128,256]{1,0:T(8,128)(2,1)S(1)}, u32[]{:S(2)}, u32[]{:S(2)}) collective-permute-start(bf16[128,256]{1,0:T(8,128)(2,1)S(1)} %collective-permute-done.5.k6), channel_id=1, source_target_pairs={{0,224},{32,0},{64,32},{96,64},{128,96},{160,128},{192,160},{224,1... | collective-permute-start | bytes 196616 | tf_op jit(solution)/shard_map/ppermute | solution.py:316
  20.6 4.3 %collective-permute-start.3 = (bf16[128,256]{1,0:T(8,128)(2,1)S(1)}, bf16[128,256]{1,0:T(8,128)(2,1)S(1)}, u32[]{:S(2)}, u32[]{:S(2)}) collective-permute-start(bf16[128,256]{1,0:T(8,128)(2,1)S(1)} %collective-permute-done.2.k3), channel_id=1, source_target_pairs={{0,32},{32,64},{64,96},{96,128},{128,160},{160,192},{192,224},{224... | collective-permute-start | bytes 196616 | tf_op jit(solution)/shard_map/ppermute | solution.py:317
  20.7 0.7 copy-start
  27.5 2.9 %collective-permute-start.10 = (f32[4,4,640]{2,1,0:T(4,128)S(1)}, f32[4,4,640]{2,1,0:T(4,128)S(1)}, u32[]{:S(2)}, u32[]{:S(2)}) collective-permute-start(f32[4,4,640]{2,1,0:T(4,128)S(1)} %get-tuple-element.32.stat_ref.mine_ref), channel_id=1, source_target_pairs={{0,8},{8,0},{16,24},{24,16},{1,9},{9,1},{17,25},{25,17},{2,10},{10... | collective-permute-start | bytes 122888 | tf_op jit(solution)/shard_map/ppermute | solution.py:339
  31.2 4.2 %collective-permute-start.11 = (f32[4,4,640]{2,1,0:T(4,128)S(1)}, f32[4,4,640]{2,1,0:T(4,128)S(1)}, u32[]{:S(2)}, u32[]{:S(2)}) collective-permute-start(f32[4,4,640]{2,1,0:T(4,128)S(1)} %merge.1.mine_ref), channel_id=1, source_target_pairs={{0,24},{8,16},{16,8},{24,0},{1,25},{9,17},{17,9},{25,1},{2,26},{10... | collective-permute-start | bytes 122888 | tf_op jit(solution)/shard_map/ppermute | solution.py:343
  38.5 12.1 %copy-start.1 = (s32[32,17]{0,1:T(8,128)S(1)}, s32[32,17]{0,1:T(8,128)}, u32[]{:S(2)}) copy-start(s32[32,17]{0,1:T(8,128)} %param.12) | copy-start | bytes 6532
  39.4 22.1 %all-to-all-start = ((bf16[8,128,256]{2,1,0:T(8,128)(2,1)}), bf16[8,128,256]{2,1,0:T(8,128)(2,1)S(1)}, u32[]{:S(2)}, u32[]{:S(2)}) async-start(bf16[8,128,256]{2,1,0:T(8,128)(2,1)} %flush.1), calls=%async_computation | async-start | bytes 1048576 | tf_op jit(solution)/shard_map/all_to_all | solution.py:360
  49.1 5.2 %collective-permute-start.12 = (bf16[128,640]{1,0:T(8,128)(2,1)S(1)}, bf16[128,640]{1,0:T(8,128)(2,1)S(1)}, u32[]{:S(2)}, u32[]{:S(2)}) collective-permute-start(bf16[128,640]{1,0:T(8,128)(2,1)S(1)} %get-tuple-element.39), channel_id=1, source_target_pairs={{0,24},{8,0},{16,8},{24,16},{1,25},{9,1},{17,9},{25,17},{2,26},{10... | collective-permute-start | bytes 491528 | tf_op jit(solution)/shard_map/ppermute | solution.py:356
  49.1 5.9 %collective-permute-start.13 = (bf16[128,640]{1,0:T(8,128)(2,1)S(1)}, bf16[128,640]{1,0:T(8,128)(2,1)S(1)}, u32[]{:S(2)}, u32[]{:S(2)}) collective-permute-start(bf16[128,640]{1,0:T(8,128)(2,1)S(1)} %get-tuple-element.40), channel_id=1, source_target_pairs={{0,16},{8,24},{16,0},{24,8},{1,17},{9,25},{17,1},{25,9},{2,18},{10... | collective-permute-start | bytes 491528 | tf_op jit(solution)/shard_map/ppermute | solution.py:356
  49.8 6.9 %collective-permute-start.14 = (bf16[128,640]{1,0:T(8,128)(2,1)S(1)}, bf16[128,640]{1,0:T(8,128)(2,1)S(1)}, u32[]{:S(2)}, u32[]{:S(2)}) collective-permute-start(bf16[128,640]{1,0:T(8,128)(2,1)S(1)} %get-tuple-element.41), channel_id=1, source_target_pairs={{0,8},{8,16},{16,24},{24,0},{1,9},{9,17},{17,25},{25,1},{2,10},{10... | collective-permute-start | bytes 491528 | tf_op jit(solution)/shard_map/ppermute | solution.py:356
  62.1 10.0 %collective-permute-start.15 = (bf16[4,640,128]{2,1,0:T(8,128)(2,1)S(1)}, bf16[4,640,128]{2,1,0:T(8,128)(2,1)S(1)}, u32[]{:S(2)}, u32[]{:S(2)}) collective-permute-start(bf16[4,640,128]{2,1,0:T(8,128)(2,1)S(1)} %get-tuple-element.54), channel_id=1, source_target_pairs={{0,1},{1,0},{2,3},{3,2},{4,5},{5,4},{6,7},{7,6},{8,9},{9,8},{10,11... | collective-permute-start | bytes 1966088 | tf_op jit(solution)/shard_map/ppermute | solution.py:388
  72.3 9.5 %collective-permute-start.18 = (bf16[640,128]{1,0:T(8,128)(2,1)S(1)}, bf16[640,128]{1,0:T(8,128)(2,1)S(1)}, u32[]{:S(2)}, u32[]{:S(2)}) collective-permute-start(bf16[640,128]{1,0:T(8,128)(2,1)S(1)} %get-tuple-element.55), channel_id=1, source_target_pairs={{0,6},{2,0},{4,2},{6,4},{1,7},{3,1},{5,3},{7,5},{8,14},{10,8},{12,... | collective-permute-start | bytes 491528 | tf_op jit(solution)/shard_map/ppermute | solution.py:398
  74.8 7.0 %collective-permute-start.17 = (bf16[640,128]{1,0:T(8,128)(2,1)S(1)}, bf16[640,128]{1,0:T(8,128)(2,1)S(1)}, u32[]{:S(2)}, u32[]{:S(2)}) collective-permute-start(bf16[640,128]{1,0:T(8,128)(2,1)S(1)} %get-tuple-element.56), channel_id=1, source_target_pairs={{0,4},{2,6},{4,0},{6,2},{1,5},{3,7},{5,1},{7,3},{8,12},{10,14},{12... | collective-permute-start | bytes 491528 | tf_op jit(solution)/shard_map/ppermute | solution.py:398
  75.3 10.6 %collective-permute-start.16 = (bf16[640,128]{1,0:T(8,128)(2,1)S(1)}, bf16[640,128]{1,0:T(8,128)(2,1)S(1)}, u32[]{:S(2)}, u32[]{:S(2)}) collective-permute-start(bf16[640,128]{1,0:T(8,128)(2,1)S(1)} %get-tuple-element.57), channel_id=1, source_target_pairs={{0,2},{2,4},{4,6},{6,0},{1,3},{3,5},{5,7},{7,1},{8,10},{10,12},{12... | collective-permute-start | bytes 491528 | tf_op jit(solution)/shard_map/ppermute | solution.py:398

commit v11 on v8

--- a/solution.py
+++ b/solution.py
@@ -21,6 +21,7 @@
 NN = (((1,), (0,)), ((), ()))
 F32, BF16, I32 = jnp.float32, jnp.bfloat16, jnp.int32
 VMEM_LIMIT = 16 << 20
+PLAN_FLOPS = 1_000_000_000
 STATS_FLOPS = 2 * 2 * (NY * ROWS) * (NZ * BLOCK) * HEAD
 GRADS_FLOPS = 3 * 2 * (NY * ROWS) * (NZ * BLOCK) * HEAD
 QUERY_FLOPS = 2 * BLOCK * ROWS * 2 * NX * ROWS
@@ -65,11 +66,16 @@
 
 def stack_kernel(q_ref, g_ref, k_ref, v_ref, rows_ref, kv_ref, sem):
     pairs = [(k_ref, kv_ref.at[:, 0:HEAD]), (v_ref, kv_ref.at[:, HEAD:2 * HEAD])]
-    for h in range(GROUP):
-        cols = slice(h * HEAD, (h + 1) * HEAD)
-        pairs.append((q_ref.at[:, cols], rows_ref.at[h * BLOCK:(h + 1) * BLOCK, :]))
-        pairs.append((g_ref.at[:, cols], rows_ref.at[ROWS + h * BLOCK:ROWS + (h + 1) * BLOCK, :]))
+    pairs += [(q_ref, rows_ref.at[:, 0:ROWS]), (g_ref, rows_ref.at[:, ROWS:2 * ROWS])]
     run_copies(pairs, sem)
+
+
+def head_rows(ref, first):
+    return jnp.concatenate([ref[:, first + h * HEAD:first + (h + 1) * HEAD] for h in range(GROUP)], axis=0)
+
+
+def side_by_side(value):
+    return jnp.concatenate([value[h * HEAD:(h + 1) * HEAD, :] for h in range(GROUP)], axis=1)
 
 
 def plan_kernel(place_ref, anc_ref, rows_ref, item_ref, list_ref):
@@ -114,8 +120,8 @@
             first = item_ref[row, 0]
             second = item_ref[row, 1]
             kv = jnp.concatenate([kv_ref[first], kv_ref[second]], axis=0)
-            scores = dot_nt(kv[:, :HEAD], group[:ROWS, :]) * FACTOR
-            prob_grads = dot_nt(kv[:, HEAD:], group[ROWS:, :])
+            scores = dot_nt(kv[:, :HEAD], head_rows(group, 0)) * FACTOR
+            prob_grads = dot_nt(kv[:, HEAD:], head_rows(group, ROWS))
             upper = jnp.where(gap >= item_ref[row, 2], scores[:BLOCK], MASKED)
             lower = jnp.where(gap >= item_ref[row, 3], scores[BLOCK:], MASKED)
             scores = jnp.concatenate([upper, lower], axis=0)
@@ -172,8 +178,8 @@
             second = item_ref[row, 1]
             probs = jnp.exp(score_ref[row] - log_totals)
             score_grads = (probs * (pgrad_ref[row] - row_dots)).astype(BF16)
-            dk_pair = dot_nn(score_grads, group[:ROWS, :])
-            dv_pair = dot_nn(probs.astype(BF16), group[ROWS:, :])
+            dk_pair = dot_nn(score_grads, head_rows(group, 0))
+            dv_pair = dot_nn(probs.astype(BF16), head_rows(group, ROWS))
             dk_acc[first] += dk_pair[:BLOCK]
             dk_acc[second] += dk_pair[BLOCK:]
             dv_acc[first] += dv_pair[:BLOCK]
@@ -258,7 +264,8 @@
     low_ref[:HEAD, :] = unrotate(total[:, :HEAD].T, cos_ref[...], sin_ref[...]).astype(BF16)
     low_ref[HEAD:, :] = total[:, HEAD:].T.astype(BF16)
     for i in range(NX):
-        out_ref[i] = (part_ref[i] + key_value_part(low_ref, wk[i], wv[i])).astype(BF16)
+        total = part_ref[i] + key_value_part(low_ref, wk[i], wv[i])
+        out_ref[i] = side_by_side(total).astype(BF16)
 
 
 def second_half_kernel(place_ref, low_ref, part_ref, wk_hbm, wv_hbm, out_ref, wk, wv, sem):
@@ -266,7 +273,7 @@
     for i in range(NX):
         for copy in copies[2 * i:2 * i + 2]:
             copy.wait()
-        out_ref[i] = part_ref[NX + i] + key_value_part(low_ref, wk[i], wv[i])
+        out_ref[i] = side_by_side(part_ref[NX + i] + key_value_part(low_ref, wk[i], wv[i]))
 
 
 def key_value_part(low_ref, wk, wv):
@@ -275,11 +282,11 @@
 
 def finish_kernel(kept_ref, arrived_ref, p0, p1, p2, out_ref):
     for h in range(GROUP):
-        rows = slice(h * HEAD, (h + 1) * HEAD)
-        total = kept_ref[rows, :]
+        cols = slice(h * HEAD, (h + 1) * HEAD)
+        total = kept_ref[:, cols]
         for part in (arrived_ref, p0, p1, p2):
-            total = total + part[rows, :].astype(F32)
-        out_ref[:, rows] = total.T.astype(BF16)
+            total = total + part[:, cols].astype(F32)
+        out_ref[:, cols] = total.T.astype(BF16)
 
 
 def shift(size, k):
@@ -291,11 +298,11 @@
     place = jnp.stack([z, y, x, c]).astype(I32)
     group, kv = call(
         stack_kernel,
-        [pltpu.VMEM((2 * ROWS, HEAD), BF16), pltpu.VMEM((BLOCK, 2 * HEAD), BF16)],
+        [pltpu.VMEM((BLOCK, 2 * ROWS), BF16), pltpu.VMEM((BLOCK, 2 * HEAD), BF16)],
         [HB] * 4,
         [VM] * 2,
         "stack",
-        [pltpu.SemaphoreType.DMA((2 * GROUP + 2,))],
+        [pltpu.SemaphoreType.DMA((4,))],
     )(*in_hbm(queries, out_grad, keys, values))
     groups = [group] + [lax.ppermute(group, "y", shift(NY, k)) for k in range(1, NY)]
     below, above = [kv], [kv]
@@ -311,6 +318,7 @@
         SM,
         "plan",
         [pltpu.SMEM((NZ + 1,), I32)],
+        PLAN_FLOPS,
     )(place, ancestry.T, group)
 
     tiles = (NY * PAIRS, 2 * BLOCK, ROWS)
@@ -363,7 +371,7 @@
     )(place, cosine, sine, *dq_own, wk, wv, *blocks)
     away, low = call(
         first_half_kernel,
-        [pltpu.VMEM((NX, ROWS, BLOCK), BF16), pltpu.VMEM((2 * HEAD, BLOCK), BF16)],
+        [pltpu.VMEM((NX, BLOCK, ROWS), BF16), pltpu.VMEM((2 * HEAD, BLOCK), BF16)],
         [VM] * 6,
         [VM] * 2,
         "first_half",
@@ -371,7 +379,7 @@
     arrived = lax.ppermute(away, "c", shift(NC, 1))
     kept = call(
         second_half_kernel,
-        pltpu.VMEM((NX, ROWS, BLOCK), F32),
+        pltpu.VMEM((NX, BLOCK, ROWS), F32),
         [SM] + [VM] * 2 + [HB] * 2,
         VM,
         "second_half",

time: 87 us -> 84.3 us (0.969)
  waiting for transfers between devices: 23.9 us -> 20.2 us
    ppermute x3, waiting for transfers between devices: 5.83 us -> 0.6 us  [shards(): below.append(lax.ppermute(below[-1], 'z', shift(NZ, 1)))]
    ppermute x1, starting transfers between devices: 9.06 us -> 6.58 us  [shards(): arrived = lax.ppermute(away, 'c', shift(NC, 1))]
    ppermute x3, waiting for transfers between devices: 0.01 us -> 2.28 us  [shards(): above.append(lax.ppermute(above[-1], 'z', shift(NZ, -1)))]
    ppermute x3, starting transfers between devices: 1.46 us -> 2.88 us  [shards(): lax.ppermute(dq_parts[k], 'y', shift(NY, -k))]
    ppermute x3, starting transfers between devices: 9.29 us -> 10.3 us  [shards(): above.append(lax.ppermute(above[-1], 'z', shift(NZ, -1)))]
    ppermute x3, starting transfers between devices: 4.68 us -> 3.77 us  [shards(): lax.ppermute(group, 'y', shift(NY, k))]
    ppermute x3, starting transfers between devices: 1.64 us -> 2.55 us  [shards(): below.append(lax.ppermute(below[-1], 'z', shift(NZ, 1)))]
where the time goes in v11:
time: 84.3 us; the launch traced here: 84 us
  starting transfers between devices  40.8 us (48%)
  Pallas kernels  22 us (26%)
  waiting for transfers between devices  20.2 us (24%)
    ppermute x3, starting transfers between devices, shards(): above.append(lax.ppermute(above[-1], 'z', shift(NZ, -1)))  10.3 us
    ppermute x3, waiting for transfers between devices, shards(): parts = [lax.ppermute(sent[k - 1], 'x', shift(NX, k)) for k in range(1, NX)]  10 us
    all_to_all x1, starting transfers between devices, shards(): dkv_own = lax.all_to_all(dkv, 'z', 0, 0, tiled=True)  8.27 us
    ppermute x1, starting transfers between devices, shards(): arrived = lax.ppermute(away, 'c', shift(NC, 1))  6.58 us
    pallas_call x1, Pallas kernels, shards(): call(query_part_kernel, [pltpu.VMEM((2 * NX, ROWS, BLOCK), BF16)] + pair_...  3.78 us
    ppermute x3, starting transfers between devices, shards(): lax.ppermute(group, 'y', shift(NY, k))  3.77 us
    pallas_call x1, Pallas kernels, shards(): call(fetch_kernel, [pltpu.VMEM((HEAD // 2, BLOCK), F32)] * 2 + [pltpu.VME...  3.68 us
    ppermute x3, starting transfers between devices, shards(): parts = [lax.ppermute(sent[k - 1], 'x', shift(NX, k)) for k in range(1, NX)]  3.67 us
  transfers between devices with their start and end apart: 21, of which 12 were waited for; matrix products, arithmetic and copies ran while one was open for 0% of the time, Pallas kernels for 15%

profile of v11, /device:TPU:1, one launch (start us, length us, event | category | flops | bytes accessed | tf_op | source)
XLA Modules:
  0.0 84.0 jit_solution(8386760458860834152)
XLA Ops:
  1.1 2.5 %collective-permute-start = (bf16[128,256]{1,0:T(8,128)(2,1)S(1)}, bf16[128,256]{1,0:T(8,128)(2,1)S(1)}, u32[]{:S(2)}, u32[]{:S(2)}) collective-permute-start(bf16[128,256]{1,0:T(8,128)(2,1)S(1)} %get-tuple-element.31.k0), channel_id=1, source_target_pairs={{0,32},{32,64},{64,96},{96,128},{128,160},{160,192},{192,224},{224... | collective-permute-start | bytes 196616 | tf_op jit(solution)/shard_map/ppermute | solution.py:310
  3.6 2.7 %collective-permute-start.9 = (bf16[128,1280]{1,0:T(8,128)(2,1)S(1)}, bf16[128,1280]{1,0:T(8,128)(2,1)S(1)}, u32[]{:S(2)}, u32[]{:S(2)}) collective-permute-start(bf16[128,1280]{1,0:T(8,128)(2,1)S(1)} %get-tuple-element.30.rows_ref.g0), channel_id=1, source_target_pairs={{0,24},{8,0},{16,8},{24,16},{1,25},{9,1},{17,9},{25,17},{2,26},{10... | collective-permute-start | bytes 983048 | tf_op jit(solution)/shard_map/ppermute | solution.py:307
  7.4 4.0 %collective-permute-start.4 = (bf16[128,256]{1,0:T(8,128)(2,1)S(1)}, bf16[128,256]{1,0:T(8,128)(2,1)S(1)}, u32[]{:S(2)}, u32[]{:S(2)}) collective-permute-start(bf16[128,256]{1,0:T(8,128)(2,1)S(1)} %get-tuple-element.31.k0), channel_id=1, source_target_pairs={{0,224},{32,0},{64,32},{96,64},{128,96},{160,128},{192,160},{224,1... | collective-permute-start | bytes 196616 | tf_op jit(solution)/shard_map/ppermute | solution.py:311
  11.4 1.3 %collective-permute-done.4.k7 = bf16[128,256]{1,0:T(8,128)(2,1)S(1)} collective-permute-done((bf16[128,256]{1,0:T(8,128)(2,1)S(1)}, bf16[128,256]{1,0:T(8,128)(2,1)S(1)}, u32[]{:S(2)}, u32[]{:S(2)}) %collective-permute-start.4) | collective-permute-done | bytes 65568 | tf_op jit(solution)/shard_map/ppermute | solution.py:311
  12.8 3.0 %collective-permute-start.5 = (bf16[128,256]{1,0:T(8,128)(2,1)S(1)}, bf16[128,256]{1,0:T(8,128)(2,1)S(1)}, u32[]{:S(2)}, u32[]{:S(2)}) collective-permute-start(bf16[128,256]{1,0:T(8,128)(2,1)S(1)} %collective-permute-done.4.k7), channel_id=1, source_target_pairs={{0,224},{32,0},{64,32},{96,64},{128,96},{160,128},{192,160},{224,1... | collective-permute-start | bytes 196616 | tf_op jit(solution)/shard_map/ppermute | solution.py:311
  17.1 3.3 %collective-permute-start.6 = (bf16[128,256]{1,0:T(8,128)(2,1)S(1)}, bf16[128,256]{1,0:T(8,128)(2,1)S(1)}, u32[]{:S(2)}, u32[]{:S(2)}) collective-permute-start(bf16[128,256]{1,0:T(8,128)(2,1)S(1)} %collective-permute-done.5.k6), channel_id=1, source_target_pairs={{0,224},{32,0},{64,32},{96,64},{128,96},{160,128},{192,160},{224,1... | collective-permute-start | bytes 196616 | tf_op jit(solution)/shard_map/ppermute | solution.py:311
  21.4 1.8 %plan.1.item_ref = s32[20,4]{1,0:T(8,128)S(1)} custom-call(s32[4]{0:T(128)S(1)} %pad_add_fusion.place_ref, s32[17,32]{1,0:T(8,128)S(1)} %bitcast.15, bf16[128,1280]{1,0:T(8,128)(2,1)S(1)} %get-tuple-element.30.rows_ref.g0), custom_call_target="tpu_custom_call" | custom-call | flops 1000000000 | tf_op jit(solution)/shard_map/plan/pallas_call | solution.py:314
  23.2 1.8 %collective-permute-done.3.k4 = bf16[128,256]{1,0:T(8,128)(2,1)S(1)} collective-permute-done((bf16[128,256]{1,0:T(8,128)(2,1)S(1)}, bf16[128,256]{1,0:T(8,128)(2,1)S(1)}, u32[]{:S(2)}, u32[]{:S(2)}) %collective-permute-start.3) | collective-permute-done | bytes 65568 | tf_op jit(solution)/shard_map/ppermute | solution.py:312
  25.0 2.5 %stats.1 = (f32[4,4,640]{2,1,0:T(4,128)S(1)}, f32[16,256,640]{2,1,0:T(8,128)S(1)}, f32[16,256,640]{2,1,0:T(8,128)S(1)}) custom-call(s32[20,4]{1,0:T(8,128)S(1)} %plan.1.item_ref, bf16[128,256]{1,0:T(8,128)(2,1)S(1)} %get-tuple-element.31.k0, bf16[128,256]{1,0:T(8,128)(2,1)S(1)} %collective-permute-done.k1, bf16[128,256]{1,0:T(8,128)(2,1)S(1)} %collective-permute-done.1.k2, ...), custom_call_target="tpu_custom_call" | custom-call | flops 1342177280 | tf_op jit(solution)/shard_map/stats/pallas_call | solution.py:325
  28.3 1.9 %collective-permute-start.11 = (f32[4,4,640]{2,1,0:T(4,128)S(1)}, f32[4,4,640]{2,1,0:T(4,128)S(1)}, u32[]{:S(2)}, u32[]{:S(2)}) collective-permute-start(f32[4,4,640]{2,1,0:T(4,128)S(1)} %get-tuple-element.32.stat_ref.s0), channel_id=1, source_target_pairs={{0,16},{8,24},{16,0},{24,8},{1,17},{9,25},{17,1},{25,9},{2,18},{10... | collective-permute-start | bytes 122888 | tf_op jit(solution)/shard_map/ppermute | solution.py:334
  31.1 1.6 %collective-permute-done.11.s2 = f32[4,4,640]{2,1,0:T(4,128)S(1)} collective-permute-done((f32[4,4,640]{2,1,0:T(4,128)S(1)}, f32[4,4,640]{2,1,0:T(4,128)S(1)}, u32[]{:S(2)}, u32[]{:S(2)}) %collective-permute-start.11) | collective-permute-done | bytes 40992 | tf_op jit(solution)/shard_map/ppermute | solution.py:334
  32.7 1.6 %collective-permute-done.10.s1 = f32[4,4,640]{2,1,0:T(4,128)S(1)} collective-permute-done((f32[4,4,640]{2,1,0:T(4,128)S(1)}, f32[4,4,640]{2,1,0:T(4,128)S(1)}, u32[]{:S(2)}, u32[]{:S(2)}) %collective-permute-start.10) | collective-permute-done | bytes 40992 | tf_op jit(solution)/shard_map/ppermute | solution.py:334
  34.3 3.2 %grads.1 = (bf16[8,128,256]{2,1,0:T(8,128)(2,1)S(1)}, bf16[128,640]{1,0:T(8,128)(2,1)S(1)}, bf16[128,640]{1,0:T(8,128)(2,1)S(1)}, bf16[128,640]{1,0:T(8,128)(2,1)S(1)}, bf16[128,640]{1,0:T(8,128)(2,1)S(1)}) custom-call(s32[20,4]{1,0:T(8,128)S(1)} %plan.1.item_ref, bf16[8,128,128]{2,1,0:T(8,128)(2,1)S(1)} %turn.1.cols_ref, ...), custom_call_target="tpu_custom_call" | custom-call | flops 2013265920 | tf_op jit(solution)/shard_map/grads/pallas_call | solution.py:338
  38.4 8.3 %all-to-all-start = ((bf16[8,128,256]{2,1,0:T(8,128)(2,1)}), bf16[8,128,256]{2,1,0:T(8,128)(2,1)S(1)}, u32[]{:S(2)}, u32[]{:S(2)}) async-start(bf16[8,128,256]{2,1,0:T(8,128)(2,1)} %flush.1), calls=%async_computation | async-start | bytes 1048576 | tf_op jit(solution)/shard_map/all_to_all | solution.py:351
  46.6 1.5 %collective-permute-start.13 = (bf16[128,640]{1,0:T(8,128)(2,1)S(1)}, bf16[128,640]{1,0:T(8,128)(2,1)S(1)}, u32[]{:S(2)}, u32[]{:S(2)}) collective-permute-start(bf16[128,640]{1,0:T(8,128)(2,1)S(1)} %get-tuple-element.39), channel_id=1, source_target_pairs={{0,24},{8,0},{16,8},{24,16},{1,25},{9,1},{17,9},{25,17},{2,26},{10... | collective-permute-start | bytes 491528 | tf_op jit(solution)/shard_map/ppermute | solution.py:347
  48.1 1.4 %collective-permute-start.14 = (bf16[128,640]{1,0:T(8,128)(2,1)S(1)}, bf16[128,640]{1,0:T(8,128)(2,1)S(1)}, u32[]{:S(2)}, u32[]{:S(2)}) collective-permute-start(bf16[128,640]{1,0:T(8,128)(2,1)S(1)} %get-tuple-element.40), channel_id=1, source_target_pairs={{0,16},{8,24},{16,0},{24,8},{1,17},{9,25},{17,1},{25,9},{2,18},{10... | collective-permute-start | bytes 491528 | tf_op jit(solution)/shard_map/ppermute | solution.py:347
  49.5 3.7 %fetch.1 = (f32[64,128]{1,0:T(8,128)S(1)}, f32[64,128]{1,0:T(8,128)S(1)}, bf16[640,640]{1,0:T(8,128)(2,1)S(1)}, bf16[640,640]{1,0:T(8,128)(2,1)S(1)}, bf16[640,6...) custom-call(s32[4]{0:T(128)S(1)} %pad_add_fusion.place_ref, ...), custom_call_target="tpu_custom_call" | custom-call | tf_op jit(solution)/shard_map/fetch/pallas_call | solution.py:354
  53.8 1.7 %collective-permute-done.15.q3 = bf16[128,640]{1,0:T(8,128)(2,1)S(1)} collective-permute-done((bf16[128,640]{1,0:T(8,128)(2,1)S(1)}, bf16[128,640]{1,0:T(8,128)(2,1)S(1)}, u32[]{:S(2)}, u32[]{:S(2)}) %collective-permute-start.15) | collective-permute-done | bytes 163872 | tf_op jit(solution)/shard_map/ppermute | solution.py:347
  55.5 3.8 %query_part.1 = (bf16[8,640,128]{2,1,0:T(8,128)(2,1)S(1)}, bf16[4,640,128]{2,1,0:T(8,128)(2,1)S(1)}, bf16[4,640,128]{2,1,0:T(8,128)(2,1)S(1)}) custom-call(s32[4]{0:T(128)S(1)} %pad_add_fusion.place_ref, f32[64,128]{1,0:T(8,128)S(1)} %get-tuple-element.36.cos_ref, f32[64,128]{1,0:T(8,128)S(1)} %get-tuple-element.37.sin_ref, ...), custom_call_target="tpu_custom_call" | custom-call | flops 838860800 | tf_op jit(solution)/shard_map/query_part/pallas_call | solution.py:363
  59.9 6.6 %collective-permute-start.16 = (bf16[4,128,640]{2,1,0:T(8,128)(2,1)S(1)}, bf16[4,128,640]{2,1,0:T(8,128)(2,1)S(1)}, u32[]{:S(2)}, u32[]{:S(2)}) collective-permute-start(bf16[4,128,640]{2,1,0:T(8,128)(2,1)S(1)} %get-tuple-element.54), channel_id=1, source_target_pairs={{0,1},{1,0},{2,3},{3,2},{4,5},{5,4},{6,7},{7,6},{8,9},{9,8},{10,11... | collective-permute-start | bytes 1966088 | tf_op jit(solution)/shard_map/ppermute | solution.py:379
  66.5 2.8 %second_half.1 = f32[4,128,640]{2,1,0:T(8,128)S(1)} custom-call(s32[4]{0:T(128)S(1)} %pad_add_fusion.place_ref, bf16[256,128]{1,0:T(8,128)(2,1)S(1)} %get-tuple-element.53.low_ref, bf16[8,640,128]{2,1,0:T(8,128)(2,1)S(1)} %get-tuple-element.50.part_ref, bf16[5120,128]{1,0:T(8,128)(2,1)} %wk_hbm.3, bf16[5120,128]{1,0:T(8,128)(2,1)} %wv_hbm.3), custom_call_target="tpu_custom_call" | custom-call | tf_op jit(solution)/shard_map/second_half/pallas_call | solution.py:380
  69.5 2.6 %collective-permute-start.19 = (bf16[128,640]{1,0:T(8,128)(2,1)S(1)}, bf16[128,640]{1,0:T(8,128)(2,1)S(1)}, u32[]{:S(2)}, u32[]{:S(2)}) collective-permute-start(bf16[128,640]{1,0:T(8,128)(2,1)S(1)} %get-tuple-element.55), channel_id=1, source_target_pairs={{0,6},{2,0},{4,2},{6,4},{1,7},{3,1},{5,3},{7,5},{8,14},{10,8},{12,... | collective-permute-start | bytes 491528 | tf_op jit(solution)/shard_map/ppermute | solution.py:389
  73.2 5.9 %collective-permute-done.19.p2 = bf16[128,640]{1,0:T(8,128)(2,1)S(1)} collective-permute-done((bf16[128,640]{1,0:T(8,128)(2,1)S(1)}, bf16[128,640]{1,0:T(8,128)(2,1)S(1)}, u32[]{:S(2)}, u32[]{:S(2)}) %collective-permute-start.19) | collective-permute-done | bytes 163872 | tf_op jit(solution)/shard_map/ppermute | solution.py:389
  79.1 4.1 %collective-permute-done.17.p0 = bf16[128,640]{1,0:T(8,128)(2,1)S(1)} collective-permute-done((bf16[128,640]{1,0:T(8,128)(2,1)S(1)}, bf16[128,640]{1,0:T(8,128)(2,1)S(1)}, u32[]{:S(2)}, u32[]{:S(2)}) %collective-permute-start.17) | collective-permute-done | bytes 163872 | tf_op jit(solution)/shard_map/ppermute | solution.py:389
  (36 shorter events, 10.4 us)
Async XLA Ops:
  1.1 10.4 %collective-permute-start = (bf16[128,256]{1,0:T(8,128)(2,1)S(1)}, bf16[128,256]{1,0:T(8,128)(2,1)S(1)}, u32[]{:S(2)}, u32[]{:S(2)}) collective-permute-start(bf16[128,256]{1,0:T(8,128)(2,1)S(1)} %get-tuple-element.31.k0), channel_id=1, source_target_pairs={{0,32},{32,64},{64,96},{96,128},{128,160},{160,192},{192,224},{224... | collective-permute-start | bytes 196616 | tf_op jit(solution)/shard_map/ppermute | solution.py:310
  3.6 21.4 %collective-permute-start.9 = (bf16[128,1280]{1,0:T(8,128)(2,1)S(1)}, bf16[128,1280]{1,0:T(8,128)(2,1)S(1)}, u32[]{:S(2)}, u32[]{:S(2)}) collective-permute-start(bf16[128,1280]{1,0:T(8,128)(2,1)S(1)} %get-tuple-element.30.rows_ref.g0), channel_id=1, source_target_pairs={{0,24},{8,0},{16,8},{24,16},{1,25},{9,1},{17,9},{25,17},{2,26},{10... | collective-permute-start | bytes 983048 | tf_op jit(solution)/shard_map/ppermute | solution.py:307
  6.4 18.7 %collective-permute-start.8 = (bf16[128,1280]{1,0:T(8,128)(2,1)S(1)}, bf16[128,1280]{1,0:T(8,128)(2,1)S(1)}, u32[]{:S(2)}, u32[]{:S(2)}) collective-permute-start(bf16[128,1280]{1,0:T(8,128)(2,1)S(1)} %get-tuple-element.30.rows_ref.g0), channel_id=1, source_target_pairs={{0,16},{8,24},{16,0},{24,8},{1,17},{9,25},{17,1},{25,9},{2,18},{10... | collective-permute-start | bytes 983048 | tf_op jit(solution)/shard_map/ppermute | solution.py:307
  6.7 18.3 %collective-permute-start.7 = (bf16[128,1280]{1,0:T(8,128)(2,1)S(1)}, bf16[128,1280]{1,0:T(8,128)(2,1)S(1)}, u32[]{:S(2)}, u32[]{:S(2)}) collective-permute-start(bf16[128,1280]{1,0:T(8,128)(2,1)S(1)} %get-tuple-element.30.rows_ref.g0), channel_id=1, source_target_pairs={{0,8},{8,16},{16,24},{24,0},{1,9},{9,17},{17,25},{25,1},{2,10},{10... | collective-permute-start | bytes 983048 | tf_op jit(solution)/shard_map/ppermute | solution.py:307
  7.4 5.4 %collective-permute-start.4 = (bf16[128,256]{1,0:T(8,128)(2,1)S(1)}, bf16[128,256]{1,0:T(8,128)(2,1)S(1)}, u32[]{:S(2)}, u32[]{:S(2)}) collective-permute-start(bf16[128,256]{1,0:T(8,128)(2,1)S(1)} %get-tuple-element.31.k0), channel_id=1, source_target_pairs={{0,224},{32,0},{64,32},{96,64},{128,96},{160,128},{192,160},{224,1... | collective-permute-start | bytes 196616 | tf_op jit(solution)/shard_map/ppermute | solution.py:311
  11.4 4.6 %collective-permute-start.1 = (bf16[128,256]{1,0:T(8,128)(2,1)S(1)}, bf16[128,256]{1,0:T(8,128)(2,1)S(1)}, u32[]{:S(2)}, u32[]{:S(2)}) collective-permute-start(bf16[128,256]{1,0:T(8,128)(2,1)S(1)} %collective-permute-done.k1), channel_id=1, source_target_pairs={{0,32},{32,64},{64,96},{96,128},{128,160},{160,192},{192,224},{224... | collective-permute-start | bytes 196616 | tf_op jit(solution)/shard_map/ppermute | solution.py:310
  12.8 4.3 %collective-permute-start.5 = (bf16[128,256]{1,0:T(8,128)(2,1)S(1)}, bf16[128,256]{1,0:T(8,128)(2,1)S(1)}, u32[]{:S(2)}, u32[]{:S(2)}) collective-permute-start(bf16[128,256]{1,0:T(8,128)(2,1)S(1)} %collective-permute-done.4.k7), channel_id=1, source_target_pairs={{0,224},{32,0},{64,32},{96,64},{128,96},{160,128},{192,160},{224,1... | collective-permute-start | bytes 196616 | tf_op jit(solution)/shard_map/ppermute | solution.py:311
  16.1 4.6 %collective-permute-start.2 = (bf16[128,256]{1,0:T(8,128)(2,1)S(1)}, bf16[128,256]{1,0:T(8,128)(2,1)S(1)}, u32[]{:S(2)}, u32[]{:S(2)}) collective-permute-start(bf16[128,256]{1,0:T(8,128)(2,1)S(1)} %collective-permute-done.1.k2), channel_id=1, source_target_pairs={{0,32},{32,64},{64,96},{96,128},{128,160},{160,192},{192,224},{224... | collective-permute-start | bytes 196616 | tf_op jit(solution)/shard_map/ppermute | solution.py:310
  17.1 6.1 %collective-permute-start.6 = (bf16[128,256]{1,0:T(8,128)(2,1)S(1)}, bf16[128,256]{1,0:T(8,128)(2,1)S(1)}, u32[]{:S(2)}, u32[]{:S(2)}) collective-permute-start(bf16[128,256]{1,0:T(8,128)(2,1)S(1)} %collective-permute-done.5.k6), channel_id=1, source_target_pairs={{0,224},{32,0},{64,32},{96,64},{128,96},{160,128},{192,160},{224,1... | collective-permute-start | bytes 196616 | tf_op jit(solution)/shard_map/ppermute | solution.py:311
  20.7 4.3 %collective-permute-start.3 = (bf16[128,256]{1,0:T(8,128)(2,1)S(1)}, bf16[128,256]{1,0:T(8,128)(2,1)S(1)}, u32[]{:S(2)}, u32[]{:S(2)}) collective-permute-start(bf16[128,256]{1,0:T(8,128)(2,1)S(1)} %collective-permute-done.2.k3), channel_id=1, source_target_pairs={{0,32},{32,64},{64,96},{96,128},{128,160},{160,192},{192,224},{224... | collective-permute-start | bytes 196616 | tf_op jit(solution)/shard_map/ppermute | solution.py:312
  20.7 0.7 copy-start
  27.5 3.6 %collective-permute-start.12 = (f32[4,4,640]{2,1,0:T(4,128)S(1)}, f32[4,4,640]{2,1,0:T(4,128)S(1)}, u32[]{:S(2)}, u32[]{:S(2)}) collective-permute-start(f32[4,4,640]{2,1,0:T(4,128)S(1)} %get-tuple-element.32.stat_ref.s0), channel_id=1, source_target_pairs={{0,24},{8,0},{16,8},{24,16},{1,25},{9,1},{17,9},{25,17},{2,26},{10... | collective-permute-start | bytes 122888 | tf_op jit(solution)/shard_map/ppermute | solution.py:334
  28.3 4.4 %collective-permute-start.11 = (f32[4,4,640]{2,1,0:T(4,128)S(1)}, f32[4,4,640]{2,1,0:T(4,128)S(1)}, u32[]{:S(2)}, u32[]{:S(2)}) collective-permute-start(f32[4,4,640]{2,1,0:T(4,128)S(1)} %get-tuple-element.32.stat_ref.s0), channel_id=1, source_target_pairs={{0,16},{8,24},{16,0},{24,8},{1,17},{9,25},{17,1},{25,9},{2,18},{10... | collective-permute-start | bytes 122888 | tf_op jit(solution)/shard_map/ppermute | solution.py:334
  30.2 4.1 %collective-permute-start.10 = (f32[4,4,640]{2,1,0:T(4,128)S(1)}, f32[4,4,640]{2,1,0:T(4,128)S(1)}, u32[]{:S(2)}, u32[]{:S(2)}) collective-permute-start(f32[4,4,640]{2,1,0:T(4,128)S(1)} %get-tuple-element.32.stat_ref.s0), channel_id=1, source_target_pairs={{0,8},{8,16},{16,24},{24,0},{1,9},{9,17},{17,25},{25,1},{2,10},{10... | collective-permute-start | bytes 122888 | tf_op jit(solution)/shard_map/ppermute | solution.py:334
  37.5 12.0 %copy-start.1 = (s32[32,17]{0,1:T(8,128)S(1)}, s32[32,17]{0,1:T(8,128)}, u32[]{:S(2)}) copy-start(s32[32,17]{0,1:T(8,128)} %param.12) | copy-start | bytes 6532
  38.4 20.9 %all-to-all-start = ((bf16[8,128,256]{2,1,0:T(8,128)(2,1)}), bf16[8,128,256]{2,1,0:T(8,128)(2,1)S(1)}, u32[]{:S(2)}, u32[]{:S(2)}) async-start(bf16[8,128,256]{2,1,0:T(8,128)(2,1)} %flush.1), calls=%async_computation | async-start | bytes 1048576 | tf_op jit(solution)/shard_map/all_to_all | solution.py:351
  46.6 6.6 %collective-permute-start.13 = (bf16[128,640]{1,0:T(8,128)(2,1)S(1)}, bf16[128,640]{1,0:T(8,128)(2,1)S(1)}, u32[]{:S(2)}, u32[]{:S(2)}) collective-permute-start(bf16[128,640]{1,0:T(8,128)(2,1)S(1)} %get-tuple-element.39), channel_id=1, source_target_pairs={{0,24},{8,0},{16,8},{24,16},{1,25},{9,1},{17,9},{25,17},{2,26},{10... | collective-permute-start | bytes 491528 | tf_op jit(solution)/shard_map/ppermute | solution.py:347
  48.1 5.7 %collective-permute-start.14 = (bf16[128,640]{1,0:T(8,128)(2,1)S(1)}, bf16[128,640]{1,0:T(8,128)(2,1)S(1)}, u32[]{:S(2)}, u32[]{:S(2)}) collective-permute-start(bf16[128,640]{1,0:T(8,128)(2,1)S(1)} %get-tuple-element.40), channel_id=1, source_target_pairs={{0,16},{8,24},{16,0},{24,8},{1,17},{9,25},{17,1},{25,9},{2,18},{10... | collective-permute-start | bytes 491528 | tf_op jit(solution)/shard_map/ppermute | solution.py:347
  49.5 6.0 %collective-permute-start.15 = (bf16[128,640]{1,0:T(8,128)(2,1)S(1)}, bf16[128,640]{1,0:T(8,128)(2,1)S(1)}, u32[]{:S(2)}, u32[]{:S(2)}) collective-permute-start(bf16[128,640]{1,0:T(8,128)(2,1)S(1)} %get-tuple-element.41), channel_id=1, source_target_pairs={{0,8},{8,16},{16,24},{24,0},{1,9},{9,17},{17,25},{25,1},{2,10},{10... | collective-permute-start | bytes 491528 | tf_op jit(solution)/shard_map/ppermute | solution.py:347
  59.9 9.4 %collective-permute-start.16 = (bf16[4,128,640]{2,1,0:T(8,128)(2,1)S(1)}, bf16[4,128,640]{2,1,0:T(8,128)(2,1)S(1)}, u32[]{:S(2)}, u32[]{:S(2)}) collective-permute-start(bf16[4,128,640]{2,1,0:T(8,128)(2,1)S(1)} %get-tuple-element.54), channel_id=1, source_target_pairs={{0,1},{1,0},{2,3},{3,2},{4,5},{5,4},{6,7},{7,6},{8,9},{9,8},{10,11... | collective-permute-start | bytes 1966088 | tf_op jit(solution)/shard_map/ppermute | solution.py:379
  69.5 9.5 %collective-permute-start.19 = (bf16[128,640]{1,0:T(8,128)(2,1)S(1)}, bf16[128,640]{1,0:T(8,128)(2,1)S(1)}, u32[]{:S(2)}, u32[]{:S(2)}) collective-permute-start(bf16[128,640]{1,0:T(8,128)(2,1)S(1)} %get-tuple-element.55), channel_id=1, source_target_pairs={{0,6},{2,0},{4,2},{6,4},{1,7},{3,1},{5,3},{7,5},{8,14},{10,8},{12,... | collective-permute-start | bytes 491528 | tf_op jit(solution)/shard_map/ppermute | solution.py:389
  72.1 7.0 %collective-permute-start.18 = (bf16[128,640]{1,0:T(8,128)(2,1)S(1)}, bf16[128,640]{1,0:T(8,128)(2,1)S(1)}, u32[]{:S(2)}, u32[]{:S(2)}) collective-permute-start(bf16[128,640]{1,0:T(8,128)(2,1)S(1)} %get-tuple-element.56), channel_id=1, source_target_pairs={{0,4},{2,6},{4,0},{6,2},{1,5},{3,7},{5,1},{7,3},{8,12},{10,14},{12... | collective-permute-start | bytes 491528 | tf_op jit(solution)/shard_map/ppermute | solution.py:389
  72.6 10.6 %collective-permute-start.17 = (bf16[128,640]{1,0:T(8,128)(2,1)S(1)}, bf16[128,640]{1,0:T(8,128)(2,1)S(1)}, u32[]{:S(2)}, u32[]{:S(2)}) collective-permute-start(bf16[128,640]{1,0:T(8,128)(2,1)S(1)} %get-tuple-element.57), channel_id=1, source_target_pairs={{0,2},{2,4},{4,6},{6,0},{1,3},{3,5},{5,7},{7,1},{8,10},{10,12},{12... | collective-permute-start | bytes 491528 | tf_op jit(solution)/shard_map/ppermute | solution.py:389

commit v12 on v11

--- a/solution.py
+++ b/solution.py
@@ -105,7 +105,7 @@
         item_ref[NY * PAIRS + j, 1] = z
 
 
-def stats_kernel(item_ref, k0, k1, k2, k3, k4, k5, k6, k7, g0, g1, g2, g3, stat_ref, score_ref, pgrad_ref, kv_ref):
+def stats_kernel(item_ref, k0, k1, k2, k3, k4, k5, k6, k7, g0, g3, g2, g1, stat_ref, score_ref, pgrad_ref, kv_ref):
     z = item_ref[NY * PAIRS, 1]
     for r, part in enumerate((k0, k1, k2, k3, k4, k5, k6, k7)):
         kv_ref[(z - r) & (NZ - 1)] = part[...]
@@ -153,7 +153,7 @@
     run_copies([(low_ref, out_ref)], sem)
 
 
-def grads_kernel(item_ref, cols_ref, score_ref, pgrad_ref, g0, g1, g2, g3, s0, s1, s2, s3,
+def grads_kernel(item_ref, cols_ref, score_ref, pgrad_ref, g0, g1, g2, g3, s0, s3, s2, s1,
                  dkv_ref, dq0, dq1, dq2, dq3, dk_acc, dv_acc):
     stats = (s0, s1, s2, s3)
     dk_acc[...] = jnp.zeros_like(dk_acc)
@@ -280,7 +280,7 @@
     return dot_nn(wk, low_ref[:HEAD, :]) + dot_nn(wv, low_ref[HEAD:, :])
 
 
-def finish_kernel(kept_ref, arrived_ref, p0, p1, p2, out_ref):
+def finish_kernel(kept_ref, p2, p1, p0, arrived_ref, out_ref):
     for h in range(GROUP):
         cols = slice(h * HEAD, (h + 1) * HEAD)
         total = kept_ref[:, cols]
@@ -330,7 +330,7 @@
         "stats",
         [pltpu.VMEM((NZ, BLOCK, 2 * HEAD), BF16)],
         STATS_FLOPS,
-    )(items, *kvs, *groups)
+    )(items, *kvs, group, *groups[:0:-1])
     all_stats = [stats] + [lax.ppermute(stats, "y", shift(NY, k)) for k in range(1, NY)]
     key_cols = call(
         turn_kernel, pltpu.VMEM((NZ, HEAD, BLOCK), BF16), [SM] + [VM] * (NZ + 1), VM, "turn",
@@ -343,7 +343,7 @@
         "grads",
         [pltpu.VMEM((NZ, BLOCK, HEAD), F32), pltpu.VMEM((NZ, BLOCK, HEAD), F32)],
         GRADS_FLOPS,
-    )(items, key_cols, scores, prob_grads, *groups, *all_stats)
+    )(items, key_cols, scores, prob_grads, *groups, all_stats[0], *all_stats[:0:-1])
     dq_own = [dq_parts[0]] + [lax.ppermute(dq_parts[k], "y", shift(NY, -k)) for k in range(1, NY)]
     dkv = call(
         flush_kernel, pltpu.HBM(dkv.shape, BF16), [VM], HB, "flush", [pltpu.SemaphoreType.DMA((1,))],
@@ -389,7 +389,7 @@
     parts = [lax.ppermute(sent[k - 1], "x", shift(NX, k)) for k in range(1, NX)]
     return call(
         finish_kernel, jax.ShapeDtypeStruct((BLOCK, ROWS), BF16), [VM] * (2 + len(parts)), VM, "finish",
-    )(kept[0], arrived[0], *parts)
+    )(kept[0], *parts[::-1], arrived[0])
 
 
 def solution(mesh):

time: 84.3 us -> 82.2 us (0.975)
  waiting for transfers between devices: 20.2 us -> 15.6 us
  starting transfers between devices: 40.8 us -> 43.2 us
    ppermute x3, waiting for transfers between devices: 10 us -> 6.7 us  [shards(): parts = [lax.ppermute(sent[k - 1], 'x', shift(NX, k)) for k in range(1, NX)]]
    ppermute x3, waiting for transfers between devices: 3.19 us -> 1.54 us  [shards(): lax.ppermute(stats, 'y', shift(NY, k))]
    ppermute x3, starting transfers between devices: 3.67 us -> 4.88 us  [shards(): parts = [lax.ppermute(sent[k - 1], 'x', shift(NX, k)) for k in range(1, NX)]]
    ppermute x3, starting transfers between devices: 3.77 us -> 4.99 us  [shards(): lax.ppermute(group, 'y', shift(NY, k))]
    ppermute x1, starting transfers between devices: 6.58 us -> 7.51 us  [shards(): arrived = lax.ppermute(away, 'c', shift(NC, 1))]
  transfers between devices with their start and end apart: 21 -> 21, of which waited for: 12 -> 10; matrix products, arithmetic and copies ran while one was open for 0% -> 0% of each run, Pallas kernels for 15% -> 16%
where the time goes in v12:
time: 82.2 us; the launch traced here: 81.9 us
  starting transfers between devices  43.2 us (53%)
  Pallas kernels  22 us (27%)
  waiting for transfers between devices  15.6 us (19%)
    ppermute x3, starting transfers between devices, shards(): above.append(lax.ppermute(above[-1], 'z', shift(NZ, -1)))  10.6 us
    all_to_all x1, starting transfers between devices, shards(): dkv_own = lax.all_to_all(dkv, 'z', 0, 0, tiled=True)  7.53 us
    ppermute x1, starting transfers between devices, shards(): arrived = lax.ppermute(away, 'c', shift(NC, 1))  7.51 us
    ppermute x3, waiting for transfers between devices, shards(): parts = [lax.ppermute(sent[k - 1], 'x', shift(NX, k)) for k in range(1, NX)]  6.7 us
    ppermute x3, starting transfers between devices, shards(): lax.ppermute(group, 'y', shift(NY, k))  4.99 us
    ppermute x3, starting transfers between devices, shards(): parts = [lax.ppermute(sent[k - 1], 'x', shift(NX, k)) for k in range(1, NX)]  4.88 us
    pallas_call x1, Pallas kernels, shards(): call(query_part_kernel, [pltpu.VMEM((2 * NX, ROWS, BLOCK), BF16)] + pair_...  3.78 us
    pallas_call x1, Pallas kernels, shards(): call(fetch_kernel, [pltpu.VMEM((HEAD // 2, BLOCK), F32)] * 2 + [pltpu.VME...  3.68 us
  transfers between devices with their start and end apart: 21, of which 10 were waited for; matrix products, arithmetic and copies ran while one was open for 0% of the time, Pallas kernels for 16%

profile of v12, /device:TPU:1, one launch (start us, length us, event | category | flops | bytes accessed | tf_op | source)
XLA Modules:
  0.0 81.9 jit_solution(1677785876706565852)
XLA Ops:
  1.1 2.5 %collective-permute-start = (bf16[128,256]{1,0:T(8,128)(2,1)S(1)}, bf16[128,256]{1,0:T(8,128)(2,1)S(1)}, u32[]{:S(2)}, u32[]{:S(2)}) collective-permute-start(bf16[128,256]{1,0:T(8,128)(2,1)S(1)} %get-tuple-element.31.k0), channel_id=1, source_target_pairs={{0,32},{32,64},{64,96},{96,128},{128,160},{160,192},{192,224},{224... | collective-permute-start | bytes 196616 | tf_op jit(solution)/shard_map/ppermute | solution.py:310
  3.6 1.3 %collective-permute-start.9 = (bf16[128,1280]{1,0:T(8,128)(2,1)S(1)}, bf16[128,1280]{1,0:T(8,128)(2,1)S(1)}, u32[]{:S(2)}, u32[]{:S(2)}) collective-permute-start(bf16[128,1280]{1,0:T(8,128)(2,1)S(1)} %get-tuple-element.30.rows_ref.g0), channel_id=1, source_target_pairs={{0,8},{8,16},{16,24},{24,0},{1,9},{9,17},{17,25},{25,1},{2,10},{10... | collective-permute-start | bytes 983048 | tf_op jit(solution)/shard_map/ppermute | solution.py:307
  4.9 2.6 %collective-permute-start.8 = (bf16[128,1280]{1,0:T(8,128)(2,1)S(1)}, bf16[128,1280]{1,0:T(8,128)(2,1)S(1)}, u32[]{:S(2)}, u32[]{:S(2)}) collective-permute-start(bf16[128,1280]{1,0:T(8,128)(2,1)S(1)} %get-tuple-element.30.rows_ref.g0), channel_id=1, source_target_pairs={{0,16},{8,24},{16,0},{24,8},{1,17},{9,25},{17,1},{25,9},{2,18},{10... | collective-permute-start | bytes 983048 | tf_op jit(solution)/shard_map/ppermute | solution.py:307
  8.6 4.0 %collective-permute-start.4 = (bf16[128,256]{1,0:T(8,128)(2,1)S(1)}, bf16[128,256]{1,0:T(8,128)(2,1)S(1)}, u32[]{:S(2)}, u32[]{:S(2)}) collective-permute-start(bf16[128,256]{1,0:T(8,128)(2,1)S(1)} %get-tuple-element.31.k0), channel_id=1, source_target_pairs={{0,224},{32,0},{64,32},{96,64},{128,96},{160,128},{192,160},{224,1... | collective-permute-start | bytes 196616 | tf_op jit(solution)/shard_map/ppermute | solution.py:311
  12.6 1.3 %collective-permute-done.4.k7 = bf16[128,256]{1,0:T(8,128)(2,1)S(1)} collective-permute-done((bf16[128,256]{1,0:T(8,128)(2,1)S(1)}, bf16[128,256]{1,0:T(8,128)(2,1)S(1)}, u32[]{:S(2)}, u32[]{:S(2)}) %collective-permute-start.4) | collective-permute-done | bytes 65568 | tf_op jit(solution)/shard_map/ppermute | solution.py:311
  14.0 3.3 %collective-permute-start.5 = (bf16[128,256]{1,0:T(8,128)(2,1)S(1)}, bf16[128,256]{1,0:T(8,128)(2,1)S(1)}, u32[]{:S(2)}, u32[]{:S(2)}) collective-permute-start(bf16[128,256]{1,0:T(8,128)(2,1)S(1)} %collective-permute-done.4.k7), channel_id=1, source_target_pairs={{0,224},{32,0},{64,32},{96,64},{128,96},{160,128},{192,160},{224,1... | collective-permute-start | bytes 196616 | tf_op jit(solution)/shard_map/ppermute | solution.py:311
  18.6 3.3 %collective-permute-start.6 = (bf16[128,256]{1,0:T(8,128)(2,1)S(1)}, bf16[128,256]{1,0:T(8,128)(2,1)S(1)}, u32[]{:S(2)}, u32[]{:S(2)}) collective-permute-start(bf16[128,256]{1,0:T(8,128)(2,1)S(1)} %collective-permute-done.5.k6), channel_id=1, source_target_pairs={{0,224},{32,0},{64,32},{96,64},{128,96},{160,128},{192,160},{224,1... | collective-permute-start | bytes 196616 | tf_op jit(solution)/shard_map/ppermute | solution.py:311
  22.6 1.8 %plan.1.item_ref = s32[20,4]{1,0:T(8,128)S(1)} custom-call(s32[4]{0:T(128)S(1)} %pad_add_fusion.place_ref, s32[17,32]{1,0:T(8,128)S(1)} %bitcast.15, bf16[128,1280]{1,0:T(8,128)(2,1)S(1)} %get-tuple-element.30.rows_ref.g0), custom_call_target="tpu_custom_call" | custom-call | flops 1000000000 | tf_op jit(solution)/shard_map/plan/pallas_call | solution.py:314
  24.4 1.8 %collective-permute-done.3.k4 = bf16[128,256]{1,0:T(8,128)(2,1)S(1)} collective-permute-done((bf16[128,256]{1,0:T(8,128)(2,1)S(1)}, bf16[128,256]{1,0:T(8,128)(2,1)S(1)}, u32[]{:S(2)}, u32[]{:S(2)}) %collective-permute-start.3) | collective-permute-done | bytes 65568 | tf_op jit(solution)/shard_map/ppermute | solution.py:312
  26.2 2.5 %stats.1 = (f32[4,4,640]{2,1,0:T(4,128)S(1)}, f32[16,256,640]{2,1,0:T(8,128)S(1)}, f32[16,256,640]{2,1,0:T(8,128)S(1)}) custom-call(s32[20,4]{1,0:T(8,128)S(1)} %plan.1.item_ref, bf16[128,256]{1,0:T(8,128)(2,1)S(1)} %get-tuple-element.31.k0, bf16[128,256]{1,0:T(8,128)(2,1)S(1)} %collective-permute-done.k1, bf16[128,256]{1,0:T(8,128)(2,1)S(1)} %collective-permute-done.1.k2, ...), custom_call_target="tpu_custom_call" | custom-call | flops 1342177280 | tf_op jit(solution)/shard_map/stats/pallas_call | solution.py:325
  28.9 2.6 %collective-permute-start.10 = (f32[4,4,640]{2,1,0:T(4,128)S(1)}, f32[4,4,640]{2,1,0:T(4,128)S(1)}, u32[]{:S(2)}, u32[]{:S(2)}) collective-permute-start(f32[4,4,640]{2,1,0:T(4,128)S(1)} %get-tuple-element.32.stat_ref.s0), channel_id=1, source_target_pairs={{0,24},{8,0},{16,8},{24,16},{1,25},{9,1},{17,9},{25,17},{2,26},{10... | collective-permute-start | bytes 122888 | tf_op jit(solution)/shard_map/ppermute | solution.py:334
  33.9 3.2 %grads.1 = (bf16[8,128,256]{2,1,0:T(8,128)(2,1)S(1)}, bf16[128,640]{1,0:T(8,128)(2,1)S(1)}, bf16[128,640]{1,0:T(8,128)(2,1)S(1)}, bf16[128,640]{1,0:T(8,128)(2,1)S(1)}, bf16[128,640]{1,0:T(8,128)(2,1)S(1)}) custom-call(s32[20,4]{1,0:T(8,128)S(1)} %plan.1.item_ref, bf16[8,128,128]{2,1,0:T(8,128)(2,1)S(1)} %turn.1.cols_ref, ...), custom_call_target="tpu_custom_call" | custom-call | flops 2013265920 | tf_op jit(solution)/shard_map/grads/pallas_call | solution.py:338
  37.9 7.5 %all-to-all-start = ((bf16[8,128,256]{2,1,0:T(8,128)(2,1)}), bf16[8,128,256]{2,1,0:T(8,128)(2,1)S(1)}, u32[]{:S(2)}, u32[]{:S(2)}) async-start(bf16[8,128,256]{2,1,0:T(8,128)(2,1)} %flush.1), calls=%async_computation | async-start | bytes 1048576 | tf_op jit(solution)/shard_map/all_to_all | solution.py:351
  45.4 1.7 %collective-permute-start.13 = (bf16[128,640]{1,0:T(8,128)(2,1)S(1)}, bf16[128,640]{1,0:T(8,128)(2,1)S(1)}, u32[]{:S(2)}, u32[]{:S(2)}) collective-permute-start(bf16[128,640]{1,0:T(8,128)(2,1)S(1)} %get-tuple-element.39), channel_id=1, source_target_pairs={{0,24},{8,0},{16,8},{24,16},{1,25},{9,1},{17,9},{25,17},{2,26},{10... | collective-permute-start | bytes 491528 | tf_op jit(solution)/shard_map/ppermute | solution.py:347
  47.9 3.7 %fetch.1 = (f32[64,128]{1,0:T(8,128)S(1)}, f32[64,128]{1,0:T(8,128)S(1)}, bf16[640,640]{1,0:T(8,128)(2,1)S(1)}, bf16[640,640]{1,0:T(8,128)(2,1)S(1)}, bf16[640,6...) custom-call(s32[4]{0:T(128)S(1)} %pad_add_fusion.place_ref, ...), custom_call_target="tpu_custom_call" | custom-call | tf_op jit(solution)/shard_map/fetch/pallas_call | solution.py:354
  51.6 1.4 %collective-permute-done.14.q2 = bf16[128,640]{1,0:T(8,128)(2,1)S(1)} collective-permute-done((bf16[128,640]{1,0:T(8,128)(2,1)S(1)}, bf16[128,640]{1,0:T(8,128)(2,1)S(1)}, u32[]{:S(2)}, u32[]{:S(2)}) %collective-permute-start.14) | collective-permute-done | bytes 163872 | tf_op jit(solution)/shard_map/ppermute | solution.py:347
  52.9 1.7 %collective-permute-done.15.q3 = bf16[128,640]{1,0:T(8,128)(2,1)S(1)} collective-permute-done((bf16[128,640]{1,0:T(8,128)(2,1)S(1)}, bf16[128,640]{1,0:T(8,128)(2,1)S(1)}, u32[]{:S(2)}, u32[]{:S(2)}) %collective-permute-start.15) | collective-permute-done | bytes 163872 | tf_op jit(solution)/shard_map/ppermute | solution.py:347
  54.6 3.8 %query_part.1 = (bf16[8,640,128]{2,1,0:T(8,128)(2,1)S(1)}, bf16[4,640,128]{2,1,0:T(8,128)(2,1)S(1)}, bf16[4,640,128]{2,1,0:T(8,128)(2,1)S(1)}) custom-call(s32[4]{0:T(128)S(1)} %pad_add_fusion.place_ref, f32[64,128]{1,0:T(8,128)S(1)} %get-tuple-element.36.cos_ref, f32[64,128]{1,0:T(8,128)S(1)} %get-tuple-element.37.sin_ref, ...), custom_call_target="tpu_custom_call" | custom-call | flops 838860800 | tf_op jit(solution)/shard_map/query_part/pallas_call | solution.py:363
  59.0 7.5 %collective-permute-start.16 = (bf16[4,128,640]{2,1,0:T(8,128)(2,1)S(1)}, bf16[4,128,640]{2,1,0:T(8,128)(2,1)S(1)}, u32[]{:S(2)}, u32[]{:S(2)}) collective-permute-start(bf16[4,128,640]{2,1,0:T(8,128)(2,1)S(1)} %get-tuple-element.54), channel_id=1, source_target_pairs={{0,1},{1,0},{2,3},{3,2},{4,5},{5,4},{6,7},{7,6},{8,9},{9,8},{10,11... | collective-permute-start | bytes 1966088 | tf_op jit(solution)/shard_map/ppermute | solution.py:379
  66.5 2.8 %second_half.1 = f32[4,128,640]{2,1,0:T(8,128)S(1)} custom-call(s32[4]{0:T(128)S(1)} %pad_add_fusion.place_ref, bf16[256,128]{1,0:T(8,128)(2,1)S(1)} %get-tuple-element.53.low_ref, bf16[8,640,128]{2,1,0:T(8,128)(2,1)S(1)} %get-tuple-element.50.part_ref, bf16[5120,128]{1,0:T(8,128)(2,1)} %wk_hbm.3, bf16[5120,128]{1,0:T(8,128)(2,1)} %wv_hbm.3), custom_call_target="tpu_custom_call" | custom-call | tf_op jit(solution)/shard_map/second_half/pallas_call | solution.py:380
  69.5 1.3 %collective-permute-start.19 = (bf16[128,640]{1,0:T(8,128)(2,1)S(1)}, bf16[128,640]{1,0:T(8,128)(2,1)S(1)}, u32[]{:S(2)}, u32[]{:S(2)}) collective-permute-start(bf16[128,640]{1,0:T(8,128)(2,1)S(1)} %get-tuple-element.55), channel_id=1, source_target_pairs={{0,2},{2,4},{4,6},{6,0},{1,3},{3,5},{5,7},{7,1},{8,10},{10,12},{12... | collective-permute-start | bytes 491528 | tf_op jit(solution)/shard_map/ppermute | solution.py:389
  70.8 2.5 %collective-permute-start.18 = (bf16[128,640]{1,0:T(8,128)(2,1)S(1)}, bf16[128,640]{1,0:T(8,128)(2,1)S(1)}, u32[]{:S(2)}, u32[]{:S(2)}) collective-permute-start(bf16[128,640]{1,0:T(8,128)(2,1)S(1)} %get-tuple-element.56), channel_id=1, source_target_pairs={{0,4},{2,6},{4,0},{6,2},{1,5},{3,7},{5,1},{7,3},{8,12},{10,14},{12... | collective-permute-start | bytes 491528 | tf_op jit(solution)/shard_map/ppermute | solution.py:389
  74.4 2.2 %collective-permute-done.19.p0 = bf16[128,640]{1,0:T(8,128)(2,1)S(1)} collective-permute-done((bf16[128,640]{1,0:T(8,128)(2,1)S(1)}, bf16[128,640]{1,0:T(8,128)(2,1)S(1)}, u32[]{:S(2)}, u32[]{:S(2)}) %collective-permute-start.19) | collective-permute-done | bytes 163872 | tf_op jit(solution)/shard_map/ppermute | solution.py:389
  76.6 4.5 %collective-permute-done.18.p1 = bf16[128,640]{1,0:T(8,128)(2,1)S(1)} collective-permute-done((bf16[128,640]{1,0:T(8,128)(2,1)S(1)}, bf16[128,640]{1,0:T(8,128)(2,1)S(1)}, u32[]{:S(2)}, u32[]{:S(2)}) %collective-permute-start.18) | collective-permute-done | bytes 163872 | tf_op jit(solution)/shard_map/ppermute | solution.py:389
  (36 shorter events, 11.1 us)
Async XLA Ops:
  1.1 11.6 %collective-permute-start = (bf16[128,256]{1,0:T(8,128)(2,1)S(1)}, bf16[128,256]{1,0:T(8,128)(2,1)S(1)}, u32[]{:S(2)}, u32[]{:S(2)}) collective-permute-start(bf16[128,256]{1,0:T(8,128)(2,1)S(1)} %get-tuple-element.31.k0), channel_id=1, source_target_pairs={{0,32},{32,64},{64,96},{96,128},{128,160},{160,192},{192,224},{224... | collective-permute-start | bytes 196616 | tf_op jit(solution)/shard_map/ppermute | solution.py:310
  3.6 22.6 %collective-permute-start.9 = (bf16[128,1280]{1,0:T(8,128)(2,1)S(1)}, bf16[128,1280]{1,0:T(8,128)(2,1)S(1)}, u32[]{:S(2)}, u32[]{:S(2)}) collective-permute-start(bf16[128,1280]{1,0:T(8,128)(2,1)S(1)} %get-tuple-element.30.rows_ref.g0), channel_id=1, source_target_pairs={{0,8},{8,16},{16,24},{24,0},{1,9},{9,17},{17,25},{25,1},{2,10},{10... | collective-permute-start | bytes 983048 | tf_op jit(solution)/shard_map/ppermute | solution.py:307
  4.9 21.3 %collective-permute-start.8 = (bf16[128,1280]{1,0:T(8,128)(2,1)S(1)}, bf16[128,1280]{1,0:T(8,128)(2,1)S(1)}, u32[]{:S(2)}, u32[]{:S(2)}) collective-permute-start(bf16[128,1280]{1,0:T(8,128)(2,1)S(1)} %get-tuple-element.30.rows_ref.g0), channel_id=1, source_target_pairs={{0,16},{8,24},{16,0},{24,8},{1,17},{9,25},{17,1},{25,9},{2,18},{10... | collective-permute-start | bytes 983048 | tf_op jit(solution)/shard_map/ppermute | solution.py:307
  7.5 18.7 %collective-permute-start.7 = (bf16[128,1280]{1,0:T(8,128)(2,1)S(1)}, bf16[128,1280]{1,0:T(8,128)(2,1)S(1)}, u32[]{:S(2)}, u32[]{:S(2)}) collective-permute-start(bf16[128,1280]{1,0:T(8,128)(2,1)S(1)} %get-tuple-element.30.rows_ref.g0), channel_id=1, source_target_pairs={{0,24},{8,0},{16,8},{24,16},{1,25},{9,1},{17,9},{25,17},{2,26},{10... | collective-permute-start | bytes 983048 | tf_op jit(solution)/shard_map/ppermute | solution.py:307
  8.6 5.4 %collective-permute-start.4 = (bf16[128,256]{1,0:T(8,128)(2,1)S(1)}, bf16[128,256]{1,0:T(8,128)(2,1)S(1)}, u32[]{:S(2)}, u32[]{:S(2)}) collective-permute-start(bf16[128,256]{1,0:T(8,128)(2,1)S(1)} %get-tuple-element.31.k0), channel_id=1, source_target_pairs={{0,224},{32,0},{64,32},{96,64},{128,96},{160,128},{192,160},{224,1... | collective-permute-start | bytes 196616 | tf_op jit(solution)/shard_map/ppermute | solution.py:311
  12.6 4.6 %collective-permute-start.1 = (bf16[128,256]{1,0:T(8,128)(2,1)S(1)}, bf16[128,256]{1,0:T(8,128)(2,1)S(1)}, u32[]{:S(2)}, u32[]{:S(2)}) collective-permute-start(bf16[128,256]{1,0:T(8,128)(2,1)S(1)} %collective-permute-done.k1), channel_id=1, source_target_pairs={{0,32},{32,64},{64,96},{96,128},{128,160},{160,192},{192,224},{224... | collective-permute-start | bytes 196616 | tf_op jit(solution)/shard_map/ppermute | solution.py:310
  14.0 4.6 %collective-permute-start.5 = (bf16[128,256]{1,0:T(8,128)(2,1)S(1)}, bf16[128,256]{1,0:T(8,128)(2,1)S(1)}, u32[]{:S(2)}, u32[]{:S(2)}) collective-permute-start(bf16[128,256]{1,0:T(8,128)(2,1)S(1)} %collective-permute-done.4.k7), channel_id=1, source_target_pairs={{0,224},{32,0},{64,32},{96,64},{128,96},{160,128},{192,160},{224,1... | collective-permute-start | bytes 196616 | tf_op jit(solution)/shard_map/ppermute | solution.py:311
  17.3 4.6 %collective-permute-start.2 = (bf16[128,256]{1,0:T(8,128)(2,1)S(1)}, bf16[128,256]{1,0:T(8,128)(2,1)S(1)}, u32[]{:S(2)}, u32[]{:S(2)}) collective-permute-start(bf16[128,256]{1,0:T(8,128)(2,1)S(1)} %collective-permute-done.1.k2), channel_id=1, source_target_pairs={{0,32},{32,64},{64,96},{96,128},{128,160},{160,192},{192,224},{224... | collective-permute-start | bytes 196616 | tf_op jit(solution)/shard_map/ppermute | solution.py:310
  18.6 5.8 %collective-permute-start.6 = (bf16[128,256]{1,0:T(8,128)(2,1)S(1)}, bf16[128,256]{1,0:T(8,128)(2,1)S(1)}, u32[]{:S(2)}, u32[]{:S(2)}) collective-permute-start(bf16[128,256]{1,0:T(8,128)(2,1)S(1)} %collective-permute-done.5.k6), channel_id=1, source_target_pairs={{0,224},{32,0},{64,32},{96,64},{128,96},{160,128},{192,160},{224,1... | collective-permute-start | bytes 196616 | tf_op jit(solution)/shard_map/ppermute | solution.py:311
  21.9 4.3 %collective-permute-start.3 = (bf16[128,256]{1,0:T(8,128)(2,1)S(1)}, bf16[128,256]{1,0:T(8,128)(2,1)S(1)}, u32[]{:S(2)}, u32[]{:S(2)}) collective-permute-start(bf16[128,256]{1,0:T(8,128)(2,1)S(1)} %collective-permute-done.2.k3), channel_id=1, source_target_pairs={{0,32},{32,64},{64,96},{96,128},{128,160},{160,192},{192,224},{224... | collective-permute-start | bytes 196616 | tf_op jit(solution)/shard_map/ppermute | solution.py:312
  21.9 0.7 copy-start
  28.7 4.2 %collective-permute-start.12 = (f32[4,4,640]{2,1,0:T(4,128)S(1)}, f32[4,4,640]{2,1,0:T(4,128)S(1)}, u32[]{:S(2)}, u32[]{:S(2)}) collective-permute-start(f32[4,4,640]{2,1,0:T(4,128)S(1)} %get-tuple-element.32.stat_ref.s0), channel_id=1, source_target_pairs={{0,8},{8,16},{16,24},{24,0},{1,9},{9,17},{17,25},{25,1},{2,10},{10... | collective-permute-start | bytes 122888 | tf_op jit(solution)/shard_map/ppermute | solution.py:334
  28.8 4.5 %collective-permute-start.11 = (f32[4,4,640]{2,1,0:T(4,128)S(1)}, f32[4,4,640]{2,1,0:T(4,128)S(1)}, u32[]{:S(2)}, u32[]{:S(2)}) collective-permute-start(f32[4,4,640]{2,1,0:T(4,128)S(1)} %get-tuple-element.32.stat_ref.s0), channel_id=1, source_target_pairs={{0,16},{8,24},{16,0},{24,8},{1,17},{9,25},{17,1},{25,9},{2,18},{10... | collective-permute-start | bytes 122888 | tf_op jit(solution)/shard_map/ppermute | solution.py:334
  28.9 5.0 %collective-permute-start.10 = (f32[4,4,640]{2,1,0:T(4,128)S(1)}, f32[4,4,640]{2,1,0:T(4,128)S(1)}, u32[]{:S(2)}, u32[]{:S(2)}) collective-permute-start(f32[4,4,640]{2,1,0:T(4,128)S(1)} %get-tuple-element.32.stat_ref.s0), channel_id=1, source_target_pairs={{0,24},{8,0},{16,8},{24,16},{1,25},{9,1},{17,9},{25,17},{2,26},{10... | collective-permute-start | bytes 122888 | tf_op jit(solution)/shard_map/ppermute | solution.py:334
  37.1 10.8 %copy-start.1 = (s32[32,17]{0,1:T(8,128)S(1)}, s32[32,17]{0,1:T(8,128)}, u32[]{:S(2)}) copy-start(s32[32,17]{0,1:T(8,128)} %param.12) | copy-start | bytes 6532
  37.9 20.4 %all-to-all-start = ((bf16[8,128,256]{2,1,0:T(8,128)(2,1)}), bf16[8,128,256]{2,1,0:T(8,128)(2,1)S(1)}, u32[]{:S(2)}, u32[]{:S(2)}) async-start(bf16[8,128,256]{2,1,0:T(8,128)(2,1)} %flush.1), calls=%async_computation | async-start | bytes 1048576 | tf_op jit(solution)/shard_map/all_to_all | solution.py:351
  45.4 6.1 %collective-permute-start.13 = (bf16[128,640]{1,0:T(8,128)(2,1)S(1)}, bf16[128,640]{1,0:T(8,128)(2,1)S(1)}, u32[]{:S(2)}, u32[]{:S(2)}) collective-permute-start(bf16[128,640]{1,0:T(8,128)(2,1)S(1)} %get-tuple-element.39), channel_id=1, source_target_pairs={{0,24},{8,0},{16,8},{24,16},{1,25},{9,1},{17,9},{25,17},{2,26},{10... | collective-permute-start | bytes 491528 | tf_op jit(solution)/shard_map/ppermute | solution.py:347
  47.1 5.8 %collective-permute-start.14 = (bf16[128,640]{1,0:T(8,128)(2,1)S(1)}, bf16[128,640]{1,0:T(8,128)(2,1)S(1)}, u32[]{:S(2)}, u32[]{:S(2)}) collective-permute-start(bf16[128,640]{1,0:T(8,128)(2,1)S(1)} %get-tuple-element.40), channel_id=1, source_target_pairs={{0,16},{8,24},{16,0},{24,8},{1,17},{9,25},{17,1},{25,9},{2,18},{10... | collective-permute-start | bytes 491528 | tf_op jit(solution)/shard_map/ppermute | solution.py:347
  47.9 6.7 %collective-permute-start.15 = (bf16[128,640]{1,0:T(8,128)(2,1)S(1)}, bf16[128,640]{1,0:T(8,128)(2,1)S(1)}, u32[]{:S(2)}, u32[]{:S(2)}) collective-permute-start(bf16[128,640]{1,0:T(8,128)(2,1)S(1)} %get-tuple-element.41), channel_id=1, source_target_pairs={{0,8},{8,16},{16,24},{24,0},{1,9},{9,17},{17,25},{25,1},{2,10},{10... | collective-permute-start | bytes 491528 | tf_op jit(solution)/shard_map/ppermute | solution.py:347
  59.0 10.3 %collective-permute-start.16 = (bf16[4,128,640]{2,1,0:T(8,128)(2,1)S(1)}, bf16[4,128,640]{2,1,0:T(8,128)(2,1)S(1)}, u32[]{:S(2)}, u32[]{:S(2)}) collective-permute-start(bf16[4,128,640]{2,1,0:T(8,128)(2,1)S(1)} %get-tuple-element.54), channel_id=1, source_target_pairs={{0,1},{1,0},{2,3},{3,2},{4,5},{5,4},{6,7},{7,6},{8,9},{9,8},{10,11... | collective-permute-start | bytes 1966088 | tf_op jit(solution)/shard_map/ppermute | solution.py:379
  69.5 7.1 %collective-permute-start.19 = (bf16[128,640]{1,0:T(8,128)(2,1)S(1)}, bf16[128,640]{1,0:T(8,128)(2,1)S(1)}, u32[]{:S(2)}, u32[]{:S(2)}) collective-permute-start(bf16[128,640]{1,0:T(8,128)(2,1)S(1)} %get-tuple-element.55), channel_id=1, source_target_pairs={{0,2},{2,4},{4,6},{6,0},{1,3},{3,5},{5,7},{7,1},{8,10},{10,12},{12... | collective-permute-start | bytes 491528 | tf_op jit(solution)/shard_map/ppermute | solution.py:389
  70.8 10.3 %collective-permute-start.18 = (bf16[128,640]{1,0:T(8,128)(2,1)S(1)}, bf16[128,640]{1,0:T(8,128)(2,1)S(1)}, u32[]{:S(2)}, u32[]{:S(2)}) collective-permute-start(bf16[128,640]{1,0:T(8,128)(2,1)S(1)} %get-tuple-element.56), channel_id=1, source_target_pairs={{0,4},{2,6},{4,0},{6,2},{1,5},{3,7},{5,1},{7,3},{8,12},{10,14},{12... | collective-permute-start | bytes 491528 | tf_op jit(solution)/shard_map/ppermute | solution.py:389
  73.2 7.9 %collective-permute-start.17 = (bf16[128,640]{1,0:T(8,128)(2,1)S(1)}, bf16[128,640]{1,0:T(8,128)(2,1)S(1)}, u32[]{:S(2)}, u32[]{:S(2)}) collective-permute-start(bf16[128,640]{1,0:T(8,128)(2,1)S(1)} %get-tuple-element.57), channel_id=1, source_target_pairs={{0,6},{2,0},{4,2},{6,4},{1,7},{3,1},{5,3},{7,5},{8,14},{10,8},{12,... | collective-permute-start | bytes 491528 | tf_op jit(solution)/shard_map/ppermute | solution.py:389

commit v13 on v12

--- a/solution.py
+++ b/solution.py
@@ -238,7 +238,7 @@
     return copies
 
 
-def query_part_kernel(place_ref, cos_ref, sin_ref, q0, q1, q2, q3, wk_hbm, wv_hbm, *refs):
+def query_part_kernel(place_ref, cos_ref, sin_ref, q0, q3, q2, q1, wk_hbm, wv_hbm, *refs):
     blocks, out_ref, wk, wv, sem = refs[:2 * NX], *refs[2 * NX:]
     copies = start_pair(place_ref, 0, wk_hbm, wv_hbm, wk, wv, sem)
     cosine = cos_ref[...]
@@ -280,7 +280,7 @@
     return dot_nn(wk, low_ref[:HEAD, :]) + dot_nn(wv, low_ref[HEAD:, :])
 
 
-def finish_kernel(kept_ref, p2, p1, p0, arrived_ref, out_ref):
+def finish_kernel(kept_ref, p2, p0, p1, arrived_ref, out_ref):
     for h in range(GROUP):
         cols = slice(h * HEAD, (h + 1) * HEAD)
         total = kept_ref[:, cols]
@@ -368,7 +368,7 @@
         "query_part",
         [pltpu.SemaphoreType.DMA((2 * NX,))],
         QUERY_FLOPS,
-    )(place, cosine, sine, *dq_own, wk, wv, *blocks)
+    )(place, cosine, sine, dq_own[0], *dq_own[:0:-1], wk, wv, *blocks)
     away, low = call(
         first_half_kernel,
         [pltpu.VMEM((NX, BLOCK, ROWS), BF16), pltpu.VMEM((2 * HEAD, BLOCK), BF16)],
@@ -389,7 +389,7 @@
     parts = [lax.ppermute(sent[k - 1], "x", shift(NX, k)) for k in range(1, NX)]
     return call(
         finish_kernel, jax.ShapeDtypeStruct((BLOCK, ROWS), BF16), [VM] * (2 + len(parts)), VM, "finish",
-    )(kept[0], *parts[::-1], arrived[0])
+    )(kept[0], parts[2], parts[0], parts[1], arrived[0])
 
 
 def solution(mesh):

time: 82.2 us -> 83.6 us (1.017)
  starting transfers between devices: 43.2 us -> 46.7 us
  waiting for transfers between devices: 15.6 us -> 13.4 us
    ppermute x3, waiting for transfers between devices: 3.01 us -> 0.96 us  [shards(): lax.ppermute(dq_parts[k], 'y', shift(NY, -k))]
    all_to_all x1, starting transfers between devices: 7.53 us -> 9.47 us  [shards(): dkv_own = lax.all_to_all(dkv, 'z', 0, 0, tiled=True)]
    ppermute x3, waiting for transfers between devices: 6.7 us -> 5.73 us  [shards(): parts = [lax.ppermute(sent[k - 1], 'x', shift(NX, k)) for k in range(1, NX)]]
  transfers between devices with their start and end apart: 21 -> 21, of which waited for: 10 -> 11; matrix products, arithmetic and copies ran while one was open for 0% -> 0% of each run, Pallas kernels for 16% -> 16%
where the time goes in v13:
time: 83.6 us; the launch traced here: 83.1 us
  starting transfers between devices  46.7 us (56%)
  Pallas kernels  22 us (26%)
  waiting for transfers between devices  13.4 us (16%)
    ppermute x3, starting transfers between devices, shards(): above.append(lax.ppermute(above[-1], 'z', shift(NZ, -1)))  10.6 us
    all_to_all x1, starting transfers between devices, shards(): dkv_own = lax.all_to_all(dkv, 'z', 0, 0, tiled=True)  9.47 us
    ppermute x1, starting transfers between devices, shards(): arrived = lax.ppermute(away, 'c', shift(NC, 1))  7.78 us
    ppermute x3, waiting for transfers between devices, shards(): parts = [lax.ppermute(sent[k - 1], 'x', shift(NX, k)) for k in range(1, NX)]  5.73 us
    ppermute x3, starting transfers between devices, shards(): parts = [lax.ppermute(sent[k - 1], 'x', shift(NX, k)) for k in range(1, NX)]  5.5 us
    ppermute x3, starting transfers between devices, shards(): lax.ppermute(group, 'y', shift(NY, k))  4.99 us
    pallas_call x1, Pallas kernels, shards(): call(query_part_kernel, [pltpu.VMEM((2 * NX, ROWS, BLOCK), BF16)] + pair_...  3.78 us
    pallas_call x1, Pallas kernels, shards(): call(fetch_kernel, [pltpu.VMEM((HEAD // 2, BLOCK), F32)] * 2 + [pltpu.VME...  3.68 us
  transfers between devices with their start and end apart: 21, of which 11 were waited for; matrix products, arithmetic and copies ran while one was open for 0% of the time, Pallas kernels for 16%

profile of v13, /device:TPU:1, one launch (start us, length us, event | category | flops | bytes accessed | tf_op | source)
XLA Modules:
  0.0 83.1 jit_solution(3329199902055403269)
XLA Ops:
  1.1 2.5 %collective-permute-start = (bf16[128,256]{1,0:T(8,128)(2,1)S(1)}, bf16[128,256]{1,0:T(8,128)(2,1)S(1)}, u32[]{:S(2)}, u32[]{:S(2)}) collective-permute-start(bf16[128,256]{1,0:T(8,128)(2,1)S(1)} %get-tuple-element.31.k0), channel_id=1, source_target_pairs={{0,32},{32,64},{64,96},{96,128},{128,160},{160,192},{192,224},{224... | collective-permute-start | bytes 196616 | tf_op jit(solution)/shard_map/ppermute | solution.py:310
  3.6 1.3 %collective-permute-start.9 = (bf16[128,1280]{1,0:T(8,128)(2,1)S(1)}, bf16[128,1280]{1,0:T(8,128)(2,1)S(1)}, u32[]{:S(2)}, u32[]{:S(2)}) collective-permute-start(bf16[128,1280]{1,0:T(8,128)(2,1)S(1)} %get-tuple-element.30.rows_ref.g0), channel_id=1, source_target_pairs={{0,8},{8,16},{16,24},{24,0},{1,9},{9,17},{17,25},{25,1},{2,10},{10... | collective-permute-start | bytes 983048 | tf_op jit(solution)/shard_map/ppermute | solution.py:307
  4.9 2.6 %collective-permute-start.8 = (bf16[128,1280]{1,0:T(8,128)(2,1)S(1)}, bf16[128,1280]{1,0:T(8,128)(2,1)S(1)}, u32[]{:S(2)}, u32[]{:S(2)}) collective-permute-start(bf16[128,1280]{1,0:T(8,128)(2,1)S(1)} %get-tuple-element.30.rows_ref.g0), channel_id=1, source_target_pairs={{0,16},{8,24},{16,0},{24,8},{1,17},{9,25},{17,1},{25,9},{2,18},{10... | collective-permute-start | bytes 983048 | tf_op jit(solution)/shard_map/ppermute | solution.py:307
  8.6 4.0 %collective-permute-start.4 = (bf16[128,256]{1,0:T(8,128)(2,1)S(1)}, bf16[128,256]{1,0:T(8,128)(2,1)S(1)}, u32[]{:S(2)}, u32[]{:S(2)}) collective-permute-start(bf16[128,256]{1,0:T(8,128)(2,1)S(1)} %get-tuple-element.31.k0), channel_id=1, source_target_pairs={{0,224},{32,0},{64,32},{96,64},{128,96},{160,128},{192,160},{224,1... | collective-permute-start | bytes 196616 | tf_op jit(solution)/shard_map/ppermute | solution.py:311
  12.6 1.3 %collective-permute-done.4.k7 = bf16[128,256]{1,0:T(8,128)(2,1)S(1)} collective-permute-done((bf16[128,256]{1,0:T(8,128)(2,1)S(1)}, bf16[128,256]{1,0:T(8,128)(2,1)S(1)}, u32[]{:S(2)}, u32[]{:S(2)}) %collective-permute-start.4) | collective-permute-done | bytes 65568 | tf_op jit(solution)/shard_map/ppermute | solution.py:311
  14.0 3.3 %collective-permute-start.5 = (bf16[128,256]{1,0:T(8,128)(2,1)S(1)}, bf16[128,256]{1,0:T(8,128)(2,1)S(1)}, u32[]{:S(2)}, u32[]{:S(2)}) collective-permute-start(bf16[128,256]{1,0:T(8,128)(2,1)S(1)} %collective-permute-done.4.k7), channel_id=1, source_target_pairs={{0,224},{32,0},{64,32},{96,64},{128,96},{160,128},{192,160},{224,1... | collective-permute-start | bytes 196616 | tf_op jit(solution)/shard_map/ppermute | solution.py:311
  17.3 1.2 %collective-permute-done.5.k6 = bf16[128,256]{1,0:T(8,128)(2,1)S(1)} collective-permute-done((bf16[128,256]{1,0:T(8,128)(2,1)S(1)}, bf16[128,256]{1,0:T(8,128)(2,1)S(1)}, u32[]{:S(2)}, u32[]{:S(2)}) %collective-permute-start.5) | collective-permute-done | bytes 65568 | tf_op jit(solution)/shard_map/ppermute | solution.py:311
  18.6 3.3 %collective-permute-start.6 = (bf16[128,256]{1,0:T(8,128)(2,1)S(1)}, bf16[128,256]{1,0:T(8,128)(2,1)S(1)}, u32[]{:S(2)}, u32[]{:S(2)}) collective-permute-start(bf16[128,256]{1,0:T(8,128)(2,1)S(1)} %collective-permute-done.5.k6), channel_id=1, source_target_pairs={{0,224},{32,0},{64,32},{96,64},{128,96},{160,128},{192,160},{224,1... | collective-permute-start | bytes 196616 | tf_op jit(solution)/shard_map/ppermute | solution.py:311
  22.6 1.8 %plan.1.item_ref = s32[20,4]{1,0:T(8,128)S(1)} custom-call(s32[4]{0:T(128)S(1)} %pad_add_fusion.place_ref, s32[17,32]{1,0:T(8,128)S(1)} %bitcast.15, bf16[128,1280]{1,0:T(8,128)(2,1)S(1)} %get-tuple-element.30.rows_ref.g0), custom_call_target="tpu_custom_call" | custom-call | flops 1000000000 | tf_op jit(solution)/shard_map/plan/pallas_call | solution.py:314
  24.4 1.8 %collective-permute-done.3.k4 = bf16[128,256]{1,0:T(8,128)(2,1)S(1)} collective-permute-done((bf16[128,256]{1,0:T(8,128)(2,1)S(1)}, bf16[128,256]{1,0:T(8,128)(2,1)S(1)}, u32[]{:S(2)}, u32[]{:S(2)}) %collective-permute-start.3) | collective-permute-done | bytes 65568 | tf_op jit(solution)/shard_map/ppermute | solution.py:312
  26.2 2.5 %stats.1 = (f32[4,4,640]{2,1,0:T(4,128)S(1)}, f32[16,256,640]{2,1,0:T(8,128)S(1)}, f32[16,256,640]{2,1,0:T(8,128)S(1)}) custom-call(s32[20,4]{1,0:T(8,128)S(1)} %plan.1.item_ref, bf16[128,256]{1,0:T(8,128)(2,1)S(1)} %get-tuple-element.31.k0, bf16[128,256]{1,0:T(8,128)(2,1)S(1)} %collective-permute-done.k1, bf16[128,256]{1,0:T(8,128)(2,1)S(1)} %collective-permute-done.1.k2, ...), custom_call_target="tpu_custom_call" | custom-call | flops 1342177280 | tf_op jit(solution)/shard_map/stats/pallas_call | solution.py:325
  28.9 2.6 %collective-permute-start.10 = (f32[4,4,640]{2,1,0:T(4,128)S(1)}, f32[4,4,640]{2,1,0:T(4,128)S(1)}, u32[]{:S(2)}, u32[]{:S(2)}) collective-permute-start(f32[4,4,640]{2,1,0:T(4,128)S(1)} %get-tuple-element.32.stat_ref.s0), channel_id=1, source_target_pairs={{0,24},{8,0},{16,8},{24,16},{1,25},{9,1},{17,9},{25,17},{2,26},{10... | collective-permute-start | bytes 122888 | tf_op jit(solution)/shard_map/ppermute | solution.py:334
  33.9 3.2 %grads.1 = (bf16[8,128,256]{2,1,0:T(8,128)(2,1)S(1)}, bf16[128,640]{1,0:T(8,128)(2,1)S(1)}, bf16[128,640]{1,0:T(8,128)(2,1)S(1)}, bf16[128,640]{1,0:T(8,128)(2,1)S(1)}, bf16[128,640]{1,0:T(8,128)(2,1)S(1)}) custom-call(s32[20,4]{1,0:T(8,128)S(1)} %plan.1.item_ref, bf16[8,128,128]{2,1,0:T(8,128)(2,1)S(1)} %turn.1.cols_ref, ...), custom_call_target="tpu_custom_call" | custom-call | flops 2013265920 | tf_op jit(solution)/shard_map/grads/pallas_call | solution.py:338
  37.9 9.5 %all-to-all-start = ((bf16[8,128,256]{2,1,0:T(8,128)(2,1)}), bf16[8,128,256]{2,1,0:T(8,128)(2,1)S(1)}, u32[]{:S(2)}, u32[]{:S(2)}) async-start(bf16[8,128,256]{2,1,0:T(8,128)(2,1)} %flush.1), calls=%async_computation | async-start | bytes 1048576 | tf_op jit(solution)/shard_map/all_to_all | solution.py:351
  48.0 1.4 %collective-permute-start.14 = (bf16[128,640]{1,0:T(8,128)(2,1)S(1)}, bf16[128,640]{1,0:T(8,128)(2,1)S(1)}, u32[]{:S(2)}, u32[]{:S(2)}) collective-permute-start(bf16[128,640]{1,0:T(8,128)(2,1)S(1)} %get-tuple-element.40), channel_id=1, source_target_pairs={{0,16},{8,24},{16,0},{24,8},{1,17},{9,25},{17,1},{25,9},{2,18},{10... | collective-permute-start | bytes 491528 | tf_op jit(solution)/shard_map/ppermute | solution.py:347
  49.3 1.1 %collective-permute-start.15 = (bf16[128,640]{1,0:T(8,128)(2,1)S(1)}, bf16[128,640]{1,0:T(8,128)(2,1)S(1)}, u32[]{:S(2)}, u32[]{:S(2)}) collective-permute-start(bf16[128,640]{1,0:T(8,128)(2,1)S(1)} %get-tuple-element.41), channel_id=1, source_target_pairs={{0,24},{8,0},{16,8},{24,16},{1,25},{9,1},{17,9},{25,17},{2,26},{10... | collective-permute-start | bytes 491528 | tf_op jit(solution)/shard_map/ppermute | solution.py:347
  50.5 3.7 %fetch.1 = (f32[64,128]{1,0:T(8,128)S(1)}, f32[64,128]{1,0:T(8,128)S(1)}, bf16[640,640]{1,0:T(8,128)(2,1)S(1)}, bf16[640,640]{1,0:T(8,128)(2,1)S(1)}, bf16[640,6...) custom-call(s32[4]{0:T(128)S(1)} %pad_add_fusion.place_ref, ...), custom_call_target="tpu_custom_call" | custom-call | tf_op jit(solution)/shard_map/fetch/pallas_call | solution.py:354
  55.1 3.8 %query_part.1 = (bf16[8,640,128]{2,1,0:T(8,128)(2,1)S(1)}, bf16[4,640,128]{2,1,0:T(8,128)(2,1)S(1)}, bf16[4,640,128]{2,1,0:T(8,128)(2,1)S(1)}) custom-call(s32[4]{0:T(128)S(1)} %pad_add_fusion.place_ref, f32[64,128]{1,0:T(8,128)S(1)} %get-tuple-element.36.cos_ref, f32[64,128]{1,0:T(8,128)S(1)} %get-tuple-element.37.sin_ref, ...), custom_call_target="tpu_custom_call" | custom-call | flops 838860800 | tf_op jit(solution)/shard_map/query_part/pallas_call | solution.py:363
  60.3 7.8 %collective-permute-start.16 = (bf16[4,128,640]{2,1,0:T(8,128)(2,1)S(1)}, bf16[4,128,640]{2,1,0:T(8,128)(2,1)S(1)}, u32[]{:S(2)}, u32[]{:S(2)}) collective-permute-start(bf16[4,128,640]{2,1,0:T(8,128)(2,1)S(1)} %get-tuple-element.54), channel_id=1, source_target_pairs={{0,1},{1,0},{2,3},{3,2},{4,5},{5,4},{6,7},{7,6},{8,9},{9,8},{10,11... | collective-permute-start | bytes 1966088 | tf_op jit(solution)/shard_map/ppermute | solution.py:379
  68.0 2.8 %second_half.1 = f32[4,128,640]{2,1,0:T(8,128)S(1)} custom-call(s32[4]{0:T(128)S(1)} %pad_add_fusion.place_ref, bf16[256,128]{1,0:T(8,128)(2,1)S(1)} %get-tuple-element.53.low_ref, bf16[8,640,128]{2,1,0:T(8,128)(2,1)S(1)} %get-tuple-element.50.part_ref, bf16[5120,128]{1,0:T(8,128)(2,1)} %wk_hbm.3, bf16[5120,128]{1,0:T(8,128)(2,1)} %wv_hbm.3), custom_call_target="tpu_custom_call" | custom-call | tf_op jit(solution)/shard_map/second_half/pallas_call | solution.py:380
  71.0 2.8 %collective-permute-start.19 = (bf16[128,640]{1,0:T(8,128)(2,1)S(1)}, bf16[128,640]{1,0:T(8,128)(2,1)S(1)}, u32[]{:S(2)}, u32[]{:S(2)}) collective-permute-start(bf16[128,640]{1,0:T(8,128)(2,1)S(1)} %get-tuple-element.55), channel_id=1, source_target_pairs={{0,4},{2,6},{4,0},{6,2},{1,5},{3,7},{5,1},{7,3},{8,12},{10,14},{12... | collective-permute-start | bytes 491528 | tf_op jit(solution)/shard_map/ppermute | solution.py:389
  74.2 2.4 %collective-permute-start.17 = (bf16[128,640]{1,0:T(8,128)(2,1)S(1)}, bf16[128,640]{1,0:T(8,128)(2,1)S(1)}, u32[]{:S(2)}, u32[]{:S(2)}) collective-permute-start(bf16[128,640]{1,0:T(8,128)(2,1)S(1)} %get-tuple-element.57), channel_id=1, source_target_pairs={{0,6},{2,0},{4,2},{6,4},{1,7},{3,1},{5,3},{7,5},{8,14},{10,8},{12,... | collective-permute-start | bytes 491528 | tf_op jit(solution)/shard_map/ppermute | solution.py:389
  76.5 1.9 %collective-permute-done.19.p1 = bf16[128,640]{1,0:T(8,128)(2,1)S(1)} collective-permute-done((bf16[128,640]{1,0:T(8,128)(2,1)S(1)}, bf16[128,640]{1,0:T(8,128)(2,1)S(1)}, u32[]{:S(2)}, u32[]{:S(2)}) %collective-permute-start.19) | collective-permute-done | bytes 163872 | tf_op jit(solution)/shard_map/ppermute | solution.py:389
  78.4 3.8 %collective-permute-done.18.p0 = bf16[128,640]{1,0:T(8,128)(2,1)S(1)} collective-permute-done((bf16[128,640]{1,0:T(8,128)(2,1)S(1)}, bf16[128,640]{1,0:T(8,128)(2,1)S(1)}, u32[]{:S(2)}, u32[]{:S(2)}) %collective-permute-start.18) | collective-permute-done | bytes 163872 | tf_op jit(solution)/shard_map/ppermute | solution.py:389
  (36 shorter events, 10.6 us)
Async XLA Ops:
  1.1 11.6 %collective-permute-start = (bf16[128,256]{1,0:T(8,128)(2,1)S(1)}, bf16[128,256]{1,0:T(8,128)(2,1)S(1)}, u32[]{:S(2)}, u32[]{:S(2)}) collective-permute-start(bf16[128,256]{1,0:T(8,128)(2,1)S(1)} %get-tuple-element.31.k0), channel_id=1, source_target_pairs={{0,32},{32,64},{64,96},{96,128},{128,160},{160,192},{192,224},{224... | collective-permute-start | bytes 196616 | tf_op jit(solution)/shard_map/ppermute | solution.py:310
  3.6 22.6 %collective-permute-start.9 = (bf16[128,1280]{1,0:T(8,128)(2,1)S(1)}, bf16[128,1280]{1,0:T(8,128)(2,1)S(1)}, u32[]{:S(2)}, u32[]{:S(2)}) collective-permute-start(bf16[128,1280]{1,0:T(8,128)(2,1)S(1)} %get-tuple-element.30.rows_ref.g0), channel_id=1, source_target_pairs={{0,8},{8,16},{16,24},{24,0},{1,9},{9,17},{17,25},{25,1},{2,10},{10... | collective-permute-start | bytes 983048 | tf_op jit(solution)/shard_map/ppermute | solution.py:307
  4.9 21.3 %collective-permute-start.8 = (bf16[128,1280]{1,0:T(8,128)(2,1)S(1)}, bf16[128,1280]{1,0:T(8,128)(2,1)S(1)}, u32[]{:S(2)}, u32[]{:S(2)}) collective-permute-start(bf16[128,1280]{1,0:T(8,128)(2,1)S(1)} %get-tuple-element.30.rows_ref.g0), channel_id=1, source_target_pairs={{0,16},{8,24},{16,0},{24,8},{1,17},{9,25},{17,1},{25,9},{2,18},{10... | collective-permute-start | bytes 983048 | tf_op jit(solution)/shard_map/ppermute | solution.py:307
  7.5 18.7 %collective-permute-start.7 = (bf16[128,1280]{1,0:T(8,128)(2,1)S(1)}, bf16[128,1280]{1,0:T(8,128)(2,1)S(1)}, u32[]{:S(2)}, u32[]{:S(2)}) collective-permute-start(bf16[128,1280]{1,0:T(8,128)(2,1)S(1)} %get-tuple-element.30.rows_ref.g0), channel_id=1, source_target_pairs={{0,24},{8,0},{16,8},{24,16},{1,25},{9,1},{17,9},{25,17},{2,26},{10... | collective-permute-start | bytes 983048 | tf_op jit(solution)/shard_map/ppermute | solution.py:307
  8.6 5.4 %collective-permute-start.4 = (bf16[128,256]{1,0:T(8,128)(2,1)S(1)}, bf16[128,256]{1,0:T(8,128)(2,1)S(1)}, u32[]{:S(2)}, u32[]{:S(2)}) collective-permute-start(bf16[128,256]{1,0:T(8,128)(2,1)S(1)} %get-tuple-element.31.k0), channel_id=1, source_target_pairs={{0,224},{32,0},{64,32},{96,64},{128,96},{160,128},{192,160},{224,1... | collective-permute-start | bytes 196616 | tf_op jit(solution)/shard_map/ppermute | solution.py:311
  12.6 4.6 %collective-permute-start.1 = (bf16[128,256]{1,0:T(8,128)(2,1)S(1)}, bf16[128,256]{1,0:T(8,128)(2,1)S(1)}, u32[]{:S(2)}, u32[]{:S(2)}) collective-permute-start(bf16[128,256]{1,0:T(8,128)(2,1)S(1)} %collective-permute-done.k1), channel_id=1, source_target_pairs={{0,32},{32,64},{64,96},{96,128},{128,160},{160,192},{192,224},{224... | collective-permute-start | bytes 196616 | tf_op jit(solution)/shard_map/ppermute | solution.py:310
  14.0 4.6 %collective-permute-start.5 = (bf16[128,256]{1,0:T(8,128)(2,1)S(1)}, bf16[128,256]{1,0:T(8,128)(2,1)S(1)}, u32[]{:S(2)}, u32[]{:S(2)}) collective-permute-start(bf16[128,256]{1,0:T(8,128)(2,1)S(1)} %collective-permute-done.4.k7), channel_id=1, source_target_pairs={{0,224},{32,0},{64,32},{96,64},{128,96},{160,128},{192,160},{224,1... | collective-permute-start | bytes 196616 | tf_op jit(solution)/shard_map/ppermute | solution.py:311
  17.3 4.6 %collective-permute-start.2 = (bf16[128,256]{1,0:T(8,128)(2,1)S(1)}, bf16[128,256]{1,0:T(8,128)(2,1)S(1)}, u32[]{:S(2)}, u32[]{:S(2)}) collective-permute-start(bf16[128,256]{1,0:T(8,128)(2,1)S(1)} %collective-permute-done.1.k2), channel_id=1, source_target_pairs={{0,32},{32,64},{64,96},{96,128},{128,160},{160,192},{192,224},{224... | collective-permute-start | bytes 196616 | tf_op jit(solution)/shard_map/ppermute | solution.py:310
  18.6 5.8 %collective-permute-start.6 = (bf16[128,256]{1,0:T(8,128)(2,1)S(1)}, bf16[128,256]{1,0:T(8,128)(2,1)S(1)}, u32[]{:S(2)}, u32[]{:S(2)}) collective-permute-start(bf16[128,256]{1,0:T(8,128)(2,1)S(1)} %collective-permute-done.5.k6), channel_id=1, source_target_pairs={{0,224},{32,0},{64,32},{96,64},{128,96},{160,128},{192,160},{224,1... | collective-permute-start | bytes 196616 | tf_op jit(solution)/shard_map/ppermute | solution.py:311
  21.9 4.3 %collective-permute-start.3 = (bf16[128,256]{1,0:T(8,128)(2,1)S(1)}, bf16[128,256]{1,0:T(8,128)(2,1)S(1)}, u32[]{:S(2)}, u32[]{:S(2)}) collective-permute-start(bf16[128,256]{1,0:T(8,128)(2,1)S(1)} %collective-permute-done.2.k3), channel_id=1, source_target_pairs={{0,32},{32,64},{64,96},{96,128},{128,160},{160,192},{192,224},{224... | collective-permute-start | bytes 196616 | tf_op jit(solution)/shard_map/ppermute | solution.py:312
  21.9 0.7 copy-start
  28.7 4.2 %collective-permute-start.12 = (f32[4,4,640]{2,1,0:T(4,128)S(1)}, f32[4,4,640]{2,1,0:T(4,128)S(1)}, u32[]{:S(2)}, u32[]{:S(2)}) collective-permute-start(f32[4,4,640]{2,1,0:T(4,128)S(1)} %get-tuple-element.32.stat_ref.s0), channel_id=1, source_target_pairs={{0,8},{8,16},{16,24},{24,0},{1,9},{9,17},{17,25},{25,1},{2,10},{10... | collective-permute-start | bytes 122888 | tf_op jit(solution)/shard_map/ppermute | solution.py:334
  28.8 4.5 %collective-permute-start.11 = (f32[4,4,640]{2,1,0:T(4,128)S(1)}, f32[4,4,640]{2,1,0:T(4,128)S(1)}, u32[]{:S(2)}, u32[]{:S(2)}) collective-permute-start(f32[4,4,640]{2,1,0:T(4,128)S(1)} %get-tuple-element.32.stat_ref.s0), channel_id=1, source_target_pairs={{0,16},{8,24},{16,0},{24,8},{1,17},{9,25},{17,1},{25,9},{2,18},{10... | collective-permute-start | bytes 122888 | tf_op jit(solution)/shard_map/ppermute | solution.py:334
  28.9 5.0 %collective-permute-start.10 = (f32[4,4,640]{2,1,0:T(4,128)S(1)}, f32[4,4,640]{2,1,0:T(4,128)S(1)}, u32[]{:S(2)}, u32[]{:S(2)}) collective-permute-start(f32[4,4,640]{2,1,0:T(4,128)S(1)} %get-tuple-element.32.stat_ref.s0), channel_id=1, source_target_pairs={{0,24},{8,0},{16,8},{24,16},{1,25},{9,1},{17,9},{25,17},{2,26},{10... | collective-permute-start | bytes 122888 | tf_op jit(solution)/shard_map/ppermute | solution.py:334
  37.1 13.4 %copy-start.1 = (s32[32,17]{0,1:T(8,128)S(1)}, s32[32,17]{0,1:T(8,128)}, u32[]{:S(2)}) copy-start(s32[32,17]{0,1:T(8,128)} %param.12) | copy-start | bytes 6532
  37.9 21.7 %all-to-all-start = ((bf16[8,128,256]{2,1,0:T(8,128)(2,1)}), bf16[8,128,256]{2,1,0:T(8,128)(2,1)S(1)}, u32[]{:S(2)}, u32[]{:S(2)}) async-start(bf16[8,128,256]{2,1,0:T(8,128)(2,1)} %flush.1), calls=%async_computation | async-start | bytes 1048576 | tf_op jit(solution)/shard_map/all_to_all | solution.py:351
  47.4 7.1 %collective-permute-start.13 = (bf16[128,640]{1,0:T(8,128)(2,1)S(1)}, bf16[128,640]{1,0:T(8,128)(2,1)S(1)}, u32[]{:S(2)}, u32[]{:S(2)}) collective-permute-start(bf16[128,640]{1,0:T(8,128)(2,1)S(1)} %get-tuple-element.39), channel_id=1, source_target_pairs={{0,8},{8,16},{16,24},{24,0},{1,9},{9,17},{17,25},{25,1},{2,10},{10... | collective-permute-start | bytes 491528 | tf_op jit(solution)/shard_map/ppermute | solution.py:347
  48.0 6.6 %collective-permute-start.14 = (bf16[128,640]{1,0:T(8,128)(2,1)S(1)}, bf16[128,640]{1,0:T(8,128)(2,1)S(1)}, u32[]{:S(2)}, u32[]{:S(2)}) collective-permute-start(bf16[128,640]{1,0:T(8,128)(2,1)S(1)} %get-tuple-element.40), channel_id=1, source_target_pairs={{0,16},{8,24},{16,0},{24,8},{1,17},{9,25},{17,1},{25,9},{2,18},{10... | collective-permute-start | bytes 491528 | tf_op jit(solution)/shard_map/ppermute | solution.py:347
  49.3 5.8 %collective-permute-start.15 = (bf16[128,640]{1,0:T(8,128)(2,1)S(1)}, bf16[128,640]{1,0:T(8,128)(2,1)S(1)}, u32[]{:S(2)}, u32[]{:S(2)}) collective-permute-start(bf16[128,640]{1,0:T(8,128)(2,1)S(1)} %get-tuple-element.41), channel_id=1, source_target_pairs={{0,24},{8,0},{16,8},{24,16},{1,25},{9,1},{17,9},{25,17},{2,26},{10... | collective-permute-start | bytes 491528 | tf_op jit(solution)/shard_map/ppermute | solution.py:347
  60.3 10.6 %collective-permute-start.16 = (bf16[4,128,640]{2,1,0:T(8,128)(2,1)S(1)}, bf16[4,128,640]{2,1,0:T(8,128)(2,1)S(1)}, u32[]{:S(2)}, u32[]{:S(2)}) collective-permute-start(bf16[4,128,640]{2,1,0:T(8,128)(2,1)S(1)} %get-tuple-element.54), channel_id=1, source_target_pairs={{0,1},{1,0},{2,3},{3,2},{4,5},{5,4},{6,7},{7,6},{8,9},{9,8},{10,11... | collective-permute-start | bytes 1966088 | tf_op jit(solution)/shard_map/ppermute | solution.py:379
  71.0 7.4 %collective-permute-start.19 = (bf16[128,640]{1,0:T(8,128)(2,1)S(1)}, bf16[128,640]{1,0:T(8,128)(2,1)S(1)}, u32[]{:S(2)}, u32[]{:S(2)}) collective-permute-start(bf16[128,640]{1,0:T(8,128)(2,1)S(1)} %get-tuple-element.55), channel_id=1, source_target_pairs={{0,4},{2,6},{4,0},{6,2},{1,5},{3,7},{5,1},{7,3},{8,12},{10,14},{12... | collective-permute-start | bytes 491528 | tf_op jit(solution)/shard_map/ppermute | solution.py:389
  73.8 8.4 %collective-permute-start.18 = (bf16[128,640]{1,0:T(8,128)(2,1)S(1)}, bf16[128,640]{1,0:T(8,128)(2,1)S(1)}, u32[]{:S(2)}, u32[]{:S(2)}) collective-permute-start(bf16[128,640]{1,0:T(8,128)(2,1)S(1)} %get-tuple-element.56), channel_id=1, source_target_pairs={{0,2},{2,4},{4,6},{6,0},{1,3},{3,5},{5,7},{7,1},{8,10},{10,12},{12... | collective-permute-start | bytes 491528 | tf_op jit(solution)/shard_map/ppermute | solution.py:389
  74.2 8.1 %collective-permute-start.17 = (bf16[128,640]{1,0:T(8,128)(2,1)S(1)}, bf16[128,640]{1,0:T(8,128)(2,1)S(1)}, u32[]{:S(2)}, u32[]{:S(2)}) collective-permute-start(bf16[128,640]{1,0:T(8,128)(2,1)S(1)} %get-tuple-element.57), channel_id=1, source_target_pairs={{0,6},{2,0},{4,2},{6,4},{1,7},{3,1},{5,3},{7,5},{8,14},{10,8},{12,... | collective-permute-start | bytes 491528 | tf_op jit(solution)/shard_map/ppermute | solution.py:389

commit v14 on v13

--- a/solution.py
+++ b/solution.py
@@ -105,7 +105,7 @@
         item_ref[NY * PAIRS + j, 1] = z
 
 
-def stats_kernel(item_ref, k0, k1, k2, k3, k4, k5, k6, k7, g0, g3, g2, g1, stat_ref, score_ref, pgrad_ref, kv_ref):
+def stats_kernel(item_ref, k0, k1, k2, k3, k4, k5, k6, k7, g0, g1, g2, g3, stat_ref, score_ref, pgrad_ref, kv_ref):
     z = item_ref[NY * PAIRS, 1]
     for r, part in enumerate((k0, k1, k2, k3, k4, k5, k6, k7)):
         kv_ref[(z - r) & (NZ - 1)] = part[...]
@@ -330,7 +330,7 @@
         "stats",
         [pltpu.VMEM((NZ, BLOCK, 2 * HEAD), BF16)],
         STATS_FLOPS,
-    )(items, *kvs, group, *groups[:0:-1])
+    )(items, *kvs, *groups)
     all_stats = [stats] + [lax.ppermute(stats, "y", shift(NY, k)) for k in range(1, NY)]
     key_cols = call(
         turn_kernel, pltpu.VMEM((NZ, HEAD, BLOCK), BF16), [SM] + [VM] * (NZ + 1), VM, "turn",

time: 83.6 us -> 84 us (level); the launches traced: 83.1 us -> 84.4 us
  waiting for transfers between devices: 13.4 us -> 15.5 us
  starting transfers between devices: 46.7 us -> 45.8 us
    all_to_all x1, starting transfers between devices: 9.47 us -> 13.3 us  [shards(): dkv_own = lax.all_to_all(dkv, 'z', 0, 0, tiled=True)]
    ppermute x1, starting transfers between devices: 7.78 us -> 4.17 us  [shards(): arrived = lax.ppermute(away, 'c', shift(NC, 1))]
    all_to_all x1, waiting for transfers between devices: 0.73 us -> 2.53 us  [shards(): dkv_own = lax.all_to_all(dkv, 'z', 0, 0, tiled=True)]
    ppermute x3, starting transfers between devices: 4.99 us -> 3.77 us  [shards(): lax.ppermute(group, 'y', shift(NY, k))]
  transfers between devices with their start and end apart: 21 -> 21, of which waited for: 11 -> 11; matrix products, arithmetic and copies ran while one was open for 0% -> 0% of each run, Pallas kernels for 16% -> 15%
where the time goes in v14:
time: 84 us; the launch traced here: 84.4 us
  starting transfers between devices  45.8 us (55%)
  Pallas kernels  22 us (26%)
  waiting for transfers between devices  15.5 us (18%)
    all_to_all x1, starting transfers between devices, shards(): dkv_own = lax.all_to_all(dkv, 'z', 0, 0, tiled=True)  13.3 us
    ppermute x3, starting transfers between devices, shards(): above.append(lax.ppermute(above[-1], 'z', shift(NZ, -1)))  10.3 us
    ppermute x3, waiting for transfers between devices, shards(): parts = [lax.ppermute(sent[k - 1], 'x', shift(NX, k)) for k in range(1, NX)]  5.72 us
    ppermute x3, starting transfers between devices, shards(): parts = [lax.ppermute(sent[k - 1], 'x', shift(NX, k)) for k in range(1, NX)]  5.51 us
    ppermute x1, starting transfers between devices, shards(): arrived = lax.ppermute(away, 'c', shift(NC, 1))  4.17 us
    pallas_call x1, Pallas kernels, shards(): call(query_part_kernel, [pltpu.VMEM((2 * NX, ROWS, BLOCK), BF16)] + pair_...  3.78 us
    ppermute x3, starting transfers between devices, shards(): lax.ppermute(group, 'y', shift(NY, k))  3.77 us
    pallas_call x1, Pallas kernels, shards(): call(fetch_kernel, [pltpu.VMEM((HEAD // 2, BLOCK), F32)] * 2 + [pltpu.VME...  3.68 us
  transfers between devices with their start and end apart: 21, of which 11 were waited for; matrix products, arithmetic and copies ran while one was open for 0% of the time, Pallas kernels for 15%

profile of v14, /device:TPU:1, one launch (start us, length us, event | category | flops | bytes accessed | tf_op | source)
XLA Modules:
  0.0 84.4 jit_solution(5099877374240396389)
XLA Ops:
  0.0 1.1 %stack.21 = (bf16[128,1280]{1,0:T(8,128)(2,1)S(1)}, bf16[128,256]{1,0:T(8,128)(2,1)S(1)}) custom-call(bf16[128,640]{1,0:T(8,128)(2,1)} %q_ref.1, bf16[128,640]{1,0:T(8,128)(2,1)} %g_ref.1, bf16[128,128]{1,0:T(8,128)(2,1)} %k_ref.1, bf16[128,128]{1,0:T(8,128)(2,1)} %v_ref.1), custom_call_target="tpu_custom_call" | custom-call | tf_op jit(solution)/shard_map/stack/pallas_call | solution.py:299
  1.1 2.5 %collective-permute-start = (bf16[128,256]{1,0:T(8,128)(2,1)S(1)}, bf16[128,256]{1,0:T(8,128)(2,1)S(1)}, u32[]{:S(2)}, u32[]{:S(2)}) collective-permute-start(bf16[128,256]{1,0:T(8,128)(2,1)S(1)} %get-tuple-element.31.k0), channel_id=1, source_target_pairs={{0,32},{32,64},{64,96},{96,128},{128,160},{160,192},{192,224},{224... | collective-permute-start | bytes 196616 | tf_op jit(solution)/shard_map/ppermute | solution.py:310
  3.6 2.7 %collective-permute-start.9 = (bf16[128,1280]{1,0:T(8,128)(2,1)S(1)}, bf16[128,1280]{1,0:T(8,128)(2,1)S(1)}, u32[]{:S(2)}, u32[]{:S(2)}) collective-permute-start(bf16[128,1280]{1,0:T(8,128)(2,1)S(1)} %get-tuple-element.30.rows_ref.g0), channel_id=1, source_target_pairs={{0,24},{8,0},{16,8},{24,16},{1,25},{9,1},{17,9},{25,17},{2,26},{10... | collective-permute-start | bytes 983048 | tf_op jit(solution)/shard_map/ppermute | solution.py:307
  7.4 4.0 %collective-permute-start.4 = (bf16[128,256]{1,0:T(8,128)(2,1)S(1)}, bf16[128,256]{1,0:T(8,128)(2,1)S(1)}, u32[]{:S(2)}, u32[]{:S(2)}) collective-permute-start(bf16[128,256]{1,0:T(8,128)(2,1)S(1)} %get-tuple-element.31.k0), channel_id=1, source_target_pairs={{0,224},{32,0},{64,32},{96,64},{128,96},{160,128},{192,160},{224,1... | collective-permute-start | bytes 196616 | tf_op jit(solution)/shard_map/ppermute | solution.py:311
  11.4 1.3 %collective-permute-done.4.k7 = bf16[128,256]{1,0:T(8,128)(2,1)S(1)} collective-permute-done((bf16[128,256]{1,0:T(8,128)(2,1)S(1)}, bf16[128,256]{1,0:T(8,128)(2,1)S(1)}, u32[]{:S(2)}, u32[]{:S(2)}) %collective-permute-start.4) | collective-permute-done | bytes 65568 | tf_op jit(solution)/shard_map/ppermute | solution.py:311
  12.8 3.0 %collective-permute-start.5 = (bf16[128,256]{1,0:T(8,128)(2,1)S(1)}, bf16[128,256]{1,0:T(8,128)(2,1)S(1)}, u32[]{:S(2)}, u32[]{:S(2)}) collective-permute-start(bf16[128,256]{1,0:T(8,128)(2,1)S(1)} %collective-permute-done.4.k7), channel_id=1, source_target_pairs={{0,224},{32,0},{64,32},{96,64},{128,96},{160,128},{192,160},{224,1... | collective-permute-start | bytes 196616 | tf_op jit(solution)/shard_map/ppermute | solution.py:311
  17.1 3.3 %collective-permute-start.6 = (bf16[128,256]{1,0:T(8,128)(2,1)S(1)}, bf16[128,256]{1,0:T(8,128)(2,1)S(1)}, u32[]{:S(2)}, u32[]{:S(2)}) collective-permute-start(bf16[128,256]{1,0:T(8,128)(2,1)S(1)} %collective-permute-done.5.k6), channel_id=1, source_target_pairs={{0,224},{32,0},{64,32},{96,64},{128,96},{160,128},{192,160},{224,1... | collective-permute-start | bytes 196616 | tf_op jit(solution)/shard_map/ppermute | solution.py:311
  21.4 1.8 %plan.1.item_ref = s32[20,4]{1,0:T(8,128)S(1)} custom-call(s32[4]{0:T(128)S(1)} %pad_add_fusion.place_ref, s32[17,32]{1,0:T(8,128)S(1)} %bitcast.15, bf16[128,1280]{1,0:T(8,128)(2,1)S(1)} %get-tuple-element.30.rows_ref.g0), custom_call_target="tpu_custom_call" | custom-call | flops 1000000000 | tf_op jit(solution)/shard_map/plan/pallas_call | solution.py:314
  23.2 1.8 %collective-permute-done.3.k4 = bf16[128,256]{1,0:T(8,128)(2,1)S(1)} collective-permute-done((bf16[128,256]{1,0:T(8,128)(2,1)S(1)}, bf16[128,256]{1,0:T(8,128)(2,1)S(1)}, u32[]{:S(2)}, u32[]{:S(2)}) %collective-permute-start.3) | collective-permute-done | bytes 65568 | tf_op jit(solution)/shard_map/ppermute | solution.py:312
  25.0 2.5 %stats.1 = (f32[4,4,640]{2,1,0:T(4,128)S(1)}, f32[16,256,640]{2,1,0:T(8,128)S(1)}, f32[16,256,640]{2,1,0:T(8,128)S(1)}) custom-call(s32[20,4]{1,0:T(8,128)S(1)} %plan.1.item_ref, bf16[128,256]{1,0:T(8,128)(2,1)S(1)} %get-tuple-element.31.k0, bf16[128,256]{1,0:T(8,128)(2,1)S(1)} %collective-permute-done.k1, bf16[128,256]{1,0:T(8,128)(2,1)S(1)} %collective-permute-done.1.k2, ...), custom_call_target="tpu_custom_call" | custom-call | flops 1342177280 | tf_op jit(solution)/shard_map/stats/pallas_call | solution.py:325
  28.5 1.1 %collective-permute-start.11 = (f32[4,4,640]{2,1,0:T(4,128)S(1)}, f32[4,4,640]{2,1,0:T(4,128)S(1)}, u32[]{:S(2)}, u32[]{:S(2)}) collective-permute-start(f32[4,4,640]{2,1,0:T(4,128)S(1)} %get-tuple-element.32.stat_ref.s0), channel_id=1, source_target_pairs={{0,16},{8,24},{16,0},{24,8},{1,17},{9,25},{17,1},{25,9},{2,18},{10... | collective-permute-start | bytes 122888 | tf_op jit(solution)/shard_map/ppermute | solution.py:334
  29.5 1.4 %collective-permute-start.10 = (f32[4,4,640]{2,1,0:T(4,128)S(1)}, f32[4,4,640]{2,1,0:T(4,128)S(1)}, u32[]{:S(2)}, u32[]{:S(2)}) collective-permute-start(f32[4,4,640]{2,1,0:T(4,128)S(1)} %get-tuple-element.32.stat_ref.s0), channel_id=1, source_target_pairs={{0,24},{8,0},{16,8},{24,16},{1,25},{9,1},{17,9},{25,17},{2,26},{10... | collective-permute-start | bytes 122888 | tf_op jit(solution)/shard_map/ppermute | solution.py:334
  32.8 3.2 %grads.1 = (bf16[8,128,256]{2,1,0:T(8,128)(2,1)S(1)}, bf16[128,640]{1,0:T(8,128)(2,1)S(1)}, bf16[128,640]{1,0:T(8,128)(2,1)S(1)}, bf16[128,640]{1,0:T(8,128)(2,1)S(1)}, bf16[128,640]{1,0:T(8,128)(2,1)S(1)}) custom-call(s32[20,4]{1,0:T(8,128)S(1)} %plan.1.item_ref, bf16[8,128,128]{2,1,0:T(8,128)(2,1)S(1)} %turn.1.cols_ref, ...), custom_call_target="tpu_custom_call" | custom-call | flops 2013265920 | tf_op jit(solution)/shard_map/grads/pallas_call | solution.py:338
  36.9 13.3 %all-to-all-start = ((bf16[8,128,256]{2,1,0:T(8,128)(2,1)}), bf16[8,128,256]{2,1,0:T(8,128)(2,1)S(1)}, u32[]{:S(2)}, u32[]{:S(2)}) async-start(bf16[8,128,256]{2,1,0:T(8,128)(2,1)} %flush.1), calls=%async_computation | async-start | bytes 1048576 | tf_op jit(solution)/shard_map/all_to_all | solution.py:351
  51.4 1.6 %collective-permute-start.15 = (bf16[128,640]{1,0:T(8,128)(2,1)S(1)}, bf16[128,640]{1,0:T(8,128)(2,1)S(1)}, u32[]{:S(2)}, u32[]{:S(2)}) collective-permute-start(bf16[128,640]{1,0:T(8,128)(2,1)S(1)} %get-tuple-element.41), channel_id=1, source_target_pairs={{0,24},{8,0},{16,8},{24,16},{1,25},{9,1},{17,9},{25,17},{2,26},{10... | collective-permute-start | bytes 491528 | tf_op jit(solution)/shard_map/ppermute | solution.py:347
  52.9 3.7 %fetch.1 = (f32[64,128]{1,0:T(8,128)S(1)}, f32[64,128]{1,0:T(8,128)S(1)}, bf16[640,640]{1,0:T(8,128)(2,1)S(1)}, bf16[640,640]{1,0:T(8,128)(2,1)S(1)}, bf16[640,6...) custom-call(s32[4]{0:T(128)S(1)} %pad_add_fusion.place_ref, ...), custom_call_target="tpu_custom_call" | custom-call | tf_op jit(solution)/shard_map/fetch/pallas_call | solution.py:354
  58.2 3.8 %query_part.1 = (bf16[8,640,128]{2,1,0:T(8,128)(2,1)S(1)}, bf16[4,640,128]{2,1,0:T(8,128)(2,1)S(1)}, bf16[4,640,128]{2,1,0:T(8,128)(2,1)S(1)}) custom-call(s32[4]{0:T(128)S(1)} %pad_add_fusion.place_ref, f32[64,128]{1,0:T(8,128)S(1)} %get-tuple-element.36.cos_ref, f32[64,128]{1,0:T(8,128)S(1)} %get-tuple-element.37.sin_ref, ...), custom_call_target="tpu_custom_call" | custom-call | flops 838860800 | tf_op jit(solution)/shard_map/query_part/pallas_call | solution.py:363
  62.0 2.5 %all-to-all-done.dkv_ref = bf16[8,128,256]{2,1,0:T(8,128)(2,1)S(1)} async-done(((bf16[8,128,256]{2,1,0:T(8,128)(2,1)}), bf16[8,128,256]{2,1,0:T(8,128)(2,1)S(1)}, u32[]{:S(2)}, u32[]{:S(2)}) %all-to-all-start) | async-done | bytes 524320 | tf_op jit(solution)/shard_map/all_to_all | solution.py:351
  65.2 4.2 %collective-permute-start.16 = (bf16[4,128,640]{2,1,0:T(8,128)(2,1)S(1)}, bf16[4,128,640]{2,1,0:T(8,128)(2,1)S(1)}, u32[]{:S(2)}, u32[]{:S(2)}) collective-permute-start(bf16[4,128,640]{2,1,0:T(8,128)(2,1)S(1)} %get-tuple-element.54), channel_id=1, source_target_pairs={{0,1},{1,0},{2,3},{3,2},{4,5},{5,4},{6,7},{7,6},{8,9},{9,8},{10,11... | collective-permute-start | bytes 1966088 | tf_op jit(solution)/shard_map/ppermute | solution.py:379
  69.3 2.8 %second_half.1 = f32[4,128,640]{2,1,0:T(8,128)S(1)} custom-call(s32[4]{0:T(128)S(1)} %pad_add_fusion.place_ref, bf16[256,128]{1,0:T(8,128)(2,1)S(1)} %get-tuple-element.53.low_ref, bf16[8,640,128]{2,1,0:T(8,128)(2,1)S(1)} %get-tuple-element.50.part_ref, bf16[5120,128]{1,0:T(8,128)(2,1)} %wk_hbm.3, bf16[5120,128]{1,0:T(8,128)(2,1)} %wv_hbm.3), custom_call_target="tpu_custom_call" | custom-call | tf_op jit(solution)/shard_map/second_half/pallas_call | solution.py:380
  72.3 2.8 %collective-permute-start.19 = (bf16[128,640]{1,0:T(8,128)(2,1)S(1)}, bf16[128,640]{1,0:T(8,128)(2,1)S(1)}, u32[]{:S(2)}, u32[]{:S(2)}) collective-permute-start(bf16[128,640]{1,0:T(8,128)(2,1)S(1)} %get-tuple-element.55), channel_id=1, source_target_pairs={{0,4},{2,6},{4,0},{6,2},{1,5},{3,7},{5,1},{7,3},{8,12},{10,14},{12... | collective-permute-start | bytes 491528 | tf_op jit(solution)/shard_map/ppermute | solution.py:389
  75.5 2.4 %collective-permute-start.17 = (bf16[128,640]{1,0:T(8,128)(2,1)S(1)}, bf16[128,640]{1,0:T(8,128)(2,1)S(1)}, u32[]{:S(2)}, u32[]{:S(2)}) collective-permute-start(bf16[128,640]{1,0:T(8,128)(2,1)S(1)} %get-tuple-element.57), channel_id=1, source_target_pairs={{0,6},{2,0},{4,2},{6,4},{1,7},{3,1},{5,3},{7,5},{8,14},{10,8},{12,... | collective-permute-start | bytes 491528 | tf_op jit(solution)/shard_map/ppermute | solution.py:389
  77.8 1.9 %collective-permute-done.19.p1 = bf16[128,640]{1,0:T(8,128)(2,1)S(1)} collective-permute-done((bf16[128,640]{1,0:T(8,128)(2,1)S(1)}, bf16[128,640]{1,0:T(8,128)(2,1)S(1)}, u32[]{:S(2)}, u32[]{:S(2)}) %collective-permute-start.19) | collective-permute-done | bytes 163872 | tf_op jit(solution)/shard_map/ppermute | solution.py:389
  79.7 3.8 %collective-permute-done.18.p0 = bf16[128,640]{1,0:T(8,128)(2,1)S(1)} collective-permute-done((bf16[128,640]{1,0:T(8,128)(2,1)S(1)}, bf16[128,640]{1,0:T(8,128)(2,1)S(1)}, u32[]{:S(2)}, u32[]{:S(2)}) %collective-permute-start.18) | collective-permute-done | bytes 163872 | tf_op jit(solution)/shard_map/ppermute | solution.py:389
  (36 shorter events, 11.8 us)
Async XLA Ops:
  1.1 10.4 %collective-permute-start = (bf16[128,256]{1,0:T(8,128)(2,1)S(1)}, bf16[128,256]{1,0:T(8,128)(2,1)S(1)}, u32[]{:S(2)}, u32[]{:S(2)}) collective-permute-start(bf16[128,256]{1,0:T(8,128)(2,1)S(1)} %get-tuple-element.31.k0), channel_id=1, source_target_pairs={{0,32},{32,64},{64,96},{96,128},{128,160},{160,192},{192,224},{224... | collective-permute-start | bytes 196616 | tf_op jit(solution)/shard_map/ppermute | solution.py:310
  3.6 21.4 %collective-permute-start.9 = (bf16[128,1280]{1,0:T(8,128)(2,1)S(1)}, bf16[128,1280]{1,0:T(8,128)(2,1)S(1)}, u32[]{:S(2)}, u32[]{:S(2)}) collective-permute-start(bf16[128,1280]{1,0:T(8,128)(2,1)S(1)} %get-tuple-element.30.rows_ref.g0), channel_id=1, source_target_pairs={{0,24},{8,0},{16,8},{24,16},{1,25},{9,1},{17,9},{25,17},{2,26},{10... | collective-permute-start | bytes 983048 | tf_op jit(solution)/shard_map/ppermute | solution.py:307
  6.4 18.7 %collective-permute-start.8 = (bf16[128,1280]{1,0:T(8,128)(2,1)S(1)}, bf16[128,1280]{1,0:T(8,128)(2,1)S(1)}, u32[]{:S(2)}, u32[]{:S(2)}) collective-permute-start(bf16[128,1280]{1,0:T(8,128)(2,1)S(1)} %get-tuple-element.30.rows_ref.g0), channel_id=1, source_target_pairs={{0,16},{8,24},{16,0},{24,8},{1,17},{9,25},{17,1},{25,9},{2,18},{10... | collective-permute-start | bytes 983048 | tf_op jit(solution)/shard_map/ppermute | solution.py:307
  6.7 18.3 %collective-permute-start.7 = (bf16[128,1280]{1,0:T(8,128)(2,1)S(1)}, bf16[128,1280]{1,0:T(8,128)(2,1)S(1)}, u32[]{:S(2)}, u32[]{:S(2)}) collective-permute-start(bf16[128,1280]{1,0:T(8,128)(2,1)S(1)} %get-tuple-element.30.rows_ref.g0), channel_id=1, source_target_pairs={{0,8},{8,16},{16,24},{24,0},{1,9},{9,17},{17,25},{25,1},{2,10},{10... | collective-permute-start | bytes 983048 | tf_op jit(solution)/shard_map/ppermute | solution.py:307
  7.4 5.4 %collective-permute-start.4 = (bf16[128,256]{1,0:T(8,128)(2,1)S(1)}, bf16[128,256]{1,0:T(8,128)(2,1)S(1)}, u32[]{:S(2)}, u32[]{:S(2)}) collective-permute-start(bf16[128,256]{1,0:T(8,128)(2,1)S(1)} %get-tuple-element.31.k0), channel_id=1, source_target_pairs={{0,224},{32,0},{64,32},{96,64},{128,96},{160,128},{192,160},{224,1... | collective-permute-start | bytes 196616 | tf_op jit(solution)/shard_map/ppermute | solution.py:311
  11.4 4.6 %collective-permute-start.1 = (bf16[128,256]{1,0:T(8,128)(2,1)S(1)}, bf16[128,256]{1,0:T(8,128)(2,1)S(1)}, u32[]{:S(2)}, u32[]{:S(2)}) collective-permute-start(bf16[128,256]{1,0:T(8,128)(2,1)S(1)} %collective-permute-done.k1), channel_id=1, source_target_pairs={{0,32},{32,64},{64,96},{96,128},{128,160},{160,192},{192,224},{224... | collective-permute-start | bytes 196616 | tf_op jit(solution)/shard_map/ppermute | solution.py:310
  12.8 4.3 %collective-permute-start.5 = (bf16[128,256]{1,0:T(8,128)(2,1)S(1)}, bf16[128,256]{1,0:T(8,128)(2,1)S(1)}, u32[]{:S(2)}, u32[]{:S(2)}) collective-permute-start(bf16[128,256]{1,0:T(8,128)(2,1)S(1)} %collective-permute-done.4.k7), channel_id=1, source_target_pairs={{0,224},{32,0},{64,32},{96,64},{128,96},{160,128},{192,160},{224,1... | collective-permute-start | bytes 196616 | tf_op jit(solution)/shard_map/ppermute | solution.py:311
  16.1 4.6 %collective-permute-start.2 = (bf16[128,256]{1,0:T(8,128)(2,1)S(1)}, bf16[128,256]{1,0:T(8,128)(2,1)S(1)}, u32[]{:S(2)}, u32[]{:S(2)}) collective-permute-start(bf16[128,256]{1,0:T(8,128)(2,1)S(1)} %collective-permute-done.1.k2), channel_id=1, source_target_pairs={{0,32},{32,64},{64,96},{96,128},{128,160},{160,192},{192,224},{224... | collective-permute-start | bytes 196616 | tf_op jit(solution)/shard_map/ppermute | solution.py:310
  17.1 6.1 %collective-permute-start.6 = (bf16[128,256]{1,0:T(8,128)(2,1)S(1)}, bf16[128,256]{1,0:T(8,128)(2,1)S(1)}, u32[]{:S(2)}, u32[]{:S(2)}) collective-permute-start(bf16[128,256]{1,0:T(8,128)(2,1)S(1)} %collective-permute-done.5.k6), channel_id=1, source_target_pairs={{0,224},{32,0},{64,32},{96,64},{128,96},{160,128},{192,160},{224,1... | collective-permute-start | bytes 196616 | tf_op jit(solution)/shard_map/ppermute | solution.py:311
  20.7 4.3 %collective-permute-start.3 = (bf16[128,256]{1,0:T(8,128)(2,1)S(1)}, bf16[128,256]{1,0:T(8,128)(2,1)S(1)}, u32[]{:S(2)}, u32[]{:S(2)}) collective-permute-start(bf16[128,256]{1,0:T(8,128)(2,1)S(1)} %collective-permute-done.2.k3), channel_id=1, source_target_pairs={{0,32},{32,64},{64,96},{96,128},{128,160},{160,192},{192,224},{224... | collective-permute-start | bytes 196616 | tf_op jit(solution)/shard_map/ppermute | solution.py:312
  20.7 0.7 copy-start
  27.5 4.3 %collective-permute-start.12 = (f32[4,4,640]{2,1,0:T(4,128)S(1)}, f32[4,4,640]{2,1,0:T(4,128)S(1)}, u32[]{:S(2)}, u32[]{:S(2)}) collective-permute-start(f32[4,4,640]{2,1,0:T(4,128)S(1)} %get-tuple-element.32.stat_ref.s0), channel_id=1, source_target_pairs={{0,8},{8,16},{16,24},{24,0},{1,9},{9,17},{17,25},{25,1},{2,10},{10... | collective-permute-start | bytes 122888 | tf_op jit(solution)/shard_map/ppermute | solution.py:334
  28.5 4.4 %collective-permute-start.11 = (f32[4,4,640]{2,1,0:T(4,128)S(1)}, f32[4,4,640]{2,1,0:T(4,128)S(1)}, u32[]{:S(2)}, u32[]{:S(2)}) collective-permute-start(f32[4,4,640]{2,1,0:T(4,128)S(1)} %get-tuple-element.32.stat_ref.s0), channel_id=1, source_target_pairs={{0,16},{8,24},{16,0},{24,8},{1,17},{9,25},{17,1},{25,9},{2,18},{10... | collective-permute-start | bytes 122888 | tf_op jit(solution)/shard_map/ppermute | solution.py:334
  29.5 3.3 %collective-permute-start.10 = (f32[4,4,640]{2,1,0:T(4,128)S(1)}, f32[4,4,640]{2,1,0:T(4,128)S(1)}, u32[]{:S(2)}, u32[]{:S(2)}) collective-permute-start(f32[4,4,640]{2,1,0:T(4,128)S(1)} %get-tuple-element.32.stat_ref.s0), channel_id=1, source_target_pairs={{0,24},{8,0},{16,8},{24,16},{1,25},{9,1},{17,9},{25,17},{2,26},{10... | collective-permute-start | bytes 122888 | tf_op jit(solution)/shard_map/ppermute | solution.py:334
  36.0 16.9 %copy-start.1 = (s32[32,17]{0,1:T(8,128)S(1)}, s32[32,17]{0,1:T(8,128)}, u32[]{:S(2)}) copy-start(s32[32,17]{0,1:T(8,128)} %param.12) | copy-start | bytes 6532
  36.9 27.7 %all-to-all-start = ((bf16[8,128,256]{2,1,0:T(8,128)(2,1)}), bf16[8,128,256]{2,1,0:T(8,128)(2,1)S(1)}, u32[]{:S(2)}, u32[]{:S(2)}) async-start(bf16[8,128,256]{2,1,0:T(8,128)(2,1)} %flush.1), calls=%async_computation | async-start | bytes 1048576 | tf_op jit(solution)/shard_map/all_to_all | solution.py:351
  50.2 7.1 %collective-permute-start.13 = (bf16[128,640]{1,0:T(8,128)(2,1)S(1)}, bf16[128,640]{1,0:T(8,128)(2,1)S(1)}, u32[]{:S(2)}, u32[]{:S(2)}) collective-permute-start(bf16[128,640]{1,0:T(8,128)(2,1)S(1)} %get-tuple-element.39), channel_id=1, source_target_pairs={{0,8},{8,16},{16,24},{24,0},{1,9},{9,17},{17,25},{25,1},{2,10},{10... | collective-permute-start | bytes 491528 | tf_op jit(solution)/shard_map/ppermute | solution.py:347
  50.4 6.8 %collective-permute-start.14 = (bf16[128,640]{1,0:T(8,128)(2,1)S(1)}, bf16[128,640]{1,0:T(8,128)(2,1)S(1)}, u32[]{:S(2)}, u32[]{:S(2)}) collective-permute-start(bf16[128,640]{1,0:T(8,128)(2,1)S(1)} %get-tuple-element.40), channel_id=1, source_target_pairs={{0,16},{8,24},{16,0},{24,8},{1,17},{9,25},{17,1},{25,9},{2,18},{10... | collective-permute-start | bytes 491528 | tf_op jit(solution)/shard_map/ppermute | solution.py:347
  51.4 6.8 %collective-permute-start.15 = (bf16[128,640]{1,0:T(8,128)(2,1)S(1)}, bf16[128,640]{1,0:T(8,128)(2,1)S(1)}, u32[]{:S(2)}, u32[]{:S(2)}) collective-permute-start(bf16[128,640]{1,0:T(8,128)(2,1)S(1)} %get-tuple-element.41), channel_id=1, source_target_pairs={{0,24},{8,0},{16,8},{24,16},{1,25},{9,1},{17,9},{25,17},{2,26},{10... | collective-permute-start | bytes 491528 | tf_op jit(solution)/shard_map/ppermute | solution.py:347
  65.2 7.0 %collective-permute-start.16 = (bf16[4,128,640]{2,1,0:T(8,128)(2,1)S(1)}, bf16[4,128,640]{2,1,0:T(8,128)(2,1)S(1)}, u32[]{:S(2)}, u32[]{:S(2)}) collective-permute-start(bf16[4,128,640]{2,1,0:T(8,128)(2,1)S(1)} %get-tuple-element.54), channel_id=1, source_target_pairs={{0,1},{1,0},{2,3},{3,2},{4,5},{5,4},{6,7},{7,6},{8,9},{9,8},{10,11... | collective-permute-start | bytes 1966088 | tf_op jit(solution)/shard_map/ppermute | solution.py:379
  72.3 7.4 %collective-permute-start.19 = (bf16[128,640]{1,0:T(8,128)(2,1)S(1)}, bf16[128,640]{1,0:T(8,128)(2,1)S(1)}, u32[]{:S(2)}, u32[]{:S(2)}) collective-permute-start(bf16[128,640]{1,0:T(8,128)(2,1)S(1)} %get-tuple-element.55), channel_id=1, source_target_pairs={{0,4},{2,6},{4,0},{6,2},{1,5},{3,7},{5,1},{7,3},{8,12},{10,14},{12... | collective-permute-start | bytes 491528 | tf_op jit(solution)/shard_map/ppermute | solution.py:389
  75.1 8.4 %collective-permute-start.18 = (bf16[128,640]{1,0:T(8,128)(2,1)S(1)}, bf16[128,640]{1,0:T(8,128)(2,1)S(1)}, u32[]{:S(2)}, u32[]{:S(2)}) collective-permute-start(bf16[128,640]{1,0:T(8,128)(2,1)S(1)} %get-tuple-element.56), channel_id=1, source_target_pairs={{0,2},{2,4},{4,6},{6,0},{1,3},{3,5},{5,7},{7,1},{8,10},{10,12},{12... | collective-permute-start | bytes 491528 | tf_op jit(solution)/shard_map/ppermute | solution.py:389
  75.5 8.1 %collective-permute-start.17 = (bf16[128,640]{1,0:T(8,128)(2,1)S(1)}, bf16[128,640]{1,0:T(8,128)(2,1)S(1)}, u32[]{:S(2)}, u32[]{:S(2)}) collective-permute-start(bf16[128,640]{1,0:T(8,128)(2,1)S(1)} %get-tuple-element.57), channel_id=1, source_target_pairs={{0,6},{2,0},{4,2},{6,4},{1,7},{3,1},{5,3},{7,5},{8,14},{10,8},{12,... | collective-permute-start | bytes 491528 | tf_op jit(solution)/shard_map/ppermute | solution.py:389
